TPU v7x, 256 devices: a whole 4x4x8 slice. The times are simulated.
256 devices in a mesh: depth: 64 (over x, y, z_hi), comp: 4 (over z_lo, core).
Axes of the slice: x: 4, y: 4, z: 8 (z_hi: 4, z_lo: 2; z = z_hi * 2 + z_lo), core: 2. Of those that a mesh axis runs over, the one named last changes fastest.
Arguments:
- density: float32 [64, 512, 256], P('depth', 'comp'), may hold values from -4 to 4
- observed: float32 [4, 512, 256], P('comp', 'depth'), may hold values from -6 to 6
- data_weight: float32 [4, 512, 256], P('comp', 'depth'), may hold values from 0.3 to 7.5
- layer_top: float32 [64], P('depth'), may hold values from 0.5 to 8
Outputs:
- density_new: float32 [64, 512, 256], P('depth', 'comp')
- weighted_error: float32 [4, 512, 256], P('comp', 'depth')
All inputs are finite; a program needn't handle non-finite values.
Results may differ from a plain program's by a relative error of at most 0.0001.
Values sent between devices are 32-bit elements; how exact they have to be, the bound alone decides.
No kernel may reach another device: no remote copies, remote signals or barrier semaphores. Data moves between devices by JAX's collectives and lax.ppermute only.
A program may use at most 64 MiB of HBM per device.

v0:
```python
import math

import jax
import jax.numpy as jnp
from jax import lax
from jax.sharding import PartitionSpec as P

ITERS = 2


TWO_PI = 2.0 * math.pi


def matmul(left, right):
    return jnp.dot(left, right, precision=lax.Precision.HIGHEST, preferred_element_type=jnp.float32)


def tables(count):
    index = lax.iota(jnp.int32, count)
    product = index[:, None] * index[None, :] % count
    angle = product.astype(jnp.float32) * (TWO_PI / count)
    return (jnp.cos(angle), jnp.sin(angle))


def wavenumbers(count):
    index = lax.iota(jnp.int32, count)
    signed = jnp.where(index < (count - 1) // 2 + 1, index, index - count)
    return signed.astype(jnp.float32) * (TWO_PI / count)


def kernel_parts(top, comp_index, rows_all, cols_all):
    kx = wavenumbers(rows_all)[:, None]
    ky = wavenumbers(cols_all)[None, :]
    kabs = jnp.sqrt(kx * kx + ky * ky)
    floor_k = jnp.maximum(kabs, TWO_PI / max(rows_all, cols_all))
    decay = 4.0 * jnp.exp(-kabs * top) * (1.0 - jnp.exp(-kabs))
    zeros = jnp.zeros_like(kabs)
    real_part = jnp.where(
        comp_index == 0,
        decay,
        jnp.where(comp_index == 3, decay * (-(kx * kx) / (floor_k * floor_k)), zeros),
    )
    imag_part = jnp.where(
        comp_index == 1,
        decay * (kx / floor_k),
        jnp.where(comp_index == 2, decay * (ky / floor_k), zeros),
    )
    return (real_part, imag_part)


def along_rows(field, cos_y, sin_y):
    return (matmul(field, cos_y), -matmul(field, sin_y))


def add_columns(part_re, part_im, cos_cols, sin_cols):
    new_re = matmul(cos_cols, part_re) + matmul(sin_cols, part_im)
    new_im = matmul(cos_cols, part_im) - matmul(sin_cols, part_re)
    return (new_re, new_im)


def inverse_rows(spec_re, spec_im, cos_rows, sin_rows, cos_y, sin_y, scale):
    mixed_re = matmul(cos_rows, spec_re) - matmul(sin_rows, spec_im)
    mixed_im = matmul(cos_rows, spec_im) + matmul(sin_rows, spec_re)
    return (matmul(mixed_re, cos_y) - matmul(mixed_im, sin_y)) * scale


def body(density, observed, data_weight, layer_top):
    own_rows = density.shape[1]
    comps = lax.axis_size("comp")
    rows_all = own_rows * comps
    cols_all = density.shape[2]
    comp_index = lax.axis_index("comp")
    cos_x, sin_x = tables(rows_all)
    cos_y, sin_y = tables(cols_all)
    scale = 1.0 / (rows_all * cols_all)
    kernels = [kernel_parts(layer_top[0], comp_index, rows_all, cols_all)]
    weight = data_weight[0]
    measured = observed[0]

    def spectrum(field):
        part_re, part_im = along_rows(field, cos_y, sin_y)
        return add_columns(part_re, part_im, cos_x, sin_x)

    def forward_once(fields):
        spec_re, spec_im = spectrum(fields[0])
        kre, kim = kernels[0]
        total_re = kre * spec_re - kim * spec_im
        total_im = kre * spec_im + kim * spec_re
        return lax.psum_scatter(
            inverse_rows(total_re, total_im, cos_x, sin_x, cos_y, sin_y, scale),
            "depth",
            scatter_dimension=0,
            tiled=True,
        )

    def forward(fields):
        return forward_once(fields)

    dens_full = lax.all_gather(density, "comp", axis=1, tiled=True)
    dens_strip = density
    predicted = forward([dens_full[0]])
    weighted_error = weight * (predicted - measured)
    for step in range(ITERS):
        weighted_res = weight * weighted_error
        add_part_re, add_part_im = along_rows(
            lax.all_gather(weighted_res, "depth", axis=0, tiled=True), cos_y, sin_y
        )
        res_re, res_im = add_columns(add_part_re, add_part_im, cos_x, sin_x)
        kre, kim = kernels[0]
        grad_re = kre * res_re + kim * res_im
        grad_im = kre * res_im - kim * res_re
        terms = [inverse_rows(grad_re, grad_im, cos_x, sin_x, cos_y, sin_y, scale)]
        data_grad = jnp.stack(terms)
        quad_strip = 1.0 / (dens_strip * dens_strip + 0.25)
        grad_strip = lax.psum_scatter(data_grad, "comp", scatter_dimension=1, tiled=True) + 0.5 * (
            quad_strip * dens_strip
        )
        grad_full = lax.all_gather(grad_strip, "comp", axis=1, tiled=True)
        grad_sq = jnp.sum(grad_strip * grad_strip)
        quad_sq = jnp.sum(quad_strip * grad_strip * grad_strip)
        grad_sq, quad_sq = lax.psum((grad_sq, quad_sq), ("depth", "comp"))
        image = forward([grad_full[0]])
        weighted_image = weight * image
        curv = jnp.sum(weighted_image * weighted_image)
        curv = lax.psum(curv, ("depth", "comp"))
        alpha = grad_sq / (curv + 0.5 * quad_sq)
        dens_strip = dens_strip - alpha * grad_strip
        predicted = predicted - alpha * image
        weighted_error = weight * (predicted - measured)
    return (dens_strip, weighted_error[None])


def solution(mesh):
    return jax.shard_map(
        body,
        mesh=mesh,
        in_specs=(
            P("depth", "comp", None),
            P("comp", "depth", None),
            P("comp", "depth", None),
            P("depth"),
        ),
        out_specs=(P("depth", "comp", None), P("comp", "depth", None)),
        check_vma=False,
    )
```

profile of v0, /device:TPU:1, one launch (start us, length us, event | category | flops | bytes accessed | tf_op | source)
XLA Modules:
  0.0 2017.7 jit_solution(2522826895115508715)
XLA Ops:
  7.3 9.8 all_gather.15
  52.4 5.7 convolution_subtract_fusion.8
  59.6 5.9 convolution_add_fusion.8
  68.0 334.6 %reduce-scatter.6.cloned.1.call-done = f32[8,256]{1,0:T(8,128)} async-done(((f32[512,256]{1,0:T(8,128)}), f32[8,256]{1,0:T(8,128)}) %reduce-scatter.6.cloned.1.call-update) | async-done | bytes 8208 | tf_op jit(solution)/shard_map/reduce_scatter | solution.py:89
  403.3 161.1 %all_gather.16 = f32[512,256]{1,0:T(8,128)S(1)} all-gather(f32[8,256]{1,0:T(8,128)S(1)} %multiply_multiply_fusion.3), channel_id=1, replica_groups=mesh['depth'=64,'comp'=4] {'depth'}, dimensions={0}, use_global_device_ids=true | all-gather | bytes 532480 | tf_op jit(solution)/shard_map/all_gather | solution.py:106
  567.6 5.6 fusion.55
  578.8 5.6 convolution_add_fusion.7
  584.5 5.8 convolution_subtract_fusion.7
  601.2 5.7 convolution_subtract_fusion.6
  608.5 5.9 convolution_add_fusion.6
  616.9 93.4 %reduce-scatter.8.cloned.1.call-done = f32[1,128,256]{2,1,0:T(8,128)} async-done(((f32[1,512,256]{2,1,0:T(8,128)}), f32[1,128,256]{2,1,0:T(8,128)}) %reduce-scatter.8.cloned.1.call-update) | async-done | bytes 131088 | tf_op jit(solution)/shard_map/reduce_scatter | solution.py:115
  711.9 7.3 all_gather.17
  727.9 5.6 fusion.45
  733.5 5.6 convolution_add_fusion.5
  739.1 5.8 convolution_subtract_fusion.5
  755.9 5.7 convolution_subtract_fusion.4
  763.2 5.9 convolution_add_fusion.4
  771.5 333.5 %reduce-scatter.10.cloned.1.call-done = f32[8,256]{1,0:T(8,128)} async-done(((f32[512,256]{1,0:T(8,128)}), f32[8,256]{1,0:T(8,128)}) %reduce-scatter.10.cloned.1.call-update) | async-done | bytes 8208 | tf_op jit(solution)/shard_map/reduce_scatter | solution.py:89
  1106.4 123.9 %all-reduce.1 = (f32[]{:T(128)}, f32[]{:T(128)}, f32[]{:T(128)}) all-reduce(f32[]{:T(128)} %get-tuple-element.5, f32[]{:T(128)} %fusion.127, f32[]{:T(128)} %get-tuple-element.4), channel_id=1, replica_groups=mesh['depth'=64,'comp'=4] {'depth','comp'}, use_global_device_ids=true, to_apply=%region_3.4 | all-reduce | flops 3 | bytes 24 | tf_op jit(solution)/shard_map/psum | solution.py:121
  1232.1 161.9 %all_gather.18 = f32[512,256]{1,0:T(8,128)S(1)} all-gather(f32[8,256]{1,0:T(8,128)S(1)} %multiply_multiply_fusion.2), channel_id=1, replica_groups=mesh['depth'=64,'comp'=4] {'depth'}, dimensions={0}, use_global_device_ids=true | all-gather | bytes 532480 | tf_op jit(solution)/shard_map/all_gather | solution.py:106
  1408.4 5.6 convolution_add_fusion.3
  1414.0 5.8 convolution_subtract_fusion.3
  1430.8 5.7 convolution_subtract_fusion.2
  1438.1 5.9 convolution_add_fusion.2
  1446.4 41.4 %reduce-scatter.12.cloned.1.call-done = f32[1,128,256]{2,1,0:T(8,128)} async-done(((f32[1,512,256]{2,1,0:T(8,128)}), f32[1,128,256]{2,1,0:T(8,128)}) %reduce-scatter.12.cloned.1.call-update) | async-done | bytes 131088 | tf_op jit(solution)/shard_map/reduce_scatter | solution.py:115
  1489.4 7.3 all_gather.19
  1511.0 5.6 convolution_add_fusion.1
  1516.6 5.8 convolution_subtract_fusion.1
  1533.4 5.7 convolution_subtract_fusion
  1540.7 5.8 convolution_add_fusion
  1548.8 333.5 %reduce-scatter.14.cloned.1.call-done = f32[8,256]{1,0:T(8,128)} async-done(((f32[512,256]{1,0:T(8,128)}), f32[8,256]{1,0:T(8,128)}) %reduce-scatter.14.cloned.1.call-update) | async-done | bytes 8208 | tf_op jit(solution)/shard_map/reduce_scatter | solution.py:89
  1883.6 123.9 %all-reduce = (f32[]{:T(128)}, f32[]{:T(128)}, f32[]{:T(128)}) all-reduce(f32[]{:T(128)} %get-tuple-element.3, f32[]{:T(128)} %fusion.125, f32[]{:T(128)} %get-tuple-element.2), channel_id=1, replica_groups=mesh['depth'=64,'comp'=4] {'depth','comp'}, use_global_device_ids=true, to_apply=%region_11.12 | all-reduce | flops 3 | bytes 24 | tf_op jit(solution)/shard_map/psum | solution.py:121
  (73 shorter events, 152.3 us)
Async XLA Ops:
  7.2 395.5 %reduce-scatter.6.cloned.1.call-start = ((), (), s32[]{:S(2)}) async-start(), calls=%async_computation.5 | async-start | bytes 532480 | tf_op jit(solution)/shard_map/reduce_scatter | solution.py:89
  67.9 334.7 %copy-start.1 = (f32[1,8,256]{2,1,0:T(8,128)S(1)}, f32[1,8,256]{2,1,0:T(8,128)}, u32[]{:S(2)}) copy-start(f32[1,8,256]{2,1,0:T(8,128)} %param.6) | copy-start | bytes 24580
  67.9 334.7 %copy-start.3 = (f32[1,8,256]{2,1,0:T(8,128)S(1)}, f32[1,8,256]{2,1,0:T(8,128)}, u32[]{:S(2)}) copy-start(f32[1,8,256]{2,1,0:T(8,128)} %param.5) | copy-start | bytes 24580
  68.0 642.3 %reduce-scatter.8.cloned.1.call-start = ((), (), s32[]{:S(2)}) async-start(), calls=%async_computation.6 | async-start | bytes 655360 | tf_op jit(solution)/shard_map/reduce_scatter | solution.py:115
  616.8 93.4 %copy-start = (f32[1,128,256]{2,1,0:T(8,128)S(1)}, f32[1,128,256]{2,1,0:T(8,128)}, u32[]{:S(2)}) copy-start(f32[1,128,256]{2,1,0:T(8,128)} %param.4) | copy-start | bytes 393220
  616.8 488.1 %reduce-scatter.10.cloned.1.call-start = ((), (), s32[]{:S(2)}) async-start(), calls=%async_computation.7 | async-start | bytes 532480 | tf_op jit(solution)/shard_map/reduce_scatter | solution.py:89
  771.5 716.3 %reduce-scatter.12.cloned.1.call-start = ((), (), s32[]{:S(2)}) async-start(), calls=%async_computation.8 | async-start | bytes 655360 | tf_op jit(solution)/shard_map/reduce_scatter | solution.py:115
  1106.3 125.8 %copy-start.4 = (f32[8,256]{1,0:T(8,128)S(1)}, f32[8,256]{1,0:T(8,128)}, u32[]{:S(2)}) copy-start(f32[8,256]{1,0:T(8,128)} %reduce-scatter.6.cloned.1.call-done) | copy-start | bytes 24580
  1106.4 125.8 %copy-start.2 = (f32[8,256]{1,0:T(8,128)S(1)}, f32[8,256]{1,0:T(8,128)}, u32[]{:S(2)}) copy-start(f32[8,256]{1,0:T(8,128)} %reduce-scatter.10.cloned.1.call-done) | copy-start | bytes 24580
  1446.4 436.0 %reduce-scatter.14.cloned.1.call-start = ((), (), s32[]{:S(2)}) async-start(), calls=%async_computation.9 | async-start | bytes 532480 | tf_op jit(solution)/shard_map/reduce_scatter | solution.py:89
  2009.4 0.7 copy-start.5
Sparse Core Ops, SparseCore 0:
  68.1 334.4 reduce-scatter.5
  616.9 93.2 reduce-scatter.7
  771.6 333.3 reduce-scatter.9
  1446.5 41.2 reduce-scatter.11
  1548.9 333.3 reduce-scatter.13
where the time goes:
time: 2030 us; the launch traced here: 2020 us
  waiting for transfers between devices  1140 us (56%)
  blocking collectives  595 us (29%)
  matrix products  259 us (13%)
    reduce_scatter x3, waiting for transfers between devices, forward_once(): lax.psum_scatter(inverse_rows(total_re, total_im, cos_x, sin_x, cos_y, si...  1000 us
    all_gather x2, blocking collectives, body(): lax.all_gather(weighted_res, 'depth', axis=0, tiled=True)  323 us
    dot_general x60, matrix products, matmul(): jnp.dot(left, right, precision=lax.Precision.HIGHEST, preferred_element_t...  259 us
    psum x2, blocking collectives, body(): grad_sq, quad_sq = lax.psum((grad_sq, quad_sq), ('depth', 'comp'))  248 us
    reduce_scatter x2, waiting for transfers between devices, body(): lax.psum_scatter(data_grad, 'comp', scatter_dimension=1, tiled=True)  135 us
  transfers between devices with their start and end apart: 5, of which 5 were waited for; matrix products, arithmetic and copies ran while one was open for 0% of the time, Pallas kernels for 0%

commit v1 on v0

v1 whole, which is shorter than its diff:
```python
import functools
import math

import jax
import jax.numpy as jnp
import numpy as np
from jax import lax
from jax.experimental import pallas as pl
from jax.experimental.pallas import tpu as pltpu
from jax.sharding import Mesh
from jax.sharding import PartitionSpec as P

TWO_PI = 2.0 * math.pi
F32 = jnp.float32
BF16 = jnp.bfloat16
XY = ("x", "y")
DEPTH = ("x", "y", "h")
COMP = ("l", "k")
ALL = ("x", "y", "h", "l", "k")

NX = 512
NY = 256
HX = NX // 2
QX = NX // 4
HY = NY // 2


def split_table(table):
    high = table.astype(jnp.bfloat16)
    low = (table - high.astype(np.float64)).astype(jnp.bfloat16)
    return np.stack([high, low])


def basis(count, waves):
    place = np.arange(count)
    rows = []
    for wave in waves:
        norm = math.sqrt((1.0 if wave == 0 else 2.0) / count)
        rows.append(norm * np.cos(TWO_PI * (wave * place % count) / count))
    for wave in waves:
        if wave == 0:
            rows.append(math.sqrt(1.0 / count) * (1.0 - 2.0 * (place % 2)))
        else:
            rows.append(math.sqrt(2.0 / count) * np.sin(TWO_PI * (wave * place % count) / count))
    return np.stack(rows)


def make_tables():
    even = basis(NX, range(0, HX, 2))[:, :HX]
    odd = basis(NX, range(1, HX, 2))[:, :HX]
    col = basis(NY, range(HY))
    return (
        np.concatenate([split_table(even), split_table(odd)]),
        np.concatenate([split_table(even.T), split_table(odd.T)]),
        np.concatenate([split_table(col.T), split_table(col)]),
    )


def split(value):
    high = value.astype(BF16)
    low = (value - high.astype(F32)).astype(BF16)
    return high, low


def dot(left, right):
    return jnp.dot(left, right, preferred_element_type=F32)


def times_table(value, high, low):
    vh, vl = split(value)
    return dot(vh, high) + (dot(vl, high) + dot(vh, low))


def table_times(high, low, value):
    vh, vl = split(value)
    return dot(high, vh) + (dot(high, vl) + dot(low, vh))


def to_waves(field, fx, ty):
    cols = times_table(field, ty[0], ty[1])
    upper, lower = cols[:HX], cols[HX:]
    return (
        table_times(fx[0], fx[1], upper + lower),
        table_times(fx[2], fx[3], upper - lower),
    )


def from_waves(even, odd, bx, ty):
    first = table_times(bx[0], bx[1], even)
    second = table_times(bx[2], bx[3], odd)
    rows = jnp.concatenate([first + second, first - second], axis=0)
    return times_table(rows, ty[2], ty[3])


def swap_x(half):
    return jnp.concatenate([half[HX // 2 :], half[: HX // 2]], axis=0)


def swap_y(half):
    return jnp.concatenate([half[:, HY:], half[:, :HY]], axis=1)


def component(even, odd, own, comp):
    def one(half, coefficients):
        met = jnp.where(comp == 1, swap_x(half), jnp.where(comp == 2, swap_y(half), half))
        return met * coefficients

    return one(even, own[:HX]), one(odd, own[HX:])


def comp_index():
    return lax.axis_index("l") * 2 + lax.axis_index("k")


def wave_grid(rows):
    shape = (rows, NY)
    row = lax.broadcasted_iota(jnp.int32, shape, 0)
    col = lax.broadcasted_iota(jnp.int32, shape, 1)
    odd = (row >= HX).astype(jnp.int32)
    slot = row % QX
    wave_x = 2 * slot + odd
    sine_x = (row % HX) >= QX
    nyquist_x = sine_x & (wave_x == 0)
    wave_x = jnp.where(nyquist_x, HX, wave_x)
    wave_y = col % HY
    sine_y = col >= HY
    nyquist_y = sine_y & (wave_y == 0)
    wave_y = jnp.where(nyquist_y, HY, wave_y)
    kx = wave_x.astype(F32) * (TWO_PI / NX)
    ky = wave_y.astype(F32) * (TWO_PI / NY)
    return kx, ky, sine_x, sine_y, nyquist_x, nyquist_y


def prepare_kernel(top_ref, decay_ref, own_ref, factors_ref):
    comp = comp_index()
    kx, ky, sine_x, sine_y, nyquist_x, nyquist_y = wave_grid(NX)
    kabs = jnp.sqrt(kx * kx + ky * ky)
    inverse = 1.0 / jnp.maximum(kabs, TWO_PI / max(NX, NY))
    decay_ref[...] = 4.0 * jnp.exp(-kabs * top_ref[0]) * (1.0 - jnp.exp(-kabs))
    rx = kx * inverse
    ry = ky * inverse
    first = jnp.where(nyquist_x, 0.0, jnp.where(sine_x, -rx, rx))
    second = jnp.where(nyquist_y, 0.0, jnp.where(sine_y, -ry, ry))
    third = -(rx * rx)
    factors_ref[0] = first
    factors_ref[1] = second
    factors_ref[2] = third
    own_ref[...] = jnp.where(
        comp == 0, 1.0, jnp.where(comp == 1, first, jnp.where(comp == 2, second, third))
    )


def gather_rows(pieces, full_ref):
    comp = comp_index()
    for step, piece in enumerate(pieces):
        full_ref[pl.ds(pl.multiple_of(jnp.bitwise_xor(comp, step) * QX, QX), QX), :] = piece[...]


def start_kernel(
    nxy, m0, m1, m2, m3, top_ref, decay_ref, own_ref, fx, bx, ty, out_ref, full_ref
):
    rows = NX // nxy
    comp = comp_index()
    gather_rows((m0, m1, m2, m3), full_ref)
    dens = full_ref[...]
    pull = 0.5 * (dens * (1.0 / (dens * dens + 0.25)))
    for place, field in enumerate((dens, pull)):
        even, odd = to_waves(field, fx, ty)
        even, odd = component(even * decay_ref[:HX], odd * decay_ref[HX:], own_ref, comp)
        plane = from_waves(even, odd, bx, ty)
        for target in range(nxy):
            out_ref[target, place * rows : (place + 1) * rows, :] = plane[
                target * rows : (target + 1) * rows
            ]
    for target in range(nxy):
        out_ref[target, 2 * rows : 2 * rows + 8, :] = jnp.full((8, NY), top_ref[0], F32)


def collect_kernel(nxy, got_ref, sum_ref, pull_ref):
    rows = NX // nxy
    total = got_ref[0, : 2 * rows, :]
    for source in range(1, nxy):
        total = total + got_ref[source, : 2 * rows, :]
    sum_ref[:rows] = total[:rows]
    pull_ref[...] = total[rows:]
    for source in range(nxy):
        sum_ref[rows + source : rows + source + 1, :] = got_ref[source, 2 * rows : 2 * rows + 1, :]


def residual_kernel(nxy, nh, *refs):
    rows = NX // nxy
    part = rows // nh
    sums = refs[:nh]
    data = refs[nh : 2 * nh]
    pred_ref, weight_ref, tops_ref, send_ref = refs[2 * nh : 2 * nh + 4]
    meas_ref = refs[2 * nh + 4]
    chip = lax.axis_index("h")
    total = sums[0][:rows]
    for step in range(1, nh):
        total = total + sums[step][:rows]
    for step in range(nh):
        tops_ref[step * nxy : (step + 1) * nxy] = sums[step][rows:]
        place = pl.ds(pl.multiple_of(lax.rem(chip + (nh - step), nh) * part, part), part)
        weight_ref[place, :] = data[step][:part]
        meas_ref[place, :] = data[step][part:]
    weight = weight_ref[...]
    pred_ref[...] = total
    res = weight * (weight * (total - meas_ref[...]))
    for target in range(nxy):
        send_ref[target] = res


def power_kernel(layers, tops_ref, power_ref):
    kx, ky, *_ = wave_grid(NX)
    for start in range(0, NX, 64):
        ks = jnp.sqrt(kx[start : start + 64] ** 2 + ky[start : start + 64] ** 2)
        double = -2.0 * ks

        def add(layer, total):
            return total + jnp.exp(double * tops_ref[pl.ds(layer, 1), :])

        total = lax.fori_loop(0, layers, add, jnp.zeros_like(ks))
        rise = 1.0 - jnp.exp(-ks)
        power_ref[start : start + 64] = (16.0 * (rise * rise)) * total


def adjoint_kernel(
    nxy, res_ref, decay_ref, own_ref, power_ref, factors_ref, fx, bx, ty, o0, o1, o2, o3, z_ref, i_ref
):
    rows = NX // nxy
    comp = comp_index()
    res = res_ref[...].reshape(NX, NY)
    even, odd = to_waves(res, fx, ty)
    even, odd = component(even, odd, own_ref, comp)
    sign = jnp.where((comp == 1) | (comp == 2), -1.0, 1.0)
    even = even * sign
    odd = odd * sign
    z_ref[...] = from_waves(even * decay_ref[:HX], odd * decay_ref[HX:], bx, ty)
    even = even * power_ref[:HX]
    odd = odd * power_ref[HX:]
    block = lax.axis_index("x") * lax.axis_size("y") + lax.axis_index("y")
    upper = block * rows < HX
    begin = pl.multiple_of(lax.rem(block * rows, HX), rows)
    near = pl.ds(begin, rows)
    flip = jnp.where(upper, 1.0, -1.0)
    for target in range(4):
        if target == 0:
            e, o = even, odd
        elif target == 1:
            e, o = swap_x(even) * factors_ref[0, :HX], swap_x(odd) * factors_ref[0, HX:]
        elif target == 2:
            e, o = swap_y(even) * factors_ref[1, :HX], swap_y(odd) * factors_ref[1, HX:]
        else:
            e, o = even * factors_ref[2, :HX], odd * factors_ref[2, HX:]
        line = table_times(bx[0, near, :], bx[1, near, :], e)
        line = line + flip * table_times(bx[2, near, :], bx[3, near, :], o)
        i_ref[target * rows : (target + 1) * rows, :] = line
    i_ref[...] = times_table(i_ref[...], ty[2], ty[3])
    for step, out in enumerate((o0, o1, o2, o3)):
        other = jnp.bitwise_xor(comp, step)
        out[:QX] = z_ref[pl.ds(pl.multiple_of(other * QX, QX), QX), :]
        out[QX:] = i_ref[pl.ds(pl.multiple_of(other * rows, rows), rows), :]


def share(grad, quad, image, weight, scratch, part):
    scratch[...] = weight * image
    place = pl.ds(pl.multiple_of(lax.axis_index("h") * part, part), part)
    mine = scratch[place, :]
    lane = lax.broadcasted_iota(jnp.int32, (1, 128), 1)
    square = grad * grad
    gg = jnp.sum(square)
    qgg = jnp.sum(quad * square)
    curv = jnp.sum(mine * mine)
    return jnp.where(lane == 0, gg, jnp.where(lane == 1, qgg, jnp.where(lane == 2, curv, 0.0)))


def step_length(shares):
    total = jnp.sum(shares, axis=0, keepdims=True)
    lane = lax.broadcasted_iota(jnp.int32, total.shape, 1)
    pick = lambda place: jnp.sum(jnp.where(lane == place, total, 0.0), keepdims=True)
    return pick(0) / (pick(2) + 0.5 * pick(1))


def gradient_kernel(nxy, nh, *refs):
    rows = NX // nxy
    part = rows // nh
    pieces = refs[:4]
    pulls = refs[4 : 4 + nh]
    dens_ref, weight_ref = refs[4 + nh : 6 + nh]
    share_ref, send_ref, data_ref, grad_ref, line_ref, image_ref, scratch = refs[6 + nh :]
    total = pieces[0][...] + pieces[1][...] + (pieces[2][...] + pieces[3][...])
    data = total[:QX]
    line = total[QX:]
    dens = dens_ref[0]
    quad = 1.0 / (dens * dens + 0.25)
    grad = data + 0.5 * (quad * dens)
    pulled = pulls[0][...]
    for step in range(1, nh):
        pulled = pulled + pulls[step][...]
    image = line + pulled
    weight = weight_ref[...]
    share_ref[...] = jnp.broadcast_to(
        share(grad, quad, image, weight, scratch, part), share_ref.shape
    )
    data_ref[...] = data
    grad_ref[...] = grad
    line_ref[...] = line
    image_ref[...] = image
    back = weight * (weight * image)
    for target in range(nxy):
        send_ref[target] = back


def move_kernel(shares_ref, dens_ref, grad_ref, dens_out, pull_out, alpha_ref):
    alpha = step_length(shares_ref[...])
    dens = dens_ref[0] - alpha * grad_ref[...]
    dens_out[...] = dens
    pull_out[...] = 0.5 * (dens * (1.0 / (dens * dens + 0.25)))
    alpha_ref[...] = jnp.broadcast_to(alpha, alpha_ref.shape)


def second_kernel(nxy, p0, p1, p2, p3, decay_ref, own_ref, fx, bx, ty, out_ref, full_ref):
    comp = comp_index()
    gather_rows((p0, p1, p2, p3), full_ref)
    even, odd = to_waves(full_ref[...], fx, ty)
    even, odd = component(even * decay_ref[:HX], odd * decay_ref[HX:], own_ref, comp)
    out_ref[...] = from_waves(even, odd, bx, ty).reshape(out_ref.shape)


def sum_kernel(nxy, got_ref, sum_ref):
    total = got_ref[0]
    for source in range(1, nxy):
        total = total + got_ref[source]
    sum_ref[...] = total


def second_gradient_kernel(
    u0, u1, u2, u3, alpha_ref, data_ref, pull_ref, dens_ref, line_ref, grad_ref, image_ref, share_ref
):
    alpha = alpha_ref[:1, :1]
    total = u0[...] + u1[...] + (u2[...] + u3[...])
    dens = dens_ref[...]
    grad = data_ref[...] - alpha * total[:QX] + pull_ref[...]
    quad = 1.0 / (dens * dens + 0.25)
    grad_ref[...] = grad
    image_ref[...] = line_ref[...] - alpha * total[QX:]
    square = grad * grad
    lane = lax.broadcasted_iota(jnp.int32, (8, 128), 1)
    share_ref[...] = jnp.where(
        lane == 0, jnp.sum(square), jnp.where(lane == 1, jnp.sum(quad * square), 0.0)
    )


def curvature_kernel(nxy, nh, *refs):
    rows = NX // nxy
    part = rows // nh
    pulls = refs[:nh]
    image_ref, weight_ref, part_ref, share_ref, out_ref, scratch = refs[nh:]
    image = image_ref[...]
    for step in range(nh):
        image = image + pulls[step][...]
    out_ref[...] = image
    scratch[...] = weight_ref[...] * image
    mine = scratch[pl.ds(pl.multiple_of(lax.axis_index("h") * part, part), part), :]
    lane = lax.broadcasted_iota(jnp.int32, (1, 128), 1)
    share_ref[...] = jnp.broadcast_to(
        jnp.where(lane == 2, jnp.sum(mine * mine), part_ref[:1]), share_ref.shape
    )


def finish_kernel(
    shares_ref, dens_ref, grad_ref, alpha_ref, pred_ref, first_ref, second_ref, obs_ref, w_ref, dens_out, err_out
):
    part = obs_ref.shape[1]
    alpha = step_length(shares_ref[...])
    dens_out[0] = dens_ref[...] - alpha * grad_ref[...]
    place = pl.ds(pl.multiple_of(lax.axis_index("h") * part, part), part)
    pred = pred_ref[place, :] - alpha_ref[:1, :1] * first_ref[place, :]
    pred = pred - alpha * second_ref[place, :]
    err_out[0] = w_ref[0] * (pred - obs_ref[0])


VMEM = pl.BlockSpec(memory_space=pltpu.VMEM)
SMEM = pl.BlockSpec(memory_space=pltpu.SMEM)


def call(kernel, outs, *args, scratch=(), scalars=()):
    shapes = [jax.ShapeDtypeStruct(shape, F32) for shape in outs]
    return pl.pallas_call(
        kernel,
        out_shape=shapes,
        in_specs=[SMEM if place in scalars else VMEM for place in range(len(args))],
        out_specs=[VMEM] * len(outs),
        scratch_shapes=[pltpu.VMEM(shape, F32) for shape in scratch],
    )(*args)


def from_comps(values):
    return [values[0]] + [
        lax.ppermute(values[step], COMP, [(i, i ^ step) for i in range(4)]) for step in (1, 2, 3)
    ]


def from_chips(value, nh):
    return [value] + [
        lax.ppermute(value, "h", [(i, (i + step) % nh) for i in range(nh)]) for step in range(1, nh)
    ]


def exchange(value, axes):
    return lax.all_to_all(value, axes, 0, 0, tiled=True)


def after(value, *others):
    return lax.optimization_barrier((value, *others))[0]


def body(density, observed, data_weight, layer_top):
    nxy = lax.axis_size("x") * lax.axis_size("y")
    nh = lax.axis_size("h")
    devices = nxy * nh * 4
    rows = NX // nxy
    fx, bx, ty = (jnp.asarray(table) for table in make_tables())
    bind = functools.partial

    decay, own, factors = call(
        prepare_kernel, [(NX, NY), (NX, NY), (3, NX, NY)], layer_top, scalars=(0,)
    )
    strip = density[0]
    layers = from_comps([strip] * 4)
    (message,) = call(
        bind(start_kernel, nxy),
        [(nxy, 2 * rows + 8, NY)],
        *layers, layer_top, decay, own, fx, bx, ty,
        scratch=[(NX, NY)], scalars=(4,),
    )
    data = from_chips(jnp.concatenate([data_weight[0], observed[0]], axis=0), nh)
    got = exchange(message, XY)
    sums, pulled = call(bind(collect_kernel, nxy), [(rows + nxy, NY), (rows, NY)], got)
    sums = from_chips(sums, nh)
    pred, weight, tops, message = call(
        bind(residual_kernel, nxy, nh),
        [(rows, NY), (rows, NY), (nxy * nh, NY), (nxy, rows, NY)],
        *sums, *data, scratch=[(rows, NY)],
    )
    got = exchange(message, XY)
    pulls = from_chips(after(pulled, message), nh)
    (power,) = call(bind(power_kernel, nxy * nh), [(NX, NY)], tops)
    adjoint = lambda plane: from_comps(
        call(
            bind(adjoint_kernel, nxy),
            [(QX + rows, NY)] * 4,
            plane, decay, own, power, factors, fx, bx, ty,
            scratch=[(NX, NY), (4 * rows, NY)],
        )
    )
    pieces = adjoint(got)
    shares, message, data_grad, grad, line, image = call(
        bind(gradient_kernel, nxy, nh),
        [(devices, 128), (nxy, rows, NY), (QX, NY), (QX, NY), (rows, NY), (rows, NY)],
        *pieces, *pulls, density, weight, scratch=[(rows, NY)],
    )
    shares = exchange(shares, ALL)
    dens, pull, alpha = call(
        move_kernel, [(QX, NY), (QX, NY), (8, 128)], shares, density, grad
    )
    back = exchange(after(message, pull), XY)
    pull_full = from_comps([pull] * 4)
    (message,) = call(
        bind(second_kernel, nxy), [(nxy, rows, NY)],
        *pull_full, decay, own, fx, bx, ty, scratch=[(NX, NY)],
    )
    got = exchange(message, XY)
    pieces = adjoint(back)
    grad2, image2, half = call(
        second_gradient_kernel, [(QX, NY), (rows, NY), (8, 128)],
        *pieces, alpha, data_grad, pull, dens, line,
    )
    (pulled,) = call(bind(sum_kernel, nxy), [(rows, NY)], got)
    pulls = from_chips(pulled, nh)
    shares, image2 = call(
        bind(curvature_kernel, nxy, nh), [(devices, 128), (rows, NY)],
        *pulls, image2, weight, half, scratch=[(rows, NY)],
    )
    shares = exchange(shares, ALL)
    return tuple(
        call(
            finish_kernel, [density.shape, observed.shape],
            shares, dens, grad2, alpha, pred, image, image2, observed, data_weight,
        )
    )


def solution(mesh):
    depth = mesh.shape["depth"]
    sizes = {64: (4, 4, 4), 4: (2, 1, 2)}[depth]
    fine = Mesh(mesh.devices.reshape(*sizes, 2, 2), ALL)
    data = P(COMP, DEPTH, None)
    layer = P(DEPTH, COMP, None)
    return jax.shard_map(
        body,
        mesh=fine,
        in_specs=(layer, data, data, P(DEPTH)),
        out_specs=(layer, data),
        check_vma=False,
    )
```

time: 2030 us -> 213 us (0.10)
  waiting for transfers between devices: 1140 us -> 28.3 us
  blocking collectives: 595 us -> 75.9 us
  matrix products: 259 us -> 0 us
  Pallas kernels: 0 us -> 51.4 us
  starting transfers between devices: 0.21 us -> 49.2 us
    reduce_scatter x5 -> x0, waiting for transfers between devices: 1140 us -> none  [the longest x3 1000 us: forward_once(): lax.psum_scatter(inverse_rows(total_re, total_im, cos_x, sin_x, cos_y, si...]
    all_gather x5 -> x0, blocking collectives: 347 us -> none  [the longest x2 323 us: body(): lax.all_gather(weighted_res, 'depth', axis=0, tiled=True)]
    dot_general x60 -> x0, matrix products: 259 us -> none  [matmul(): jnp.dot(left, right, precision=lax.Precision.HIGHEST, preferred_element_t...]
    psum x2 -> x0, blocking collectives: 248 us -> none  [body(): grad_sq, quad_sq = lax.psum((grad_sq, quad_sq), ('depth', 'comp'))]
    all_to_all x0 -> x3, blocking collectives: none -> 75.9 us  [exchange(): return lax.all_to_all(value, axes, 0, 0, tiled=True)]
    pallas_call x0 -> x14, Pallas kernels: none -> 51.4 us  [call(): pl.pallas_call(kernel, out_shape=shapes, in_specs=[SMEM if place in scala...]
    ppermute x0 -> x24, starting transfers between devices: none -> 35.6 us  [the longest x12 20.1 us: from_chips(): lax.ppermute(value, 'h', [(i, (i + step) % nh) for i in range(nh)])]
    ppermute x0 -> x24, waiting for transfers between devices: none -> 25.8 us  [the longest x12 15.1 us: from_chips(): lax.ppermute(value, 'h', [(i, (i + step) % nh) for i in range(nh)])]
  transfers between devices with their start and end apart: 5 -> 27, of which waited for: 5 -> 13; matrix products, arithmetic and copies ran while one was open for 0% -> 0% of each run, Pallas kernels for 0% -> 13%
where the time goes in v1:
time: 213 us; the launch traced here: 212 us
  blocking collectives  75.9 us (36%)
  Pallas kernels  51.4 us (24%)
  starting transfers between devices  49.2 us (23%)
  waiting for transfers between devices  28.3 us (13%)
  local copies, waits for them, and re-layouts  6.23 us (3%)
    all_to_all x3, blocking collectives, exchange(): return lax.all_to_all(value, axes, 0, 0, tiled=True)  75.9 us
    pallas_call x14, Pallas kernels, call(): pl.pallas_call(kernel, out_shape=shapes, in_specs=[SMEM if place in scala...  51.4 us
    ppermute x12, starting transfers between devices, from_chips(): lax.ppermute(value, 'h', [(i, (i + step) % nh) for i in range(nh)])  20.1 us
    ppermute x12, starting transfers between devices, from_comps(): lax.ppermute(values[step], COMP, [(i, i ^ step) for i in range(4)])  15.5 us
    ppermute x12, waiting for transfers between devices, from_chips(): lax.ppermute(value, 'h', [(i, (i + step) % nh) for i in range(nh)])  15.1 us
    all_to_all x3, starting transfers between devices, exchange(): return lax.all_to_all(value, axes, 0, 0, tiled=True)  13.6 us
    ppermute x12, waiting for transfers between devices, from_comps(): lax.ppermute(values[step], COMP, [(i, i ^ step) for i in range(4)])  10.7 us
    unnamed x62, local copies, waits for them, and re-layouts  6.23 us
  transfers between devices with their start and end apart: 27, of which 13 were waited for; matrix products, arithmetic and copies ran while one was open for 0% of the time, Pallas kernels for 13%

profile of v1, /device:TPU:1, one launch (start us, length us, event | category | flops | bytes accessed | tf_op | source)
XLA Modules:
  0.0 212.4 jit_solution(6048153156032935224)
XLA Ops:
  0.6 3.3 %collective-permute-start = (f32[128,256]{1,0:T(8,128)}, f32[128,256]{1,0:T(8,128)S(1)}, u32[]{:S(2)}, u32[]{:S(2)}) collective-permute-start(f32[128,256]{1,0:T(8,128)} %bitcast.11), channel_id=1, source_target_pairs={{0,1},{1,0},{2,3},{3,2},{4,5},{5,4},{6,7},{7,6},{8,9},{9,8},{10,11... | collective-permute-start | bytes 393224 | tf_op jit(solution)/shard_map/ppermute | solution.py:400
  6.3 1.9 shard_map.86
  9.1 3.1 %collective-permute-done.2.m3 = f32[128,256]{1,0:T(8,128)S(1)} collective-permute-done((f32[128,256]{1,0:T(8,128)}, f32[128,256]{1,0:T(8,128)S(1)}, u32[]{:S(2)}, u32[]{:S(2)}) %collective-permute-start.2) | collective-permute-done | bytes 131104 | tf_op jit(solution)/shard_map/ppermute | solution.py:400
  12.8 5.8 %shard_map.87 = f32[16,72,256]{2,1,0:T(8,128)} custom-call(f32[128,256]{1,0:T(8,128)} %bitcast.14, f32[128,256]{1,0:T(8,128)} %copy-done.9, f32[128,256]{1,0:T(8,128)} %copy-done.10, f32[128,256]{1,0:T(8,128)} %copy-done.12, f32[1]{0:T(128)S(6)} %copy.11.top_ref, f32[512,256]{1,0:T(8,128)} %get-tuple-element.35.decay_ref, ...), custom_call_target="tpu_custom_call" | custom-call | tf_op jit(solution)/shard_map/pallas_call | solution.py:389
  18.7 23.0 %all_to_all.42.got_ref = f32[16,72,256]{2,1,0:T(8,128)} all-to-all(f32[16,72,256]{2,1,0:T(8,128)} %shard_map.87), channel_id=1, replica_groups=mesh['x'=4,'y'=4,'h'=4,'l'=2,'k'=2] {'x','y'}, dimensions={0} | all-to-all | bytes 2359296 | tf_op jit(solution)/shard_map/all_to_all | solution.py:411
  41.7 2.0 shard_map.88
  43.7 3.0 %collective-permute-start.3 = (f32[48,256]{1,0:T(8,128)}, f32[48,256]{1,0:T(8,128)S(1)}, u32[]{:S(2)}, u32[]{:S(2)}) collective-permute-start(f32[48,256]{1,0:T(8,128)} %get-tuple-element.37.refs_0_), channel_id=1, source_target_pairs={{0,4},{4,8},{8,12},{12,0},{1,5},{5,9},{9,13},{13,1},{2,6},{6,10},{... | collective-permute-start | bytes 147464 | tf_op jit(solution)/shard_map/ppermute | solution.py:406
  46.6 5.1 %collective-permute-start.4 = (f32[48,256]{1,0:T(8,128)}, f32[48,256]{1,0:T(8,128)S(1)}, u32[]{:S(2)}, u32[]{:S(2)}) collective-permute-start(f32[48,256]{1,0:T(8,128)} %get-tuple-element.37.refs_0_), channel_id=1, source_target_pairs={{0,8},{4,12},{8,0},{12,4},{1,9},{5,13},{9,1},{13,5},{2,10},{6,14},... | collective-permute-start | bytes 147464 | tf_op jit(solution)/shard_map/ppermute | solution.py:406
  51.8 2.4 %collective-permute-start.5 = (f32[48,256]{1,0:T(8,128)}, f32[48,256]{1,0:T(8,128)S(1)}, u32[]{:S(2)}, u32[]{:S(2)}) collective-permute-start(f32[48,256]{1,0:T(8,128)} %get-tuple-element.37.refs_0_), channel_id=1, source_target_pairs={{0,12},{4,0},{8,4},{12,8},{1,13},{5,1},{9,5},{13,9},{2,14},{6,2},{... | collective-permute-start | bytes 147464 | tf_op jit(solution)/shard_map/ppermute | solution.py:406
  54.2 2.1 collective-permute-start.7
  56.3 2.6 %collective-permute-done.6.refs_5_ = f32[16,256]{1,0:T(8,128)S(1)} collective-permute-done((f32[16,256]{1,0:T(8,128)S(1)}, f32[16,256]{1,0:T(8,128)S(1)}, u32[]{:S(2)}, u32[]{:S(2)}) %collective-permute-start.6) | collective-permute-done | bytes 16416 | tf_op jit(solution)/shard_map/ppermute | solution.py:406
  58.9 1.9 collective-permute-done.7.refs_6_
  65.7 3.6 %all-to-all-start.1 = ((f32[16,32,256]{2,1,0:T(8,128)}), f32[16,32,256]{2,1,0:T(8,128)S(1)}, u32[]{:S(2)}, u32[]{:S(2)}) async-start(f32[16,32,256]{2,1,0:T(8,128)} %get-tuple-element.38), calls=%async_computation.1 | async-start | bytes 1048576 | tf_op jit(solution)/shard_map/all_to_all | solution.py:411
  69.3 12.8 %shard_map.90.power_ref = f32[512,256]{1,0:T(8,128)} custom-call(f32[64,256]{1,0:T(8,128)} %get-tuple-element.39.tops_ref), custom_call_target="tpu_custom_call" | custom-call | tf_op jit(solution)/shard_map/pallas_call | solution.py:389
  82.9 5.6 %shard_map.91 = (f32[160,256]{1,0:T(8,128)}, f32[160,256]{1,0:T(8,128)}, f32[160,256]{1,0:T(8,128)}, f32[160,256]{1,0:T(8,128)}) custom-call(f32[16,32,256]{2,1,0:T(8,128)} %copy-done.1, f32[512,256]{1,0:T(8,128)} %get-tuple-element.35.decay_ref, f32[512,256]{1,0:T(8,128)} %get-tuple-element.36.own_ref, f32[512,256]{1,0:T(8,128)} %shard_map.90.power_ref, ...), custom_call_target="tpu_custom_call" | custom-call | tf_op jit(solution)/shard_map/pallas_call | solution.py:389
  89.2 5.2 %collective-permute-start.11 = (f32[160,256]{1,0:T(8,128)}, f32[160,256]{1,0:T(8,128)S(1)}, u32[]{:S(2)}, u32[]{:S(2)}) collective-permute-start(f32[160,256]{1,0:T(8,128)} %get-tuple-element.44), channel_id=1, source_target_pairs={{0,3},{1,2},{2,1},{3,0},{4,7},{5,6},{6,5},{7,4},{8,11},{9,10},{10,... | collective-permute-start | bytes 491528 | tf_op jit(solution)/shard_map/ppermute | solution.py:400
  97.6 4.0 %collective-permute-done.12.refs_5_ = f32[32,256]{1,0:T(8,128)S(1)} collective-permute-done((f32[32,256]{1,0:T(8,128)S(1)}, f32[32,256]{1,0:T(8,128)S(1)}, u32[]{:S(2)}, u32[]{:S(2)}) %collective-permute-start.12) | collective-permute-done | bytes 32800 | tf_op jit(solution)/shard_map/ppermute | solution.py:406
  103.0 2.2 %collective-permute-done.14.refs_7_ = f32[32,256]{1,0:T(8,128)S(1)} collective-permute-done((f32[32,256]{1,0:T(8,128)S(1)}, f32[32,256]{1,0:T(8,128)S(1)}, u32[]{:S(2)}, u32[]{:S(2)}) %collective-permute-start.14) | collective-permute-done | bytes 32800 | tf_op jit(solution)/shard_map/ppermute | solution.py:406
  106.0 2.3 %shard_map.92 = (f32[256,128]{1,0:T(8,128)}, f32[16,32,256]{2,1,0:T(8,128)}, f32[128,256]{1,0:T(8,128)}, f32[128,256]{1,0:T(8,128)}, f32[32,256]{1,0:T(8,128)}, /*index=5*/f32[32,256]{1,0:T(8,128)}) custom-call(f32[160,256]{1,0:T(8,128)} %get-tuple-element.41.refs_0_, f32[160,256]{1,0:T(8,128)} %copy-done.6, f32[160,256]{1,0:T(8,128)} %copy-done.3, ...), custom_call_target="tpu_custom_call" | custom-call | tf_op jit(solution)/shard_map/pallas_call | solution.py:389
  108.3 28.8 %all_to_all.43 = f32[256,1,128]{2,1,0:T(1,128)} all-to-all(f32[256,1,128]{2,1,0:T(1,128)} %bitcast.17), channel_id=1, replica_groups=mesh['x'=4,'y'=4,'h'=4,'l'=2,'k'=2] {'x','y','h','l','k'}, dimensions={0} | all-to-all | bytes 262144 | tf_op jit(solution)/shard_map/all_to_all | solution.py:411
  137.1 1.9 shard_map.93
  139.0 3.6 %all-to-all-start.4 = ((f32[16,32,256]{2,1,0:T(8,128)}), f32[16,32,256]{2,1,0:T(8,128)S(1)}, u32[]{:S(2)}, u32[]{:S(2)}) async-start(f32[16,32,256]{2,1,0:T(8,128)} %get-tuple-element.52), calls=%async_computation.4 | async-start | bytes 1048576 | tf_op jit(solution)/shard_map/all_to_all | solution.py:411
  145.0 3.4 %collective-permute-done.16.p2 = f32[128,256]{1,0:T(8,128)S(1)} collective-permute-done((f32[128,256]{1,0:T(8,128)}, f32[128,256]{1,0:T(8,128)S(1)}, u32[]{:S(2)}, u32[]{:S(2)}) %collective-permute-start.16) | collective-permute-done | bytes 131104 | tf_op jit(solution)/shard_map/ppermute | solution.py:400
  148.4 3.4 %collective-permute-done.17.p3 = f32[128,256]{1,0:T(8,128)S(1)} collective-permute-done((f32[128,256]{1,0:T(8,128)}, f32[128,256]{1,0:T(8,128)S(1)}, u32[]{:S(2)}, u32[]{:S(2)}) %collective-permute-start.17) | collective-permute-done | bytes 131104 | tf_op jit(solution)/shard_map/ppermute | solution.py:400
  152.4 4.4 %shard_map.94 = f32[16,32,256]{2,1,0:T(8,128)} custom-call(f32[128,256]{1,0:T(8,128)} %get-tuple-element.50.p0.pull_ref, f32[128,256]{1,0:T(8,128)} %copy-done.11, f32[128,256]{1,0:T(8,128)} %copy-done.13, f32[128,256]{1,0:T(8,128)} %copy-done.14, f32[512,256]{1,0:T(8,128)} %get-tuple-element.35.decay_ref, f32[512,256]{1,0:T(8,128)} %get-tuple-element.36.own_ref, ...), custom_call_target="tpu_custom_call" | custom-call | tf_op jit(solution)/shard_map/pallas_call | solution.py:389
  156.8 6.5 %all-to-all-start.3 = ((f32[16,32,256]{2,1,0:T(8,128)}), f32[16,32,256]{2,1,0:T(8,128)S(1)}, u32[]{:S(2)}, u32[]{:S(2)}) async-start(f32[16,32,256]{2,1,0:T(8,128)} %shard_map.94), calls=%async_computation.3 | async-start | bytes 1048576 | tf_op jit(solution)/shard_map/all_to_all | solution.py:411
  163.4 5.6 %shard_map.96 = (f32[160,256]{1,0:T(8,128)}, f32[160,256]{1,0:T(8,128)}, f32[160,256]{1,0:T(8,128)}, f32[160,256]{1,0:T(8,128)}) custom-call(f32[16,32,256]{2,1,0:T(8,128)} %copy-done, f32[512,256]{1,0:T(8,128)} %get-tuple-element.35.decay_ref, f32[512,256]{1,0:T(8,128)} %get-tuple-element.36.own_ref, f32[512,256]{1,0:T(8,128)} %shard_map.90.power_ref, ...), custom_call_target="tpu_custom_call" | custom-call | tf_op jit(solution)/shard_map/pallas_call | solution.py:389
  171.1 2.4 %all-to-all-done.3.got_ref = f32[16,32,256]{2,1,0:T(8,128)S(1)} async-done(((f32[16,32,256]{2,1,0:T(8,128)}), f32[16,32,256]{2,1,0:T(8,128)S(1)}, u32[]{:S(2)}, u32[]{:S(2)}) %all-to-all-start.3) | async-done | bytes 524320 | tf_op jit(solution)/shard_map/all_to_all | solution.py:411
  178.3 2.1 collective-permute-start.20
  181.1 2.1 shard_map.97
  186.5 24.0 %all_to_all.44 = f32[256,1,128]{2,1,0:T(1,128)} all-to-all(f32[256,1,128]{2,1,0:T(1,128)} %bitcast.18), channel_id=1, replica_groups=mesh['x'=4,'y'=4,'h'=4,'l'=2,'k'=2] {'x','y','h','l','k'}, dimensions={0} | all-to-all | bytes 262144 | tf_op jit(solution)/shard_map/all_to_all | solution.py:411
  210.5 1.9 shard_map.99
  (102 shorter events, 29.1 us)
Async XLA Ops:
  0.6 7.6 %collective-permute-start = (f32[128,256]{1,0:T(8,128)}, f32[128,256]{1,0:T(8,128)S(1)}, u32[]{:S(2)}, u32[]{:S(2)}) collective-permute-start(f32[128,256]{1,0:T(8,128)} %bitcast.11), channel_id=1, source_target_pairs={{0,1},{1,0},{2,3},{3,2},{4,5},{5,4},{6,7},{7,6},{8,9},{9,8},{10,11... | collective-permute-start | bytes 393224 | tf_op jit(solution)/shard_map/ppermute | solution.py:400
  3.9 5.2 %collective-permute-start.1 = (f32[128,256]{1,0:T(8,128)}, f32[128,256]{1,0:T(8,128)S(1)}, u32[]{:S(2)}, u32[]{:S(2)}) collective-permute-start(f32[128,256]{1,0:T(8,128)} %bitcast.12), channel_id=1, source_target_pairs={{0,2},{1,3},{2,0},{3,1},{4,6},{5,7},{6,4},{7,5},{8,10},{9,11},{10,... | collective-permute-start | bytes 393224 | tf_op jit(solution)/shard_map/ppermute | solution.py:400
  3.9 8.2 %collective-permute-start.2 = (f32[128,256]{1,0:T(8,128)}, f32[128,256]{1,0:T(8,128)S(1)}, u32[]{:S(2)}, u32[]{:S(2)}) collective-permute-start(f32[128,256]{1,0:T(8,128)} %bitcast.13), channel_id=1, source_target_pairs={{0,3},{1,2},{2,1},{3,0},{4,7},{5,6},{6,5},{7,4},{8,11},{9,10},{10,... | collective-permute-start | bytes 393224 | tf_op jit(solution)/shard_map/ppermute | solution.py:400
  41.7 12.5 %copy-start.19 = (f32[1,8,256]{2,1,0:T(8,128)S(1)}, f32[1,8,256]{2,1,0:T(8,128)}, u32[]{:S(2)}) copy-start(f32[1,8,256]{2,1,0:T(8,128)} %obs_ref.1) | copy-start | bytes 24580
  41.7 12.5 %copy-start.20 = (f32[1,8,256]{2,1,0:T(8,128)S(1)}, f32[1,8,256]{2,1,0:T(8,128)}, u32[]{:S(2)}) copy-start(f32[1,8,256]{2,1,0:T(8,128)} %w_ref.1) | copy-start | bytes 24580
  43.7 19.1 %collective-permute-start.3 = (f32[48,256]{1,0:T(8,128)}, f32[48,256]{1,0:T(8,128)S(1)}, u32[]{:S(2)}, u32[]{:S(2)}) collective-permute-start(f32[48,256]{1,0:T(8,128)} %get-tuple-element.37.refs_0_), channel_id=1, source_target_pairs={{0,4},{4,8},{8,12},{12,0},{1,5},{5,9},{9,13},{13,1},{2,6},{6,10},{... | collective-permute-start | bytes 147464 | tf_op jit(solution)/shard_map/ppermute | solution.py:406
  46.6 16.1 %collective-permute-start.4 = (f32[48,256]{1,0:T(8,128)}, f32[48,256]{1,0:T(8,128)S(1)}, u32[]{:S(2)}, u32[]{:S(2)}) collective-permute-start(f32[48,256]{1,0:T(8,128)} %get-tuple-element.37.refs_0_), channel_id=1, source_target_pairs={{0,8},{4,12},{8,0},{12,4},{1,9},{5,13},{9,1},{13,5},{2,10},{6,14},... | collective-permute-start | bytes 147464 | tf_op jit(solution)/shard_map/ppermute | solution.py:406
  51.8 11.0 %collective-permute-start.5 = (f32[48,256]{1,0:T(8,128)}, f32[48,256]{1,0:T(8,128)S(1)}, u32[]{:S(2)}, u32[]{:S(2)}) collective-permute-start(f32[48,256]{1,0:T(8,128)} %get-tuple-element.37.refs_0_), channel_id=1, source_target_pairs={{0,12},{4,0},{8,4},{12,8},{1,13},{5,1},{9,5},{13,9},{2,14},{6,2},{... | collective-permute-start | bytes 147464 | tf_op jit(solution)/shard_map/ppermute | solution.py:406
  54.1 8.6 %copy-start.15 = (f32[16,256]{1,0:T(8,128)}, f32[16,256]{1,0:T(8,128)S(1)}, u32[]{:S(2)}) copy-start(f32[16,256]{1,0:T(8,128)S(1)} %pad_maximum_fusion.refs_4_) | copy-start | bytes 49156
  54.2 4.8 %collective-permute-start.6 = (f32[16,256]{1,0:T(8,128)S(1)}, f32[16,256]{1,0:T(8,128)S(1)}, u32[]{:S(2)}, u32[]{:S(2)}) collective-permute-start(f32[16,256]{1,0:T(8,128)S(1)} %pad_maximum_fusion.refs_4_), channel_id=1, source_target_pairs={{0,4},{4,8},{8,12},{12,0},{1,5},{5,9},{9,13},{13,1},{2,6},{6,10},{... | collective-permute-start | bytes 49160 | tf_op jit(solution)/shard_map/ppermute | solution.py:406
  54.2 6.6 %collective-permute-start.7 = (f32[16,256]{1,0:T(8,128)S(1)}, f32[16,256]{1,0:T(8,128)S(1)}, u32[]{:S(2)}, u32[]{:S(2)}) collective-permute-start(f32[16,256]{1,0:T(8,128)S(1)} %pad_maximum_fusion.refs_4_), channel_id=1, source_target_pairs={{0,8},{4,12},{8,0},{12,4},{1,9},{5,13},{9,1},{13,5},{2,10},{6,14},... | collective-permute-start | bytes 49160 | tf_op jit(solution)/shard_map/ppermute | solution.py:406
  58.9 3.8 %collective-permute-start.8 = (f32[16,256]{1,0:T(8,128)S(1)}, f32[16,256]{1,0:T(8,128)S(1)}, u32[]{:S(2)}, u32[]{:S(2)}) collective-permute-start(f32[16,256]{1,0:T(8,128)S(1)} %pad_maximum_fusion.refs_4_), channel_id=1, source_target_pairs={{0,12},{4,0},{8,4},{12,8},{1,13},{5,1},{9,5},{13,9},{2,14},{6,2},{... | collective-permute-start | bytes 49160 | tf_op jit(solution)/shard_map/ppermute | solution.py:406
  65.7 16.4 %all-to-all-start.1 = ((f32[16,32,256]{2,1,0:T(8,128)}), f32[16,32,256]{2,1,0:T(8,128)S(1)}, u32[]{:S(2)}, u32[]{:S(2)}) async-start(f32[16,32,256]{2,1,0:T(8,128)} %get-tuple-element.38), calls=%async_computation.1 | async-start | bytes 1048576 | tf_op jit(solution)/shard_map/all_to_all | solution.py:411
  82.9 11.5 %copy-start.24 = (f32[32,256]{1,0:T(8,128)S(1)}, f32[32,256]{1,0:T(8,128)}, u32[]{:S(2)}) copy-start(f32[32,256]{1,0:T(8,128)} %get-tuple-element.46.refs_4_) | copy-start | bytes 98308
  88.5 16.7 %collective-permute-start.10 = (f32[160,256]{1,0:T(8,128)}, f32[160,256]{1,0:T(8,128)S(1)}, u32[]{:S(2)}, u32[]{:S(2)}) collective-permute-start(f32[160,256]{1,0:T(8,128)} %get-tuple-element.43), channel_id=1, source_target_pairs={{0,2},{1,3},{2,0},{3,1},{4,6},{5,7},{6,4},{7,5},{8,10},{9,11},{10,... | collective-permute-start | bytes 491528 | tf_op jit(solution)/shard_map/ppermute | solution.py:400
  89.2 16.0 %collective-permute-start.11 = (f32[160,256]{1,0:T(8,128)}, f32[160,256]{1,0:T(8,128)S(1)}, u32[]{:S(2)}, u32[]{:S(2)}) collective-permute-start(f32[160,256]{1,0:T(8,128)} %get-tuple-element.44), channel_id=1, source_target_pairs={{0,3},{1,2},{2,1},{3,0},{4,7},{5,6},{6,5},{7,4},{8,11},{9,10},{10,... | collective-permute-start | bytes 491528 | tf_op jit(solution)/shard_map/ppermute | solution.py:400
  94.4 10.8 %collective-permute-start.9 = (f32[160,256]{1,0:T(8,128)}, f32[160,256]{1,0:T(8,128)S(1)}, u32[]{:S(2)}, u32[]{:S(2)}) collective-permute-start(f32[160,256]{1,0:T(8,128)} %get-tuple-element.42), channel_id=1, source_target_pairs={{0,1},{1,0},{2,3},{3,2},{4,5},{5,4},{6,7},{7,6},{8,9},{9,8},{10,11... | collective-permute-start | bytes 491528 | tf_op jit(solution)/shard_map/ppermute | solution.py:400
  94.4 7.1 %collective-permute-start.12 = (f32[32,256]{1,0:T(8,128)S(1)}, f32[32,256]{1,0:T(8,128)S(1)}, u32[]{:S(2)}, u32[]{:S(2)}) collective-permute-start(f32[32,256]{1,0:T(8,128)S(1)} %copy-done.24), channel_id=1, source_target_pairs={{0,4},{4,8},{8,12},{12,0},{1,5},{5,9},{9,13},{13,1},{2,6},{6,10},{... | collective-permute-start | bytes 98312 | tf_op jit(solution)/shard_map/ppermute | solution.py:406
  96.0 7.0 %collective-permute-start.13 = (f32[32,256]{1,0:T(8,128)S(1)}, f32[32,256]{1,0:T(8,128)S(1)}, u32[]{:S(2)}, u32[]{:S(2)}) collective-permute-start(f32[32,256]{1,0:T(8,128)S(1)} %copy-done.24), channel_id=1, source_target_pairs={{0,8},{4,12},{8,0},{12,4},{1,9},{5,13},{9,1},{13,5},{2,10},{6,14},... | collective-permute-start | bytes 98312 | tf_op jit(solution)/shard_map/ppermute | solution.py:406
  101.5 3.7 %collective-permute-start.14 = (f32[32,256]{1,0:T(8,128)S(1)}, f32[32,256]{1,0:T(8,128)S(1)}, u32[]{:S(2)}, u32[]{:S(2)}) collective-permute-start(f32[32,256]{1,0:T(8,128)S(1)} %copy-done.24), channel_id=1, source_target_pairs={{0,12},{4,0},{8,4},{12,8},{1,13},{5,1},{9,5},{13,9},{2,14},{6,2},{... | collective-permute-start | bytes 98312 | tf_op jit(solution)/shard_map/ppermute | solution.py:406
  139.0 17.8 %all-to-all-start.4 = ((f32[16,32,256]{2,1,0:T(8,128)}), f32[16,32,256]{2,1,0:T(8,128)S(1)}, u32[]{:S(2)}, u32[]{:S(2)}) async-start(f32[16,32,256]{2,1,0:T(8,128)} %get-tuple-element.52), calls=%async_computation.4 | async-start | bytes 1048576 | tf_op jit(solution)/shard_map/all_to_all | solution.py:411
  142.6 2.4 %collective-permute-start.15 = (f32[128,256]{1,0:T(8,128)}, f32[128,256]{1,0:T(8,128)S(1)}, u32[]{:S(2)}, u32[]{:S(2)}) collective-permute-start(f32[128,256]{1,0:T(8,128)} %get-tuple-element.50.p0.pull_ref), channel_id=1, source_target_pairs={{0,1},{1,0},{2,3},{3,2},{4,5},{5,4},{6,7},{7,6},{8,9},{9,8},{10,11... | collective-permute-start | bytes 393224 | tf_op jit(solution)/shard_map/ppermute | solution.py:400
  143.2 5.2 %collective-permute-start.16 = (f32[128,256]{1,0:T(8,128)}, f32[128,256]{1,0:T(8,128)S(1)}, u32[]{:S(2)}, u32[]{:S(2)}) collective-permute-start(f32[128,256]{1,0:T(8,128)} %get-tuple-element.50.p0.pull_ref), channel_id=1, source_target_pairs={{0,2},{1,3},{2,0},{3,1},{4,6},{5,7},{6,4},{7,5},{8,10},{9,11},{10,... | collective-permute-start | bytes 393224 | tf_op jit(solution)/shard_map/ppermute | solution.py:400
  143.6 8.1 %collective-permute-start.17 = (f32[128,256]{1,0:T(8,128)}, f32[128,256]{1,0:T(8,128)S(1)}, u32[]{:S(2)}, u32[]{:S(2)}) collective-permute-start(f32[128,256]{1,0:T(8,128)} %get-tuple-element.50.p0.pull_ref), channel_id=1, source_target_pairs={{0,3},{1,2},{2,1},{3,0},{4,7},{5,6},{6,5},{7,4},{8,11},{9,10},{10,... | collective-permute-start | bytes 393224 | tf_op jit(solution)/shard_map/ppermute | solution.py:400
  144.9 6.8 %copy-start.11 = (f32[128,256]{1,0:T(8,128)}, f32[128,256]{1,0:T(8,128)S(1)}, u32[]{:S(2)}) copy-start(f32[128,256]{1,0:T(8,128)S(1)} %collective-permute-done.15.p1) | copy-start | bytes 393220
  156.8 16.7 %all-to-all-start.3 = ((f32[16,32,256]{2,1,0:T(8,128)}), f32[16,32,256]{2,1,0:T(8,128)S(1)}, u32[]{:S(2)}, u32[]{:S(2)}) async-start(f32[16,32,256]{2,1,0:T(8,128)} %shard_map.94), calls=%async_computation.3 | async-start | bytes 1048576 | tf_op jit(solution)/shard_map/all_to_all | solution.py:411
  168.9 9.3 %collective-permute-start.21 = (f32[160,256]{1,0:T(8,128)}, f32[160,256]{1,0:T(8,128)S(1)}, u32[]{:S(2)}, u32[]{:S(2)}) collective-permute-start(f32[160,256]{1,0:T(8,128)} %get-tuple-element.54), channel_id=1, source_target_pairs={{0,1},{1,0},{2,3},{3,2},{4,5},{5,4},{6,7},{7,6},{8,9},{9,8},{10,11... | collective-permute-start | bytes 491528 | tf_op jit(solution)/shard_map/ppermute | solution.py:400
  169.3 11.0 %collective-permute-start.22 = (f32[160,256]{1,0:T(8,128)}, f32[160,256]{1,0:T(8,128)S(1)}, u32[]{:S(2)}, u32[]{:S(2)}) collective-permute-start(f32[160,256]{1,0:T(8,128)} %get-tuple-element.55), channel_id=1, source_target_pairs={{0,2},{1,3},{2,0},{3,1},{4,6},{5,7},{6,4},{7,5},{8,10},{9,11},{10,... | collective-permute-start | bytes 491528 | tf_op jit(solution)/shard_map/ppermute | solution.py:400
  169.7 10.6 %collective-permute-start.23 = (f32[160,256]{1,0:T(8,128)}, f32[160,256]{1,0:T(8,128)S(1)}, u32[]{:S(2)}, u32[]{:S(2)}) collective-permute-start(f32[160,256]{1,0:T(8,128)} %get-tuple-element.56), channel_id=1, source_target_pairs={{0,3},{1,2},{2,1},{3,0},{4,7},{5,6},{6,5},{7,4},{8,11},{9,10},{10,... | collective-permute-start | bytes 491528 | tf_op jit(solution)/shard_map/ppermute | solution.py:400
  176.0 7.2 %collective-permute-start.18 = (f32[32,256]{1,0:T(8,128)}, f32[32,256]{1,0:T(8,128)S(1)}, u32[]{:S(2)}, u32[]{:S(2)}) collective-permute-start(f32[32,256]{1,0:T(8,128)} %shard_map.95.refs_0_), channel_id=1, source_target_pairs={{0,4},{4,8},{8,12},{12,0},{1,5},{5,9},{9,13},{13,1},{2,6},{6,10},{... | collective-permute-start | bytes 98312 | tf_op jit(solution)/shard_map/ppermute | solution.py:406
  176.7 7.3 %collective-permute-start.19 = (f32[32,256]{1,0:T(8,128)}, f32[32,256]{1,0:T(8,128)S(1)}, u32[]{:S(2)}, u32[]{:S(2)}) collective-permute-start(f32[32,256]{1,0:T(8,128)} %shard_map.95.refs_0_), channel_id=1, source_target_pairs={{0,8},{4,12},{8,0},{12,4},{1,9},{5,13},{9,1},{13,5},{2,10},{6,14},... | collective-permute-start | bytes 98312 | tf_op jit(solution)/shard_map/ppermute | solution.py:406
  178.3 6.0 %collective-permute-start.20 = (f32[32,256]{1,0:T(8,128)}, f32[32,256]{1,0:T(8,128)S(1)}, u32[]{:S(2)}, u32[]{:S(2)}) collective-permute-start(f32[32,256]{1,0:T(8,128)} %shard_map.95.refs_0_), channel_id=1, source_target_pairs={{0,12},{4,0},{8,4},{12,8},{1,13},{5,1},{9,5},{13,9},{2,14},{6,2},{... | collective-permute-start | bytes 98312 | tf_op jit(solution)/shard_map/ppermute | solution.py:406
  (26 other events, 42.5 us)

commit v2 on v1

--- a/solution.py
+++ b/solution.py
@@ -157,71 +157,94 @@
 
 
 def start_kernel(
-    nxy, m0, m1, m2, m3, top_ref, decay_ref, own_ref, fx, bx, ty, out_ref, full_ref
+    nxy, m0, m1, m2, m3, top_ref, decay_ref, own_ref, fx, bx, ty, out_ref, full_ref, other_ref
 ):
     rows = NX // nxy
     comp = comp_index()
     gather_rows((m0, m1, m2, m3), full_ref)
     dens = full_ref[...]
     pull = 0.5 * (dens * (1.0 / (dens * dens + 0.25)))
-    for place, field in enumerate((dens, pull)):
-        even, odd = to_waves(field, fx, ty)
+    full_ref[...] = dens
+    other_ref[...] = pull
+
+    def plane_of(field_ref, place):
+        even, odd = to_waves(field_ref[...], fx, ty)
         even, odd = component(even * decay_ref[:HX], odd * decay_ref[HX:], own_ref, comp)
         plane = from_waves(even, odd, bx, ty)
         for target in range(nxy):
             out_ref[target, place * rows : (place + 1) * rows, :] = plane[
                 target * rows : (target + 1) * rows
             ]
+
+    plane_of(full_ref, 0)
+    plane_of(other_ref, 1)
     for target in range(nxy):
         out_ref[target, 2 * rows : 2 * rows + 8, :] = jnp.full((8, NY), top_ref[0], F32)
 
 
-def collect_kernel(nxy, got_ref, sum_ref, pull_ref):
+def collect_kernel(nxy, got_ref, weight_ref, obs_ref, sum_ref):
     rows = NX // nxy
     total = got_ref[0, : 2 * rows, :]
     for source in range(1, nxy):
         total = total + got_ref[source, : 2 * rows, :]
-    sum_ref[:rows] = total[:rows]
+    sum_ref[: 2 * rows] = total
+    for source in range(nxy):
+        place = 2 * rows + source
+        sum_ref[place : place + 1, :] = got_ref[source, 2 * rows : 2 * rows + 1, :]
+    part = weight_ref.shape[1]
+    start = 2 * rows + nxy
+    sum_ref[start : start + part] = weight_ref[0]
+    sum_ref[start + part : start + 2 * part] = obs_ref[0]
+
+
+def residual_kernel(nxy, nh, *refs):
+    rows = NX // nxy
+    part = rows // nh
+    start = 2 * rows + nxy
+    sums = refs[:nh]
+    pred_ref, pull_ref, weight_ref, tops_ref, send_ref, meas_ref = refs[nh:]
+    chip = lax.axis_index("h")
+    total = sums[0][: 2 * rows]
+    for step in range(1, nh):
+        total = total + sums[step][: 2 * rows]
+    for step in range(nh):
+        tops_ref[step * nxy : (step + 1) * nxy] = sums[step][2 * rows : start]
+        place = pl.ds(pl.multiple_of(lax.rem(chip + (nh - step), nh) * part, part), part)
+        weight_ref[place, :] = sums[step][start : start + part]
+        meas_ref[place, :] = sums[step][start + part :]
+    weight = weight_ref[...]
+    pred = total[:rows]
+    pred_ref[...] = pred
     pull_ref[...] = total[rows:]
-    for source in range(nxy):
-        sum_ref[rows + source : rows + source + 1, :] = got_ref[source, 2 * rows : 2 * rows + 1, :]
-
-
-def residual_kernel(nxy, nh, *refs):
-    rows = NX // nxy
-    part = rows // nh
-    sums = refs[:nh]
-    data = refs[nh : 2 * nh]
-    pred_ref, weight_ref, tops_ref, send_ref = refs[2 * nh : 2 * nh + 4]
-    meas_ref = refs[2 * nh + 4]
-    chip = lax.axis_index("h")
-    total = sums[0][:rows]
-    for step in range(1, nh):
-        total = total + sums[step][:rows]
-    for step in range(nh):
-        tops_ref[step * nxy : (step + 1) * nxy] = sums[step][rows:]
-        place = pl.ds(pl.multiple_of(lax.rem(chip + (nh - step), nh) * part, part), part)
-        weight_ref[place, :] = data[step][:part]
-        meas_ref[place, :] = data[step][part:]
-    weight = weight_ref[...]
-    pred_ref[...] = total
-    res = weight * (weight * (total - meas_ref[...]))
+    res = weight * (weight * (pred - meas_ref[...]))
     for target in range(nxy):
         send_ref[target] = res
 
 
 def power_kernel(layers, tops_ref, power_ref):
     kx, ky, *_ = wave_grid(NX)
-    for start in range(0, NX, 64):
-        ks = jnp.sqrt(kx[start : start + 64] ** 2 + ky[start : start + 64] ** 2)
+
+    def block(start, count):
+        ks = jnp.sqrt(kx[start : start + count] ** 2 + ky[start : start + count] ** 2)
         double = -2.0 * ks
 
-        def add(layer, total):
-            return total + jnp.exp(double * tops_ref[pl.ds(layer, 1), :])
-
-        total = lax.fori_loop(0, layers, add, jnp.zeros_like(ks))
+        def add(step, total):
+            for layer in range(4):
+                total = total + jnp.exp(double * tops_ref[pl.ds(4 * step + layer, 1), :])
+            return total
+
+        total = lax.fori_loop(0, layers // 4, add, jnp.zeros_like(ks))
         rise = 1.0 - jnp.exp(-ks)
-        power_ref[start : start + 64] = (16.0 * (rise * rise)) * total
+        return (16.0 * (rise * rise)) * total
+
+    for half in (0, HX):
+        for start in range(half, half + QX, 64):
+            value = block(start, 64)
+            power_ref[start : start + 64] = value
+            power_ref[start + QX : start + QX + 64] = value
+    value = block(QX, 8)
+    row = lax.broadcasted_iota(jnp.int32, value.shape, 0)
+    power_ref[QX : QX + 8] = jnp.where(row == 0, value, power_ref[QX : QX + 8])
 
 
 def adjoint_kernel(
@@ -285,19 +308,15 @@
     rows = NX // nxy
     part = rows // nh
     pieces = refs[:4]
-    pulls = refs[4 : 4 + nh]
-    dens_ref, weight_ref = refs[4 + nh : 6 + nh]
-    share_ref, send_ref, data_ref, grad_ref, line_ref, image_ref, scratch = refs[6 + nh :]
+    pull_ref, dens_ref, weight_ref = refs[4:7]
+    share_ref, send_ref, data_ref, grad_ref, line_ref, image_ref, scratch = refs[7:]
     total = pieces[0][...] + pieces[1][...] + (pieces[2][...] + pieces[3][...])
     data = total[:QX]
     line = total[QX:]
     dens = dens_ref[0]
     quad = 1.0 / (dens * dens + 0.25)
     grad = data + 0.5 * (quad * dens)
-    pulled = pulls[0][...]
-    for step in range(1, nh):
-        pulled = pulled + pulls[step][...]
-    image = line + pulled
+    image = line + pull_ref[...]
     weight = weight_ref[...]
     share_ref[...] = jnp.broadcast_to(
         share(grad, quad, image, weight, scratch, part), share_ref.shape
@@ -384,7 +403,7 @@
 SMEM = pl.BlockSpec(memory_space=pltpu.SMEM)
 
 
-def call(kernel, outs, *args, scratch=(), scalars=()):
+def call(kernel, outs, *args, scratch=(), scalars=(), mib=8):
     shapes = [jax.ShapeDtypeStruct(shape, F32) for shape in outs]
     return pl.pallas_call(
         kernel,
@@ -392,6 +411,7 @@
         in_specs=[SMEM if place in scalars else VMEM for place in range(len(args))],
         out_specs=[VMEM] * len(outs),
         scratch_shapes=[pltpu.VMEM(shape, F32) for shape in scratch],
+        compiler_params=pltpu.CompilerParams(vmem_limit_bytes=mib << 20),
     )(*args)
 
 
@@ -432,19 +452,19 @@
         bind(start_kernel, nxy),
         [(nxy, 2 * rows + 8, NY)],
         *layers, layer_top, decay, own, fx, bx, ty,
-        scratch=[(NX, NY)], scalars=(4,),
-    )
-    data = from_chips(jnp.concatenate([data_weight[0], observed[0]], axis=0), nh)
+        scratch=[(NX, NY)] * 2, scalars=(4,),
+    )
     got = exchange(message, XY)
-    sums, pulled = call(bind(collect_kernel, nxy), [(rows + nxy, NY), (rows, NY)], got)
+    (sums,) = call(
+        bind(collect_kernel, nxy), [(2 * rows + nxy + 2 * rows // nh, NY)], got, data_weight, observed
+    )
     sums = from_chips(sums, nh)
-    pred, weight, tops, message = call(
+    pred, pulled, weight, tops, message = call(
         bind(residual_kernel, nxy, nh),
-        [(rows, NY), (rows, NY), (nxy * nh, NY), (nxy, rows, NY)],
-        *sums, *data, scratch=[(rows, NY)],
+        [(rows, NY), (rows, NY), (rows, NY), (nxy * nh, NY), (nxy, rows, NY)],
+        *sums, scratch=[(rows, NY)],
     )
     got = exchange(message, XY)
-    pulls = from_chips(after(pulled, message), nh)
     (power,) = call(bind(power_kernel, nxy * nh), [(NX, NY)], tops)
     adjoint = lambda plane: from_comps(
         call(
@@ -458,7 +478,7 @@
     shares, message, data_grad, grad, line, image = call(
         bind(gradient_kernel, nxy, nh),
         [(devices, 128), (nxy, rows, NY), (QX, NY), (QX, NY), (rows, NY), (rows, NY)],
-        *pieces, *pulls, density, weight, scratch=[(rows, NY)],
+        *pieces, pulled, density, weight, scratch=[(rows, NY)],
     )
     shares = exchange(shares, ALL)
     dens, pull, alpha = call(

time: 213 us -> 182 us (0.85)
  Pallas kernels: 51.4 us -> 20 us
  blocking collectives: 75.9 us -> 66.6 us
  local copies, waits for them, and re-layouts: 6.23 us -> 13.8 us
  waiting for transfers between devices: 28.3 us -> 32.5 us
  starting transfers between devices: 49.2 us -> 46.3 us
    pallas_call x14, Pallas kernels: 51.4 us -> 20 us  [call(): pl.pallas_call(kernel, out_shape=shapes, in_specs=[SMEM if place in scala...]
    all_to_all x3, blocking collectives: 75.9 us -> 66.6 us  [exchange(): return lax.all_to_all(value, axes, 0, 0, tiled=True)]
    ppermute x12 -> x6, waiting for transfers between devices: 15.1 us -> 6.07 us  [from_chips(): lax.ppermute(value, 'h', [(i, (i + step) % nh) for i in range(nh)])]
    ppermute x12, waiting for transfers between devices: 10.7 us -> 19.4 us  [from_comps(): lax.ppermute(values[step], COMP, [(i, i ^ step) for i in range(4)])]
    unnamed x62 -> x56, local copies, waits for them, and re-layouts: 6.23 us -> 13.8 us
    ppermute x12 -> x6, starting transfers between devices: 20.1 us -> 15 us  [from_chips(): lax.ppermute(value, 'h', [(i, (i + step) % nh) for i in range(nh)])]
    all_to_all x3, waiting for transfers between devices: 2.45 us -> 7.08 us  [exchange(): return lax.all_to_all(value, axes, 0, 0, tiled=True)]
  transfers between devices with their start and end apart: 27 -> 21, of which waited for: 13 -> 11; matrix products, arithmetic and copies ran while one was open for 0% -> 0% of each run, Pallas kernels for 13% -> 6%
where the time goes in v2:
time: 182 us; the launch traced here: 181 us
  blocking collectives  66.6 us (37%)
  starting transfers between devices  46.3 us (25%)
  waiting for transfers between devices  32.5 us (18%)
  Pallas kernels  20 us (11%)
  local copies, waits for them, and re-layouts  13.8 us (8%)
    all_to_all x3, blocking collectives, exchange(): return lax.all_to_all(value, axes, 0, 0, tiled=True)  66.6 us
    pallas_call x14, Pallas kernels, call(): pl.pallas_call(kernel, out_shape=shapes, in_specs=[SMEM if place in scala...  20 us
    ppermute x12, waiting for transfers between devices, from_comps(): lax.ppermute(values[step], COMP, [(i, i ^ step) for i in range(4)])  19.4 us
    ppermute x12, starting transfers between devices, from_comps(): lax.ppermute(values[step], COMP, [(i, i ^ step) for i in range(4)])  16.5 us
    ppermute x6, starting transfers between devices, from_chips(): lax.ppermute(value, 'h', [(i, (i + step) % nh) for i in range(nh)])  15 us
    all_to_all x3, starting transfers between devices, exchange(): return lax.all_to_all(value, axes, 0, 0, tiled=True)  14.7 us
    unnamed x56, local copies, waits for them, and re-layouts  13.8 us
    all_to_all x3, waiting for transfers between devices, exchange(): return lax.all_to_all(value, axes, 0, 0, tiled=True)  7.08 us
  transfers between devices with their start and end apart: 21, of which 11 were waited for; matrix products, arithmetic and copies ran while one was open for 0% of the time, Pallas kernels for 6%

profile of v2, /device:TPU:1, one launch (start us, length us, event | category | flops | bytes accessed | tf_op | source)
XLA Modules:
  0.0 180.8 jit_solution(4981493366654926881)
XLA Ops:
  0.6 3.1 %collective-permute-start.2 = (f32[128,256]{1,0:T(8,128)}, f32[128,256]{1,0:T(8,128)S(1)}, u32[]{:S(2)}, u32[]{:S(2)}) collective-permute-start(f32[128,256]{1,0:T(8,128)} %bitcast.9), channel_id=1, source_target_pairs={{0,3},{1,2},{2,1},{3,0},{4,7},{5,6},{6,5},{7,4},{8,11},{9,10},{10,... | collective-permute-start | bytes 393224 | tf_op jit(solution)/shard_map/ppermute | solution.py:420
  3.7 1.5 collective-permute-start.1
  6.6 1.2 copy-done.6
  7.8 3.1 %collective-permute-done.1.m2 = f32[128,256]{1,0:T(8,128)S(1)} collective-permute-done((f32[128,256]{1,0:T(8,128)}, f32[128,256]{1,0:T(8,128)S(1)}, u32[]{:S(2)}, u32[]{:S(2)}) %collective-permute-start.1) | collective-permute-done | bytes 131104 | tf_op jit(solution)/shard_map/ppermute | solution.py:420
  14.8 2.9 %shard_map.87 = f32[16,72,256]{2,1,0:T(8,128)S(1)} custom-call(f32[128,256]{1,0:T(8,128)S(1)} %bitcast.12, f32[128,256]{1,0:T(8,128)S(1)} %collective-permute-done.m1, f32[128,256]{1,0:T(8,128)S(1)} %collective-permute-done.1.m2, f32[128,256]{1,0:T(8,128)S(1)} %collective-permute-done.2.m3, f32[1]{0:T(128)S(6)} %copy.11.top_ref, ...), custom_call_target="tpu_custom_call" | custom-call | tf_op jit(solution)/shard_map/pallas_call | solution.py:408
  17.8 22.7 %all_to_all.42.got_ref = f32[16,72,256]{2,1,0:T(8,128)S(1)} all-to-all(f32[16,72,256]{2,1,0:T(8,128)S(1)} %shard_map.87), channel_id=1, replica_groups=mesh['x'=4,'y'=4,'h'=4,'l'=2,'k'=2] {'x','y'}, dimensions={0} | all-to-all | bytes 2359296 | tf_op jit(solution)/shard_map/all_to_all | solution.py:431
  40.6 7.3 %collective-permute-start.5 = (f32[96,256]{1,0:T(8,128)S(1)}, f32[96,256]{1,0:T(8,128)S(1)}, u32[]{:S(2)}, u32[]{:S(2)}) collective-permute-start(f32[96,256]{1,0:T(8,128)S(1)} %shard_map.88.refs_0_), channel_id=1, source_target_pairs={{0,12},{4,0},{8,4},{12,8},{1,13},{5,1},{9,5},{13,9},{2,14},{6,2},{... | collective-permute-start | bytes 294920 | tf_op jit(solution)/shard_map/ppermute | solution.py:426
  48.9 2.3 %collective-permute-start.3 = (f32[96,256]{1,0:T(8,128)S(1)}, f32[96,256]{1,0:T(8,128)S(1)}, u32[]{:S(2)}, u32[]{:S(2)}) collective-permute-start(f32[96,256]{1,0:T(8,128)S(1)} %shard_map.88.refs_0_), channel_id=1, source_target_pairs={{0,4},{4,8},{8,12},{12,0},{1,5},{5,9},{9,13},{13,1},{2,6},{6,10},{... | collective-permute-start | bytes 294920 | tf_op jit(solution)/shard_map/ppermute | solution.py:426
  51.1 4.4 %collective-permute-done.5.refs_3_ = f32[96,256]{1,0:T(8,128)S(1)} collective-permute-done((f32[96,256]{1,0:T(8,128)S(1)}, f32[96,256]{1,0:T(8,128)S(1)}, u32[]{:S(2)}, u32[]{:S(2)}) %collective-permute-start.5) | collective-permute-done | bytes 98336 | tf_op jit(solution)/shard_map/ppermute | solution.py:426
  57.9 4.2 %all-to-all-start.1 = ((f32[16,32,256]{2,1,0:T(8,128)}), f32[16,32,256]{2,1,0:T(8,128)}, u32[]{:S(2)}, u32[]{:S(2)}) async-start(f32[16,32,256]{2,1,0:T(8,128)} %get-tuple-element.35), calls=%async_computation.1 | async-start | bytes 1048576 | tf_op jit(solution)/shard_map/all_to_all | solution.py:431
  62.1 3.6 %shard_map.90.power_ref = f32[512,256]{1,0:T(8,128)S(1)} custom-call(f32[64,256]{1,0:T(8,128)S(1)} %get-tuple-element.36.tops_ref), custom_call_target="tpu_custom_call" | custom-call | tf_op jit(solution)/shard_map/pallas_call | solution.py:408
  65.7 5.4 %all-to-all-done.1.res_ref = f32[16,32,256]{2,1,0:T(8,128)} async-done(((f32[16,32,256]{2,1,0:T(8,128)}), f32[16,32,256]{2,1,0:T(8,128)}, u32[]{:S(2)}, u32[]{:S(2)}) %all-to-all-start.1) | async-done | bytes 524320 | tf_op jit(solution)/shard_map/all_to_all | solution.py:431
  71.1 1.4 copy-done.7
  72.5 3.4 %shard_map.91 = (f32[160,256]{1,0:T(8,128)S(1)}, f32[160,256]{1,0:T(8,128)S(1)}, f32[160,256]{1,0:T(8,128)S(1)}, f32[160,256]{1,0:T(8,128)S(1)}) custom-call(f32[16,32,256]{2,1,0:T(8,128)} %all-to-all-done.1.res_ref, f32[512,256]{1,0:T(8,128)S(1)} %get-tuple-element.33.decay_ref, f32[512,256]{1,0:T(8,128)S(1)} %get-tuple-element.34.own_ref, ...), custom_call_target="tpu_custom_call" | custom-call | tf_op jit(solution)/shard_map/pallas_call | solution.py:408
  75.9 5.4 %collective-permute-start.6 = (f32[160,256]{1,0:T(8,128)S(1)}, f32[160,256]{1,0:T(8,128)S(1)}, u32[]{:S(2)}, u32[]{:S(2)}) collective-permute-start(f32[160,256]{1,0:T(8,128)S(1)} %get-tuple-element.39), channel_id=1, source_target_pairs={{0,1},{1,0},{2,3},{3,2},{4,5},{5,4},{6,7},{7,6},{8,9},{9,8},{10,11... | collective-permute-start | bytes 491528 | tf_op jit(solution)/shard_map/ppermute | solution.py:420
  81.3 1.5 collective-permute-start.7
  83.1 4.0 %collective-permute-done.7.refs_2_ = f32[160,256]{1,0:T(8,128)S(1)} collective-permute-done((f32[160,256]{1,0:T(8,128)S(1)}, f32[160,256]{1,0:T(8,128)S(1)}, u32[]{:S(2)}, u32[]{:S(2)}) %collective-permute-start.7) | collective-permute-done | bytes 163872 | tf_op jit(solution)/shard_map/ppermute | solution.py:420
  87.1 3.7 %collective-permute-done.8.refs_3_ = f32[160,256]{1,0:T(8,128)S(1)} collective-permute-done((f32[160,256]{1,0:T(8,128)S(1)}, f32[160,256]{1,0:T(8,128)S(1)}, u32[]{:S(2)}, u32[]{:S(2)}) %collective-permute-start.8) | collective-permute-done | bytes 163872 | tf_op jit(solution)/shard_map/ppermute | solution.py:420
  91.9 21.2 %all_to_all.43 = f32[256,1,128]{2,1,0:T(1,128)S(1)} all-to-all(f32[256,1,128]{2,1,0:T(1,128)S(1)} %bitcast.15), channel_id=1, replica_groups=mesh['x'=4,'y'=4,'h'=4,'l'=2,'k'=2] {'x','y','h','l','k'}, dimensions={0} | all-to-all | bytes 262144 | tf_op jit(solution)/shard_map/all_to_all | solution.py:431
  113.9 4.2 %all-to-all-start.4 = ((f32[16,32,256]{2,1,0:T(8,128)}), f32[16,32,256]{2,1,0:T(8,128)}, u32[]{:S(2)}, u32[]{:S(2)}) async-start(f32[16,32,256]{2,1,0:T(8,128)} %copy-done.12), calls=%async_computation.4 | async-start | bytes 1048576 | tf_op jit(solution)/shard_map/all_to_all | solution.py:431
  118.1 1.7 collective-permute-start.11
  120.4 3.9 %collective-permute-done.11.p3 = f32[128,256]{1,0:T(8,128)S(1)} collective-permute-done((f32[128,256]{1,0:T(8,128)S(1)}, f32[128,256]{1,0:T(8,128)S(1)}, u32[]{:S(2)}, u32[]{:S(2)}) %collective-permute-start.11) | collective-permute-done | bytes 131104 | tf_op jit(solution)/shard_map/ppermute | solution.py:420
  124.2 3.0 %collective-permute-done.10.p2 = f32[128,256]{1,0:T(8,128)S(1)} collective-permute-done((f32[128,256]{1,0:T(8,128)S(1)}, f32[128,256]{1,0:T(8,128)S(1)}, u32[]{:S(2)}, u32[]{:S(2)}) %collective-permute-start.10) | collective-permute-done | bytes 131104 | tf_op jit(solution)/shard_map/ppermute | solution.py:420
  127.2 1.7 shard_map.94
  129.7 6.2 %all-to-all-start.3 = ((f32[16,32,256]{2,1,0:T(8,128)}), f32[16,32,256]{2,1,0:T(8,128)}, u32[]{:S(2)}, u32[]{:S(2)}) async-start(f32[16,32,256]{2,1,0:T(8,128)} %copy-done.9), calls=%async_computation.3 | async-start | bytes 1048576 | tf_op jit(solution)/shard_map/all_to_all | solution.py:431
  136.0 1.4 copy-done.8
  137.4 4.1 %shard_map.96 = (f32[160,256]{1,0:T(8,128)S(1)}, f32[160,256]{1,0:T(8,128)}, f32[160,256]{1,0:T(8,128)}, f32[160,256]{1,0:T(8,128)}) custom-call(f32[16,32,256]{2,1,0:T(8,128)} %all-to-all-done.4.res_ref, f32[512,256]{1,0:T(8,128)S(1)} %get-tuple-element.33.decay_ref, f32[512,256]{1,0:T(8,128)S(1)} %get-tuple-element.34.own_ref, ...), custom_call_target="tpu_custom_call" | custom-call | tf_op jit(solution)/shard_map/pallas_call | solution.py:408
  143.6 1.1 collective-permute-start.17
  144.7 1.7 all-to-all-done.3.got_ref
  147.6 4.4 %collective-permute-start.13 = (f32[32,256]{1,0:T(8,128)S(1)}, f32[32,256]{1,0:T(8,128)S(1)}, u32[]{:S(2)}, u32[]{:S(2)}) collective-permute-start(f32[32,256]{1,0:T(8,128)S(1)} %shard_map.95.refs_0_), channel_id=1, source_target_pairs={{0,8},{4,12},{8,0},{12,4},{1,9},{5,13},{9,1},{13,5},{2,10},{6,14},... | collective-permute-start | bytes 98312 | tf_op jit(solution)/shard_map/ppermute | solution.py:426
  152.0 1.7 collective-permute-done.17.u3
  157.3 22.7 %all_to_all.44 = f32[256,1,128]{2,1,0:T(1,128)S(1)} all-to-all(f32[256,1,128]{2,1,0:T(1,128)S(1)} %bitcast.16), channel_id=1, replica_groups=mesh['x'=4,'y'=4,'h'=4,'l'=2,'k'=2] {'x','y','h','l','k'}, dimensions={0} | all-to-all | bytes 262144 | tf_op jit(solution)/shard_map/all_to_all | solution.py:431
  (83 shorter events, 19.1 us)
Async XLA Ops:
  0.6 7.1 %collective-permute-start.2 = (f32[128,256]{1,0:T(8,128)}, f32[128,256]{1,0:T(8,128)S(1)}, u32[]{:S(2)}, u32[]{:S(2)}) collective-permute-start(f32[128,256]{1,0:T(8,128)} %bitcast.9), channel_id=1, source_target_pairs={{0,3},{1,2},{2,1},{3,0},{4,7},{5,6},{6,5},{7,4},{8,11},{9,10},{10,... | collective-permute-start | bytes 393224 | tf_op jit(solution)/shard_map/ppermute | solution.py:420
  3.7 7.1 %collective-permute-start.1 = (f32[128,256]{1,0:T(8,128)}, f32[128,256]{1,0:T(8,128)S(1)}, u32[]{:S(2)}, u32[]{:S(2)}) collective-permute-start(f32[128,256]{1,0:T(8,128)} %bitcast.10), channel_id=1, source_target_pairs={{0,2},{1,3},{2,0},{3,1},{4,6},{5,7},{6,4},{7,5},{8,10},{9,11},{10,... | collective-permute-start | bytes 393224 | tf_op jit(solution)/shard_map/ppermute | solution.py:420
  5.3 5.5 %collective-permute-start = (f32[128,256]{1,0:T(8,128)}, f32[128,256]{1,0:T(8,128)S(1)}, u32[]{:S(2)}, u32[]{:S(2)}) collective-permute-start(f32[128,256]{1,0:T(8,128)} %bitcast.11), channel_id=1, source_target_pairs={{0,1},{1,0},{2,3},{3,2},{4,5},{5,4},{6,7},{7,6},{8,9},{9,8},{10,11... | collective-permute-start | bytes 393224 | tf_op jit(solution)/shard_map/ppermute | solution.py:420
  17.7 22.7 %copy-start.17 = (f32[1,8,256]{2,1,0:T(8,128)S(1)}, f32[1,8,256]{2,1,0:T(8,128)}, u32[]{:S(2)}) copy-start(f32[1,8,256]{2,1,0:T(8,128)} %w_ref.1) | copy-start | bytes 24580
  17.8 22.7 %copy-start.18 = (f32[1,8,256]{2,1,0:T(8,128)S(1)}, f32[1,8,256]{2,1,0:T(8,128)}, u32[]{:S(2)}) copy-start(f32[1,8,256]{2,1,0:T(8,128)} %obs_ref.3) | copy-start | bytes 24580
  40.5 30.6 %copy-start.1 = (bf16[4,256,256]{2,1,0:T(8,128)(2,1)S(1)}, bf16[4,256,256]{2,1,0:T(8,128)(2,1)}, u32[]{:S(2)}) copy-start(bf16[4,256,256]{2,1,0:T(8,128)(2,1)} %constant.8.clone.ty) | copy-start | bytes 1572868
  40.6 30.5 %copy-start.3 = (bf16[4,256,256]{2,1,0:T(8,128)(2,1)S(1)}, bf16[4,256,256]{2,1,0:T(8,128)(2,1)}, u32[]{:S(2)}) copy-start(bf16[4,256,256]{2,1,0:T(8,128)(2,1)} %constant.7.clone.bx) | copy-start | bytes 1572868
  40.6 30.5 %copy-start.5 = (bf16[4,256,256]{2,1,0:T(8,128)(2,1)S(1)}, bf16[4,256,256]{2,1,0:T(8,128)(2,1)}, u32[]{:S(2)}) copy-start(bf16[4,256,256]{2,1,0:T(8,128)(2,1)} %constant.6.clone.fx) | copy-start | bytes 1572868
  40.6 14.9 %collective-permute-start.5 = (f32[96,256]{1,0:T(8,128)S(1)}, f32[96,256]{1,0:T(8,128)S(1)}, u32[]{:S(2)}, u32[]{:S(2)}) collective-permute-start(f32[96,256]{1,0:T(8,128)S(1)} %shard_map.88.refs_0_), channel_id=1, source_target_pairs={{0,12},{4,0},{8,4},{12,8},{1,13},{5,1},{9,5},{13,9},{2,14},{6,2},{... | collective-permute-start | bytes 294920 | tf_op jit(solution)/shard_map/ppermute | solution.py:426
  47.9 8.5 %collective-permute-start.4 = (f32[96,256]{1,0:T(8,128)S(1)}, f32[96,256]{1,0:T(8,128)S(1)}, u32[]{:S(2)}, u32[]{:S(2)}) collective-permute-start(f32[96,256]{1,0:T(8,128)S(1)} %shard_map.88.refs_0_), channel_id=1, source_target_pairs={{0,8},{4,12},{8,0},{12,4},{1,9},{5,13},{9,1},{13,5},{2,10},{6,14},... | collective-permute-start | bytes 294920 | tf_op jit(solution)/shard_map/ppermute | solution.py:426
  48.9 7.5 %collective-permute-start.3 = (f32[96,256]{1,0:T(8,128)S(1)}, f32[96,256]{1,0:T(8,128)S(1)}, u32[]{:S(2)}, u32[]{:S(2)}) collective-permute-start(f32[96,256]{1,0:T(8,128)S(1)} %shard_map.88.refs_0_), channel_id=1, source_target_pairs={{0,4},{4,8},{8,12},{12,0},{1,5},{5,9},{9,13},{13,1},{2,6},{6,10},{... | collective-permute-start | bytes 294920 | tf_op jit(solution)/shard_map/ppermute | solution.py:426
  57.9 32.9 %copy-start.15 = (f32[32,256]{1,0:T(8,128)}, f32[32,256]{1,0:T(8,128)S(1)}, u32[]{:S(2)}) copy-start(f32[32,256]{1,0:T(8,128)S(1)} %get-tuple-element.43.refs_6_.refs_5_) | copy-start | bytes 98308
  57.9 13.2 %all-to-all-start.1 = ((f32[16,32,256]{2,1,0:T(8,128)}), f32[16,32,256]{2,1,0:T(8,128)}, u32[]{:S(2)}, u32[]{:S(2)}) async-start(f32[16,32,256]{2,1,0:T(8,128)} %get-tuple-element.35), calls=%async_computation.1 | async-start | bytes 1048576 | tf_op jit(solution)/shard_map/all_to_all | solution.py:431
  75.9 7.1 %collective-permute-start.6 = (f32[160,256]{1,0:T(8,128)S(1)}, f32[160,256]{1,0:T(8,128)S(1)}, u32[]{:S(2)}, u32[]{:S(2)}) collective-permute-start(f32[160,256]{1,0:T(8,128)S(1)} %get-tuple-element.39), channel_id=1, source_target_pairs={{0,1},{1,0},{2,3},{3,2},{4,5},{5,4},{6,7},{7,6},{8,9},{9,8},{10,11... | collective-permute-start | bytes 491528 | tf_op jit(solution)/shard_map/ppermute | solution.py:420
  81.3 5.8 %collective-permute-start.7 = (f32[160,256]{1,0:T(8,128)S(1)}, f32[160,256]{1,0:T(8,128)S(1)}, u32[]{:S(2)}, u32[]{:S(2)}) collective-permute-start(f32[160,256]{1,0:T(8,128)S(1)} %get-tuple-element.40), channel_id=1, source_target_pairs={{0,2},{1,3},{2,0},{3,1},{4,6},{5,7},{6,4},{7,5},{8,10},{9,11},{10,... | collective-permute-start | bytes 491528 | tf_op jit(solution)/shard_map/ppermute | solution.py:420
  82.8 8.0 %collective-permute-start.8 = (f32[160,256]{1,0:T(8,128)S(1)}, f32[160,256]{1,0:T(8,128)S(1)}, u32[]{:S(2)}, u32[]{:S(2)}) collective-permute-start(f32[160,256]{1,0:T(8,128)S(1)} %get-tuple-element.41), channel_id=1, source_target_pairs={{0,3},{1,2},{2,1},{3,0},{4,7},{5,6},{6,5},{7,4},{8,11},{9,10},{10,... | collective-permute-start | bytes 491528 | tf_op jit(solution)/shard_map/ppermute | solution.py:420
  91.8 21.2 %copy-start.23 = (f32[32,256]{1,0:T(8,128)}, f32[32,256]{1,0:T(8,128)S(1)}, u32[]{:S(2)}) copy-start(f32[32,256]{1,0:T(8,128)S(1)} %get-tuple-element.56.line_ref) | copy-start | bytes 98308
  91.8 21.4 %copy-start.21 = (f32[32,256]{1,0:T(8,128)}, f32[32,256]{1,0:T(8,128)S(1)}, u32[]{:S(2)}) copy-start(f32[32,256]{1,0:T(8,128)S(1)} %get-tuple-element.62.first_ref) | copy-start | bytes 98308
  113.9 15.9 %all-to-all-start.4 = ((f32[16,32,256]{2,1,0:T(8,128)}), f32[16,32,256]{2,1,0:T(8,128)}, u32[]{:S(2)}, u32[]{:S(2)}) async-start(f32[16,32,256]{2,1,0:T(8,128)} %copy-done.12), calls=%async_computation.4 | async-start | bytes 1048576 | tf_op jit(solution)/shard_map/all_to_all | solution.py:431
  118.1 6.1 %collective-permute-start.11 = (f32[128,256]{1,0:T(8,128)S(1)}, f32[128,256]{1,0:T(8,128)S(1)}, u32[]{:S(2)}, u32[]{:S(2)}) collective-permute-start(f32[128,256]{1,0:T(8,128)S(1)} %get-tuple-element.46.p0.pull_ref), channel_id=1, source_target_pairs={{0,3},{1,2},{2,1},{3,0},{4,7},{5,6},{6,5},{7,4},{8,11},{9,10},{10,... | collective-permute-start | bytes 393224 | tf_op jit(solution)/shard_map/ppermute | solution.py:420
  119.8 7.4 %collective-permute-start.10 = (f32[128,256]{1,0:T(8,128)S(1)}, f32[128,256]{1,0:T(8,128)S(1)}, u32[]{:S(2)}, u32[]{:S(2)}) collective-permute-start(f32[128,256]{1,0:T(8,128)S(1)} %get-tuple-element.46.p0.pull_ref), channel_id=1, source_target_pairs={{0,2},{1,3},{2,0},{3,1},{4,6},{5,7},{6,4},{7,5},{8,10},{9,11},{10,... | collective-permute-start | bytes 393224 | tf_op jit(solution)/shard_map/ppermute | solution.py:420
  120.4 6.8 %collective-permute-start.9 = (f32[128,256]{1,0:T(8,128)S(1)}, f32[128,256]{1,0:T(8,128)S(1)}, u32[]{:S(2)}, u32[]{:S(2)}) collective-permute-start(f32[128,256]{1,0:T(8,128)S(1)} %get-tuple-element.46.p0.pull_ref), channel_id=1, source_target_pairs={{0,1},{1,0},{2,3},{3,2},{4,5},{5,4},{6,7},{7,6},{8,9},{9,8},{10,11... | collective-permute-start | bytes 393224 | tf_op jit(solution)/shard_map/ppermute | solution.py:420
  129.7 16.7 %all-to-all-start.3 = ((f32[16,32,256]{2,1,0:T(8,128)}), f32[16,32,256]{2,1,0:T(8,128)}, u32[]{:S(2)}, u32[]{:S(2)}) async-start(f32[16,32,256]{2,1,0:T(8,128)} %copy-done.9), calls=%async_computation.3 | async-start | bytes 1048576 | tf_op jit(solution)/shard_map/all_to_all | solution.py:431
  142.2 37.8 %copy-start.20 = (f32[32,256]{1,0:T(8,128)S(1)}, f32[32,256]{1,0:T(8,128)}, u32[]{:S(2)}) copy-start(f32[32,256]{1,0:T(8,128)} %copy-done.19) | copy-start | bytes 98308
  142.2 37.8 %copy-start.22 = (f32[32,256]{1,0:T(8,128)S(1)}, f32[32,256]{1,0:T(8,128)}, u32[]{:S(2)}) copy-start(f32[32,256]{1,0:T(8,128)} %copy-done.21) | copy-start | bytes 98308
  142.2 37.8 %copy-start.27 = (f32[8,128]{1,0:T(8,128)S(1)}, f32[8,128]{1,0:T(8,128)}, u32[]{:S(2)}) copy-start(f32[8,128]{1,0:T(8,128)} %copy-done.25) | copy-start | bytes 12292
  142.2 9.8 %collective-permute-start.15 = (f32[160,256]{1,0:T(8,128)}, f32[160,256]{1,0:T(8,128)S(1)}, u32[]{:S(2)}, u32[]{:S(2)}) collective-permute-start(f32[160,256]{1,0:T(8,128)} %get-tuple-element.50), channel_id=1, source_target_pairs={{0,1},{1,0},{2,3},{3,2},{4,5},{5,4},{6,7},{7,6},{8,9},{9,8},{10,11... | collective-permute-start | bytes 491528 | tf_op jit(solution)/shard_map/ppermute | solution.py:420
  143.0 9.0 %collective-permute-start.16 = (f32[160,256]{1,0:T(8,128)}, f32[160,256]{1,0:T(8,128)S(1)}, u32[]{:S(2)}, u32[]{:S(2)}) collective-permute-start(f32[160,256]{1,0:T(8,128)} %get-tuple-element.51), channel_id=1, source_target_pairs={{0,2},{1,3},{2,0},{3,1},{4,6},{5,7},{6,4},{7,5},{8,10},{9,11},{10,... | collective-permute-start | bytes 491528 | tf_op jit(solution)/shard_map/ppermute | solution.py:420
  143.6 10.1 %collective-permute-start.17 = (f32[160,256]{1,0:T(8,128)}, f32[160,256]{1,0:T(8,128)S(1)}, u32[]{:S(2)}, u32[]{:S(2)}) collective-permute-start(f32[160,256]{1,0:T(8,128)} %get-tuple-element.52), channel_id=1, source_target_pairs={{0,3},{1,2},{2,1},{3,0},{4,7},{5,6},{6,5},{7,4},{8,11},{9,10},{10,... | collective-permute-start | bytes 491528 | tf_op jit(solution)/shard_map/ppermute | solution.py:420
  147.5 8.8 %collective-permute-start.14 = (f32[32,256]{1,0:T(8,128)S(1)}, f32[32,256]{1,0:T(8,128)S(1)}, u32[]{:S(2)}, u32[]{:S(2)}) collective-permute-start(f32[32,256]{1,0:T(8,128)S(1)} %shard_map.95.refs_0_), channel_id=1, source_target_pairs={{0,12},{4,0},{8,4},{12,8},{1,13},{5,1},{9,5},{13,9},{2,14},{6,2},{... | collective-permute-start | bytes 98312 | tf_op jit(solution)/shard_map/ppermute | solution.py:426
  147.6 8.7 %collective-permute-start.13 = (f32[32,256]{1,0:T(8,128)S(1)}, f32[32,256]{1,0:T(8,128)S(1)}, u32[]{:S(2)}, u32[]{:S(2)}) collective-permute-start(f32[32,256]{1,0:T(8,128)S(1)} %shard_map.95.refs_0_), channel_id=1, source_target_pairs={{0,8},{4,12},{8,0},{12,4},{1,9},{5,13},{9,1},{13,5},{2,10},{6,14},... | collective-permute-start | bytes 98312 | tf_op jit(solution)/shard_map/ppermute | solution.py:426
  152.0 5.2 %collective-permute-start.12 = (f32[32,256]{1,0:T(8,128)S(1)}, f32[32,256]{1,0:T(8,128)S(1)}, u32[]{:S(2)}, u32[]{:S(2)}) collective-permute-start(f32[32,256]{1,0:T(8,128)S(1)} %shard_map.95.refs_0_), channel_id=1, source_target_pairs={{0,4},{4,8},{8,12},{12,0},{1,5},{5,9},{9,13},{13,1},{2,6},{6,10},{... | collective-permute-start | bytes 98312 | tf_op jit(solution)/shard_map/ppermute | solution.py:426
  (17 other events, 47.1 us)

commit v3 on v2

--- a/solution.py
+++ b/solution.py
@@ -131,7 +131,13 @@
     return kx, ky, sine_x, sine_y, nyquist_x, nyquist_y
 
 
-def prepare_kernel(top_ref, decay_ref, own_ref, factors_ref):
+def prepare_kernel(top_ref, *refs):
+    count = 6
+    sources, outs, sems = refs[:count], refs[count : 2 * count], refs[-1]
+    decay_ref, own_ref, factors_ref = refs[2 * count : 2 * count + 3]
+    copies = [pltpu.make_async_copy(sources[i], outs[i], sems.at[i]) for i in range(count)]
+    for copy in copies:
+        copy.start()
     comp = comp_index()
     kx, ky, sine_x, sine_y, nyquist_x, nyquist_y = wave_grid(NX)
     kabs = jnp.sqrt(kx * kx + ky * ky)
@@ -148,6 +154,8 @@
     own_ref[...] = jnp.where(
         comp == 0, 1.0, jnp.where(comp == 1, first, jnp.where(comp == 2, second, third))
     )
+    for copy in copies:
+        copy.wait()
 
 
 def gather_rows(pieces, full_ref):
@@ -156,43 +164,79 @@
         full_ref[pl.ds(pl.multiple_of(jnp.bitwise_xor(comp, step) * QX, QX), QX), :] = piece[...]
 
 
+def forward_plane(field, decay_ref, own_ref, fx, bx, ty):
+    even, odd = to_waves(field, fx, ty)
+    even, odd = component(even * decay_ref[:HX], odd * decay_ref[HX:], own_ref, comp_index())
+    return from_waves(even, odd, bx, ty)
+
+
 def start_kernel(
-    nxy, m0, m1, m2, m3, top_ref, decay_ref, own_ref, fx, bx, ty, out_ref, full_ref, other_ref
+    nxy, m0, m1, m2, m3, top_ref, decay_ref, own_ref, fx, bx, ty, out_ref, full_ref
 ):
     rows = NX // nxy
-    comp = comp_index()
     gather_rows((m0, m1, m2, m3), full_ref)
+    plane = forward_plane(full_ref[...], decay_ref, own_ref, fx, bx, ty)
+    for target in range(nxy):
+        out_ref[target, :rows, :] = plane[target * rows : (target + 1) * rows]
+        out_ref[target, rows : rows + 8, :] = jnp.full((8, NY), top_ref[0], F32)
+
+
+def shift_place(axis, step, rows):
+    size = lax.axis_size(axis)
+    return pl.ds(pl.multiple_of(lax.rem(lax.axis_index(axis) + step, size) * rows, rows), rows)
+
+
+def pull_kernel(full_ref, decay_ref, own_ref, fx, bx, ty, *refs):
+    outs, plane_ref = refs[:-1], refs[-1]
     dens = full_ref[...]
     pull = 0.5 * (dens * (1.0 / (dens * dens + 0.25)))
-    full_ref[...] = dens
-    other_ref[...] = pull
-
-    def plane_of(field_ref, place):
-        even, odd = to_waves(field_ref[...], fx, ty)
-        even, odd = component(even * decay_ref[:HX], odd * decay_ref[HX:], own_ref, comp)
-        plane = from_waves(even, odd, bx, ty)
-        for target in range(nxy):
-            out_ref[target, place * rows : (place + 1) * rows, :] = plane[
-                target * rows : (target + 1) * rows
+    plane_ref[...] = forward_plane(pull, decay_ref, own_ref, fx, bx, ty)
+    for step, out in enumerate(outs):
+        out[...] = plane_ref[shift_place("x", step, out.shape[0]), :]
+
+
+def fold_kernel(count, *refs):
+    parts, outs, total_ref = refs[:count], refs[count:-1], refs[-1]
+    total = parts[0][...]
+    for part in parts[1:]:
+        total = total + part[...]
+    if len(outs) == 1:
+        outs[0][...] = total
+    else:
+        total_ref[...] = total
+        for step, out in enumerate(outs):
+            out[...] = total_ref[shift_place("y", step, out.shape[0]), :]
+
+
+def join_kernel(*refs):
+    out = refs[-1]
+    rows = refs[0].shape[0]
+    for place, part in enumerate(refs[:-1]):
+        out[place * rows : (place + 1) * rows] = part[...]
+
+
+def place_kernel(ny, nx, *refs):
+    out = refs[-1]
+    rows = refs[0].shape[0] // nx
+    x, y = lax.axis_index("x"), lax.axis_index("y")
+    for back_y in range(ny):
+        for back_x in range(nx):
+            block = lax.rem(x + (nx - back_x), nx) * ny + lax.rem(y + (ny - back_y), ny)
+            out[pl.ds(pl.multiple_of(block * rows, rows), rows), :] = refs[back_y][
+                back_x * rows : (back_x + 1) * rows
             ]
-
-    plane_of(full_ref, 0)
-    plane_of(other_ref, 1)
-    for target in range(nxy):
-        out_ref[target, 2 * rows : 2 * rows + 8, :] = jnp.full((8, NY), top_ref[0], F32)
 
 
 def collect_kernel(nxy, got_ref, weight_ref, obs_ref, sum_ref):
     rows = NX // nxy
-    total = got_ref[0, : 2 * rows, :]
+    total = got_ref[0, :rows, :]
     for source in range(1, nxy):
-        total = total + got_ref[source, : 2 * rows, :]
-    sum_ref[: 2 * rows] = total
+        total = total + got_ref[source, :rows, :]
+    sum_ref[:rows] = total
     for source in range(nxy):
-        place = 2 * rows + source
-        sum_ref[place : place + 1, :] = got_ref[source, 2 * rows : 2 * rows + 1, :]
+        sum_ref[rows + source : rows + source + 1, :] = got_ref[source, rows : rows + 1, :]
     part = weight_ref.shape[1]
-    start = 2 * rows + nxy
+    start = rows + nxy
     sum_ref[start : start + part] = weight_ref[0]
     sum_ref[start + part : start + 2 * part] = obs_ref[0]
 
@@ -200,22 +244,20 @@
 def residual_kernel(nxy, nh, *refs):
     rows = NX // nxy
     part = rows // nh
-    start = 2 * rows + nxy
+    start = rows + nxy
     sums = refs[:nh]
-    pred_ref, pull_ref, weight_ref, tops_ref, send_ref, meas_ref = refs[nh:]
+    pred_ref, weight_ref, tops_ref, send_ref, meas_ref = refs[nh:]
     chip = lax.axis_index("h")
-    total = sums[0][: 2 * rows]
+    pred = sums[0][:rows]
     for step in range(1, nh):
-        total = total + sums[step][: 2 * rows]
+        pred = pred + sums[step][:rows]
     for step in range(nh):
-        tops_ref[step * nxy : (step + 1) * nxy] = sums[step][2 * rows : start]
+        tops_ref[step * nxy : (step + 1) * nxy] = sums[step][rows:start]
         place = pl.ds(pl.multiple_of(lax.rem(chip + (nh - step), nh) * part, part), part)
         weight_ref[place, :] = sums[step][start : start + part]
         meas_ref[place, :] = sums[step][start + part :]
     weight = weight_ref[...]
-    pred = total[:rows]
     pred_ref[...] = pred
-    pull_ref[...] = total[rows:]
     res = weight * (weight * (pred - meas_ref[...]))
     for target in range(nxy):
         send_ref[target] = res
@@ -252,8 +294,7 @@
 ):
     rows = NX // nxy
     comp = comp_index()
-    res = res_ref[...].reshape(NX, NY)
-    even, odd = to_waves(res, fx, ty)
+    even, odd = to_waves(res_ref[...], fx, ty)
     even, odd = component(even, odd, own_ref, comp)
     sign = jnp.where((comp == 1) | (comp == 2), -1.0, 1.0)
     even = even * sign
@@ -307,16 +348,19 @@
 def gradient_kernel(nxy, nh, *refs):
     rows = NX // nxy
     part = rows // nh
-    pieces = refs[:4]
-    pull_ref, dens_ref, weight_ref = refs[4:7]
-    share_ref, send_ref, data_ref, grad_ref, line_ref, image_ref, scratch = refs[7:]
+    pieces, pulls = refs[:4], refs[4 : 4 + nh]
+    dens_ref, weight_ref = refs[4 + nh : 6 + nh]
+    share_ref, back_ref, data_ref, grad_ref, line_ref, image_ref, scratch = refs[6 + nh :]
     total = pieces[0][...] + pieces[1][...] + (pieces[2][...] + pieces[3][...])
     data = total[:QX]
     line = total[QX:]
     dens = dens_ref[0]
     quad = 1.0 / (dens * dens + 0.25)
     grad = data + 0.5 * (quad * dens)
-    image = line + pull_ref[...]
+    pulled = pulls[0][...]
+    for step in range(1, nh):
+        pulled = pulled + pulls[step][...]
+    image = line + pulled
     weight = weight_ref[...]
     share_ref[...] = jnp.broadcast_to(
         share(grad, quad, image, weight, scratch, part), share_ref.shape
@@ -325,9 +369,7 @@
     grad_ref[...] = grad
     line_ref[...] = line
     image_ref[...] = image
-    back = weight * (weight * image)
-    for target in range(nxy):
-        send_ref[target] = back
+    back_ref[...] = weight * (weight * image)
 
 
 def move_kernel(shares_ref, dens_ref, grad_ref, dens_out, pull_out, alpha_ref):
@@ -338,19 +380,10 @@
     alpha_ref[...] = jnp.broadcast_to(alpha, alpha_ref.shape)
 
 
-def second_kernel(nxy, p0, p1, p2, p3, decay_ref, own_ref, fx, bx, ty, out_ref, full_ref):
-    comp = comp_index()
+def second_kernel(p0, p1, p2, p3, decay_ref, own_ref, fx, bx, ty, out_ref, full_ref):
     gather_rows((p0, p1, p2, p3), full_ref)
-    even, odd = to_waves(full_ref[...], fx, ty)
-    even, odd = component(even * decay_ref[:HX], odd * decay_ref[HX:], own_ref, comp)
-    out_ref[...] = from_waves(even, odd, bx, ty).reshape(out_ref.shape)
-
-
-def sum_kernel(nxy, got_ref, sum_ref):
-    total = got_ref[0]
-    for source in range(1, nxy):
-        total = total + got_ref[source]
-    sum_ref[...] = total
+    plane = forward_plane(full_ref[...], decay_ref, own_ref, fx, bx, ty)
+    out_ref[...] = plane.reshape(out_ref.shape)
 
 
 def second_gradient_kernel(
@@ -370,17 +403,15 @@
     )
 
 
-def curvature_kernel(nxy, nh, *refs):
-    rows = NX // nxy
-    part = rows // nh
-    pulls = refs[:nh]
-    image_ref, weight_ref, part_ref, share_ref, out_ref, scratch = refs[nh:]
-    image = image_ref[...]
-    for step in range(nh):
-        image = image + pulls[step][...]
+def curvature_kernel(got_ref, image_ref, weight_ref, part_ref, share_ref, out_ref):
+    part = weight_ref.shape[1]
+    image = image_ref[pl.ds(pl.multiple_of(lax.axis_index("h") * part, part), part), :]
+    total = got_ref[0]
+    for source in range(1, got_ref.shape[0]):
+        total = total + got_ref[source]
+    image = image + total
     out_ref[...] = image
-    scratch[...] = weight_ref[...] * image
-    mine = scratch[pl.ds(pl.multiple_of(lax.axis_index("h") * part, part), part), :]
+    mine = weight_ref[0] * image
     lane = lax.broadcasted_iota(jnp.int32, (1, 128), 1)
     share_ref[...] = jnp.broadcast_to(
         jnp.where(lane == 2, jnp.sum(mine * mine), part_ref[:1]), share_ref.shape
@@ -395,22 +426,26 @@
     dens_out[0] = dens_ref[...] - alpha * grad_ref[...]
     place = pl.ds(pl.multiple_of(lax.axis_index("h") * part, part), part)
     pred = pred_ref[place, :] - alpha_ref[:1, :1] * first_ref[place, :]
-    pred = pred - alpha * second_ref[place, :]
+    pred = pred - alpha * second_ref[...]
     err_out[0] = w_ref[0] * (pred - obs_ref[0])
 
 
 VMEM = pl.BlockSpec(memory_space=pltpu.VMEM)
 SMEM = pl.BlockSpec(memory_space=pltpu.SMEM)
-
-
-def call(kernel, outs, *args, scratch=(), scalars=(), mib=8):
-    shapes = [jax.ShapeDtypeStruct(shape, F32) for shape in outs]
+ANY = pl.BlockSpec(memory_space=pl.ANY)
+
+
+def call(kernel, outs, *args, scratch=(), places=(), out=pltpu.VMEM, mib=8):
+    places = dict(places)
+    kinds = [(item, F32) if isinstance(item, tuple) else (item.shape, item.dtype) for item in outs]
     return pl.pallas_call(
         kernel,
-        out_shape=shapes,
-        in_specs=[SMEM if place in scalars else VMEM for place in range(len(args))],
+        out_shape=[out(shape, dtype) for shape, dtype in kinds],
+        in_specs=[places.get(place, VMEM) for place in range(len(args))],
         out_specs=[VMEM] * len(outs),
-        scratch_shapes=[pltpu.VMEM(shape, F32) for shape in scratch],
+        scratch_shapes=[
+            pltpu.VMEM(item, F32) if isinstance(item, tuple) else item for item in scratch
+        ],
         compiler_params=pltpu.CompilerParams(vmem_limit_bytes=mib << 20),
     )(*args)
 
@@ -421,9 +456,11 @@
     ]
 
 
-def from_chips(value, nh):
-    return [value] + [
-        lax.ppermute(value, "h", [(i, (i + step) % nh) for i in range(nh)]) for step in range(1, nh)
+def from_axis(values, axis):
+    size = len(values)
+    return [values[0]] + [
+        lax.ppermute(values[step], axis, [(i, (i + step) % size) for i in range(size)])
+        for step in range(1, size)
     ]
 
 
@@ -431,82 +468,95 @@
     return lax.all_to_all(value, axes, 0, 0, tiled=True)
 
 
-def after(value, *others):
-    return lax.optimization_barrier((value, *others))[0]
+def after(values, *others):
+    if isinstance(values, (list, tuple)):
+        return list(lax.optimization_barrier((tuple(values), others))[0])
+    return lax.optimization_barrier((values, others))[0]
 
 
 def body(density, observed, data_weight, layer_top):
-    nxy = lax.axis_size("x") * lax.axis_size("y")
-    nh = lax.axis_size("h")
+    nx, ny, nh = (lax.axis_size(axis) for axis in DEPTH)
+    nxy = nx * ny
     devices = nxy * nh * 4
     rows = NX // nxy
-    fx, bx, ty = (jnp.asarray(table) for table in make_tables())
+    part = rows // nh
+    tables = [jnp.asarray(table) for table in make_tables()]
     bind = functools.partial
 
-    decay, own, factors = call(
-        prepare_kernel, [(NX, NY), (NX, NY), (3, NX, NY)], layer_top, scalars=(0,)
-    )
-    strip = density[0]
-    layers = from_comps([strip] * 4)
-    (message,) = call(
-        bind(start_kernel, nxy),
-        [(nxy, 2 * rows + 8, NY)],
-        *layers, layer_top, decay, own, fx, bx, ty,
-        scratch=[(NX, NY)] * 2, scalars=(4,),
+    layers = from_comps([density[0]] * 4)
+    kept = [*tables, density, data_weight, observed]
+    *tables, density, data_weight, observed, decay, own, factors = call(
+        prepare_kernel, [*kept, (NX, NY), (NX, NY), (3, NX, NY)], layer_top, *kept,
+        scratch=[pltpu.SemaphoreType.DMA((6,))],
+        places=[(0, SMEM), *((place, ANY) for place in range(1, 7))],
+    )
+    message, full = call(
+        bind(start_kernel, nxy), [(nxy, rows + 8, NY), (NX, NY)],
+        density[0], *layers[1:], layer_top, decay, own, *tables, places=[(4, SMEM)],
     )
     got = exchange(message, XY)
+    parts = call(
+        pull_kernel, [(NX // nx, NY)] * nx, after(full, message), decay, own, *tables,
+        scratch=[(NX, NY)],
+    )
+    parts = call(
+        bind(fold_kernel, nx), [(rows, NY)] * ny, *from_axis(parts, "x"), scratch=[(NX // nx, NY)]
+    )
+    got = after(got, *parts)
     (sums,) = call(
-        bind(collect_kernel, nxy), [(2 * rows + nxy + 2 * rows // nh, NY)], got, data_weight, observed
-    )
-    sums = from_chips(sums, nh)
-    pred, pulled, weight, tops, message = call(
+        bind(collect_kernel, nxy), [(rows + nxy + 2 * part, NY)], got, data_weight, observed
+    )
+    sums = from_axis([sums] * nh, "h")
+    pred, weight, tops, message = call(
         bind(residual_kernel, nxy, nh),
-        [(rows, NY), (rows, NY), (rows, NY), (nxy * nh, NY), (nxy, rows, NY)],
+        [(rows, NY), (rows, NY), (nxy * nh, NY), (nxy, rows, NY)],
         *sums, scratch=[(rows, NY)],
     )
     got = exchange(message, XY)
+    parts = from_axis(after(parts, message), "y")
+    (pulled,) = call(bind(fold_kernel, ny), [(rows, NY)], *parts, scratch=[(rows, NY)])
+    pulls = from_axis([pulled] * nh, "h")
     (power,) = call(bind(power_kernel, nxy * nh), [(NX, NY)], tops)
-    adjoint = lambda plane: from_comps(
-        call(
-            bind(adjoint_kernel, nxy),
-            [(QX + rows, NY)] * 4,
-            plane, decay, own, power, factors, fx, bx, ty,
-            scratch=[(NX, NY), (4 * rows, NY)],
-        )
-    )
-    pieces = adjoint(got)
-    shares, message, data_grad, grad, line, image = call(
+    adjoint = lambda plane: call(
+        bind(adjoint_kernel, nxy), [(QX + rows, NY)] * 4,
+        plane, decay, own, power, factors, *tables, scratch=[(NX, NY), (4 * rows, NY)],
+    )
+    got = after(got, *pulls)
+    pieces = from_comps(adjoint(got.reshape(NX, NY)))
+    shares, back, data_grad, grad, line, image = call(
         bind(gradient_kernel, nxy, nh),
-        [(devices, 128), (nxy, rows, NY), (QX, NY), (QX, NY), (rows, NY), (rows, NY)],
-        *pieces, pulled, density, weight, scratch=[(rows, NY)],
+        [(devices, 128), (rows, NY), (QX, NY), (QX, NY), (rows, NY), (rows, NY)],
+        *pieces, *pulls, density, weight, scratch=[(rows, NY)],
     )
     shares = exchange(shares, ALL)
+    (joined,) = call(join_kernel, [(nx * rows, NY)], *from_axis([back] * nx, "x"))
+    (plane,) = call(bind(place_kernel, ny, nx), [(NX, NY)], *from_axis([joined] * ny, "y"))
+    shares = after(shares, plane)
     dens, pull, alpha = call(
         move_kernel, [(QX, NY), (QX, NY), (8, 128)], shares, density, grad
     )
-    back = exchange(after(message, pull), XY)
     pull_full = from_comps([pull] * 4)
+    pieces = adjoint(after(plane, pull))
+    pull_full = after(pull_full, *pieces)
     (message,) = call(
-        bind(second_kernel, nxy), [(nxy, rows, NY)],
-        *pull_full, decay, own, fx, bx, ty, scratch=[(NX, NY)],
-    )
-    got = exchange(message, XY)
-    pieces = adjoint(back)
+        second_kernel, [(nxy * nh, part, NY)], *pull_full, decay, own, *tables, scratch=[(NX, NY)]
+    )
+    got = exchange(message, DEPTH)
+    pieces = from_comps(after(pieces, message))
     grad2, image2, half = call(
         second_gradient_kernel, [(QX, NY), (rows, NY), (8, 128)],
         *pieces, alpha, data_grad, pull, dens, line,
     )
-    (pulled,) = call(bind(sum_kernel, nxy), [(rows, NY)], got)
-    pulls = from_chips(pulled, nh)
+    got = after(got, half)
     shares, image2 = call(
-        bind(curvature_kernel, nxy, nh), [(devices, 128), (rows, NY)],
-        *pulls, image2, weight, half, scratch=[(rows, NY)],
+        curvature_kernel, [(devices, 128), (part, NY)], got, image2, data_weight, half
     )
     shares = exchange(shares, ALL)
     return tuple(
         call(
             finish_kernel, [density.shape, observed.shape],
             shares, dens, grad2, alpha, pred, image, image2, observed, data_weight,
+            out=jax.ShapeDtypeStruct,
         )
     )
 

time: 182 us -> 202 us (1.11)
  blocking collectives: 66.6 us -> 24.4 us
  starting transfers between devices: 46.3 us -> 79.2 us
  waiting for transfers between devices: 32.5 us -> 52.6 us
  local copies, waits for them, and re-layouts: 13.8 us -> 22.6 us
    all_to_all x3 -> x1, blocking collectives: 66.6 us -> 24.4 us  [exchange(): return lax.all_to_all(value, axes, 0, 0, tiled=True)]
    ppermute x6 -> x18, waiting for transfers between devices: 6.07 us -> 27.7 us  [from_axis(): lax.ppermute(values[step], axis, [(i, (i + step) % size) for i in range(s...]
    ppermute x6 -> x18, starting transfers between devices: 15 us -> 35.3 us  [from_axis(): lax.ppermute(values[step], axis, [(i, (i + step) % size) for i in range(s...]
    all_to_all x3 -> x4, starting transfers between devices: 14.7 us -> 28.6 us  [exchange(): return lax.all_to_all(value, axes, 0, 0, tiled=True)]
    unnamed x56 -> x72, local copies, waits for them, and re-layouts: 13.8 us -> 22.6 us
    all_to_all x3 -> x4, waiting for transfers between devices: 7.08 us -> 0.01 us  [exchange(): return lax.all_to_all(value, axes, 0, 0, tiled=True)]
    ppermute x12, waiting for transfers between devices: 19.4 us -> 24.9 us  [from_comps(): lax.ppermute(values[step], COMP, [(i, i ^ step) for i in range(4)])]
    pallas_call x14 -> x18, Pallas kernels: 20 us -> 20.3 us  [call(): pl.pallas_call(kernel, out_shape=[out(shape, dtype) for shape, dtype in k...]
  transfers between devices with their start and end apart: 21 -> 34, of which waited for: 11 -> 15; matrix products, arithmetic and copies ran while one was open for 0% -> 0% of each run, Pallas kernels for 6% -> 5%
where the time goes in v3:
time: 202 us; the launch traced here: 201 us
  starting transfers between devices  79.2 us (39%)
  waiting for transfers between devices  52.6 us (26%)
  blocking collectives  24.4 us (12%)
  local copies, waits for them, and re-layouts  22.6 us (11%)
  Pallas kernels  20.3 us (10%)
    ppermute x18, starting transfers between devices, from_axis(): lax.ppermute(values[step], axis, [(i, (i + step) % size) for i in range(s...  35.3 us
    all_to_all x4, starting transfers between devices, exchange(): return lax.all_to_all(value, axes, 0, 0, tiled=True)  28.6 us
    ppermute x18, waiting for transfers between devices, from_axis(): lax.ppermute(values[step], axis, [(i, (i + step) % size) for i in range(s...  27.7 us
    ppermute x12, waiting for transfers between devices, from_comps(): lax.ppermute(values[step], COMP, [(i, i ^ step) for i in range(4)])  24.9 us
    all_to_all x1, blocking collectives, exchange(): return lax.all_to_all(value, axes, 0, 0, tiled=True)  24.4 us
    unnamed x72, local copies, waits for them, and re-layouts  22.6 us
    pallas_call x18, Pallas kernels, call(): pl.pallas_call(kernel, out_shape=[out(shape, dtype) for shape, dtype in k...  20.3 us
    ppermute x12, starting transfers between devices, from_comps(): lax.ppermute(values[step], COMP, [(i, i ^ step) for i in range(4)])  15.3 us
  transfers between devices with their start and end apart: 34, of which 15 were waited for; matrix products, arithmetic and copies ran while one was open for 0% of the time, Pallas kernels for 5%

profile of v3, /device:TPU:1, one launch (start us, length us, event | category | flops | bytes accessed | tf_op | source)
XLA Modules:
  0.0 200.8 jit_solution(14934845957638752155)
XLA Ops:
  0.6 3.1 %collective-permute-start.2 = (f32[128,256]{1,0:T(8,128)}, f32[128,256]{1,0:T(8,128)S(1)}, u32[]{:S(2)}, u32[]{:S(2)}) collective-permute-start(f32[128,256]{1,0:T(8,128)} %bitcast.14), channel_id=1, source_target_pairs={{0,3},{1,2},{2,1},{3,0},{4,7},{5,6},{6,5},{7,4},{8,11},{9,10},{10,... | collective-permute-start | bytes 393224 | tf_op jit(solution)/shard_map/ppermute | solution.py:455
  16.9 5.7 %all-to-all-start = ((f32[16,40,256]{2,1,0:T(8,128)}), f32[16,40,256]{2,1,0:T(8,128)S(1)}, u32[]{:S(2)}, u32[]{:S(2)}) async-start(f32[16,40,256]{2,1,0:T(8,128)} %copy-done.5), calls=%async_computation | async-start | bytes 1310720 | tf_op jit(solution)/shard_map/all_to_all | solution.py:468
  23.7 1.8 shard_map.88
  26.9 2.4 %collective-permute-start.4 = (f32[128,256]{1,0:T(8,128)S(1)}, f32[128,256]{1,0:T(8,128)S(1)}, u32[]{:S(2)}, u32[]{:S(2)}) collective-permute-start(f32[128,256]{1,0:T(8,128)S(1)} %get-tuple-element.76), channel_id=1, source_target_pairs={{0,128},{64,192},{128,0},{192,64},{1,129},{65,193},{129,1},{193,65... | collective-permute-start | bytes 393224 | tf_op jit(solution)/shard_map/ppermute | solution.py:462
  30.5 5.2 %collective-permute-done.3.refs_1_ = f32[128,256]{1,0:T(8,128)S(1)} collective-permute-done((f32[128,256]{1,0:T(8,128)S(1)}, f32[128,256]{1,0:T(8,128)S(1)}, u32[]{:S(2)}, u32[]{:S(2)}) %collective-permute-start.3) | collective-permute-done | bytes 131104 | tf_op jit(solution)/shard_map/ppermute | solution.py:462
  35.7 3.1 %collective-permute-done.4.refs_2_ = f32[128,256]{1,0:T(8,128)S(1)} collective-permute-done((f32[128,256]{1,0:T(8,128)S(1)}, f32[128,256]{1,0:T(8,128)S(1)}, u32[]{:S(2)}, u32[]{:S(2)}) %collective-permute-start.4) | collective-permute-done | bytes 131104 | tf_op jit(solution)/shard_map/ppermute | solution.py:462
  40.1 5.2 %collective-permute-start.8 = (f32[64,256]{1,0:T(8,128)S(1)}, f32[64,256]{1,0:T(8,128)S(1)}, u32[]{:S(2)}, u32[]{:S(2)}) collective-permute-start(f32[64,256]{1,0:T(8,128)S(1)} %shard_map.90.refs_0_), channel_id=1, source_target_pairs={{0,12},{4,0},{8,4},{12,8},{1,13},{5,1},{9,5},{13,9},{2,14},{6,2},{... | collective-permute-start | bytes 196616 | tf_op jit(solution)/shard_map/ppermute | solution.py:462
  46.5 2.1 %collective-permute-start.6 = (f32[64,256]{1,0:T(8,128)S(1)}, f32[64,256]{1,0:T(8,128)S(1)}, u32[]{:S(2)}, u32[]{:S(2)}) collective-permute-start(f32[64,256]{1,0:T(8,128)S(1)} %shard_map.90.refs_0_), channel_id=1, source_target_pairs={{0,4},{4,8},{8,12},{12,0},{1,5},{5,9},{9,13},{13,1},{2,6},{6,10},{... | collective-permute-start | bytes 196616 | tf_op jit(solution)/shard_map/ppermute | solution.py:462
  48.6 4.0 %collective-permute-done.7.refs_2_ = f32[64,256]{1,0:T(8,128)S(1)} collective-permute-done((f32[64,256]{1,0:T(8,128)S(1)}, f32[64,256]{1,0:T(8,128)S(1)}, u32[]{:S(2)}, u32[]{:S(2)}) %collective-permute-start.7) | collective-permute-done | bytes 65568 | tf_op jit(solution)/shard_map/ppermute | solution.py:462
  53.8 4.8 %all-to-all-start.1 = ((f32[16,32,256]{2,1,0:T(8,128)}), f32[16,32,256]{2,1,0:T(8,128)}, u32[]{:S(2)}, u32[]{:S(2)}) async-start(f32[16,32,256]{2,1,0:T(8,128)} %get-tuple-element.85), calls=%async_computation.1 | async-start | bytes 1048576 | tf_op jit(solution)/shard_map/all_to_all | solution.py:468
  59.9 2.4 %collective-permute-start.10 = (f32[32,256]{1,0:T(8,128)}, f32[32,256]{1,0:T(8,128)S(1)}, u32[]{:S(2)}, u32[]{:S(2)}) collective-permute-start(f32[32,256]{1,0:T(8,128)} %get-tuple-element.88), channel_id=1, source_target_pairs={{0,32},{16,48},{32,0},{48,16},{1,33},{17,49},{33,1},{49,17},{2,34}... | collective-permute-start | bytes 98312 | tf_op jit(solution)/shard_map/ppermute | solution.py:462
  64.8 2.0 collective-permute-done.11.refs_3_
  67.2 6.8 %collective-permute-start.13 = (f32[32,256]{1,0:T(8,128)S(1)}, f32[32,256]{1,0:T(8,128)S(1)}, u32[]{:S(2)}, u32[]{:S(2)}) collective-permute-start(f32[32,256]{1,0:T(8,128)S(1)} %shard_map.92.refs_4_), channel_id=1, source_target_pairs={{0,8},{4,12},{8,0},{12,4},{1,9},{5,13},{9,1},{13,5},{2,10},{6,14},... | collective-permute-start | bytes 98312 | tf_op jit(solution)/shard_map/ppermute | solution.py:462
  74.0 2.3 %collective-permute-start.12 = (f32[32,256]{1,0:T(8,128)S(1)}, f32[32,256]{1,0:T(8,128)S(1)}, u32[]{:S(2)}, u32[]{:S(2)}) collective-permute-start(f32[32,256]{1,0:T(8,128)S(1)} %shard_map.92.refs_4_), channel_id=1, source_target_pairs={{0,4},{4,8},{8,12},{12,0},{1,5},{5,9},{9,13},{13,1},{2,6},{6,10},{... | collective-permute-start | bytes 98312 | tf_op jit(solution)/shard_map/ppermute | solution.py:462
  76.2 3.6 %shard_map.93.power_ref = f32[512,256]{1,0:T(8,128)S(1)} custom-call(f32[64,256]{1,0:T(8,128)S(1)} %get-tuple-element.91.tops_ref), custom_call_target="tpu_custom_call" | custom-call | tf_op jit(solution)/shard_map/pallas_call | solution.py:441
  81.3 3.4 %shard_map.94 = (f32[160,256]{1,0:T(8,128)S(1)}, f32[160,256]{1,0:T(8,128)S(1)}, f32[160,256]{1,0:T(8,128)S(1)}, f32[160,256]{1,0:T(8,128)S(1)}) custom-call(f32[512,256]{1,0:T(8,128)} %bitcast.2.res_ref, f32[512,256]{1,0:T(8,128)S(1)} %get-tuple-element.66.decay_ref, f32[512,256]{1,0:T(8,128)S(1)} %get-tuple-element.67.own_ref, ...), custom_call_target="tpu_custom_call" | custom-call | tf_op jit(solution)/shard_map/pallas_call | solution.py:441
  84.7 3.1 %collective-permute-start.15 = (f32[160,256]{1,0:T(8,128)S(1)}, f32[160,256]{1,0:T(8,128)S(1)}, u32[]{:S(2)}, u32[]{:S(2)}) collective-permute-start(f32[160,256]{1,0:T(8,128)S(1)} %get-tuple-element.94), channel_id=1, source_target_pairs={{0,1},{1,0},{2,3},{3,2},{4,5},{5,4},{6,7},{7,6},{8,9},{9,8},{10,11... | collective-permute-start | bytes 491528 | tf_op jit(solution)/shard_map/ppermute | solution.py:455
  89.6 3.9 %collective-permute-done.16.refs_2_ = f32[160,256]{1,0:T(8,128)S(1)} collective-permute-done((f32[160,256]{1,0:T(8,128)S(1)}, f32[160,256]{1,0:T(8,128)S(1)}, u32[]{:S(2)}, u32[]{:S(2)}) %collective-permute-start.16) | collective-permute-done | bytes 163872 | tf_op jit(solution)/shard_map/ppermute | solution.py:455
  93.5 3.8 %collective-permute-done.17.refs_3_ = f32[160,256]{1,0:T(8,128)S(1)} collective-permute-done((f32[160,256]{1,0:T(8,128)S(1)}, f32[160,256]{1,0:T(8,128)S(1)}, u32[]{:S(2)}, u32[]{:S(2)}) %collective-permute-start.17) | collective-permute-done | bytes 163872 | tf_op jit(solution)/shard_map/ppermute | solution.py:455
  100.7 9.0 %all-to-all-start.2 = ((f32[256,1,128]{2,1,0:T(1,128)}), f32[256,1,128]{2,1,0:T(1,128)S(1)}, u32[]{:S(2)}, u32[]{:S(2)}) async-start(f32[256,1,128]{2,1,0:T(1,128)} %bitcast.4), calls=%async_computation.2 | async-start | bytes 262144 | tf_op jit(solution)/shard_map/all_to_all | solution.py:468
  109.7 2.6 %collective-permute-start.20 = (f32[32,256]{1,0:T(8,128)S(1)}, f32[32,256]{1,0:T(8,128)S(1)}, u32[]{:S(2)}, u32[]{:S(2)}) collective-permute-start(f32[32,256]{1,0:T(8,128)S(1)} %get-tuple-element.99.refs_0_), channel_id=1, source_target_pairs={{0,192},{64,0},{128,64},{192,128},{1,193},{65,1},{129,65},{193,129... | collective-permute-start | bytes 98312 | tf_op jit(solution)/shard_map/ppermute | solution.py:462
  113.5 3.5 %collective-permute-done.19.refs_2_ = f32[32,256]{1,0:T(8,128)S(1)} collective-permute-done((f32[32,256]{1,0:T(8,128)S(1)}, f32[32,256]{1,0:T(8,128)S(1)}, u32[]{:S(2)}, u32[]{:S(2)}) %collective-permute-start.19) | collective-permute-done | bytes 32800 | tf_op jit(solution)/shard_map/ppermute | solution.py:462
  118.3 2.6 %collective-permute-start.23 = (f32[128,256]{1,0:T(8,128)S(1)}, f32[128,256]{1,0:T(8,128)S(1)}, u32[]{:S(2)}, u32[]{:S(2)}) collective-permute-start(f32[128,256]{1,0:T(8,128)S(1)} %shard_map.96.refs_0_), channel_id=1, source_target_pairs={{0,48},{16,0},{32,16},{48,32},{1,49},{17,1},{33,17},{49,33},{2,50}... | collective-permute-start | bytes 393224 | tf_op jit(solution)/shard_map/ppermute | solution.py:462
  123.3 3.0 %collective-permute-done.22.refs_2_ = f32[128,256]{1,0:T(8,128)S(1)} collective-permute-done((f32[128,256]{1,0:T(8,128)S(1)}, f32[128,256]{1,0:T(8,128)S(1)}, u32[]{:S(2)}, u32[]{:S(2)}) %collective-permute-start.22) | collective-permute-done | bytes 131104 | tf_op jit(solution)/shard_map/ppermute | solution.py:462
  126.3 3.3 %collective-permute-done.21.refs_1_ = f32[128,256]{1,0:T(8,128)S(1)} collective-permute-done((f32[128,256]{1,0:T(8,128)S(1)}, f32[128,256]{1,0:T(8,128)S(1)}, u32[]{:S(2)}, u32[]{:S(2)}) %collective-permute-start.21) | collective-permute-done | bytes 131104 | tf_op jit(solution)/shard_map/ppermute | solution.py:462
  132.8 2.8 %collective-permute-start.26 = (f32[128,256]{1,0:T(8,128)S(1)}, f32[128,256]{1,0:T(8,128)S(1)}, u32[]{:S(2)}, u32[]{:S(2)}) collective-permute-start(f32[128,256]{1,0:T(8,128)S(1)} %get-tuple-element.108.p0.pull_ref), channel_id=1, source_target_pairs={{0,3},{1,2},{2,1},{3,0},{4,7},{5,6},{6,5},{7,4},{8,11},{9,10},{10,... | collective-permute-start | bytes 393224 | tf_op jit(solution)/shard_map/ppermute | solution.py:455
  138.5 2.3 %shard_map.99 = (f32[160,256]{1,0:T(8,128)S(1)}, f32[160,256]{1,0:T(8,128)S(1)}, f32[160,256]{1,0:T(8,128)S(1)}, f32[160,256]{1,0:T(8,128)S(1)}) custom-call(f32[512,256]{1,0:T(8,128)S(1)} %copy-done.4, f32[512,256]{1,0:T(8,128)S(1)} %get-tuple-element.66.decay_ref, f32[512,256]{1,0:T(8,128)S(1)} %get-tuple-element.67.own_ref, ...), custom_call_target="tpu_custom_call" | custom-call | tf_op jit(solution)/shard_map/pallas_call | solution.py:441
  143.5 2.6 %shard_map.100 = f32[64,8,256]{2,1,0:T(8,128)} custom-call(f32[128,256]{1,0:T(8,128)S(1)} %get-tuple-element.108.p0.pull_ref, f32[128,256]{1,0:T(8,128)S(1)} %collective-permute-done.24.p1, f32[128,256]{1,0:T(8,128)S(1)} %collective-permute-done.25.p2, f32[128,256]{1,0:T(8,128)S(1)} %collective-permute-done.26.p3, ...), custom_call_target="tpu_custom_call" | custom-call | tf_op jit(solution)/shard_map/pallas_call | solution.py:441
  146.1 9.2 %all-to-all-start.3 = ((f32[64,8,256]{2,1,0:T(8,128)}), f32[64,8,256]{2,1,0:T(8,128)S(1)}, u32[]{:S(2)}, u32[]{:S(2)}) async-start(f32[64,8,256]{2,1,0:T(8,128)} %shard_map.100), calls=%async_computation.3 | async-start | bytes 1048576 | tf_op jit(solution)/shard_map/all_to_all | solution.py:468
  157.9 12.7 %collective-permute-done.28.u2 = f32[160,256]{1,0:T(8,128)S(1)} collective-permute-done((f32[160,256]{1,0:T(8,128)}, f32[160,256]{1,0:T(8,128)S(1)}, u32[]{:S(2)}, u32[]{:S(2)}) %collective-permute-start.28) | collective-permute-done | bytes 163872 | tf_op jit(solution)/shard_map/ppermute | solution.py:455
  170.6 4.5 %collective-permute-done.29.u3 = f32[160,256]{1,0:T(8,128)S(1)} collective-permute-done((f32[160,256]{1,0:T(8,128)}, f32[160,256]{1,0:T(8,128)S(1)}, u32[]{:S(2)}, u32[]{:S(2)}) %collective-permute-start.29) | collective-permute-done | bytes 163872 | tf_op jit(solution)/shard_map/ppermute | solution.py:455
  175.6 24.4 %all_to_all.38 = f32[256,1,128]{2,1,0:T(1,128)S(1)} all-to-all(f32[256,1,128]{2,1,0:T(1,128)S(1)} %bitcast.17), channel_id=1, replica_groups=mesh['x'=4,'y'=4,'h'=4,'l'=2,'k'=2] {'x','y','h','l','k'}, dimensions={0} | all-to-all | bytes 262144 | tf_op jit(solution)/shard_map/all_to_all | solution.py:468
  (127 shorter events, 48.1 us)
Async XLA Ops:
  0.6 12.9 %collective-permute-start.2 = (f32[128,256]{1,0:T(8,128)}, f32[128,256]{1,0:T(8,128)S(1)}, u32[]{:S(2)}, u32[]{:S(2)}) collective-permute-start(f32[128,256]{1,0:T(8,128)} %bitcast.14), channel_id=1, source_target_pairs={{0,3},{1,2},{2,1},{3,0},{4,7},{5,6},{6,5},{7,4},{8,11},{9,10},{10,... | collective-permute-start | bytes 393224 | tf_op jit(solution)/shard_map/ppermute | solution.py:455
  3.7 9.8 %collective-permute-start.1 = (f32[128,256]{1,0:T(8,128)}, f32[128,256]{1,0:T(8,128)S(1)}, u32[]{:S(2)}, u32[]{:S(2)}) collective-permute-start(f32[128,256]{1,0:T(8,128)} %bitcast.15), channel_id=1, source_target_pairs={{0,2},{1,3},{2,0},{3,1},{4,6},{5,7},{6,4},{7,5},{8,10},{9,11},{10,... | collective-permute-start | bytes 393224 | tf_op jit(solution)/shard_map/ppermute | solution.py:455
  5.3 8.2 %collective-permute-start = (f32[128,256]{1,0:T(8,128)}, f32[128,256]{1,0:T(8,128)S(1)}, u32[]{:S(2)}, u32[]{:S(2)}) collective-permute-start(f32[128,256]{1,0:T(8,128)} %bitcast.16), channel_id=1, source_target_pairs={{0,1},{1,0},{2,3},{3,2},{4,5},{5,4},{6,7},{7,6},{8,9},{9,8},{10,11... | collective-permute-start | bytes 393224 | tf_op jit(solution)/shard_map/ppermute | solution.py:455
  16.9 23.2 %all-to-all-start = ((f32[16,40,256]{2,1,0:T(8,128)}), f32[16,40,256]{2,1,0:T(8,128)S(1)}, u32[]{:S(2)}, u32[]{:S(2)}) async-start(f32[16,40,256]{2,1,0:T(8,128)} %copy-done.5), calls=%async_computation | async-start | bytes 1310720 | tf_op jit(solution)/shard_map/all_to_all | solution.py:468
  25.4 10.3 %collective-permute-start.3 = (f32[128,256]{1,0:T(8,128)S(1)}, f32[128,256]{1,0:T(8,128)S(1)}, u32[]{:S(2)}, u32[]{:S(2)}) collective-permute-start(f32[128,256]{1,0:T(8,128)S(1)} %get-tuple-element.75), channel_id=1, source_target_pairs={{0,64},{64,128},{128,192},{192,0},{1,65},{65,129},{129,193},{193,1... | collective-permute-start | bytes 393224 | tf_op jit(solution)/shard_map/ppermute | solution.py:462
  26.9 11.9 %collective-permute-start.4 = (f32[128,256]{1,0:T(8,128)S(1)}, f32[128,256]{1,0:T(8,128)S(1)}, u32[]{:S(2)}, u32[]{:S(2)}) collective-permute-start(f32[128,256]{1,0:T(8,128)S(1)} %get-tuple-element.76), channel_id=1, source_target_pairs={{0,128},{64,192},{128,0},{192,64},{1,129},{65,193},{129,1},{193,65... | collective-permute-start | bytes 393224 | tf_op jit(solution)/shard_map/ppermute | solution.py:462
  29.3 9.5 %collective-permute-start.5 = (f32[128,256]{1,0:T(8,128)S(1)}, f32[128,256]{1,0:T(8,128)S(1)}, u32[]{:S(2)}, u32[]{:S(2)}) collective-permute-start(f32[128,256]{1,0:T(8,128)S(1)} %get-tuple-element.77), channel_id=1, source_target_pairs={{0,192},{64,0},{128,64},{192,128},{1,193},{65,1},{129,65},{193,129... | collective-permute-start | bytes 393224 | tf_op jit(solution)/shard_map/ppermute | solution.py:462
  40.1 8.4 %collective-permute-start.8 = (f32[64,256]{1,0:T(8,128)S(1)}, f32[64,256]{1,0:T(8,128)S(1)}, u32[]{:S(2)}, u32[]{:S(2)}) collective-permute-start(f32[64,256]{1,0:T(8,128)S(1)} %shard_map.90.refs_0_), channel_id=1, source_target_pairs={{0,12},{4,0},{8,4},{12,8},{1,13},{5,1},{9,5},{13,9},{2,14},{6,2},{... | collective-permute-start | bytes 196616 | tf_op jit(solution)/shard_map/ppermute | solution.py:462
  45.3 7.2 %collective-permute-start.7 = (f32[64,256]{1,0:T(8,128)S(1)}, f32[64,256]{1,0:T(8,128)S(1)}, u32[]{:S(2)}, u32[]{:S(2)}) collective-permute-start(f32[64,256]{1,0:T(8,128)S(1)} %shard_map.90.refs_0_), channel_id=1, source_target_pairs={{0,8},{4,12},{8,0},{12,4},{1,9},{5,13},{9,1},{13,5},{2,10},{6,14},... | collective-permute-start | bytes 196616 | tf_op jit(solution)/shard_map/ppermute | solution.py:462
  46.5 6.5 %collective-permute-start.6 = (f32[64,256]{1,0:T(8,128)S(1)}, f32[64,256]{1,0:T(8,128)S(1)}, u32[]{:S(2)}, u32[]{:S(2)}) collective-permute-start(f32[64,256]{1,0:T(8,128)S(1)} %shard_map.90.refs_0_), channel_id=1, source_target_pairs={{0,4},{4,8},{8,12},{12,0},{1,5},{5,9},{9,13},{13,1},{2,6},{6,10},{... | collective-permute-start | bytes 196616 | tf_op jit(solution)/shard_map/ppermute | solution.py:462
  53.8 26.1 %all-to-all-start.1 = ((f32[16,32,256]{2,1,0:T(8,128)}), f32[16,32,256]{2,1,0:T(8,128)}, u32[]{:S(2)}, u32[]{:S(2)}) async-start(f32[16,32,256]{2,1,0:T(8,128)} %get-tuple-element.85), calls=%async_computation.1 | async-start | bytes 1048576 | tf_op jit(solution)/shard_map/all_to_all | solution.py:468
  58.6 4.9 %collective-permute-start.9 = (f32[32,256]{1,0:T(8,128)}, f32[32,256]{1,0:T(8,128)S(1)}, u32[]{:S(2)}, u32[]{:S(2)}) collective-permute-start(f32[32,256]{1,0:T(8,128)} %get-tuple-element.87), channel_id=1, source_target_pairs={{0,16},{16,32},{32,48},{48,0},{1,17},{17,33},{33,49},{49,1},{2,18}... | collective-permute-start | bytes 98312 | tf_op jit(solution)/shard_map/ppermute | solution.py:462
  59.9 4.8 %collective-permute-start.10 = (f32[32,256]{1,0:T(8,128)}, f32[32,256]{1,0:T(8,128)S(1)}, u32[]{:S(2)}, u32[]{:S(2)}) collective-permute-start(f32[32,256]{1,0:T(8,128)} %get-tuple-element.88), channel_id=1, source_target_pairs={{0,32},{16,48},{32,0},{48,16},{1,33},{17,49},{33,1},{49,17},{2,34}... | collective-permute-start | bytes 98312 | tf_op jit(solution)/shard_map/ppermute | solution.py:462
  62.3 4.4 %collective-permute-start.11 = (f32[32,256]{1,0:T(8,128)}, f32[32,256]{1,0:T(8,128)S(1)}, u32[]{:S(2)}, u32[]{:S(2)}) collective-permute-start(f32[32,256]{1,0:T(8,128)} %copy-done.35), channel_id=1, source_target_pairs={{0,48},{16,0},{32,16},{48,32},{1,49},{17,1},{33,17},{49,33},{2,50}... | collective-permute-start | bytes 98312 | tf_op jit(solution)/shard_map/ppermute | solution.py:462
  66.8 13.1 %collective-permute-start.14 = (f32[32,256]{1,0:T(8,128)S(1)}, f32[32,256]{1,0:T(8,128)S(1)}, u32[]{:S(2)}, u32[]{:S(2)}) collective-permute-start(f32[32,256]{1,0:T(8,128)S(1)} %shard_map.92.refs_4_), channel_id=1, source_target_pairs={{0,12},{4,0},{8,4},{12,8},{1,13},{5,1},{9,5},{13,9},{2,14},{6,2},{... | collective-permute-start | bytes 98312 | tf_op jit(solution)/shard_map/ppermute | solution.py:462
  67.2 12.7 %collective-permute-start.13 = (f32[32,256]{1,0:T(8,128)S(1)}, f32[32,256]{1,0:T(8,128)S(1)}, u32[]{:S(2)}, u32[]{:S(2)}) collective-permute-start(f32[32,256]{1,0:T(8,128)S(1)} %shard_map.92.refs_4_), channel_id=1, source_target_pairs={{0,8},{4,12},{8,0},{12,4},{1,9},{5,13},{9,1},{13,5},{2,10},{6,14},... | collective-permute-start | bytes 98312 | tf_op jit(solution)/shard_map/ppermute | solution.py:462
  74.0 5.9 %collective-permute-start.12 = (f32[32,256]{1,0:T(8,128)S(1)}, f32[32,256]{1,0:T(8,128)S(1)}, u32[]{:S(2)}, u32[]{:S(2)}) collective-permute-start(f32[32,256]{1,0:T(8,128)S(1)} %shard_map.92.refs_4_), channel_id=1, source_target_pairs={{0,4},{4,8},{8,12},{12,0},{1,5},{5,9},{9,13},{13,1},{2,6},{6,10},{... | collective-permute-start | bytes 98312 | tf_op jit(solution)/shard_map/ppermute | solution.py:462
  84.7 4.9 %collective-permute-start.15 = (f32[160,256]{1,0:T(8,128)S(1)}, f32[160,256]{1,0:T(8,128)S(1)}, u32[]{:S(2)}, u32[]{:S(2)}) collective-permute-start(f32[160,256]{1,0:T(8,128)S(1)} %get-tuple-element.94), channel_id=1, source_target_pairs={{0,1},{1,0},{2,3},{3,2},{4,5},{5,4},{6,7},{7,6},{8,9},{9,8},{10,11... | collective-permute-start | bytes 491528 | tf_op jit(solution)/shard_map/ppermute | solution.py:455
  87.8 5.7 %collective-permute-start.16 = (f32[160,256]{1,0:T(8,128)S(1)}, f32[160,256]{1,0:T(8,128)S(1)}, u32[]{:S(2)}, u32[]{:S(2)}) collective-permute-start(f32[160,256]{1,0:T(8,128)S(1)} %get-tuple-element.95), channel_id=1, source_target_pairs={{0,2},{1,3},{2,0},{3,1},{4,6},{5,7},{6,4},{7,5},{8,10},{9,11},{10,... | collective-permute-start | bytes 491528 | tf_op jit(solution)/shard_map/ppermute | solution.py:455
  89.1 8.2 %collective-permute-start.17 = (f32[160,256]{1,0:T(8,128)S(1)}, f32[160,256]{1,0:T(8,128)S(1)}, u32[]{:S(2)}, u32[]{:S(2)}) collective-permute-start(f32[160,256]{1,0:T(8,128)S(1)} %get-tuple-element.96), channel_id=1, source_target_pairs={{0,3},{1,2},{2,1},{3,0},{4,7},{5,6},{6,5},{7,4},{8,11},{9,10},{10,... | collective-permute-start | bytes 491528 | tf_op jit(solution)/shard_map/ppermute | solution.py:455
  100.7 29.8 %all-to-all-start.2 = ((f32[256,1,128]{2,1,0:T(1,128)}), f32[256,1,128]{2,1,0:T(1,128)S(1)}, u32[]{:S(2)}, u32[]{:S(2)}) async-start(f32[256,1,128]{2,1,0:T(1,128)} %bitcast.4), calls=%async_computation.2 | async-start | bytes 262144 | tf_op jit(solution)/shard_map/all_to_all | solution.py:468
  112.3 4.7 %collective-permute-start.19 = (f32[32,256]{1,0:T(8,128)S(1)}, f32[32,256]{1,0:T(8,128)S(1)}, u32[]{:S(2)}, u32[]{:S(2)}) collective-permute-start(f32[32,256]{1,0:T(8,128)S(1)} %get-tuple-element.99.refs_0_), channel_id=1, source_target_pairs={{0,128},{64,192},{128,0},{192,64},{1,129},{65,193},{129,1},{193,65... | collective-permute-start | bytes 98312 | tf_op jit(solution)/shard_map/ppermute | solution.py:462
  112.9 4.6 %collective-permute-start.18 = (f32[32,256]{1,0:T(8,128)S(1)}, f32[32,256]{1,0:T(8,128)S(1)}, u32[]{:S(2)}, u32[]{:S(2)}) collective-permute-start(f32[32,256]{1,0:T(8,128)S(1)} %get-tuple-element.99.refs_0_), channel_id=1, source_target_pairs={{0,64},{64,128},{128,192},{192,0},{1,65},{65,129},{129,193},{193,1... | collective-permute-start | bytes 98312 | tf_op jit(solution)/shard_map/ppermute | solution.py:462
  118.3 5.0 %collective-permute-start.23 = (f32[128,256]{1,0:T(8,128)S(1)}, f32[128,256]{1,0:T(8,128)S(1)}, u32[]{:S(2)}, u32[]{:S(2)}) collective-permute-start(f32[128,256]{1,0:T(8,128)S(1)} %shard_map.96.refs_0_), channel_id=1, source_target_pairs={{0,48},{16,0},{32,16},{48,32},{1,49},{17,1},{33,17},{49,33},{2,50}... | collective-permute-start | bytes 393224 | tf_op jit(solution)/shard_map/ppermute | solution.py:462
  120.9 5.4 %collective-permute-start.22 = (f32[128,256]{1,0:T(8,128)S(1)}, f32[128,256]{1,0:T(8,128)S(1)}, u32[]{:S(2)}, u32[]{:S(2)}) collective-permute-start(f32[128,256]{1,0:T(8,128)S(1)} %shard_map.96.refs_0_), channel_id=1, source_target_pairs={{0,32},{16,48},{32,0},{48,16},{1,33},{17,49},{33,1},{49,17},{2,34}... | collective-permute-start | bytes 393224 | tf_op jit(solution)/shard_map/ppermute | solution.py:462
  121.3 8.3 %collective-permute-start.21 = (f32[128,256]{1,0:T(8,128)S(1)}, f32[128,256]{1,0:T(8,128)S(1)}, u32[]{:S(2)}, u32[]{:S(2)}) collective-permute-start(f32[128,256]{1,0:T(8,128)S(1)} %shard_map.96.refs_0_), channel_id=1, source_target_pairs={{0,16},{16,32},{32,48},{48,0},{1,17},{17,33},{33,49},{49,1},{2,18}... | collective-permute-start | bytes 393224 | tf_op jit(solution)/shard_map/ppermute | solution.py:462
  132.8 10.6 %collective-permute-start.26 = (f32[128,256]{1,0:T(8,128)S(1)}, f32[128,256]{1,0:T(8,128)S(1)}, u32[]{:S(2)}, u32[]{:S(2)}) collective-permute-start(f32[128,256]{1,0:T(8,128)S(1)} %get-tuple-element.108.p0.pull_ref), channel_id=1, source_target_pairs={{0,3},{1,2},{2,1},{3,0},{4,7},{5,6},{6,5},{7,4},{8,11},{9,10},{10,... | collective-permute-start | bytes 393224 | tf_op jit(solution)/shard_map/ppermute | solution.py:455
  135.6 7.9 %collective-permute-start.25 = (f32[128,256]{1,0:T(8,128)S(1)}, f32[128,256]{1,0:T(8,128)S(1)}, u32[]{:S(2)}, u32[]{:S(2)}) collective-permute-start(f32[128,256]{1,0:T(8,128)S(1)} %get-tuple-element.108.p0.pull_ref), channel_id=1, source_target_pairs={{0,2},{1,3},{2,0},{3,1},{4,6},{5,7},{6,4},{7,5},{8,10},{9,11},{10,... | collective-permute-start | bytes 393224 | tf_op jit(solution)/shard_map/ppermute | solution.py:455
  135.7 7.8 %collective-permute-start.24 = (f32[128,256]{1,0:T(8,128)S(1)}, f32[128,256]{1,0:T(8,128)S(1)}, u32[]{:S(2)}, u32[]{:S(2)}) collective-permute-start(f32[128,256]{1,0:T(8,128)S(1)} %get-tuple-element.108.p0.pull_ref), channel_id=1, source_target_pairs={{0,1},{1,0},{2,3},{3,2},{4,5},{5,4},{6,7},{7,6},{8,9},{9,8},{10,11... | collective-permute-start | bytes 393224 | tf_op jit(solution)/shard_map/ppermute | solution.py:455
  146.1 29.3 %all-to-all-start.3 = ((f32[64,8,256]{2,1,0:T(8,128)}), f32[64,8,256]{2,1,0:T(8,128)S(1)}, u32[]{:S(2)}, u32[]{:S(2)}) async-start(f32[64,8,256]{2,1,0:T(8,128)} %shard_map.100), calls=%async_computation.3 | async-start | bytes 1048576 | tf_op jit(solution)/shard_map/all_to_all | solution.py:468
  156.1 14.5 %collective-permute-start.28 = (f32[160,256]{1,0:T(8,128)}, f32[160,256]{1,0:T(8,128)S(1)}, u32[]{:S(2)}, u32[]{:S(2)}) collective-permute-start(f32[160,256]{1,0:T(8,128)} %copy-done.33), channel_id=1, source_target_pairs={{0,2},{1,3},{2,0},{3,1},{4,6},{5,7},{6,4},{7,5},{8,10},{9,11},{10,... | collective-permute-start | bytes 491528 | tf_op jit(solution)/shard_map/ppermute | solution.py:455
  156.7 18.4 %collective-permute-start.29 = (f32[160,256]{1,0:T(8,128)}, f32[160,256]{1,0:T(8,128)S(1)}, u32[]{:S(2)}, u32[]{:S(2)}) collective-permute-start(f32[160,256]{1,0:T(8,128)} %copy-done.32), channel_id=1, source_target_pairs={{0,3},{1,2},{2,1},{3,0},{4,7},{5,6},{6,5},{7,4},{8,11},{9,10},{10,... | collective-permute-start | bytes 491528 | tf_op jit(solution)/shard_map/ppermute | solution.py:455
  (38 other events, 342.1 us)

commit v4 on v2

v4 whole, which is shorter than its diff:
```python
import functools
import math

import jax
import jax.numpy as jnp
import numpy as np
from jax import lax
from jax.experimental import pallas as pl
from jax.experimental.pallas import tpu as pltpu
from jax.sharding import Mesh
from jax.sharding import PartitionSpec as P

TWO_PI = 2.0 * math.pi
F32 = jnp.float32
BF16 = jnp.bfloat16
XY = ("x", "y")
DEPTH = ("x", "y", "h")
COMP = ("l", "k")
ALL = ("x", "y", "h", "l", "k")

NX = 512
NY = 256
HX = NX // 2
QX = NX // 4
HY = NY // 2


def split_table(table):
    high = table.astype(jnp.bfloat16)
    low = (table - high.astype(np.float64)).astype(jnp.bfloat16)
    return np.stack([high, low])


def basis(count, waves):
    place = np.arange(count)
    rows = []
    for wave in waves:
        norm = math.sqrt((1.0 if wave == 0 else 2.0) / count)
        rows.append(norm * np.cos(TWO_PI * (wave * place % count) / count))
    for wave in waves:
        if wave == 0:
            rows.append(math.sqrt(1.0 / count) * (1.0 - 2.0 * (place % 2)))
        else:
            rows.append(math.sqrt(2.0 / count) * np.sin(TWO_PI * (wave * place % count) / count))
    return np.stack(rows)


def make_tables():
    even = basis(NX, range(0, HX, 2))[:, :HX]
    odd = basis(NX, range(1, HX, 2))[:, :HX]
    col = basis(NY, range(HY))
    return (
        np.concatenate([split_table(even), split_table(odd)]),
        split_table(col.T),
    )


def split(value):
    high = value.astype(BF16)
    low = (value - high.astype(F32)).astype(BF16)
    return high, low


def dot(left, right):
    return jnp.dot(left, right, preferred_element_type=F32)


def dot_turned(left, right):
    return lax.dot_general(left, right, (((1,), (1,)), ((), ())), preferred_element_type=F32)


def times_table(value, high, low):
    vh, vl = split(value)
    return dot(vh, high) + (dot(vl, high) + dot(vh, low))


def times_turned(value, high, low):
    vh, vl = split(value)
    return dot_turned(vh, high) + (dot_turned(vl, high) + dot_turned(vh, low))


def table_times(high, low, value):
    vh, vl = split(value)
    return dot(high, vh) + (dot(high, vl) + dot(low, vh))


def to_waves(field, fx, ty):
    cols = times_table(field, ty[0], ty[1])
    upper, lower = cols[:HX], cols[HX:]
    return (
        table_times(fx[0], fx[1], upper + lower),
        table_times(fx[2], fx[3], upper - lower),
    )


def from_waves(even, odd, bx, ty):
    first = table_times(bx[0], bx[1], even)
    second = table_times(bx[2], bx[3], odd)
    rows = jnp.concatenate([first + second, first - second], axis=0)
    return times_turned(rows, ty[0], ty[1])


def swap_x(half):
    return jnp.concatenate([half[HX // 2 :], half[: HX // 2]], axis=0)


def swap_y(half):
    return jnp.concatenate([half[:, HY:], half[:, :HY]], axis=1)


def sines(cosines, nyquist):
    row = lax.broadcasted_iota(jnp.int32, cosines.shape, 0)
    return jnp.where(row == 0, nyquist, cosines)


def spread(ref):
    even, odd = ref[:QX], ref[QX:HX]
    return (
        jnp.concatenate([even, sines(even, ref[HX : HX + 1])], axis=0),
        jnp.concatenate([odd, odd], axis=0),
    )


def x_factors(gx_ref):
    even, odd = gx_ref[:QX], gx_ref[QX:HX]
    return jnp.concatenate([even, -even], axis=0), jnp.concatenate([odd, -odd], axis=0)


def xx_factors(gx_ref):
    even, odd = spread(gx_ref)
    return -(even * even), -(odd * odd)


def component(even, odd, gx_ref, gy_ref, comp):
    halves = []
    for half, first, second, third in zip(
        (even, odd), x_factors(gx_ref), spread(gy_ref), xx_factors(gx_ref)
    ):
        met = jnp.where(comp == 1, swap_x(half), jnp.where(comp == 2, swap_y(half), half))
        factor = jnp.where(comp == 1, first, jnp.where(comp == 2, second, third))
        halves.append(met * jnp.where(comp == 0, 1.0, factor))
    return halves


def comp_index():
    return lax.axis_index("l") * 2 + lax.axis_index("k")


KEPT = HX + 8


def wave_grid():
    row = lax.broadcasted_iota(jnp.int32, (KEPT, NY), 0)
    col = lax.broadcasted_iota(jnp.int32, (KEPT, NY), 1)
    wave_x = jnp.where(row >= HX, HX, 2 * (row % QX) + (row >= QX).astype(jnp.int32))
    nyquist_y = col == HY
    wave_y = jnp.where(nyquist_y, HY, col % HY)
    kx = wave_x.astype(F32) * (TWO_PI / NX)
    ky = wave_y.astype(F32) * (TWO_PI / NY)
    return kx, ky, col >= HY, nyquist_y


def prepare_kernel(
    top_ref, fx_in, ty_in, dens_in, weight_in, obs_in,
    fx, bx, ty, dens_ref, weight_ref, obs_ref, decay_ref, gx_ref, gy_ref,
):
    dens_ref[...] = dens_in[0]
    weight_ref[...] = weight_in[0]
    obs_ref[...] = obs_in[0]
    for place in range(4):
        table = fx_in[place]
        fx[place] = table
        bx[place] = table.astype(F32).T.astype(BF16)
    for place in range(2):
        ty[place] = ty_in[place]
    kx, ky, sine_y, nyquist_y = wave_grid()
    kabs = jnp.sqrt(kx * kx + ky * ky)
    inverse = 1.0 / jnp.maximum(kabs, TWO_PI / max(NX, NY))
    decay_ref[...] = 4.0 * jnp.exp(-kabs * top_ref[0]) * (1.0 - jnp.exp(-kabs))
    gx_ref[...] = kx * inverse
    ry = ky * inverse
    gy_ref[...] = jnp.where(nyquist_y, 0.0, jnp.where(sine_y, -ry, ry))


def gather_rows(pieces, full_ref):
    comp = comp_index()
    for step, piece in enumerate(pieces):
        full_ref[pl.ds(pl.multiple_of(jnp.bitwise_xor(comp, step) * QX, QX), QX), :] = piece[...]


def forward_plane(field, decay_ref, gx_ref, gy_ref, fx, bx, ty):
    even, odd = to_waves(field, fx, ty)
    decay = spread(decay_ref)
    even, odd = component(even * decay[0], odd * decay[1], gx_ref, gy_ref, comp_index())
    return from_waves(even, odd, bx, ty)


def start_kernel(
    nxy, m0, m1, m2, m3, top_ref, decay_ref, gx_ref, gy_ref, fx, bx, ty, out_ref, full_ref, pull_ref
):
    rows = NX // nxy
    gather_rows((m0, m1, m2, m3), full_ref)
    dens = full_ref[...]
    pull_ref[...] = 0.5 * (dens * (1.0 / (dens * dens + 0.25)))
    for place, field in enumerate((full_ref, pull_ref)):
        plane = forward_plane(field[...], decay_ref, gx_ref, gy_ref, fx, bx, ty)
        for target in range(nxy):
            out_ref[target, place * rows : (place + 1) * rows, :] = plane[
                target * rows : (target + 1) * rows
            ]
    for target in range(nxy):
        out_ref[target, 2 * rows : 2 * rows + 8, :] = jnp.full((8, NY), top_ref[0], F32)


def collect_kernel(nxy, got_ref, weight_ref, obs_ref, sum_ref):
    rows = NX // nxy
    total = got_ref[0, : 2 * rows, :]
    for source in range(1, nxy):
        total = total + got_ref[source, : 2 * rows, :]
    sum_ref[: 2 * rows] = total
    for source in range(nxy):
        place = 2 * rows + source
        sum_ref[place : place + 1, :] = got_ref[source, 2 * rows : 2 * rows + 1, :]
    part = weight_ref.shape[0]
    start = 2 * rows + nxy
    sum_ref[start : start + part] = weight_ref[...]
    sum_ref[start + part : start + 2 * part] = obs_ref[...]


def residual_kernel(nxy, nh, *refs):
    rows = NX // nxy
    part = rows // nh
    start = 2 * rows + nxy
    sums = refs[:nh]
    pred_ref, pull_ref, weight_ref, tops_ref, send_ref, meas_ref = refs[nh:]
    chip = lax.axis_index("h")
    total = sums[0][: 2 * rows]
    for step in range(1, nh):
        total = total + sums[step][: 2 * rows]
    for step in range(nh):
        tops_ref[step * nxy : (step + 1) * nxy] = sums[step][2 * rows : start]
        place = pl.ds(pl.multiple_of(lax.rem(chip + (nh - step), nh) * part, part), part)
        weight_ref[place, :] = sums[step][start : start + part]
        meas_ref[place, :] = sums[step][start + part :]
    weight = weight_ref[...]
    pred = total[:rows]
    pred_ref[...] = pred
    pull_ref[...] = total[rows:]
    res = weight * (weight * (pred - meas_ref[...]))
    for target in range(nxy):
        send_ref[target] = res


def power_kernel(layers, tops_ref, power_ref):
    kx, ky, *_ = wave_grid()
    for start in range(0, KEPT, 64):
        stop = min(start + 64, KEPT)
        ks = jnp.sqrt(kx[start:stop] ** 2 + ky[start:stop] ** 2)
        double = -2.0 * ks

        def add(step, total):
            for layer in range(4):
                total = total + jnp.exp(double * tops_ref[pl.ds(4 * step + layer, 1), :])
            return total

        total = lax.fori_loop(0, layers // 4, add, jnp.zeros_like(ks))
        rise = 1.0 - jnp.exp(-ks)
        power_ref[start:stop] = (16.0 * (rise * rise)) * total


def adjoint_kernel(
    nxy, res_ref, decay_ref, gx_ref, gy_ref, power_ref, fx, bx, ty, o0, o1, o2, o3, z_ref, i_ref
):
    rows = NX // nxy
    comp = comp_index()
    even, odd = to_waves(res_ref[...], fx, ty)
    even, odd = component(even, odd, gx_ref, gy_ref, comp)
    sign = jnp.where((comp == 1) | (comp == 2), -1.0, 1.0)
    even = even * sign
    odd = odd * sign
    decay = spread(decay_ref)
    z_ref[...] = from_waves(even * decay[0], odd * decay[1], bx, ty)
    power = spread(power_ref)
    even = even * power[0]
    odd = odd * power[1]
    block = lax.axis_index("x") * lax.axis_size("y") + lax.axis_index("y")
    upper = block * rows < HX
    near = pl.ds(pl.multiple_of(lax.rem(block * rows, HX), rows), rows)
    flip = jnp.where(upper, 1.0, -1.0)
    for target in range(4):
        if target == 0:
            e, o = even, odd
        elif target == 1:
            first = x_factors(gx_ref)
            e, o = swap_x(even) * first[0], swap_x(odd) * first[1]
        elif target == 2:
            second = spread(gy_ref)
            e, o = swap_y(even) * second[0], swap_y(odd) * second[1]
        else:
            third = xx_factors(gx_ref)
            e, o = even * third[0], odd * third[1]
        line = table_times(bx[0, near, :], bx[1, near, :], e)
        line = line + flip * table_times(bx[2, near, :], bx[3, near, :], o)
        i_ref[target * rows : (target + 1) * rows, :] = line
    i_ref[...] = times_turned(i_ref[...], ty[0], ty[1])
    for step, out in enumerate((o0, o1, o2, o3)):
        other = jnp.bitwise_xor(comp, step)
        out[:QX] = z_ref[pl.ds(pl.multiple_of(other * QX, QX), QX), :]
        out[QX:] = i_ref[pl.ds(pl.multiple_of(other * rows, rows), rows), :]


def share(grad, quad, image, weight, scratch, part):
    scratch[...] = weight * image
    place = pl.ds(pl.multiple_of(lax.axis_index("h") * part, part), part)
    mine = scratch[place, :]
    lane = lax.broadcasted_iota(jnp.int32, (1, 128), 1)
    square = grad * grad
    gg = jnp.sum(square)
    qgg = jnp.sum(quad * square)
    curv = jnp.sum(mine * mine)
    return jnp.where(lane == 0, gg, jnp.where(lane == 1, qgg, jnp.where(lane == 2, curv, 0.0)))


def step_length(shares):
    total = jnp.sum(shares, axis=0, keepdims=True)
    lane = lax.broadcasted_iota(jnp.int32, total.shape, 1)
    pick = lambda place: jnp.sum(jnp.where(lane == place, total, 0.0), keepdims=True)
    return pick(0) / (pick(2) + 0.5 * pick(1))


def gradient_kernel(nxy, nh, *refs):
    rows = NX // nxy
    part = rows // nh
    pieces = refs[:4]
    pull_ref, dens_ref, weight_ref = refs[4:7]
    share_ref, send_ref, grad_ref, line_ref, image_ref, scratch = refs[7:]
    total = pieces[0][...] + pieces[1][...] + (pieces[2][...] + pieces[3][...])
    data = total[:QX]
    line = total[QX:]
    dens = dens_ref[...]
    quad = 1.0 / (dens * dens + 0.25)
    grad = data + 0.5 * (quad * dens)
    image = line + pull_ref[...]
    weight = weight_ref[...]
    share_ref[...] = jnp.broadcast_to(
        share(grad, quad, image, weight, scratch, part), share_ref.shape
    )
    grad_ref[...] = grad
    line_ref[...] = line
    image_ref[...] = image
    back = weight * (weight * image)
    for target in range(nxy):
        send_ref[target] = back


def second_kernel(
    shares_ref, dens_ref, full_ref, g0, g1, g2, g3, decay_ref, gx_ref, gy_ref, fx, bx, ty,
    out_ref, dens_out, base_out, alpha_ref, all_ref,
):
    alpha = step_length(shares_ref[...])
    alpha_ref[...] = jnp.broadcast_to(alpha, alpha_ref.shape)
    old = dens_ref[...]
    dens = old - alpha * g0[...]
    dens_out[...] = dens
    data = g0[...] - 0.5 * ((1.0 / (old * old + 0.25)) * old)
    base_out[...] = data + 0.5 * (dens * (1.0 / (dens * dens + 0.25)))
    gather_rows((g0, g1, g2, g3), all_ref)
    dens = full_ref[...] - alpha * all_ref[...]
    all_ref[...] = 0.5 * (dens * (1.0 / (dens * dens + 0.25)))
    plane = forward_plane(all_ref[...], decay_ref, gx_ref, gy_ref, fx, bx, ty)
    out_ref[...] = plane.reshape(out_ref.shape)


def second_gradient_kernel(
    u0, u1, u2, u3, alpha_ref, base_ref, dens_ref, line_ref, grad_ref, image_ref, share_ref
):
    alpha = alpha_ref[:1, :1]
    total = u0[...] + u1[...] + (u2[...] + u3[...])
    dens = dens_ref[...]
    grad = base_ref[...] - alpha * total[:QX]
    quad = 1.0 / (dens * dens + 0.25)
    grad_ref[...] = grad
    image_ref[...] = line_ref[...] - alpha * total[QX:]
    square = grad * grad
    lane = lax.broadcasted_iota(jnp.int32, (8, 128), 1)
    share_ref[...] = jnp.where(
        lane == 0, jnp.sum(square), jnp.where(lane == 1, jnp.sum(quad * square), 0.0)
    )


def curvature_kernel(got_ref, image_ref, weight_ref, part_ref, share_ref, out_ref):
    part = weight_ref.shape[0]
    image = image_ref[pl.ds(pl.multiple_of(lax.axis_index("h") * part, part), part), :]
    total = got_ref[0]
    for source in range(1, got_ref.shape[0]):
        total = total + got_ref[source]
    image = image + total
    out_ref[...] = image
    mine = weight_ref[...] * image
    lane = lax.broadcasted_iota(jnp.int32, (1, 128), 1)
    share_ref[...] = jnp.broadcast_to(
        jnp.where(lane == 2, jnp.sum(mine * mine), part_ref[:1]), share_ref.shape
    )


def finish_kernel(
    shares_ref, dens_ref, grad_ref, alpha_ref, pred_ref, first_ref, second_ref, obs_ref, w_ref, dens_out, err_out
):
    part = obs_ref.shape[0]
    alpha = step_length(shares_ref[...])
    dens_out[0] = dens_ref[...] - alpha * grad_ref[...]
    place = pl.ds(pl.multiple_of(lax.axis_index("h") * part, part), part)
    pred = pred_ref[place, :] - alpha_ref[:1, :1] * first_ref[place, :]
    pred = pred - alpha * second_ref[...]
    err_out[0] = w_ref[...] * (pred - obs_ref[...])


VMEM = pl.BlockSpec(memory_space=pltpu.VMEM)
SMEM = pl.BlockSpec(memory_space=pltpu.SMEM)
ANY = pl.BlockSpec(memory_space=pl.ANY)


class Program:
    def __init__(self):
        self.alive = []

    def hold(self, *values):
        self.alive += values

    def drop(self, *values):
        self.alive = [item for item in self.alive if all(item is not value for value in values)]

    def call(self, kernel, outs, *args, scratch=(), scalars=(), mib=8):
        used = len(args)
        keep = [item for item in self.alive if all(item is not value for value in args)]
        kept = len(keep)

        def inner(*refs):
            kernel(*refs[:used], *refs[used + kept :])

        kinds = [(item, F32) if isinstance(item, tuple) else (item.shape, item.dtype) for item in outs]
        return pl.pallas_call(
            inner,
            out_shape=[jax.ShapeDtypeStruct(shape, dtype) for shape, dtype in kinds],
            in_specs=[SMEM if place in scalars else VMEM for place in range(used)] + [ANY] * kept,
            out_specs=[VMEM] * len(outs),
            scratch_shapes=[pltpu.VMEM(shape, F32) for shape in scratch],
            compiler_params=pltpu.CompilerParams(vmem_limit_bytes=mib << 20),
        )(*args, *keep)


def from_comps(values):
    return [values[0]] + [
        lax.ppermute(values[step], COMP, [(i, i ^ step) for i in range(4)]) for step in (1, 2, 3)
    ]


def from_axis(values, axis):
    size = len(values)
    return [values[0]] + [
        lax.ppermute(values[step], axis, [(i, (i + step) % size) for i in range(size)])
        for step in range(1, size)
    ]


def exchange(value, axes):
    return lax.all_to_all(value, axes, 0, 0, tiled=True)


def after(values, *others):
    if isinstance(values, (list, tuple)):
        return list(lax.optimization_barrier((tuple(values), others))[0])
    return lax.optimization_barrier((values, others))[0]


def body(density, observed, data_weight, layer_top):
    nx, ny, nh = (lax.axis_size(axis) for axis in DEPTH)
    nxy = nx * ny
    devices = nxy * nh * 4
    rows = NX // nxy
    part = rows // nh
    fx, ty = (jnp.asarray(table) for table in make_tables())
    bind = functools.partial
    program = Program()
    call = program.call

    layers = from_comps([density[0]] * 4)
    *tables, dens, weight_own, obs_own, decay, gx, gy = call(
        prepare_kernel,
        [
            fx, fx, ty, (QX, NY), (part, NY), (part, NY), (KEPT, NY), (KEPT, NY), (KEPT, NY),
        ],
        layer_top, fx, ty, density, data_weight, observed, scalars=(0,),
    )
    factors = (decay, gx, gy)
    program.hold(*tables, *factors, dens, weight_own, obs_own)
    message, full = call(
        bind(start_kernel, nxy), [(nxy, 2 * rows + 8, NY), (NX, NY)],
        dens, *layers[1:], layer_top, *factors, *tables, scratch=[(NX, NY)], scalars=(4,),
    )
    got = exchange(message, XY)
    (sums,) = call(
        bind(collect_kernel, nxy), [(2 * rows + nxy + 2 * part, NY)], got, weight_own, obs_own
    )
    sums = from_axis([sums] * nh, "h")
    pred, pulled, weight, tops, message = call(
        bind(residual_kernel, nxy, nh),
        [(rows, NY), (rows, NY), (rows, NY), (nxy * nh, NY), (nxy, rows, NY)],
        *sums, scratch=[(rows, NY)],
    )
    program.hold(pred, pulled, weight)
    got = exchange(message, XY)
    (power,) = call(bind(power_kernel, nxy * nh), [(KEPT, NY)], tops)
    program.hold(power)
    adjoint = lambda plane: call(
        bind(adjoint_kernel, nxy), [(QX + rows, NY)] * 4,
        plane.reshape(NX, NY), *factors, power, *tables,
        scratch=[(NX, NY), (4 * rows, NY)],
    )
    pieces = from_comps(adjoint(got))
    shares, message, grad, line, image = call(
        bind(gradient_kernel, nxy, nh),
        [(devices, 128), (nxy, rows, NY), (QX, NY), (rows, NY), (rows, NY)],
        *pieces, pulled, dens, weight, scratch=[(rows, NY)],
    )
    program.drop(pulled, weight)
    program.hold(line, image)
    grads = from_comps([grad] * 4)
    shares = after(exchange(shares, ALL), *grads)
    back = exchange(after(message, shares), XY)
    message, dens, base, alpha = call(
        second_kernel, [(nxy * nh, part, NY), (QX, NY), (QX, NY), (8, 128)],
        shares, dens, full, *grads, *factors, *tables, scratch=[(NX, NY)],
    )
    program.alive = [*tables, *factors, power, weight_own, obs_own, pred, line, image]
    program.hold(dens, base, alpha)
    got = exchange(after(message, back), DEPTH)
    pieces = from_comps(adjoint(after(back, message)))
    program.alive = [weight_own, obs_own, pred, image, dens, alpha]
    grad2, image2, half = call(
        second_gradient_kernel, [(QX, NY), (rows, NY), (8, 128)],
        *pieces, alpha, base, dens, line,
    )
    program.hold(grad2)
    got = after(got, half)
    shares, image2 = call(
        curvature_kernel, [(devices, 128), (part, NY)], got, image2, weight_own, half
    )
    shares = exchange(shares, ALL)
    program.alive = []
    return tuple(
        call(
            finish_kernel, [density.shape, observed.shape],
            shares, dens, grad2, alpha, pred, image, image2, obs_own, weight_own,
        )
    )


def solution(mesh):
    depth = mesh.shape["depth"]
    sizes = {64: (4, 4, 4), 4: (2, 1, 2)}[depth]
    fine = Mesh(mesh.devices.reshape(*sizes, 2, 2), ALL)
    data = P(COMP, DEPTH, None)
    layer = P(DEPTH, COMP, None)
    return jax.shard_map(
        body,
        mesh=fine,
        in_specs=(layer, data, data, P(DEPTH)),
        out_specs=(layer, data),
        check_vma=False,
    )
```

time: 182 us -> 179 us (0.984)
  blocking collectives: 66.6 us -> 47 us
  starting transfers between devices: 46.3 us -> 56.2 us
  waiting for transfers between devices: 32.5 us -> 41.4 us
  Pallas kernels: 20 us -> 17.1 us
    all_to_all x3 -> x2, blocking collectives: 66.6 us -> 47 us  [exchange(): return lax.all_to_all(value, axes, 0, 0, tiled=True)]
    all_to_all x3 -> x4, starting transfers between devices: 14.7 us -> 26.8 us  [exchange(): return lax.all_to_all(value, axes, 0, 0, tiled=True)]
    ppermute x12, waiting for transfers between devices: 19.4 us -> 26.9 us  [from_comps(): lax.ppermute(values[step], COMP, [(i, i ^ step) for i in range(4)])]
    ppermute x6 -> x3, starting transfers between devices: 15 us -> 10.5 us  [from_axis(): lax.ppermute(values[step], axis, [(i, (i + step) % size) for i in range(s...]
    pallas_call x14 -> x12, Pallas kernels: 20 us -> 17.1 us  [call(): pl.pallas_call(inner, out_shape=[jax.ShapeDtypeStruct(shape, dtype) for s...]
    ppermute x12, starting transfers between devices: 16.5 us -> 18.9 us  [from_comps(): lax.ppermute(values[step], COMP, [(i, i ^ step) for i in range(4)])]
    all_to_all x3 -> x4, waiting for transfers between devices: 7.08 us -> 9.27 us  [exchange(): return lax.all_to_all(value, axes, 0, 0, tiled=True)]
    unnamed x56 -> x42, local copies, waits for them, and re-layouts: 13.8 us -> 15.4 us
  transfers between devices with their start and end apart: 21 -> 19, of which waited for: 11 -> 12; matrix products, arithmetic and copies ran while one was open for 0% -> 0% of each run, Pallas kernels for 6% -> 5%
where the time goes in v4:
time: 179 us
  starting transfers between devices  56.2 us (31%)
  blocking collectives  47 us (26%)
  waiting for transfers between devices  41.4 us (23%)
  Pallas kernels  17.1 us (10%)
  local copies, waits for them, and re-layouts  15.4 us (9%)
    all_to_all x2, blocking collectives, exchange(): return lax.all_to_all(value, axes, 0, 0, tiled=True)  47 us
    ppermute x12, waiting for transfers between devices, from_comps(): lax.ppermute(values[step], COMP, [(i, i ^ step) for i in range(4)])  26.9 us
    all_to_all x4, starting transfers between devices, exchange(): return lax.all_to_all(value, axes, 0, 0, tiled=True)  26.8 us
    ppermute x12, starting transfers between devices, from_comps(): lax.ppermute(values[step], COMP, [(i, i ^ step) for i in range(4)])  18.9 us
    pallas_call x12, Pallas kernels, call(): pl.pallas_call(inner, out_shape=[jax.ShapeDtypeStruct(shape, dtype) for s...  17.1 us
    unnamed x42, local copies, waits for them, and re-layouts  15.4 us
    ppermute x3, starting transfers between devices, from_axis(): lax.ppermute(values[step], axis, [(i, (i + step) % size) for i in range(s...  10.5 us
    all_to_all x4, waiting for transfers between devices, exchange(): return lax.all_to_all(value, axes, 0, 0, tiled=True)  9.27 us
  transfers between devices with their start and end apart: 19, of which 12 were waited for; matrix products, arithmetic and copies ran while one was open for 0% of the time, Pallas kernels for 5%

profile of v4, /device:TPU:1, one launch (start us, length us, event | category | flops | bytes accessed | tf_op | source)
XLA Modules:
  0.0 178.5 jit_solution(2839400720908221307)
XLA Ops:
  0.6 3.1 %collective-permute-start.2 = (f32[128,256]{1,0:T(8,128)}, f32[128,256]{1,0:T(8,128)S(1)}, u32[]{:S(2)}, u32[]{:S(2)}) collective-permute-start(f32[128,256]{1,0:T(8,128)} %bitcast.15), channel_id=1, source_target_pairs={{0,3},{1,2},{2,1},{3,0},{4,7},{5,6},{6,5},{7,4},{8,11},{9,10},{10,... | collective-permute-start | bytes 393224 | tf_op jit(solution)/shard_map/ppermute | solution.py:454
  3.7 1.5 collective-permute-start.1
  10.8 2.9 %shard_map.78 = (f32[16,72,256]{2,1,0:T(8,128)S(1)}, f32[512,256]{1,0:T(8,128)S(1)}) custom-call(f32[128,256]{1,0:T(8,128)S(1)} %get-tuple-element.45.refs_0_.refs_9_.refs_10_.refs_7_.refs_8_.refs_5_.refs_1_, f32[128,256]{1,0:T(8,128)S(1)} %collective-permute-done.refs_1_, f32[128,256]{1,0:T(8,128)S(1)} %collective-permute-done.1.refs_2_, ...), custom_call_target="tpu_custom_call" | custom-call | tf_op jit(solution)/shard_map/pallas_call | solution.py:442
  14.6 22.7 %all_to_all.43.refs_0_ = f32[16,72,256]{2,1,0:T(8,128)S(1)} all-to-all(f32[16,72,256]{2,1,0:T(8,128)S(1)} %get-tuple-element.54), channel_id=1, replica_groups=mesh['x'=4,'y'=4,'h'=4,'l'=2,'k'=2] {'x','y'}, dimensions={0} | all-to-all | bytes 2359296 | tf_op jit(solution)/shard_map/all_to_all | solution.py:467
  37.4 7.3 %collective-permute-start.5 = (f32[96,256]{1,0:T(8,128)S(1)}, f32[96,256]{1,0:T(8,128)S(1)}, u32[]{:S(2)}, u32[]{:S(2)}) collective-permute-start(f32[96,256]{1,0:T(8,128)S(1)} %shard_map.79.refs_0_), channel_id=1, source_target_pairs={{0,12},{4,0},{8,4},{12,8},{1,13},{5,1},{9,5},{13,9},{2,14},{6,2},{... | collective-permute-start | bytes 294920 | tf_op jit(solution)/shard_map/ppermute | solution.py:461
  45.7 2.3 %collective-permute-start.3 = (f32[96,256]{1,0:T(8,128)S(1)}, f32[96,256]{1,0:T(8,128)S(1)}, u32[]{:S(2)}, u32[]{:S(2)}) collective-permute-start(f32[96,256]{1,0:T(8,128)S(1)} %shard_map.79.refs_0_), channel_id=1, source_target_pairs={{0,4},{4,8},{8,12},{12,0},{1,5},{5,9},{9,13},{13,1},{2,6},{6,10},{... | collective-permute-start | bytes 294920 | tf_op jit(solution)/shard_map/ppermute | solution.py:461
  47.9 4.4 %collective-permute-done.5.refs_3_ = f32[96,256]{1,0:T(8,128)S(1)} collective-permute-done((f32[96,256]{1,0:T(8,128)S(1)}, f32[96,256]{1,0:T(8,128)S(1)}, u32[]{:S(2)}, u32[]{:S(2)}) %collective-permute-start.5) | collective-permute-done | bytes 98336 | tf_op jit(solution)/shard_map/ppermute | solution.py:461
  54.0 3.7 %all-to-all-start.1 = ((f32[16,32,256]{2,1,0:T(8,128)}), f32[16,32,256]{2,1,0:T(8,128)S(1)}, u32[]{:S(2)}, u32[]{:S(2)}) async-start(f32[16,32,256]{2,1,0:T(8,128)} %copy-done.3), calls=%async_computation.1 | async-start | bytes 1048576 | tf_op jit(solution)/shard_map/all_to_all | solution.py:467
  57.8 3.6 %shard_map.81.refs_4_.refs_16_ = f32[264,256]{1,0:T(8,128)S(1)} custom-call(f32[64,256]{1,0:T(8,128)S(1)} %get-tuple-element.56.refs_0_, bf16[4,256,256]{2,1,0:T(8,128)(2,1)S(1)} %get-tuple-element.49.refs_8_.refs_3_.refs_4_.refs_1_.refs_5_.refs_7_.refs_10_, ...), custom_call_target="tpu_custom_call" | custom-call | tf_op jit(solution)/shard_map/pallas_call | solution.py:442
  61.4 5.4 %all-to-all-done.1 = f32[16,32,256]{2,1,0:T(8,128)S(1)} async-done(((f32[16,32,256]{2,1,0:T(8,128)}), f32[16,32,256]{2,1,0:T(8,128)S(1)}, u32[]{:S(2)}, u32[]{:S(2)}) %all-to-all-start.1) | async-done | bytes 524320 | tf_op jit(solution)/shard_map/all_to_all | solution.py:467
  66.7 2.4 %shard_map.82 = (f32[160,256]{1,0:T(8,128)S(1)}, f32[160,256]{1,0:T(8,128)S(1)}, f32[160,256]{1,0:T(8,128)S(1)}, f32[160,256]{1,0:T(8,128)S(1)}) custom-call(f32[512,256]{1,0:T(8,128)S(1)} %bitcast.12, f32[264,256]{1,0:T(8,128)S(1)} %get-tuple-element.46.refs_5_.refs_6_.refs_7_.refs_4_.refs_1_.refs_10_, ...), custom_call_target="tpu_custom_call" | custom-call | tf_op jit(solution)/shard_map/pallas_call | solution.py:442
  69.2 5.6 %collective-permute-start.6 = (f32[160,256]{1,0:T(8,128)S(1)}, f32[160,256]{1,0:T(8,128)S(1)}, u32[]{:S(2)}, u32[]{:S(2)}) collective-permute-start(f32[160,256]{1,0:T(8,128)S(1)} %get-tuple-element.61), channel_id=1, source_target_pairs={{0,1},{1,0},{2,3},{3,2},{4,5},{5,4},{6,7},{7,6},{8,9},{9,8},{10,11... | collective-permute-start | bytes 491528 | tf_op jit(solution)/shard_map/ppermute | solution.py:454
  74.8 1.2 collective-permute-start.7
  76.5 3.9 %collective-permute-done.7.refs_2_ = f32[160,256]{1,0:T(8,128)S(1)} collective-permute-done((f32[160,256]{1,0:T(8,128)S(1)}, f32[160,256]{1,0:T(8,128)S(1)}, u32[]{:S(2)}, u32[]{:S(2)}) %collective-permute-start.7) | collective-permute-done | bytes 163872 | tf_op jit(solution)/shard_map/ppermute | solution.py:454
  80.4 3.8 %collective-permute-done.8.refs_3_ = f32[160,256]{1,0:T(8,128)S(1)} collective-permute-done((f32[160,256]{1,0:T(8,128)S(1)}, f32[160,256]{1,0:T(8,128)S(1)}, u32[]{:S(2)}, u32[]{:S(2)}) %collective-permute-start.8) | collective-permute-done | bytes 163872 | tf_op jit(solution)/shard_map/ppermute | solution.py:454
  85.9 8.1 %all-to-all-start.2 = ((f32[256,1,128]{2,1,0:T(1,128)}), f32[256,1,128]{2,1,0:T(1,128)S(1)}, u32[]{:S(2)}, u32[]{:S(2)}) async-start(f32[256,1,128]{2,1,0:T(1,128)} %bitcast.3), calls=%async_computation.2 | async-start | bytes 262144 | tf_op jit(solution)/shard_map/all_to_all | solution.py:467
  94.0 1.8 %collective-permute-start.11 = (f32[128,256]{1,0:T(8,128)S(1)}, f32[128,256]{1,0:T(8,128)S(1)}, u32[]{:S(2)}, u32[]{:S(2)}) collective-permute-start(f32[128,256]{1,0:T(8,128)S(1)} %get-tuple-element.65.refs_3_), channel_id=1, source_target_pairs={{0,3},{1,2},{2,1},{3,0},{4,7},{5,6},{6,5},{7,4},{8,11},{9,10},{10,... | collective-permute-start | bytes 393224 | tf_op jit(solution)/shard_map/ppermute | solution.py:454
  95.9 1.7 collective-permute-start.10
  97.6 3.0 %collective-permute-done.11.refs_6_ = f32[128,256]{1,0:T(8,128)S(1)} collective-permute-done((f32[128,256]{1,0:T(8,128)S(1)}, f32[128,256]{1,0:T(8,128)S(1)}, u32[]{:S(2)}, u32[]{:S(2)}) %collective-permute-start.11) | collective-permute-done | bytes 131104 | tf_op jit(solution)/shard_map/ppermute | solution.py:454
  101.2 2.8 %collective-permute-done.10.refs_5_ = f32[128,256]{1,0:T(8,128)S(1)} collective-permute-done((f32[128,256]{1,0:T(8,128)S(1)}, f32[128,256]{1,0:T(8,128)S(1)}, u32[]{:S(2)}, u32[]{:S(2)}) %collective-permute-start.10) | collective-permute-done | bytes 131104 | tf_op jit(solution)/shard_map/ppermute | solution.py:454
  105.4 1.6 all-to-all-done.2
  106.9 4.9 %all-to-all-start.3 = ((f32[16,32,256]{2,1,0:T(8,128)}), f32[16,32,256]{2,1,0:T(8,128)S(1)}, u32[]{:S(2)}, u32[]{:S(2)}) async-start(f32[16,32,256]{2,1,0:T(8,128)} %copy-done.1), calls=%async_computation.3 | async-start | bytes 1048576 | tf_op jit(solution)/shard_map/all_to_all | solution.py:467
  116.5 2.0 %shard_map.84 = (f32[64,8,256]{2,1,0:T(8,128)S(1)}, f32[128,256]{1,0:T(8,128)S(1)}, f32[128,256]{1,0:T(8,128)S(1)}, f32[8,128]{1,0:T(8,128)S(1)}) custom-call(f32[256,128]{1,0:T(8,128)S(1)} %bitcast.14, f32[128,256]{1,0:T(8,128)S(1)} %get-tuple-element.45.refs_0_.refs_9_.refs_10_.refs_7_.refs_8_.refs_5_.refs_1_, f32[512,256]{1,0:T(8,128)S(1)} %copy-done.5, ...), custom_call_target="tpu_custom_call" | custom-call | tf_op jit(solution)/shard_map/pallas_call | solution.py:442
  119.8 2.3 %all-to-all-done.3 = f32[16,32,256]{2,1,0:T(8,128)S(1)} async-done(((f32[16,32,256]{2,1,0:T(8,128)}), f32[16,32,256]{2,1,0:T(8,128)S(1)}, u32[]{:S(2)}, u32[]{:S(2)}) %all-to-all-start.3) | async-done | bytes 524320 | tf_op jit(solution)/shard_map/all_to_all | solution.py:467
  122.2 10.0 %all-to-all-start.4 = ((f32[64,8,256]{2,1,0:T(8,128)}), f32[64,8,256]{2,1,0:T(8,128)}, u32[]{:S(2)}, u32[]{:S(2)}) async-start(f32[64,8,256]{2,1,0:T(8,128)} %copy-done), calls=%async_computation.4 | async-start | bytes 1048576 | tf_op jit(solution)/shard_map/all_to_all | solution.py:467
  132.9 2.4 %shard_map.85 = (f32[160,256]{1,0:T(8,128)S(1)}, f32[160,256]{1,0:T(8,128)S(1)}, f32[160,256]{1,0:T(8,128)S(1)}, f32[160,256]{1,0:T(8,128)S(1)}) custom-call(f32[512,256]{1,0:T(8,128)S(1)} %bitcast.11, f32[264,256]{1,0:T(8,128)S(1)} %get-tuple-element.46.refs_5_.refs_6_.refs_7_.refs_4_.refs_1_.refs_10_, ...), custom_call_target="tpu_custom_call" | custom-call | tf_op jit(solution)/shard_map/pallas_call | solution.py:442
  135.3 1.6 collective-permute-start.12
  137.5 1.1 collective-permute-start.14
  138.7 8.3 %collective-permute-done.13.refs_2_ = f32[160,256]{1,0:T(8,128)S(1)} collective-permute-done((f32[160,256]{1,0:T(8,128)S(1)}, f32[160,256]{1,0:T(8,128)S(1)}, u32[]{:S(2)}, u32[]{:S(2)}) %collective-permute-start.13) | collective-permute-done | bytes 163872 | tf_op jit(solution)/shard_map/ppermute | solution.py:454
  146.9 5.0 %collective-permute-done.14.refs_3_ = f32[160,256]{1,0:T(8,128)S(1)} collective-permute-done((f32[160,256]{1,0:T(8,128)S(1)}, f32[160,256]{1,0:T(8,128)S(1)}, u32[]{:S(2)}, u32[]{:S(2)}) %collective-permute-start.14) | collective-permute-done | bytes 163872 | tf_op jit(solution)/shard_map/ppermute | solution.py:454
  152.2 1.2 shard_map.87
  153.4 24.3 %all_to_all.44 = f32[256,1,128]{2,1,0:T(1,128)S(1)} all-to-all(f32[256,1,128]{2,1,0:T(1,128)S(1)} %bitcast.18), channel_id=1, replica_groups=mesh['x'=4,'y'=4,'h'=4,'l'=2,'k'=2] {'x','y','h','l','k'}, dimensions={0} | all-to-all | bytes 262144 | tf_op jit(solution)/shard_map/all_to_all | solution.py:467
  (62 shorter events, 21.1 us)
Async XLA Ops:
  0.6 10.1 %collective-permute-start.2 = (f32[128,256]{1,0:T(8,128)}, f32[128,256]{1,0:T(8,128)S(1)}, u32[]{:S(2)}, u32[]{:S(2)}) collective-permute-start(f32[128,256]{1,0:T(8,128)} %bitcast.15), channel_id=1, source_target_pairs={{0,3},{1,2},{2,1},{3,0},{4,7},{5,6},{6,5},{7,4},{8,11},{9,10},{10,... | collective-permute-start | bytes 393224 | tf_op jit(solution)/shard_map/ppermute | solution.py:454
  3.7 7.1 %collective-permute-start.1 = (f32[128,256]{1,0:T(8,128)}, f32[128,256]{1,0:T(8,128)S(1)}, u32[]{:S(2)}, u32[]{:S(2)}) collective-permute-start(f32[128,256]{1,0:T(8,128)} %bitcast.16), channel_id=1, source_target_pairs={{0,2},{1,3},{2,0},{3,1},{4,6},{5,7},{6,4},{7,5},{8,10},{9,11},{10,... | collective-permute-start | bytes 393224 | tf_op jit(solution)/shard_map/ppermute | solution.py:454
  5.3 5.5 %collective-permute-start = (f32[128,256]{1,0:T(8,128)}, f32[128,256]{1,0:T(8,128)S(1)}, u32[]{:S(2)}, u32[]{:S(2)}) collective-permute-start(f32[128,256]{1,0:T(8,128)} %bitcast.17), channel_id=1, source_target_pairs={{0,1},{1,0},{2,3},{3,2},{4,5},{5,4},{6,7},{7,6},{8,9},{9,8},{10,11... | collective-permute-start | bytes 393224 | tf_op jit(solution)/shard_map/ppermute | solution.py:454
  5.9 1.0 copy-start.2
  7.0 0.9 copy-start.6
  7.9 0.9 copy-start.7
  13.8 0.8 copy-start.4
  37.4 14.9 %collective-permute-start.5 = (f32[96,256]{1,0:T(8,128)S(1)}, f32[96,256]{1,0:T(8,128)S(1)}, u32[]{:S(2)}, u32[]{:S(2)}) collective-permute-start(f32[96,256]{1,0:T(8,128)S(1)} %shard_map.79.refs_0_), channel_id=1, source_target_pairs={{0,12},{4,0},{8,4},{12,8},{1,13},{5,1},{9,5},{13,9},{2,14},{6,2},{... | collective-permute-start | bytes 294920 | tf_op jit(solution)/shard_map/ppermute | solution.py:461
  44.6 8.5 %collective-permute-start.4 = (f32[96,256]{1,0:T(8,128)S(1)}, f32[96,256]{1,0:T(8,128)S(1)}, u32[]{:S(2)}, u32[]{:S(2)}) collective-permute-start(f32[96,256]{1,0:T(8,128)S(1)} %shard_map.79.refs_0_), channel_id=1, source_target_pairs={{0,8},{4,12},{8,0},{12,4},{1,9},{5,13},{9,1},{13,5},{2,10},{6,14},... | collective-permute-start | bytes 294920 | tf_op jit(solution)/shard_map/ppermute | solution.py:461
  45.7 7.5 %collective-permute-start.3 = (f32[96,256]{1,0:T(8,128)S(1)}, f32[96,256]{1,0:T(8,128)S(1)}, u32[]{:S(2)}, u32[]{:S(2)}) collective-permute-start(f32[96,256]{1,0:T(8,128)S(1)} %shard_map.79.refs_0_), channel_id=1, source_target_pairs={{0,4},{4,8},{8,12},{12,0},{1,5},{5,9},{9,13},{13,1},{2,6},{6,10},{... | collective-permute-start | bytes 294920 | tf_op jit(solution)/shard_map/ppermute | solution.py:461
  53.2 0.8 copy-start.3
  54.0 12.7 %all-to-all-start.1 = ((f32[16,32,256]{2,1,0:T(8,128)}), f32[16,32,256]{2,1,0:T(8,128)S(1)}, u32[]{:S(2)}, u32[]{:S(2)}) async-start(f32[16,32,256]{2,1,0:T(8,128)} %copy-done.3), calls=%async_computation.1 | async-start | bytes 1048576 | tf_op jit(solution)/shard_map/all_to_all | solution.py:467
  69.2 7.3 %collective-permute-start.6 = (f32[160,256]{1,0:T(8,128)S(1)}, f32[160,256]{1,0:T(8,128)S(1)}, u32[]{:S(2)}, u32[]{:S(2)}) collective-permute-start(f32[160,256]{1,0:T(8,128)S(1)} %get-tuple-element.61), channel_id=1, source_target_pairs={{0,1},{1,0},{2,3},{3,2},{4,5},{5,4},{6,7},{7,6},{8,9},{9,8},{10,11... | collective-permute-start | bytes 491528 | tf_op jit(solution)/shard_map/ppermute | solution.py:454
  74.8 5.7 %collective-permute-start.7 = (f32[160,256]{1,0:T(8,128)S(1)}, f32[160,256]{1,0:T(8,128)S(1)}, u32[]{:S(2)}, u32[]{:S(2)}) collective-permute-start(f32[160,256]{1,0:T(8,128)S(1)} %get-tuple-element.62), channel_id=1, source_target_pairs={{0,2},{1,3},{2,0},{3,1},{4,6},{5,7},{6,4},{7,5},{8,10},{9,11},{10,... | collective-permute-start | bytes 491528 | tf_op jit(solution)/shard_map/ppermute | solution.py:454
  75.9 8.3 %collective-permute-start.8 = (f32[160,256]{1,0:T(8,128)S(1)}, f32[160,256]{1,0:T(8,128)S(1)}, u32[]{:S(2)}, u32[]{:S(2)}) collective-permute-start(f32[160,256]{1,0:T(8,128)S(1)} %get-tuple-element.63), channel_id=1, source_target_pairs={{0,3},{1,2},{2,1},{3,0},{4,7},{5,6},{6,5},{7,4},{8,11},{9,10},{10,... | collective-permute-start | bytes 491528 | tf_op jit(solution)/shard_map/ppermute | solution.py:454
  85.9 25.9 %copy-start.8 = (f32[128,256]{1,0:T(8,128)}, f32[128,256]{1,0:T(8,128)S(1)}, u32[]{:S(2)}) copy-start(f32[128,256]{1,0:T(8,128)S(1)} %get-tuple-element.65.refs_3_) | copy-start | bytes 393220
  85.9 21.1 %all-to-all-start.2 = ((f32[256,1,128]{2,1,0:T(1,128)}), f32[256,1,128]{2,1,0:T(1,128)S(1)}, u32[]{:S(2)}, u32[]{:S(2)}) async-start(f32[256,1,128]{2,1,0:T(1,128)} %bitcast.3), calls=%async_computation.2 | async-start | bytes 262144 | tf_op jit(solution)/shard_map/all_to_all | solution.py:467
  94.0 6.6 %collective-permute-start.11 = (f32[128,256]{1,0:T(8,128)S(1)}, f32[128,256]{1,0:T(8,128)S(1)}, u32[]{:S(2)}, u32[]{:S(2)}) collective-permute-start(f32[128,256]{1,0:T(8,128)S(1)} %get-tuple-element.65.refs_3_), channel_id=1, source_target_pairs={{0,3},{1,2},{2,1},{3,0},{4,7},{5,6},{6,5},{7,4},{8,11},{9,10},{10,... | collective-permute-start | bytes 393224 | tf_op jit(solution)/shard_map/ppermute | solution.py:454
  95.9 8.2 %collective-permute-start.10 = (f32[128,256]{1,0:T(8,128)S(1)}, f32[128,256]{1,0:T(8,128)S(1)}, u32[]{:S(2)}, u32[]{:S(2)}) collective-permute-start(f32[128,256]{1,0:T(8,128)S(1)} %get-tuple-element.65.refs_3_), channel_id=1, source_target_pairs={{0,2},{1,3},{2,0},{3,1},{4,6},{5,7},{6,4},{7,5},{8,10},{9,11},{10,... | collective-permute-start | bytes 393224 | tf_op jit(solution)/shard_map/ppermute | solution.py:454
  97.6 7.1 %collective-permute-start.9 = (f32[128,256]{1,0:T(8,128)S(1)}, f32[128,256]{1,0:T(8,128)S(1)}, u32[]{:S(2)}, u32[]{:S(2)}) collective-permute-start(f32[128,256]{1,0:T(8,128)S(1)} %get-tuple-element.65.refs_3_), channel_id=1, source_target_pairs={{0,1},{1,0},{2,3},{3,2},{4,5},{5,4},{6,7},{7,6},{8,9},{9,8},{10,11... | collective-permute-start | bytes 393224 | tf_op jit(solution)/shard_map/ppermute | solution.py:454
  106.9 15.2 %all-to-all-start.3 = ((f32[16,32,256]{2,1,0:T(8,128)}), f32[16,32,256]{2,1,0:T(8,128)S(1)}, u32[]{:S(2)}, u32[]{:S(2)}) async-start(f32[16,32,256]{2,1,0:T(8,128)} %copy-done.1), calls=%async_computation.3 | async-start | bytes 1048576 | tf_op jit(solution)/shard_map/all_to_all | solution.py:467
  111.8 1.0 copy-start.5
  112.9 0.9 copy-start.9
  113.8 0.9 copy-start.11
  114.7 0.9 copy-start.13
  115.6 0.9 copy-start.15
  118.4 0.8 copy-start
  122.2 30.0 %all-to-all-start.4 = ((f32[64,8,256]{2,1,0:T(8,128)}), f32[64,8,256]{2,1,0:T(8,128)}, u32[]{:S(2)}, u32[]{:S(2)}) async-start(f32[64,8,256]{2,1,0:T(8,128)} %copy-done), calls=%async_computation.4 | async-start | bytes 1048576 | tf_op jit(solution)/shard_map/all_to_all | solution.py:467
  132.9 19.3 %copy-start.18 = (f32[8,128]{1,0:T(8,128)S(1)}, f32[8,128]{1,0:T(8,128)}, u32[]{:S(2)}) copy-start(f32[8,128]{1,0:T(8,128)} %copy-done.16) | copy-start | bytes 12292
  135.3 3.3 %collective-permute-start.12 = (f32[160,256]{1,0:T(8,128)S(1)}, f32[160,256]{1,0:T(8,128)S(1)}, u32[]{:S(2)}, u32[]{:S(2)}) collective-permute-start(f32[160,256]{1,0:T(8,128)S(1)} %get-tuple-element.79), channel_id=1, source_target_pairs={{0,1},{1,0},{2,3},{3,2},{4,5},{5,4},{6,7},{7,6},{8,9},{9,8},{10,11... | collective-permute-start | bytes 491528 | tf_op jit(solution)/shard_map/ppermute | solution.py:454
  136.9 10.0 %collective-permute-start.13 = (f32[160,256]{1,0:T(8,128)S(1)}, f32[160,256]{1,0:T(8,128)S(1)}, u32[]{:S(2)}, u32[]{:S(2)}) collective-permute-start(f32[160,256]{1,0:T(8,128)S(1)} %get-tuple-element.80), channel_id=1, source_target_pairs={{0,2},{1,3},{2,0},{3,1},{4,6},{5,7},{6,4},{7,5},{8,10},{9,11},{10,... | collective-permute-start | bytes 491528 | tf_op jit(solution)/shard_map/ppermute | solution.py:454
  137.5 14.4 %collective-permute-start.14 = (f32[160,256]{1,0:T(8,128)S(1)}, f32[160,256]{1,0:T(8,128)S(1)}, u32[]{:S(2)}, u32[]{:S(2)}) collective-permute-start(f32[160,256]{1,0:T(8,128)S(1)} %get-tuple-element.81), channel_id=1, source_target_pairs={{0,3},{1,2},{2,1},{3,0},{4,7},{5,6},{6,5},{7,4},{8,11},{9,10},{10,... | collective-permute-start | bytes 491528 | tf_op jit(solution)/shard_map/ppermute | solution.py:454
  (8 other events, 5.4 us)

commit v5 on v4

--- a/solution.py
+++ b/solution.py
@@ -196,10 +196,12 @@
 
 
 def start_kernel(
-    nxy, m0, m1, m2, m3, top_ref, decay_ref, gx_ref, gy_ref, fx, bx, ty, out_ref, full_ref, pull_ref
+    nxy, m0, m1, m2, m3, top_ref, decay_ref, gx_ref, gy_ref, fx, bx, ty, out_ref, far_ref, full_ref, pull_ref, sem
 ):
     rows = NX // nxy
     gather_rows((m0, m1, m2, m3), full_ref)
+    copy = pltpu.make_async_copy(full_ref, far_ref, sem)
+    copy.start()
     dens = full_ref[...]
     pull_ref[...] = 0.5 * (dens * (1.0 / (dens * dens + 0.25)))
     for place, field in enumerate((full_ref, pull_ref)):
@@ -210,6 +212,7 @@
             ]
     for target in range(nxy):
         out_ref[target, 2 * rows : 2 * rows + 8, :] = jnp.full((8, NY), top_ref[0], F32)
+    copy.wait()
 
 
 def collect_kernel(nxy, got_ref, weight_ref, obs_ref, sum_ref):
@@ -313,7 +316,7 @@
     scratch[...] = weight * image
     place = pl.ds(pl.multiple_of(lax.axis_index("h") * part, part), part)
     mine = scratch[place, :]
-    lane = lax.broadcasted_iota(jnp.int32, (1, 128), 1)
+    lane = lax.broadcasted_iota(jnp.int32, (1, NY), 1)
     square = grad * grad
     gg = jnp.sum(square)
     qgg = jnp.sum(quad * square)
@@ -333,7 +336,7 @@
     part = rows // nh
     pieces = refs[:4]
     pull_ref, dens_ref, weight_ref = refs[4:7]
-    share_ref, send_ref, grad_ref, line_ref, image_ref, scratch = refs[7:]
+    send_ref, grad_ref, line_ref, image_ref, scratch = refs[7:]
     total = pieces[0][...] + pieces[1][...] + (pieces[2][...] + pieces[3][...])
     data = total[:QX]
     line = total[QX:]
@@ -342,33 +345,65 @@
     grad = data + 0.5 * (quad * dens)
     image = line + pull_ref[...]
     weight = weight_ref[...]
-    share_ref[...] = jnp.broadcast_to(
-        share(grad, quad, image, weight, scratch, part), share_ref.shape
-    )
+    mine = jnp.broadcast_to(share(grad, quad, image, weight, scratch, part), (8, NY))
     grad_ref[...] = grad
     line_ref[...] = line
     image_ref[...] = image
     back = weight * (weight * image)
     for target in range(nxy):
-        send_ref[target] = back
+        send_ref[target, :rows] = back
+        send_ref[target, rows:] = mine
+
+
+def part_kernel(nxy, got_ref, plane_ref, share_ref):
+    rows = NX // nxy
+    total = got_ref[0, rows:, :]
+    for source in range(1, nxy):
+        total = total + got_ref[source, rows:, :]
+    share_ref[...] = total
+    for source in range(nxy):
+        plane_ref[source * rows : (source + 1) * rows] = got_ref[source, :rows, :]
+
+
+def add_kernel(*refs):
+    total = refs[0][...]
+    for part in refs[1:-1]:
+        total = total + part[...]
+    refs[-1][...] = total
 
 
 def second_kernel(
-    shares_ref, dens_ref, full_ref, g0, g1, g2, g3, decay_ref, gx_ref, gy_ref, fx, bx, ty,
-    out_ref, dens_out, base_out, alpha_ref, all_ref,
+    s0, s1, s2, s3, dens_ref, full_ref, g0, g1, g2, g3, decay_ref, gx_ref, gy_ref, fx, bx, ty,
+    out_ref, dens_out, base_out, alpha_ref, all_ref, near_ref, sems,
 ):
-    alpha = step_length(shares_ref[...])
+    comp = comp_index()
+    copies = [pltpu.make_async_copy(full_ref, near_ref, sems.at[4])]
+    for step, piece in enumerate((g0, g1, g2, g3)):
+        place = pl.ds(pl.multiple_of(jnp.bitwise_xor(comp, step) * QX, QX), QX)
+        copies.append(pltpu.make_async_copy(piece, all_ref.at[place, :], sems.at[step]))
+    for copy in copies:
+        copy.start()
+    alpha = step_length(s0[:1] + s1[:1] + (s2[:1] + s3[:1]))
     alpha_ref[...] = jnp.broadcast_to(alpha, alpha_ref.shape)
     old = dens_ref[...]
-    dens = old - alpha * g0[...]
+    for copy in copies:
+        copy.wait()
+    grad = all_ref[pl.ds(pl.multiple_of(comp * QX, QX), QX), :]
+    dens = old - alpha * grad
     dens_out[...] = dens
-    data = g0[...] - 0.5 * ((1.0 / (old * old + 0.25)) * old)
+    data = grad - 0.5 * ((1.0 / (old * old + 0.25)) * old)
     base_out[...] = data + 0.5 * (dens * (1.0 / (dens * dens + 0.25)))
-    gather_rows((g0, g1, g2, g3), all_ref)
-    dens = full_ref[...] - alpha * all_ref[...]
+    dens = near_ref[...] - alpha * all_ref[...]
     all_ref[...] = 0.5 * (dens * (1.0 / (dens * dens + 0.25)))
     plane = forward_plane(all_ref[...], decay_ref, gx_ref, gy_ref, fx, bx, ty)
     out_ref[...] = plane.reshape(out_ref.shape)
+
+
+def sum_kernel(nxy, got_ref, sum_ref):
+    total = got_ref[0]
+    for source in range(1, nxy):
+        total = total + got_ref[source]
+    sum_ref[...] = total
 
 
 def second_gradient_kernel(
@@ -388,13 +423,14 @@
     )
 
 
-def curvature_kernel(got_ref, image_ref, weight_ref, part_ref, share_ref, out_ref):
+def curvature_kernel(nh, *refs):
+    parts = refs[:nh]
+    image_ref, weight_ref, part_ref, share_ref, out_ref = refs[nh:]
     part = weight_ref.shape[0]
-    image = image_ref[pl.ds(pl.multiple_of(lax.axis_index("h") * part, part), part), :]
-    total = got_ref[0]
-    for source in range(1, got_ref.shape[0]):
-        total = total + got_ref[source]
-    image = image + total
+    place = pl.ds(pl.multiple_of(lax.axis_index("h") * part, part), part)
+    image = image_ref[place, :]
+    for piece in parts:
+        image = image + piece[place, :]
     out_ref[...] = image
     mine = weight_ref[...] * image
     lane = lax.broadcasted_iota(jnp.int32, (1, 128), 1)
@@ -430,7 +466,7 @@
     def drop(self, *values):
         self.alive = [item for item in self.alive if all(item is not value for value in values)]
 
-    def call(self, kernel, outs, *args, scratch=(), scalars=(), mib=8):
+    def call(self, kernel, outs, *args, scratch=(), scalars=(), far=(), far_out=(), sems=0, mib=8):
         used = len(args)
         keep = [item for item in self.alive if all(item is not value for value in args)]
         kept = len(keep)
@@ -442,9 +478,13 @@
         return pl.pallas_call(
             inner,
             out_shape=[jax.ShapeDtypeStruct(shape, dtype) for shape, dtype in kinds],
-            in_specs=[SMEM if place in scalars else VMEM for place in range(used)] + [ANY] * kept,
-            out_specs=[VMEM] * len(outs),
-            scratch_shapes=[pltpu.VMEM(shape, F32) for shape in scratch],
+            in_specs=[
+                SMEM if place in scalars else ANY if place in far else VMEM for place in range(used)
+            ]
+            + [ANY] * kept,
+            out_specs=[ANY if place in far_out else VMEM for place in range(len(outs))],
+            scratch_shapes=[pltpu.VMEM(shape, F32) for shape in scratch]
+            + [pltpu.SemaphoreType.DMA((sems,) if sems > 1 else ())] * (sems > 0),
             compiler_params=pltpu.CompilerParams(vmem_limit_bytes=mib << 20),
         )(*args, *keep)
 
@@ -496,7 +536,8 @@
     program.hold(*tables, *factors, dens, weight_own, obs_own)
     message, full = call(
         bind(start_kernel, nxy), [(nxy, 2 * rows + 8, NY), (NX, NY)],
-        dens, *layers[1:], layer_top, *factors, *tables, scratch=[(NX, NY)], scalars=(4,),
+        dens, *layers[1:], layer_top, *factors, *tables,
+        scratch=[(NX, NY)] * 2, scalars=(4,), far_out=(1,), sems=1,
     )
     got = exchange(message, XY)
     (sums,) = call(
@@ -518,33 +559,37 @@
         scratch=[(NX, NY), (4 * rows, NY)],
     )
     pieces = from_comps(adjoint(got))
-    shares, message, grad, line, image = call(
+    message, grad, line, image = call(
         bind(gradient_kernel, nxy, nh),
-        [(devices, 128), (nxy, rows, NY), (QX, NY), (rows, NY), (rows, NY)],
+        [(nxy, rows + 8, NY), (QX, NY), (rows, NY), (rows, NY)],
         *pieces, pulled, dens, weight, scratch=[(rows, NY)],
     )
     program.drop(pulled, weight)
     program.hold(line, image)
     grads = from_comps([grad] * 4)
-    shares = after(exchange(shares, ALL), *grads)
-    back = exchange(after(message, shares), XY)
+    got = after(exchange(message, XY), *grads)
+    plane, shares = call(bind(part_kernel, nxy), [(NX, NY), (8, NY)], got)
+    pieces = adjoint(plane)
+    shares = after(from_axis([shares] * nh, "h"), *pieces)
+    (shares,) = call(add_kernel, [(8, NY)], *shares)
+    shares = from_comps([shares] * 4)
     message, dens, base, alpha = call(
-        second_kernel, [(nxy * nh, part, NY), (QX, NY), (QX, NY), (8, 128)],
-        shares, dens, full, *grads, *factors, *tables, scratch=[(NX, NY)],
-    )
-    program.alive = [*tables, *factors, power, weight_own, obs_own, pred, line, image]
-    program.hold(dens, base, alpha)
-    got = exchange(after(message, back), DEPTH)
-    pieces = from_comps(adjoint(after(back, message)))
-    program.alive = [weight_own, obs_own, pred, image, dens, alpha]
+        second_kernel, [(nxy, rows, NY), (QX, NY), (QX, NY), (8, 128)],
+        *shares, dens, full, *grads, *factors, *tables,
+        scratch=[(NX, NY)] * 2, far=(5, 6, 7, 8, 9), sems=5,
+    )
+    program.alive = [weight_own, obs_own, pred, line, image, dens, base, alpha]
+    got = exchange(message, XY)
+    pieces = from_comps(after(pieces, message))
     grad2, image2, half = call(
         second_gradient_kernel, [(QX, NY), (rows, NY), (8, 128)],
         *pieces, alpha, base, dens, line,
     )
-    program.hold(grad2)
-    got = after(got, half)
+    (parts,) = call(bind(sum_kernel, nxy), [(rows, NY)], got)
+    parts = after(from_axis([parts] * nh, "h"), half)
+    program.alive = [obs_own, pred, image, dens, alpha, grad2]
     shares, image2 = call(
-        curvature_kernel, [(devices, 128), (part, NY)], got, image2, weight_own, half
+        bind(curvature_kernel, nh), [(devices, 128), (part, NY)], *parts, image2, weight_own, half
     )
     shares = exchange(shares, ALL)
     program.alive = []

time: 179 us -> 170 us (0.950)
  local copies, waits for them, and re-layouts: 15.4 us -> 8.07 us
  blocking collectives: 47 us -> 44.4 us
    all_to_all x4 -> x3, starting transfers between devices: 26.8 us -> 10.9 us  [exchange(): return lax.all_to_all(value, axes, 0, 0, tiled=True)]
    ppermute x3 -> x9, starting transfers between devices: 10.5 us -> 22.6 us  [from_axis(): lax.ppermute(values[step], axis, [(i, (i + step) % size) for i in range(s...]
    ppermute x12 -> x15, waiting for transfers between devices: 26.9 us -> 15.4 us  [from_comps(): lax.ppermute(values[step], COMP, [(i, i ^ step) for i in range(4)])]
    all_to_all x4 -> x3, waiting for transfers between devices: 9.27 us -> 17.3 us  [exchange(): return lax.all_to_all(value, axes, 0, 0, tiled=True)]
    unnamed x42 -> x32, local copies, waits for them, and re-layouts: 15.4 us -> 8.07 us
    ppermute x3 -> x9, waiting for transfers between devices: 5.25 us -> 9.56 us  [from_axis(): lax.ppermute(values[step], axis, [(i, (i + step) % size) for i in range(s...]
    ppermute x12 -> x15, starting transfers between devices: 18.9 us -> 22.4 us  [from_comps(): lax.ppermute(values[step], COMP, [(i, i ^ step) for i in range(4)])]
    all_to_all x2, blocking collectives: 47 us -> 44.4 us  [exchange(): return lax.all_to_all(value, axes, 0, 0, tiled=True)]
  transfers between devices with their start and end apart: 19 -> 27, of which waited for: 12 -> 15; matrix products, arithmetic and copies ran while one was open for 0% -> 0% of each run, Pallas kernels for 5% -> 4%
where the time goes in v5:
time: 170 us; the launch traced here: 169 us
  starting transfers between devices  55.9 us (33%)
  blocking collectives  44.4 us (26%)
  waiting for transfers between devices  42.3 us (25%)
  Pallas kernels  17.3 us (10%)
  local copies, waits for them, and re-layouts  8.07 us (5%)
    all_to_all x2, blocking collectives, exchange(): return lax.all_to_all(value, axes, 0, 0, tiled=True)  44.4 us
    ppermute x9, starting transfers between devices, from_axis(): lax.ppermute(values[step], axis, [(i, (i + step) % size) for i in range(s...  22.6 us
    ppermute x15, starting transfers between devices, from_comps(): lax.ppermute(values[step], COMP, [(i, i ^ step) for i in range(4)])  22.4 us
    all_to_all x3, waiting for transfers between devices, exchange(): return lax.all_to_all(value, axes, 0, 0, tiled=True)  17.3 us
    pallas_call x15, Pallas kernels, call(): pl.pallas_call(inner, out_shape=[jax.ShapeDtypeStruct(shape, dtype) for s...  17.3 us
    ppermute x15, waiting for transfers between devices, from_comps(): lax.ppermute(values[step], COMP, [(i, i ^ step) for i in range(4)])  15.4 us
    all_to_all x3, starting transfers between devices, exchange(): return lax.all_to_all(value, axes, 0, 0, tiled=True)  10.9 us
    ppermute x9, waiting for transfers between devices, from_axis(): lax.ppermute(values[step], axis, [(i, (i + step) % size) for i in range(s...  9.56 us
  transfers between devices with their start and end apart: 27, of which 15 were waited for; matrix products, arithmetic and copies ran while one was open for 0% of the time, Pallas kernels for 4%

profile of v5, /device:TPU:1, one launch (start us, length us, event | category | flops | bytes accessed | tf_op | source)
XLA Modules:
  0.0 169.5 jit_solution(9197661685000853072)
XLA Ops:
  0.6 3.1 %collective-permute-start.2 = (f32[128,256]{1,0:T(8,128)}, f32[128,256]{1,0:T(8,128)S(1)}, u32[]{:S(2)}, u32[]{:S(2)}) collective-permute-start(f32[128,256]{1,0:T(8,128)} %bitcast.8), channel_id=1, source_target_pairs={{0,3},{1,2},{2,1},{3,0},{4,7},{5,6},{6,5},{7,4},{8,11},{9,10},{10,... | collective-permute-start | bytes 393224 | tf_op jit(solution)/shard_map/ppermute | solution.py:494
  3.7 1.5 collective-permute-start.1
  10.8 3.0 %shard_map.78 = (f32[16,72,256]{2,1,0:T(8,128)S(1)}, f32[512,256]{1,0:T(8,128)S(1)}) custom-call(f32[128,256]{1,0:T(8,128)S(1)} %get-tuple-element.54.refs_0_.refs_9_.refs_10_.refs_7_.refs_8_.refs_5_.refs_4_, f32[128,256]{1,0:T(8,128)S(1)} %collective-permute-done.refs_1_, f32[128,256]{1,0:T(8,128)S(1)} %collective-permute-done.1.refs_2_, ...), custom_call_target="tpu_custom_call" | custom-call | tf_op jit(solution)/shard_map/pallas_call | solution.py:478
  14.7 22.7 %all_to_all.31.refs_0_ = f32[16,72,256]{2,1,0:T(8,128)S(1)} all-to-all(f32[16,72,256]{2,1,0:T(8,128)S(1)} %get-tuple-element.63), channel_id=1, replica_groups=mesh['x'=4,'y'=4,'h'=4,'l'=2,'k'=2] {'x','y'}, dimensions={0} | all-to-all | bytes 2359296 | tf_op jit(solution)/shard_map/all_to_all | solution.py:507
  37.5 7.3 %collective-permute-start.5 = (f32[96,256]{1,0:T(8,128)S(1)}, f32[96,256]{1,0:T(8,128)S(1)}, u32[]{:S(2)}, u32[]{:S(2)}) collective-permute-start(f32[96,256]{1,0:T(8,128)S(1)} %shard_map.79.refs_0_), channel_id=1, source_target_pairs={{0,12},{4,0},{8,4},{12,8},{1,13},{5,1},{9,5},{13,9},{2,14},{6,2},{... | collective-permute-start | bytes 294920 | tf_op jit(solution)/shard_map/ppermute | solution.py:501
  45.7 2.3 %collective-permute-start.3 = (f32[96,256]{1,0:T(8,128)S(1)}, f32[96,256]{1,0:T(8,128)S(1)}, u32[]{:S(2)}, u32[]{:S(2)}) collective-permute-start(f32[96,256]{1,0:T(8,128)S(1)} %shard_map.79.refs_0_), channel_id=1, source_target_pairs={{0,4},{4,8},{8,12},{12,0},{1,5},{5,9},{9,13},{13,1},{2,6},{6,10},{... | collective-permute-start | bytes 294920 | tf_op jit(solution)/shard_map/ppermute | solution.py:501
  48.0 4.4 %collective-permute-done.5.refs_3_ = f32[96,256]{1,0:T(8,128)S(1)} collective-permute-done((f32[96,256]{1,0:T(8,128)S(1)}, f32[96,256]{1,0:T(8,128)S(1)}, u32[]{:S(2)}, u32[]{:S(2)}) %collective-permute-start.5) | collective-permute-done | bytes 98336 | tf_op jit(solution)/shard_map/ppermute | solution.py:501
  54.1 3.7 %all-to-all-start.1 = ((f32[16,32,256]{2,1,0:T(8,128)}), f32[16,32,256]{2,1,0:T(8,128)S(1)}, u32[]{:S(2)}, u32[]{:S(2)}) async-start(f32[16,32,256]{2,1,0:T(8,128)} %copy-done.4), calls=%async_computation.1 | async-start | bytes 1048576 | tf_op jit(solution)/shard_map/all_to_all | solution.py:507
  57.8 3.6 %shard_map.81.refs_4_.refs_16_.refs_11_.refs_14_.refs_19_ = f32[264,256]{1,0:T(8,128)S(1)} custom-call(f32[64,256]{1,0:T(8,128)S(1)} %get-tuple-element.65.refs_0_, bf16[4,256,256]{2,1,0:T(8,128)(2,1)S(1)} %get-tuple-element.58.refs_8_.refs_3_.refs_4_.refs_1_.refs_5_.refs_7_.refs_13_, ...), custom_call_target="tpu_custom_call" | custom-call | tf_op jit(solution)/shard_map/pallas_call | solution.py:478
  61.4 5.4 %all-to-all-done.1 = f32[16,32,256]{2,1,0:T(8,128)S(1)} async-done(((f32[16,32,256]{2,1,0:T(8,128)}), f32[16,32,256]{2,1,0:T(8,128)S(1)}, u32[]{:S(2)}, u32[]{:S(2)}) %all-to-all-start.1) | async-done | bytes 524320 | tf_op jit(solution)/shard_map/all_to_all | solution.py:507
  66.9 2.4 %shard_map.82 = (f32[160,256]{1,0:T(8,128)S(1)}, f32[160,256]{1,0:T(8,128)S(1)}, f32[160,256]{1,0:T(8,128)S(1)}, f32[160,256]{1,0:T(8,128)S(1)}) custom-call(f32[512,256]{1,0:T(8,128)S(1)} %bitcast.6, f32[264,256]{1,0:T(8,128)S(1)} %get-tuple-element.55.refs_5_.refs_6_.refs_7_.refs_4_.refs_1_.refs_10_, ...), custom_call_target="tpu_custom_call" | custom-call | tf_op jit(solution)/shard_map/pallas_call | solution.py:478
  69.3 5.6 %collective-permute-start.6 = (f32[160,256]{1,0:T(8,128)S(1)}, f32[160,256]{1,0:T(8,128)S(1)}, u32[]{:S(2)}, u32[]{:S(2)}) collective-permute-start(f32[160,256]{1,0:T(8,128)S(1)} %get-tuple-element.70), channel_id=1, source_target_pairs={{0,1},{1,0},{2,3},{3,2},{4,5},{5,4},{6,7},{7,6},{8,9},{9,8},{10,11... | collective-permute-start | bytes 491528 | tf_op jit(solution)/shard_map/ppermute | solution.py:494
  76.6 3.9 %collective-permute-done.7.refs_2_ = f32[160,256]{1,0:T(8,128)S(1)} collective-permute-done((f32[160,256]{1,0:T(8,128)S(1)}, f32[160,256]{1,0:T(8,128)S(1)}, u32[]{:S(2)}, u32[]{:S(2)}) %collective-permute-start.7) | collective-permute-done | bytes 163872 | tf_op jit(solution)/shard_map/ppermute | solution.py:494
  80.5 3.8 %collective-permute-done.8.refs_3_ = f32[160,256]{1,0:T(8,128)S(1)} collective-permute-done((f32[160,256]{1,0:T(8,128)S(1)}, f32[160,256]{1,0:T(8,128)S(1)}, u32[]{:S(2)}, u32[]{:S(2)}) %collective-permute-start.8) | collective-permute-done | bytes 163872 | tf_op jit(solution)/shard_map/ppermute | solution.py:494
  85.4 3.6 %all-to-all-start.2 = ((f32[16,40,256]{2,1,0:T(8,128)}), f32[16,40,256]{2,1,0:T(8,128)S(1)}, u32[]{:S(2)}, u32[]{:S(2)}) async-start(f32[16,40,256]{2,1,0:T(8,128)} %copy-done), calls=%async_computation.2 | async-start | bytes 1310720 | tf_op jit(solution)/shard_map/all_to_all | solution.py:507
  89.0 1.2 collective-permute-start.11
  91.2 3.7 %collective-permute-done.11.refs_9_ = f32[128,256]{1,0:T(8,128)S(1)} collective-permute-done((f32[128,256]{1,0:T(8,128)S(1)}, f32[128,256]{1,0:T(8,128)S(1)}, u32[]{:S(2)}, u32[]{:S(2)}) %collective-permute-start.11) | collective-permute-done | bytes 131104 | tf_op jit(solution)/shard_map/ppermute | solution.py:494
  95.0 1.9 %collective-permute-done.10.refs_8_ = f32[128,256]{1,0:T(8,128)S(1)} collective-permute-done((f32[128,256]{1,0:T(8,128)S(1)}, f32[128,256]{1,0:T(8,128)S(1)}, u32[]{:S(2)}, u32[]{:S(2)}) %collective-permute-start.10) | collective-permute-done | bytes 131104 | tf_op jit(solution)/shard_map/ppermute | solution.py:494
  98.2 3.1 %all-to-all-done.2.refs_0_ = f32[16,40,256]{2,1,0:T(8,128)S(1)} async-done(((f32[16,40,256]{2,1,0:T(8,128)}), f32[16,40,256]{2,1,0:T(8,128)S(1)}, u32[]{:S(2)}, u32[]{:S(2)}) %all-to-all-start.2) | async-done | bytes 655392 | tf_op jit(solution)/shard_map/all_to_all | solution.py:507
  101.3 2.5 %collective-permute-start.14 = (f32[8,256]{1,0:T(8,128)S(1)}, f32[8,256]{1,0:T(8,128)S(1)}, u32[]{:S(2)}, u32[]{:S(2)}) collective-permute-start(f32[8,256]{1,0:T(8,128)S(1)} %get-tuple-element.84.refs_0_), channel_id=1, source_target_pairs={{0,12},{4,0},{8,4},{12,8},{1,13},{5,1},{9,5},{13,9},{2,14},{6,2},{... | collective-permute-start | bytes 24584 | tf_op jit(solution)/shard_map/ppermute | solution.py:501
  104.9 2.2 %collective-permute-start.12 = (f32[8,256]{1,0:T(8,128)S(1)}, f32[8,256]{1,0:T(8,128)S(1)}, u32[]{:S(2)}, u32[]{:S(2)}) collective-permute-start(f32[8,256]{1,0:T(8,128)S(1)} %get-tuple-element.84.refs_0_), channel_id=1, source_target_pairs={{0,4},{4,8},{8,12},{12,0},{1,5},{5,9},{9,13},{13,1},{2,6},{6,10},{... | collective-permute-start | bytes 24584 | tf_op jit(solution)/shard_map/ppermute | solution.py:501
  107.1 2.4 %shard_map.85 = (f32[160,256]{1,0:T(8,128)S(1)}, f32[160,256]{1,0:T(8,128)S(1)}, f32[160,256]{1,0:T(8,128)S(1)}, f32[160,256]{1,0:T(8,128)S(1)}) custom-call(f32[512,256]{1,0:T(8,128)S(1)} %get-tuple-element.79.refs_0_, f32[264,256]{1,0:T(8,128)S(1)} %get-tuple-element.55.refs_5_.refs_6_.refs_7_.refs_4_.refs_1_.refs_10_, ...), custom_call_target="tpu_custom_call" | custom-call | tf_op jit(solution)/shard_map/pallas_call | solution.py:478
  110.3 5.5 %collective-permute-start.17 = (f32[8,256]{1,0:T(8,128)S(1)}, f32[8,256]{1,0:T(8,128)S(1)}, u32[]{:S(2)}, u32[]{:S(2)}) collective-permute-start(f32[8,256]{1,0:T(8,128)S(1)} %shard_map.86.refs_0_), channel_id=1, source_target_pairs={{0,3},{1,2},{2,1},{3,0},{4,7},{5,6},{6,5},{7,4},{8,11},{9,10},{10,... | collective-permute-start | bytes 24584 | tf_op jit(solution)/shard_map/ppermute | solution.py:494
  118.3 3.7 %shard_map.87 = (f32[16,32,256]{2,1,0:T(8,128)}, f32[128,256]{1,0:T(8,128)S(1)}, f32[128,256]{1,0:T(8,128)S(1)}, f32[8,128]{1,0:T(8,128)S(1)}) custom-call(f32[8,256]{1,0:T(8,128)S(1)} %shard_map.86.refs_0_, f32[8,256]{1,0:T(8,128)S(1)} %collective-permute-done.15.refs_1_, f32[8,256]{1,0:T(8,128)S(1)} %collective-permute-done.16.refs_2_, ...), custom_call_target="tpu_custom_call" | custom-call | tf_op jit(solution)/shard_map/pallas_call | solution.py:478
  122.0 3.6 %all-to-all-start.3 = ((f32[16,32,256]{2,1,0:T(8,128)}), f32[16,32,256]{2,1,0:T(8,128)S(1)}, u32[]{:S(2)}, u32[]{:S(2)}) async-start(f32[16,32,256]{2,1,0:T(8,128)} %get-tuple-element.89), calls=%async_computation.3 | async-start | bytes 1048576 | tf_op jit(solution)/shard_map/all_to_all | solution.py:507
  125.7 1.4 collective-permute-start.22
  127.8 8.8 %all-to-all-done.3.refs_0_ = f32[16,32,256]{2,1,0:T(8,128)S(1)} async-done(((f32[16,32,256]{2,1,0:T(8,128)}), f32[16,32,256]{2,1,0:T(8,128)S(1)}, u32[]{:S(2)}, u32[]{:S(2)}) %all-to-all-start.3) | async-done | bytes 524320 | tf_op jit(solution)/shard_map/all_to_all | solution.py:507
  137.6 4.1 %collective-permute-start.19 = (f32[32,256]{1,0:T(8,128)S(1)}, f32[32,256]{1,0:T(8,128)S(1)}, u32[]{:S(2)}, u32[]{:S(2)}) collective-permute-start(f32[32,256]{1,0:T(8,128)S(1)} %shard_map.88.refs_0_), channel_id=1, source_target_pairs={{0,8},{4,12},{8,0},{12,4},{1,9},{5,13},{9,1},{13,5},{2,10},{6,14},... | collective-permute-start | bytes 98312 | tf_op jit(solution)/shard_map/ppermute | solution.py:501
  141.8 1.2 collective-permute-start.18
  143.2 1.2 collective-permute-done.19.refs_2_
  144.4 2.4 %collective-permute-done.18.refs_1_ = f32[32,256]{1,0:T(8,128)S(1)} collective-permute-done((f32[32,256]{1,0:T(8,128)S(1)}, f32[32,256]{1,0:T(8,128)S(1)}, u32[]{:S(2)}, u32[]{:S(2)}) %collective-permute-start.18) | collective-permute-done | bytes 32800 | tf_op jit(solution)/shard_map/ppermute | solution.py:501
  147.0 21.7 %all_to_all.32 = f32[256,1,128]{2,1,0:T(1,128)S(1)} all-to-all(f32[256,1,128]{2,1,0:T(1,128)S(1)} %bitcast.11), channel_id=1, replica_groups=mesh['x'=4,'y'=4,'h'=4,'l'=2,'k'=2] {'x','y','h','l','k'}, dimensions={0} | all-to-all | bytes 262144 | tf_op jit(solution)/shard_map/all_to_all | solution.py:507
  (71 shorter events, 21.0 us)
Async XLA Ops:
  0.6 10.1 %collective-permute-start.2 = (f32[128,256]{1,0:T(8,128)}, f32[128,256]{1,0:T(8,128)S(1)}, u32[]{:S(2)}, u32[]{:S(2)}) collective-permute-start(f32[128,256]{1,0:T(8,128)} %bitcast.8), channel_id=1, source_target_pairs={{0,3},{1,2},{2,1},{3,0},{4,7},{5,6},{6,5},{7,4},{8,11},{9,10},{10,... | collective-permute-start | bytes 393224 | tf_op jit(solution)/shard_map/ppermute | solution.py:494
  3.7 7.1 %collective-permute-start.1 = (f32[128,256]{1,0:T(8,128)}, f32[128,256]{1,0:T(8,128)S(1)}, u32[]{:S(2)}, u32[]{:S(2)}) collective-permute-start(f32[128,256]{1,0:T(8,128)} %bitcast.9), channel_id=1, source_target_pairs={{0,2},{1,3},{2,0},{3,1},{4,6},{5,7},{6,4},{7,5},{8,10},{9,11},{10,... | collective-permute-start | bytes 393224 | tf_op jit(solution)/shard_map/ppermute | solution.py:494
  5.3 5.5 %collective-permute-start = (f32[128,256]{1,0:T(8,128)}, f32[128,256]{1,0:T(8,128)S(1)}, u32[]{:S(2)}, u32[]{:S(2)}) collective-permute-start(f32[128,256]{1,0:T(8,128)} %bitcast.10), channel_id=1, source_target_pairs={{0,1},{1,0},{2,3},{3,2},{4,5},{5,4},{6,7},{7,6},{8,9},{9,8},{10,11... | collective-permute-start | bytes 393224 | tf_op jit(solution)/shard_map/ppermute | solution.py:494
  5.9 1.0 copy-start.3
  37.5 14.9 %collective-permute-start.5 = (f32[96,256]{1,0:T(8,128)S(1)}, f32[96,256]{1,0:T(8,128)S(1)}, u32[]{:S(2)}, u32[]{:S(2)}) collective-permute-start(f32[96,256]{1,0:T(8,128)S(1)} %shard_map.79.refs_0_), channel_id=1, source_target_pairs={{0,12},{4,0},{8,4},{12,8},{1,13},{5,1},{9,5},{13,9},{2,14},{6,2},{... | collective-permute-start | bytes 294920 | tf_op jit(solution)/shard_map/ppermute | solution.py:501
  44.7 8.5 %collective-permute-start.4 = (f32[96,256]{1,0:T(8,128)S(1)}, f32[96,256]{1,0:T(8,128)S(1)}, u32[]{:S(2)}, u32[]{:S(2)}) collective-permute-start(f32[96,256]{1,0:T(8,128)S(1)} %shard_map.79.refs_0_), channel_id=1, source_target_pairs={{0,8},{4,12},{8,0},{12,4},{1,9},{5,13},{9,1},{13,5},{2,10},{6,14},... | collective-permute-start | bytes 294920 | tf_op jit(solution)/shard_map/ppermute | solution.py:501
  45.7 7.5 %collective-permute-start.3 = (f32[96,256]{1,0:T(8,128)S(1)}, f32[96,256]{1,0:T(8,128)S(1)}, u32[]{:S(2)}, u32[]{:S(2)}) collective-permute-start(f32[96,256]{1,0:T(8,128)S(1)} %shard_map.79.refs_0_), channel_id=1, source_target_pairs={{0,4},{4,8},{8,12},{12,0},{1,5},{5,9},{9,13},{13,1},{2,6},{6,10},{... | collective-permute-start | bytes 294920 | tf_op jit(solution)/shard_map/ppermute | solution.py:501
  54.1 12.7 %all-to-all-start.1 = ((f32[16,32,256]{2,1,0:T(8,128)}), f32[16,32,256]{2,1,0:T(8,128)S(1)}, u32[]{:S(2)}, u32[]{:S(2)}) async-start(f32[16,32,256]{2,1,0:T(8,128)} %copy-done.4), calls=%async_computation.1 | async-start | bytes 1048576 | tf_op jit(solution)/shard_map/all_to_all | solution.py:507
  69.3 7.3 %collective-permute-start.6 = (f32[160,256]{1,0:T(8,128)S(1)}, f32[160,256]{1,0:T(8,128)S(1)}, u32[]{:S(2)}, u32[]{:S(2)}) collective-permute-start(f32[160,256]{1,0:T(8,128)S(1)} %get-tuple-element.70), channel_id=1, source_target_pairs={{0,1},{1,0},{2,3},{3,2},{4,5},{5,4},{6,7},{7,6},{8,9},{9,8},{10,11... | collective-permute-start | bytes 491528 | tf_op jit(solution)/shard_map/ppermute | solution.py:494
  74.9 5.7 %collective-permute-start.7 = (f32[160,256]{1,0:T(8,128)S(1)}, f32[160,256]{1,0:T(8,128)S(1)}, u32[]{:S(2)}, u32[]{:S(2)}) collective-permute-start(f32[160,256]{1,0:T(8,128)S(1)} %get-tuple-element.71), channel_id=1, source_target_pairs={{0,2},{1,3},{2,0},{3,1},{4,6},{5,7},{6,4},{7,5},{8,10},{9,11},{10,... | collective-permute-start | bytes 491528 | tf_op jit(solution)/shard_map/ppermute | solution.py:494
  76.0 8.3 %collective-permute-start.8 = (f32[160,256]{1,0:T(8,128)S(1)}, f32[160,256]{1,0:T(8,128)S(1)}, u32[]{:S(2)}, u32[]{:S(2)}) collective-permute-start(f32[160,256]{1,0:T(8,128)S(1)} %get-tuple-element.72), channel_id=1, source_target_pairs={{0,3},{1,2},{2,1},{3,0},{4,7},{5,6},{6,5},{7,4},{8,11},{9,10},{10,... | collective-permute-start | bytes 491528 | tf_op jit(solution)/shard_map/ppermute | solution.py:494
  85.4 15.8 %all-to-all-start.2 = ((f32[16,40,256]{2,1,0:T(8,128)}), f32[16,40,256]{2,1,0:T(8,128)S(1)}, u32[]{:S(2)}, u32[]{:S(2)}) async-start(f32[16,40,256]{2,1,0:T(8,128)} %copy-done), calls=%async_computation.2 | async-start | bytes 1310720 | tf_op jit(solution)/shard_map/all_to_all | solution.py:507
  89.0 6.0 %collective-permute-start.11 = (f32[128,256]{1,0:T(8,128)S(1)}, f32[128,256]{1,0:T(8,128)S(1)}, u32[]{:S(2)}, u32[]{:S(2)}) collective-permute-start(f32[128,256]{1,0:T(8,128)S(1)} %get-tuple-element.74.refs_6_), channel_id=1, source_target_pairs={{0,3},{1,2},{2,1},{3,0},{4,7},{5,6},{6,5},{7,4},{8,11},{9,10},{10,... | collective-permute-start | bytes 393224 | tf_op jit(solution)/shard_map/ppermute | solution.py:494
  90.2 6.6 %collective-permute-start.10 = (f32[128,256]{1,0:T(8,128)S(1)}, f32[128,256]{1,0:T(8,128)S(1)}, u32[]{:S(2)}, u32[]{:S(2)}) collective-permute-start(f32[128,256]{1,0:T(8,128)S(1)} %get-tuple-element.74.refs_6_), channel_id=1, source_target_pairs={{0,2},{1,3},{2,0},{3,1},{4,6},{5,7},{6,4},{7,5},{8,10},{9,11},{10,... | collective-permute-start | bytes 393224 | tf_op jit(solution)/shard_map/ppermute | solution.py:494
  90.6 6.9 %collective-permute-start.9 = (f32[128,256]{1,0:T(8,128)S(1)}, f32[128,256]{1,0:T(8,128)S(1)}, u32[]{:S(2)}, u32[]{:S(2)}) collective-permute-start(f32[128,256]{1,0:T(8,128)S(1)} %get-tuple-element.74.refs_6_), channel_id=1, source_target_pairs={{0,1},{1,0},{2,3},{3,2},{4,5},{5,4},{6,7},{7,6},{8,9},{9,8},{10,11... | collective-permute-start | bytes 393224 | tf_op jit(solution)/shard_map/ppermute | solution.py:494
  101.3 8.3 %collective-permute-start.14 = (f32[8,256]{1,0:T(8,128)S(1)}, f32[8,256]{1,0:T(8,128)S(1)}, u32[]{:S(2)}, u32[]{:S(2)}) collective-permute-start(f32[8,256]{1,0:T(8,128)S(1)} %get-tuple-element.84.refs_0_), channel_id=1, source_target_pairs={{0,12},{4,0},{8,4},{12,8},{1,13},{5,1},{9,5},{13,9},{2,14},{6,2},{... | collective-permute-start | bytes 24584 | tf_op jit(solution)/shard_map/ppermute | solution.py:501
  103.8 6.4 %collective-permute-start.13 = (f32[8,256]{1,0:T(8,128)S(1)}, f32[8,256]{1,0:T(8,128)S(1)}, u32[]{:S(2)}, u32[]{:S(2)}) collective-permute-start(f32[8,256]{1,0:T(8,128)S(1)} %get-tuple-element.84.refs_0_), channel_id=1, source_target_pairs={{0,8},{4,12},{8,0},{12,4},{1,9},{5,13},{9,1},{13,5},{2,10},{6,14},... | collective-permute-start | bytes 24584 | tf_op jit(solution)/shard_map/ppermute | solution.py:501
  104.9 5.3 %collective-permute-start.12 = (f32[8,256]{1,0:T(8,128)S(1)}, f32[8,256]{1,0:T(8,128)S(1)}, u32[]{:S(2)}, u32[]{:S(2)}) collective-permute-start(f32[8,256]{1,0:T(8,128)S(1)} %get-tuple-element.84.refs_0_), channel_id=1, source_target_pairs={{0,4},{4,8},{8,12},{12,0},{1,5},{5,9},{9,13},{13,1},{2,6},{6,10},{... | collective-permute-start | bytes 24584 | tf_op jit(solution)/shard_map/ppermute | solution.py:501
  109.5 8.8 %copy-start.14 = (f32[160,256]{1,0:T(8,128)}, f32[160,256]{1,0:T(8,128)S(1)}, u32[]{:S(2)}) copy-start(f32[160,256]{1,0:T(8,128)S(1)} %get-tuple-element.95) | copy-start | bytes 491524
  110.2 8.1 %copy-start.2 = (f32[512,256]{1,0:T(8,128)S(1)}, f32[512,256]{1,0:T(8,128)}, u32[]{:S(2)}) copy-start(f32[512,256]{1,0:T(8,128)} %copy-done.1) | copy-start | bytes 1572868
  110.2 8.1 %copy-start.8 = (f32[128,256]{1,0:T(8,128)S(1)}, f32[128,256]{1,0:T(8,128)}, u32[]{:S(2)}) copy-start(f32[128,256]{1,0:T(8,128)} %copy-done.7) | copy-start | bytes 393220
  110.2 8.1 %copy-start.10 = (f32[128,256]{1,0:T(8,128)S(1)}, f32[128,256]{1,0:T(8,128)}, u32[]{:S(2)}) copy-start(f32[128,256]{1,0:T(8,128)} %copy-done.9) | copy-start | bytes 393220
  110.3 6.8 %collective-permute-start.17 = (f32[8,256]{1,0:T(8,128)S(1)}, f32[8,256]{1,0:T(8,128)S(1)}, u32[]{:S(2)}, u32[]{:S(2)}) collective-permute-start(f32[8,256]{1,0:T(8,128)S(1)} %shard_map.86.refs_0_), channel_id=1, source_target_pairs={{0,3},{1,2},{2,1},{3,0},{4,7},{5,6},{6,5},{7,4},{8,11},{9,10},{10,... | collective-permute-start | bytes 24584 | tf_op jit(solution)/shard_map/ppermute | solution.py:494
  115.8 2.5 %collective-permute-start.16 = (f32[8,256]{1,0:T(8,128)S(1)}, f32[8,256]{1,0:T(8,128)S(1)}, u32[]{:S(2)}, u32[]{:S(2)}) collective-permute-start(f32[8,256]{1,0:T(8,128)S(1)} %shard_map.86.refs_0_), channel_id=1, source_target_pairs={{0,2},{1,3},{2,0},{3,1},{4,6},{5,7},{6,4},{7,5},{8,10},{9,11},{10,... | collective-permute-start | bytes 24584 | tf_op jit(solution)/shard_map/ppermute | solution.py:494
  115.8 2.5 %collective-permute-start.15 = (f32[8,256]{1,0:T(8,128)S(1)}, f32[8,256]{1,0:T(8,128)S(1)}, u32[]{:S(2)}, u32[]{:S(2)}) collective-permute-start(f32[8,256]{1,0:T(8,128)S(1)} %shard_map.86.refs_0_), channel_id=1, source_target_pairs={{0,1},{1,0},{2,3},{3,2},{4,5},{5,4},{6,7},{7,6},{8,9},{9,8},{10,11... | collective-permute-start | bytes 24584 | tf_op jit(solution)/shard_map/ppermute | solution.py:494
  122.0 14.7 %all-to-all-start.3 = ((f32[16,32,256]{2,1,0:T(8,128)}), f32[16,32,256]{2,1,0:T(8,128)S(1)}, u32[]{:S(2)}, u32[]{:S(2)}) async-start(f32[16,32,256]{2,1,0:T(8,128)} %get-tuple-element.89), calls=%async_computation.3 | async-start | bytes 1048576 | tf_op jit(solution)/shard_map/all_to_all | solution.py:507
  125.6 16.2 %collective-permute-start.21 = (f32[160,256]{1,0:T(8,128)}, f32[160,256]{1,0:T(8,128)S(1)}, u32[]{:S(2)}, u32[]{:S(2)}) collective-permute-start(f32[160,256]{1,0:T(8,128)} %copy-done.15), channel_id=1, source_target_pairs={{0,1},{1,0},{2,3},{3,2},{4,5},{5,4},{6,7},{7,6},{8,9},{9,8},{10,11... | collective-permute-start | bytes 491528 | tf_op jit(solution)/shard_map/ppermute | solution.py:494
  125.7 17.3 %collective-permute-start.22 = (f32[160,256]{1,0:T(8,128)}, f32[160,256]{1,0:T(8,128)S(1)}, u32[]{:S(2)}, u32[]{:S(2)}) collective-permute-start(f32[160,256]{1,0:T(8,128)} %copy-done.14), channel_id=1, source_target_pairs={{0,2},{1,3},{2,0},{3,1},{4,6},{5,7},{6,4},{7,5},{8,10},{9,11},{10,... | collective-permute-start | bytes 491528 | tf_op jit(solution)/shard_map/ppermute | solution.py:494
  127.0 15.9 %collective-permute-start.23 = (f32[160,256]{1,0:T(8,128)}, f32[160,256]{1,0:T(8,128)S(1)}, u32[]{:S(2)}, u32[]{:S(2)}) collective-permute-start(f32[160,256]{1,0:T(8,128)} %copy-done.13), channel_id=1, source_target_pairs={{0,3},{1,2},{2,1},{3,0},{4,7},{5,6},{6,5},{7,4},{8,11},{9,10},{10,... | collective-permute-start | bytes 491528 | tf_op jit(solution)/shard_map/ppermute | solution.py:494
  136.7 6.5 %collective-permute-start.20 = (f32[32,256]{1,0:T(8,128)S(1)}, f32[32,256]{1,0:T(8,128)S(1)}, u32[]{:S(2)}, u32[]{:S(2)}) collective-permute-start(f32[32,256]{1,0:T(8,128)S(1)} %shard_map.88.refs_0_), channel_id=1, source_target_pairs={{0,12},{4,0},{8,4},{12,8},{1,13},{5,1},{9,5},{13,9},{2,14},{6,2},{... | collective-permute-start | bytes 98312 | tf_op jit(solution)/shard_map/ppermute | solution.py:501
  137.6 6.8 %collective-permute-start.19 = (f32[32,256]{1,0:T(8,128)S(1)}, f32[32,256]{1,0:T(8,128)S(1)}, u32[]{:S(2)}, u32[]{:S(2)}) collective-permute-start(f32[32,256]{1,0:T(8,128)S(1)} %shard_map.88.refs_0_), channel_id=1, source_target_pairs={{0,8},{4,12},{8,0},{12,4},{1,9},{5,13},{9,1},{13,5},{2,10},{6,14},... | collective-permute-start | bytes 98312 | tf_op jit(solution)/shard_map/ppermute | solution.py:501
  141.8 5.1 %collective-permute-start.18 = (f32[32,256]{1,0:T(8,128)S(1)}, f32[32,256]{1,0:T(8,128)S(1)}, u32[]{:S(2)}, u32[]{:S(2)}) collective-permute-start(f32[32,256]{1,0:T(8,128)S(1)} %shard_map.88.refs_0_), channel_id=1, source_target_pairs={{0,4},{4,8},{8,12},{12,0},{1,5},{5,9},{9,13},{13,1},{2,6},{6,10},{... | collective-permute-start | bytes 98312 | tf_op jit(solution)/shard_map/ppermute | solution.py:501
  (11 other events, 8.5 us)

commit v6 on v5

--- a/solution.py
+++ b/solution.py
@@ -196,36 +196,33 @@
 
 
 def start_kernel(
-    nxy, m0, m1, m2, m3, top_ref, decay_ref, gx_ref, gy_ref, fx, bx, ty, out_ref, far_ref, full_ref, pull_ref, sem
+    nxy, m0, m1, m2, m3, top_ref, decay_ref, gx_ref, gy_ref, fx, bx, ty, out_ref, full_ref
 ):
     rows = NX // nxy
     gather_rows((m0, m1, m2, m3), full_ref)
-    copy = pltpu.make_async_copy(full_ref, far_ref, sem)
-    copy.start()
+    plane = forward_plane(full_ref[...], decay_ref, gx_ref, gy_ref, fx, bx, ty)
+    for target in range(nxy):
+        out_ref[target, :rows, :] = plane[target * rows : (target + 1) * rows]
+        out_ref[target, rows:, :] = jnp.full((8, NY), top_ref[0], F32)
+
+
+def pull_kernel(full_ref, decay_ref, gx_ref, gy_ref, fx, bx, ty, out_ref):
     dens = full_ref[...]
-    pull_ref[...] = 0.5 * (dens * (1.0 / (dens * dens + 0.25)))
-    for place, field in enumerate((full_ref, pull_ref)):
-        plane = forward_plane(field[...], decay_ref, gx_ref, gy_ref, fx, bx, ty)
-        for target in range(nxy):
-            out_ref[target, place * rows : (place + 1) * rows, :] = plane[
-                target * rows : (target + 1) * rows
-            ]
-    for target in range(nxy):
-        out_ref[target, 2 * rows : 2 * rows + 8, :] = jnp.full((8, NY), top_ref[0], F32)
-    copy.wait()
+    pull = 0.5 * (dens * (1.0 / (dens * dens + 0.25)))
+    plane = forward_plane(pull, decay_ref, gx_ref, gy_ref, fx, bx, ty)
+    out_ref[...] = plane.reshape(out_ref.shape)
 
 
 def collect_kernel(nxy, got_ref, weight_ref, obs_ref, sum_ref):
     rows = NX // nxy
-    total = got_ref[0, : 2 * rows, :]
+    total = got_ref[0, :rows, :]
     for source in range(1, nxy):
-        total = total + got_ref[source, : 2 * rows, :]
-    sum_ref[: 2 * rows] = total
+        total = total + got_ref[source, :rows, :]
+    sum_ref[:rows] = total
     for source in range(nxy):
-        place = 2 * rows + source
-        sum_ref[place : place + 1, :] = got_ref[source, 2 * rows : 2 * rows + 1, :]
+        sum_ref[rows + source : rows + source + 1, :] = got_ref[source, rows : rows + 1, :]
     part = weight_ref.shape[0]
-    start = 2 * rows + nxy
+    start = rows + nxy
     sum_ref[start : start + part] = weight_ref[...]
     sum_ref[start + part : start + 2 * part] = obs_ref[...]
 
@@ -233,22 +230,20 @@
 def residual_kernel(nxy, nh, *refs):
     rows = NX // nxy
     part = rows // nh
-    start = 2 * rows + nxy
+    start = rows + nxy
     sums = refs[:nh]
-    pred_ref, pull_ref, weight_ref, tops_ref, send_ref, meas_ref = refs[nh:]
+    pred_ref, weight_ref, tops_ref, send_ref, meas_ref = refs[nh:]
     chip = lax.axis_index("h")
-    total = sums[0][: 2 * rows]
+    pred = sums[0][:rows]
     for step in range(1, nh):
-        total = total + sums[step][: 2 * rows]
+        pred = pred + sums[step][:rows]
     for step in range(nh):
-        tops_ref[step * nxy : (step + 1) * nxy] = sums[step][2 * rows : start]
+        tops_ref[step * nxy : (step + 1) * nxy] = sums[step][rows:start]
         place = pl.ds(pl.multiple_of(lax.rem(chip + (nh - step), nh) * part, part), part)
         weight_ref[place, :] = sums[step][start : start + part]
         meas_ref[place, :] = sums[step][start + part :]
     weight = weight_ref[...]
-    pred = total[:rows]
     pred_ref[...] = pred
-    pull_ref[...] = total[rows:]
     res = weight * (weight * (pred - meas_ref[...]))
     for target in range(nxy):
         send_ref[target] = res
@@ -334,22 +329,24 @@
 def gradient_kernel(nxy, nh, *refs):
     rows = NX // nxy
     part = rows // nh
-    pieces = refs[:4]
-    pull_ref, dens_ref, weight_ref = refs[4:7]
-    send_ref, grad_ref, line_ref, image_ref, scratch = refs[7:]
+    pieces, pulls = refs[:4], refs[4 : 4 + nh]
+    dens_ref, weight_ref = refs[4 + nh : 6 + nh]
+    send_ref, grad_ref, line_ref, image_ref, scratch = refs[6 + nh :]
     total = pieces[0][...] + pieces[1][...] + (pieces[2][...] + pieces[3][...])
     data = total[:QX]
     line = total[QX:]
     dens = dens_ref[...]
     quad = 1.0 / (dens * dens + 0.25)
     grad = data + 0.5 * (quad * dens)
-    image = line + pull_ref[...]
+    image = line
+    for pull in pulls:
+        image = image + pull[...]
     weight = weight_ref[...]
+    back = weight * (weight * image)
     mine = jnp.broadcast_to(share(grad, quad, image, weight, scratch, part), (8, NY))
     grad_ref[...] = grad
     line_ref[...] = line
     image_ref[...] = image
-    back = weight * (weight * image)
     for target in range(nxy):
         send_ref[target, :rows] = back
         send_ref[target, rows:] = mine
@@ -374,26 +371,18 @@
 
 def second_kernel(
     s0, s1, s2, s3, dens_ref, full_ref, g0, g1, g2, g3, decay_ref, gx_ref, gy_ref, fx, bx, ty,
-    out_ref, dens_out, base_out, alpha_ref, all_ref, near_ref, sems,
+    out_ref, dens_out, base_out, alpha_ref, all_ref,
 ):
-    comp = comp_index()
-    copies = [pltpu.make_async_copy(full_ref, near_ref, sems.at[4])]
-    for step, piece in enumerate((g0, g1, g2, g3)):
-        place = pl.ds(pl.multiple_of(jnp.bitwise_xor(comp, step) * QX, QX), QX)
-        copies.append(pltpu.make_async_copy(piece, all_ref.at[place, :], sems.at[step]))
-    for copy in copies:
-        copy.start()
+    gather_rows((g0, g1, g2, g3), all_ref)
     alpha = step_length(s0[:1] + s1[:1] + (s2[:1] + s3[:1]))
     alpha_ref[...] = jnp.broadcast_to(alpha, alpha_ref.shape)
     old = dens_ref[...]
-    for copy in copies:
-        copy.wait()
-    grad = all_ref[pl.ds(pl.multiple_of(comp * QX, QX), QX), :]
+    grad = g0[...]
     dens = old - alpha * grad
     dens_out[...] = dens
     data = grad - 0.5 * ((1.0 / (old * old + 0.25)) * old)
     base_out[...] = data + 0.5 * (dens * (1.0 / (dens * dens + 0.25)))
-    dens = near_ref[...] - alpha * all_ref[...]
+    dens = full_ref[...] - alpha * all_ref[...]
     all_ref[...] = 0.5 * (dens * (1.0 / (dens * dens + 0.25)))
     plane = forward_plane(all_ref[...], decay_ref, gx_ref, gy_ref, fx, bx, ty)
     out_ref[...] = plane.reshape(out_ref.shape)
@@ -466,7 +455,7 @@
     def drop(self, *values):
         self.alive = [item for item in self.alive if all(item is not value for value in values)]
 
-    def call(self, kernel, outs, *args, scratch=(), scalars=(), far=(), far_out=(), sems=0, mib=8):
+    def call(self, kernel, outs, *args, scratch=(), scalars=(), mib=8):
         used = len(args)
         keep = [item for item in self.alive if all(item is not value for value in args)]
         kept = len(keep)
@@ -479,12 +468,11 @@
             inner,
             out_shape=[jax.ShapeDtypeStruct(shape, dtype) for shape, dtype in kinds],
             in_specs=[
-                SMEM if place in scalars else ANY if place in far else VMEM for place in range(used)
+                SMEM if place in scalars else VMEM for place in range(used)
             ]
             + [ANY] * kept,
-            out_specs=[ANY if place in far_out else VMEM for place in range(len(outs))],
-            scratch_shapes=[pltpu.VMEM(shape, F32) for shape in scratch]
-            + [pltpu.SemaphoreType.DMA((sems,) if sems > 1 else ())] * (sems > 0),
+            out_specs=[VMEM] * len(outs),
+            scratch_shapes=[pltpu.VMEM(shape, F32) for shape in scratch],
             compiler_params=pltpu.CompilerParams(vmem_limit_bytes=mib << 20),
         )(*args, *keep)
 
@@ -535,22 +523,28 @@
     factors = (decay, gx, gy)
     program.hold(*tables, *factors, dens, weight_own, obs_own)
     message, full = call(
-        bind(start_kernel, nxy), [(nxy, 2 * rows + 8, NY), (NX, NY)],
-        dens, *layers[1:], layer_top, *factors, *tables,
-        scratch=[(NX, NY)] * 2, scalars=(4,), far_out=(1,), sems=1,
+        bind(start_kernel, nxy), [(nxy, rows + 8, NY), (NX, NY)],
+        dens, *layers[1:], layer_top, *factors, *tables, scalars=(4,),
     )
     got = exchange(message, XY)
+    (pull_message,) = call(
+        pull_kernel, [(nxy, rows, NY)], after(full, message), *factors, *tables
+    )
+    got = after(got, pull_message)
     (sums,) = call(
-        bind(collect_kernel, nxy), [(2 * rows + nxy + 2 * part, NY)], got, weight_own, obs_own
-    )
+        bind(collect_kernel, nxy), [(rows + nxy + 2 * part, NY)], got, weight_own, obs_own
+    )
+    pulled = exchange(after(pull_message, sums), XY)
     sums = from_axis([sums] * nh, "h")
-    pred, pulled, weight, tops, message = call(
+    pred, weight, tops, message = call(
         bind(residual_kernel, nxy, nh),
-        [(rows, NY), (rows, NY), (rows, NY), (nxy * nh, NY), (nxy, rows, NY)],
+        [(rows, NY), (rows, NY), (nxy * nh, NY), (nxy, rows, NY)],
         *sums, scratch=[(rows, NY)],
     )
-    program.hold(pred, pulled, weight)
-    got = exchange(message, XY)
+    program.hold(pred, weight)
+    got = exchange(after(message, pulled), XY)
+    (pulled,) = call(bind(sum_kernel, nxy), [(rows, NY)], after(pulled, message))
+    pulls = from_axis([pulled] * nh, "h")
     (power,) = call(bind(power_kernel, nxy * nh), [(KEPT, NY)], tops)
     program.hold(power)
     adjoint = lambda plane: call(
@@ -558,34 +552,34 @@
         plane.reshape(NX, NY), *factors, power, *tables,
         scratch=[(NX, NY), (4 * rows, NY)],
     )
+    got = after(got, *pulls)
     pieces = from_comps(adjoint(got))
     message, grad, line, image = call(
         bind(gradient_kernel, nxy, nh),
         [(nxy, rows + 8, NY), (QX, NY), (rows, NY), (rows, NY)],
-        *pieces, pulled, dens, weight, scratch=[(rows, NY)],
-    )
-    program.drop(pulled, weight)
+        *pieces, *pulls, dens, weight,
+        scratch=[(rows, NY)],
+    )
+    program.drop(weight)
     program.hold(line, image)
     grads = from_comps([grad] * 4)
     got = after(exchange(message, XY), *grads)
     plane, shares = call(bind(part_kernel, nxy), [(NX, NY), (8, NY)], got)
-    pieces = adjoint(plane)
-    shares = after(from_axis([shares] * nh, "h"), *pieces)
-    (shares,) = call(add_kernel, [(8, NY)], *shares)
+    (shares,) = call(add_kernel, [(8, NY)], *from_axis([shares] * nh, "h"))
     shares = from_comps([shares] * 4)
     message, dens, base, alpha = call(
         second_kernel, [(nxy, rows, NY), (QX, NY), (QX, NY), (8, 128)],
         *shares, dens, full, *grads, *factors, *tables,
-        scratch=[(NX, NY)] * 2, far=(5, 6, 7, 8, 9), sems=5,
+        scratch=[(NX, NY)],
     )
     program.alive = [weight_own, obs_own, pred, line, image, dens, base, alpha]
     got = exchange(message, XY)
-    pieces = from_comps(after(pieces, message))
+    pieces = from_comps(adjoint(after(plane, message)))
     grad2, image2, half = call(
         second_gradient_kernel, [(QX, NY), (rows, NY), (8, 128)],
         *pieces, alpha, base, dens, line,
     )
-    (parts,) = call(bind(sum_kernel, nxy), [(rows, NY)], got)
+    (parts,) = call(bind(sum_kernel, nxy), [(rows, NY)], after(got, *pieces))
     parts = after(from_axis([parts] * nh, "h"), half)
     program.alive = [obs_own, pred, image, dens, alpha, grad2]
     shares, image2 = call(

time: 170 us -> 179 us (1.053)
  blocking collectives: 44.4 us -> 24.1 us
  starting transfers between devices: 55.9 us -> 74.7 us
  local copies, waits for them, and re-layouts: 8.07 us -> 16.3 us
  waiting for transfers between devices: 42.3 us -> 44.7 us
    all_to_all x2 -> x1, blocking collectives: 44.4 us -> 24.1 us  [exchange(): return lax.all_to_all(value, axes, 0, 0, tiled=True)]
    all_to_all x3 -> x5, starting transfers between devices: 10.9 us -> 26.8 us  [exchange(): return lax.all_to_all(value, axes, 0, 0, tiled=True)]
    unnamed x32 -> x56, local copies, waits for them, and re-layouts: 8.07 us -> 16.3 us
    all_to_all x3 -> x5, waiting for transfers between devices: 17.3 us -> 9.63 us  [exchange(): return lax.all_to_all(value, axes, 0, 0, tiled=True)]
    ppermute x15, waiting for transfers between devices: 15.4 us -> 23 us  [from_comps(): lax.ppermute(values[step], COMP, [(i, i ^ step) for i in range(4)])]
    ppermute x9 -> x12, starting transfers between devices: 22.6 us -> 26.7 us  [from_axis(): lax.ppermute(values[step], axis, [(i, (i + step) % size) for i in range(s...]
    ppermute x9 -> x12, waiting for transfers between devices: 9.56 us -> 12.1 us  [from_axis(): lax.ppermute(values[step], axis, [(i, (i + step) % size) for i in range(s...]
    pallas_call x15 -> x17, Pallas kernels: 17.3 us -> 16.8 us  [call(): pl.pallas_call(inner, out_shape=[jax.ShapeDtypeStruct(shape, dtype) for s...]
  transfers between devices with their start and end apart: 27 -> 32, of which waited for: 15 -> 18; matrix products, arithmetic and copies ran while one was open for 0% -> 0% of each run, Pallas kernels for 4% -> 5%
where the time goes in v6:
time: 179 us; the launch traced here: 178 us
  starting transfers between devices  74.7 us (42%)
  waiting for transfers between devices  44.7 us (25%)
  blocking collectives  24.1 us (13%)
  Pallas kernels  16.8 us (9%)
  local copies, waits for them, and re-layouts  16.3 us (9%)
    all_to_all x5, starting transfers between devices, exchange(): return lax.all_to_all(value, axes, 0, 0, tiled=True)  26.8 us
    ppermute x12, starting transfers between devices, from_axis(): lax.ppermute(values[step], axis, [(i, (i + step) % size) for i in range(s...  26.7 us
    all_to_all x1, blocking collectives, exchange(): return lax.all_to_all(value, axes, 0, 0, tiled=True)  24.1 us
    ppermute x15, waiting for transfers between devices, from_comps(): lax.ppermute(values[step], COMP, [(i, i ^ step) for i in range(4)])  23 us
    ppermute x15, starting transfers between devices, from_comps(): lax.ppermute(values[step], COMP, [(i, i ^ step) for i in range(4)])  21.3 us
    pallas_call x17, Pallas kernels, call(): pl.pallas_call(inner, out_shape=[jax.ShapeDtypeStruct(shape, dtype) for s...  16.8 us
    unnamed x56, local copies, waits for them, and re-layouts  16.3 us
    ppermute x12, waiting for transfers between devices, from_axis(): lax.ppermute(values[step], axis, [(i, (i + step) % size) for i in range(s...  12.1 us
  transfers between devices with their start and end apart: 32, of which 18 were waited for; matrix products, arithmetic and copies ran while one was open for 0% of the time, Pallas kernels for 5%

profile of v6, /device:TPU:1, one launch (start us, length us, event | category | flops | bytes accessed | tf_op | source)
XLA Modules:
  0.0 178.2 jit_solution(4641443394123004908)
XLA Ops:
  0.6 3.1 %collective-permute-start.2 = (f32[128,256]{1,0:T(8,128)}, f32[128,256]{1,0:T(8,128)S(1)}, u32[]{:S(2)}, u32[]{:S(2)}) collective-permute-start(f32[128,256]{1,0:T(8,128)} %bitcast.8), channel_id=1, source_target_pairs={{0,3},{1,2},{2,1},{3,0},{4,7},{5,6},{6,5},{7,4},{8,11},{9,10},{10,... | collective-permute-start | bytes 393224 | tf_op jit(solution)/shard_map/ppermute | solution.py:482
  10.8 1.8 shard_map.78
  14.3 6.1 %all-to-all-start = ((f32[16,40,256]{2,1,0:T(8,128)}), f32[16,40,256]{2,1,0:T(8,128)S(1)}, u32[]{:S(2)}, u32[]{:S(2)}) async-start(f32[16,40,256]{2,1,0:T(8,128)} %copy-done.4), calls=%async_computation | async-start | bytes 1310720 | tf_op jit(solution)/shard_map/all_to_all | solution.py:495
  21.4 2.5 %shard_map.79 = f32[16,32,256]{2,1,0:T(8,128)} custom-call(f32[512,256]{1,0:T(8,128)S(1)} %copy-done.1, f32[264,256]{1,0:T(8,128)S(1)} %get-tuple-element.54.refs_5_.refs_1_.refs_6_.refs_7_.refs_4_.refs_13_.refs_10_, f32[264,256]{1,0:T(8,128)S(1)} %get-tuple-element.55.refs_6_.refs_2_.refs_7_.refs_8_.refs_5_.refs_14_.refs_11_, ...), custom_call_target="tpu_custom_call" | custom-call | tf_op jit(solution)/shard_map/pallas_call | solution.py:467
  24.0 8.0 %all-to-all-done.refs_0_ = f32[16,40,256]{2,1,0:T(8,128)S(1)} async-done(((f32[16,40,256]{2,1,0:T(8,128)}), f32[16,40,256]{2,1,0:T(8,128)S(1)}, u32[]{:S(2)}, u32[]{:S(2)}) %all-to-all-start) | async-done | bytes 655392 | tf_op jit(solution)/shard_map/all_to_all | solution.py:495
  32.0 3.6 %all-to-all-start.1 = ((f32[16,32,256]{2,1,0:T(8,128)}), f32[16,32,256]{2,1,0:T(8,128)S(1)}, u32[]{:S(2)}, u32[]{:S(2)}) async-start(f32[16,32,256]{2,1,0:T(8,128)} %shard_map.79), calls=%async_computation.1 | async-start | bytes 1048576 | tf_op jit(solution)/shard_map/all_to_all | solution.py:495
  35.6 6.8 %collective-permute-start.5 = (f32[64,256]{1,0:T(8,128)S(1)}, f32[64,256]{1,0:T(8,128)S(1)}, u32[]{:S(2)}, u32[]{:S(2)}) collective-permute-start(f32[64,256]{1,0:T(8,128)S(1)} %shard_map.80.refs_0_), channel_id=1, source_target_pairs={{0,12},{4,0},{8,4},{12,8},{1,13},{5,1},{9,5},{13,9},{2,14},{6,2},{... | collective-permute-start | bytes 196616 | tf_op jit(solution)/shard_map/ppermute | solution.py:489
  43.4 2.3 %collective-permute-start.3 = (f32[64,256]{1,0:T(8,128)S(1)}, f32[64,256]{1,0:T(8,128)S(1)}, u32[]{:S(2)}, u32[]{:S(2)}) collective-permute-start(f32[64,256]{1,0:T(8,128)S(1)} %shard_map.80.refs_0_), channel_id=1, source_target_pairs={{0,4},{4,8},{8,12},{12,0},{1,5},{5,9},{9,13},{13,1},{2,6},{6,10},{... | collective-permute-start | bytes 196616 | tf_op jit(solution)/shard_map/ppermute | solution.py:489
  45.7 4.0 %collective-permute-done.4.refs_2_ = f32[64,256]{1,0:T(8,128)S(1)} collective-permute-done((f32[64,256]{1,0:T(8,128)S(1)}, f32[64,256]{1,0:T(8,128)S(1)}, u32[]{:S(2)}, u32[]{:S(2)}) %collective-permute-start.4) | collective-permute-done | bytes 65568 | tf_op jit(solution)/shard_map/ppermute | solution.py:489
  50.8 6.6 %all-to-all-start.2 = ((f32[16,32,256]{2,1,0:T(8,128)}), f32[16,32,256]{2,1,0:T(8,128)S(1)}, u32[]{:S(2)}, u32[]{:S(2)}) async-start(f32[16,32,256]{2,1,0:T(8,128)} %copy-done.8), calls=%async_computation.2 | async-start | bytes 1048576 | tf_op jit(solution)/shard_map/all_to_all | solution.py:495
  59.0 3.4 %collective-permute-start.7 = (f32[32,256]{1,0:T(8,128)S(1)}, f32[32,256]{1,0:T(8,128)S(1)}, u32[]{:S(2)}, u32[]{:S(2)}) collective-permute-start(f32[32,256]{1,0:T(8,128)S(1)} %shard_map.82.refs_4_), channel_id=1, source_target_pairs={{0,8},{4,12},{8,0},{12,4},{1,9},{5,13},{9,1},{13,5},{2,10},{6,14},... | collective-permute-start | bytes 98312 | tf_op jit(solution)/shard_map/ppermute | solution.py:489
  63.6 3.6 %shard_map.83.refs_4_.refs_19_.refs_11_.refs_14_ = f32[264,256]{1,0:T(8,128)S(1)} custom-call(f32[64,256]{1,0:T(8,128)S(1)} %get-tuple-element.73.refs_0_, bf16[4,256,256]{2,1,0:T(8,128)(2,1)S(1)} %get-tuple-element.57.refs_8_.refs_4_.refs_3_.refs_1_.refs_5_.refs_10_.refs_13_, ...), custom_call_target="tpu_custom_call" | custom-call | tf_op jit(solution)/shard_map/pallas_call | solution.py:467
  67.4 2.4 %shard_map.84 = (f32[160,256]{1,0:T(8,128)S(1)}, f32[160,256]{1,0:T(8,128)S(1)}, f32[160,256]{1,0:T(8,128)S(1)}, f32[160,256]{1,0:T(8,128)S(1)}) custom-call(f32[512,256]{1,0:T(8,128)S(1)} %bitcast.6, f32[264,256]{1,0:T(8,128)S(1)} %get-tuple-element.54.refs_5_.refs_1_.refs_6_.refs_7_.refs_4_.refs_13_.refs_10_, ...), custom_call_target="tpu_custom_call" | custom-call | tf_op jit(solution)/shard_map/pallas_call | solution.py:467
  69.9 4.8 %collective-permute-start.9 = (f32[160,256]{1,0:T(8,128)S(1)}, f32[160,256]{1,0:T(8,128)S(1)}, u32[]{:S(2)}, u32[]{:S(2)}) collective-permute-start(f32[160,256]{1,0:T(8,128)S(1)} %get-tuple-element.75), channel_id=1, source_target_pairs={{0,1},{1,0},{2,3},{3,2},{4,5},{5,4},{6,7},{7,6},{8,9},{9,8},{10,11... | collective-permute-start | bytes 491528 | tf_op jit(solution)/shard_map/ppermute | solution.py:482
  76.5 3.9 %collective-permute-done.10.refs_2_ = f32[160,256]{1,0:T(8,128)S(1)} collective-permute-done((f32[160,256]{1,0:T(8,128)S(1)}, f32[160,256]{1,0:T(8,128)S(1)}, u32[]{:S(2)}, u32[]{:S(2)}) %collective-permute-start.10) | collective-permute-done | bytes 163872 | tf_op jit(solution)/shard_map/ppermute | solution.py:482
  80.4 3.8 %collective-permute-done.11.refs_3_ = f32[160,256]{1,0:T(8,128)S(1)} collective-permute-done((f32[160,256]{1,0:T(8,128)S(1)}, f32[160,256]{1,0:T(8,128)S(1)}, u32[]{:S(2)}, u32[]{:S(2)}) %collective-permute-start.11) | collective-permute-done | bytes 163872 | tf_op jit(solution)/shard_map/ppermute | solution.py:482
  87.6 6.9 %all-to-all-start.3 = ((f32[16,40,256]{2,1,0:T(8,128)}), f32[16,40,256]{2,1,0:T(8,128)S(1)}, u32[]{:S(2)}, u32[]{:S(2)}) async-start(f32[16,40,256]{2,1,0:T(8,128)} %copy-done.3), calls=%async_computation.3 | async-start | bytes 1310720 | tf_op jit(solution)/shard_map/all_to_all | solution.py:495
  94.5 1.8 collective-permute-start.14
  96.8 3.9 %collective-permute-done.14.refs_9_ = f32[128,256]{1,0:T(8,128)S(1)} collective-permute-done((f32[128,256]{1,0:T(8,128)S(1)}, f32[128,256]{1,0:T(8,128)S(1)}, u32[]{:S(2)}, u32[]{:S(2)}) %collective-permute-start.14) | collective-permute-done | bytes 131104 | tf_op jit(solution)/shard_map/ppermute | solution.py:482
  106.7 1.7 collective-permute-start.17
  108.4 3.2 %collective-permute-start.16 = (f32[8,256]{1,0:T(8,128)S(1)}, f32[8,256]{1,0:T(8,128)S(1)}, u32[]{:S(2)}, u32[]{:S(2)}) collective-permute-start(f32[8,256]{1,0:T(8,128)S(1)} %get-tuple-element.83.refs_0_), channel_id=1, source_target_pairs={{0,8},{4,12},{8,0},{12,4},{1,9},{5,13},{9,1},{13,5},{2,10},{6,14},... | collective-permute-start | bytes 24584 | tf_op jit(solution)/shard_map/ppermute | solution.py:489
  112.4 2.4 %collective-permute-done.16.refs_2_ = f32[8,256]{1,0:T(8,128)S(1)} collective-permute-done((f32[8,256]{1,0:T(8,128)S(1)}, f32[8,256]{1,0:T(8,128)S(1)}, u32[]{:S(2)}, u32[]{:S(2)}) %collective-permute-start.16) | collective-permute-done | bytes 8224 | tf_op jit(solution)/shard_map/ppermute | solution.py:489
  116.2 5.0 %collective-permute-start.20 = (f32[8,256]{1,0:T(8,128)S(1)}, f32[8,256]{1,0:T(8,128)S(1)}, u32[]{:S(2)}, u32[]{:S(2)}) collective-permute-start(f32[8,256]{1,0:T(8,128)S(1)} %shard_map.87.refs_0_), channel_id=1, source_target_pairs={{0,3},{1,2},{2,1},{3,0},{4,7},{5,6},{6,5},{7,4},{8,11},{9,10},{10,... | collective-permute-start | bytes 24584 | tf_op jit(solution)/shard_map/ppermute | solution.py:482
  123.9 1.9 %shard_map.88 = (f32[16,32,256]{2,1,0:T(8,128)S(1)}, f32[128,256]{1,0:T(8,128)S(1)}, f32[128,256]{1,0:T(8,128)S(1)}, f32[8,128]{1,0:T(8,128)S(1)}) custom-call(f32[8,256]{1,0:T(8,128)S(1)} %shard_map.87.refs_0_, f32[8,256]{1,0:T(8,128)S(1)} %collective-permute-done.18.refs_1_, f32[8,256]{1,0:T(8,128)S(1)} %collective-permute-done.19.refs_2_, ...), custom_call_target="tpu_custom_call" | custom-call | tf_op jit(solution)/shard_map/pallas_call | solution.py:467
  126.6 3.6 %all-to-all-start.4 = ((f32[16,32,256]{2,1,0:T(8,128)}), f32[16,32,256]{2,1,0:T(8,128)S(1)}, u32[]{:S(2)}, u32[]{:S(2)}) async-start(f32[16,32,256]{2,1,0:T(8,128)} %copy-done.7), calls=%async_computation.4 | async-start | bytes 1048576 | tf_op jit(solution)/shard_map/all_to_all | solution.py:495
  131.2 2.4 %shard_map.89 = (f32[160,256]{1,0:T(8,128)S(1)}, f32[160,256]{1,0:T(8,128)S(1)}, f32[160,256]{1,0:T(8,128)S(1)}, f32[160,256]{1,0:T(8,128)S(1)}) custom-call(f32[512,256]{1,0:T(8,128)S(1)} %copy-done.6, f32[264,256]{1,0:T(8,128)S(1)} %get-tuple-element.54.refs_5_.refs_1_.refs_6_.refs_7_.refs_4_.refs_13_.refs_10_, ...), custom_call_target="tpu_custom_call" | custom-call | tf_op jit(solution)/shard_map/pallas_call | solution.py:467
  136.5 4.0 %collective-permute-done.22.refs_2_ = f32[160,256]{1,0:T(8,128)S(1)} collective-permute-done((f32[160,256]{1,0:T(8,128)S(1)}, f32[160,256]{1,0:T(8,128)S(1)}, u32[]{:S(2)}, u32[]{:S(2)}) %collective-permute-start.22) | collective-permute-done | bytes 163872 | tf_op jit(solution)/shard_map/ppermute | solution.py:482
  140.5 3.7 %collective-permute-done.23.refs_3_ = f32[160,256]{1,0:T(8,128)S(1)} collective-permute-done((f32[160,256]{1,0:T(8,128)S(1)}, f32[160,256]{1,0:T(8,128)S(1)}, u32[]{:S(2)}, u32[]{:S(2)}) %collective-permute-start.23) | collective-permute-done | bytes 163872 | tf_op jit(solution)/shard_map/ppermute | solution.py:482
  144.8 2.5 %collective-permute-start.25 = (f32[32,256]{1,0:T(8,128)S(1)}, f32[32,256]{1,0:T(8,128)S(1)}, u32[]{:S(2)}, u32[]{:S(2)}) collective-permute-start(f32[32,256]{1,0:T(8,128)S(1)} %shard_map.90.refs_0_), channel_id=1, source_target_pairs={{0,8},{4,12},{8,0},{12,4},{1,9},{5,13},{9,1},{13,5},{2,10},{6,14},... | collective-permute-start | bytes 98312 | tf_op jit(solution)/shard_map/ppermute | solution.py:489
  147.2 1.8 collective-permute-start.24
  149.2 2.3 %collective-permute-done.25.refs_2_ = f32[32,256]{1,0:T(8,128)S(1)} collective-permute-done((f32[32,256]{1,0:T(8,128)S(1)}, f32[32,256]{1,0:T(8,128)S(1)}, u32[]{:S(2)}, u32[]{:S(2)}) %collective-permute-start.25) | collective-permute-done | bytes 32800 | tf_op jit(solution)/shard_map/ppermute | solution.py:489
  153.3 24.1 %all_to_all.36 = f32[256,1,128]{2,1,0:T(1,128)S(1)} all-to-all(f32[256,1,128]{2,1,0:T(1,128)S(1)} %bitcast.11), channel_id=1, replica_groups=mesh['x'=4,'y'=4,'h'=4,'l'=2,'k'=2] {'x','y','h','l','k'}, dimensions={0} | all-to-all | bytes 262144 | tf_op jit(solution)/shard_map/all_to_all | solution.py:495
  (106 shorter events, 38.8 us)
Async XLA Ops:
  0.6 10.1 %collective-permute-start.2 = (f32[128,256]{1,0:T(8,128)}, f32[128,256]{1,0:T(8,128)S(1)}, u32[]{:S(2)}, u32[]{:S(2)}) collective-permute-start(f32[128,256]{1,0:T(8,128)} %bitcast.8), channel_id=1, source_target_pairs={{0,3},{1,2},{2,1},{3,0},{4,7},{5,6},{6,5},{7,4},{8,11},{9,10},{10,... | collective-permute-start | bytes 393224 | tf_op jit(solution)/shard_map/ppermute | solution.py:482
  3.7 7.1 %collective-permute-start.1 = (f32[128,256]{1,0:T(8,128)}, f32[128,256]{1,0:T(8,128)S(1)}, u32[]{:S(2)}, u32[]{:S(2)}) collective-permute-start(f32[128,256]{1,0:T(8,128)} %bitcast.9), channel_id=1, source_target_pairs={{0,2},{1,3},{2,0},{3,1},{4,6},{5,7},{6,4},{7,5},{8,10},{9,11},{10,... | collective-permute-start | bytes 393224 | tf_op jit(solution)/shard_map/ppermute | solution.py:482
  5.3 5.5 %collective-permute-start = (f32[128,256]{1,0:T(8,128)}, f32[128,256]{1,0:T(8,128)S(1)}, u32[]{:S(2)}, u32[]{:S(2)}) collective-permute-start(f32[128,256]{1,0:T(8,128)} %bitcast.10), channel_id=1, source_target_pairs={{0,1},{1,0},{2,3},{3,2},{4,5},{5,4},{6,7},{7,6},{8,9},{9,8},{10,11... | collective-permute-start | bytes 393224 | tf_op jit(solution)/shard_map/ppermute | solution.py:482
  14.3 17.7 %all-to-all-start = ((f32[16,40,256]{2,1,0:T(8,128)}), f32[16,40,256]{2,1,0:T(8,128)S(1)}, u32[]{:S(2)}, u32[]{:S(2)}) async-start(f32[16,40,256]{2,1,0:T(8,128)} %copy-done.4), calls=%async_computation | async-start | bytes 1310720 | tf_op jit(solution)/shard_map/all_to_all | solution.py:495
  32.0 18.8 %all-to-all-start.1 = ((f32[16,32,256]{2,1,0:T(8,128)}), f32[16,32,256]{2,1,0:T(8,128)S(1)}, u32[]{:S(2)}, u32[]{:S(2)}) async-start(f32[16,32,256]{2,1,0:T(8,128)} %shard_map.79), calls=%async_computation.1 | async-start | bytes 1048576 | tf_op jit(solution)/shard_map/all_to_all | solution.py:495
  35.6 10.1 %collective-permute-start.5 = (f32[64,256]{1,0:T(8,128)S(1)}, f32[64,256]{1,0:T(8,128)S(1)}, u32[]{:S(2)}, u32[]{:S(2)}) collective-permute-start(f32[64,256]{1,0:T(8,128)S(1)} %shard_map.80.refs_0_), channel_id=1, source_target_pairs={{0,12},{4,0},{8,4},{12,8},{1,13},{5,1},{9,5},{13,9},{2,14},{6,2},{... | collective-permute-start | bytes 196616 | tf_op jit(solution)/shard_map/ppermute | solution.py:489
  42.5 7.2 %collective-permute-start.4 = (f32[64,256]{1,0:T(8,128)S(1)}, f32[64,256]{1,0:T(8,128)S(1)}, u32[]{:S(2)}, u32[]{:S(2)}) collective-permute-start(f32[64,256]{1,0:T(8,128)S(1)} %shard_map.80.refs_0_), channel_id=1, source_target_pairs={{0,8},{4,12},{8,0},{12,4},{1,9},{5,13},{9,1},{13,5},{2,10},{6,14},... | collective-permute-start | bytes 196616 | tf_op jit(solution)/shard_map/ppermute | solution.py:489
  43.4 6.5 %collective-permute-start.3 = (f32[64,256]{1,0:T(8,128)S(1)}, f32[64,256]{1,0:T(8,128)S(1)}, u32[]{:S(2)}, u32[]{:S(2)}) collective-permute-start(f32[64,256]{1,0:T(8,128)S(1)} %shard_map.80.refs_0_), channel_id=1, source_target_pairs={{0,4},{4,8},{8,12},{12,0},{1,5},{5,9},{9,13},{13,1},{2,6},{6,10},{... | collective-permute-start | bytes 196616 | tf_op jit(solution)/shard_map/ppermute | solution.py:489
  50.8 16.6 %all-to-all-start.2 = ((f32[16,32,256]{2,1,0:T(8,128)}), f32[16,32,256]{2,1,0:T(8,128)S(1)}, u32[]{:S(2)}, u32[]{:S(2)}) async-start(f32[16,32,256]{2,1,0:T(8,128)} %copy-done.8), calls=%async_computation.2 | async-start | bytes 1048576 | tf_op jit(solution)/shard_map/all_to_all | solution.py:495
  57.5 9.7 %collective-permute-start.8 = (f32[32,256]{1,0:T(8,128)S(1)}, f32[32,256]{1,0:T(8,128)S(1)}, u32[]{:S(2)}, u32[]{:S(2)}) collective-permute-start(f32[32,256]{1,0:T(8,128)S(1)} %shard_map.82.refs_4_), channel_id=1, source_target_pairs={{0,12},{4,0},{8,4},{12,8},{1,13},{5,1},{9,5},{13,9},{2,14},{6,2},{... | collective-permute-start | bytes 98312 | tf_op jit(solution)/shard_map/ppermute | solution.py:489
  59.0 8.3 %collective-permute-start.7 = (f32[32,256]{1,0:T(8,128)S(1)}, f32[32,256]{1,0:T(8,128)S(1)}, u32[]{:S(2)}, u32[]{:S(2)}) collective-permute-start(f32[32,256]{1,0:T(8,128)S(1)} %shard_map.82.refs_4_), channel_id=1, source_target_pairs={{0,8},{4,12},{8,0},{12,4},{1,9},{5,13},{9,1},{13,5},{2,10},{6,14},... | collective-permute-start | bytes 98312 | tf_op jit(solution)/shard_map/ppermute | solution.py:489
  62.3 5.1 %collective-permute-start.6 = (f32[32,256]{1,0:T(8,128)S(1)}, f32[32,256]{1,0:T(8,128)S(1)}, u32[]{:S(2)}, u32[]{:S(2)}) collective-permute-start(f32[32,256]{1,0:T(8,128)S(1)} %shard_map.82.refs_4_), channel_id=1, source_target_pairs={{0,4},{4,8},{8,12},{12,0},{1,5},{5,9},{9,13},{13,1},{2,6},{6,10},{... | collective-permute-start | bytes 98312 | tf_op jit(solution)/shard_map/ppermute | solution.py:489
  69.9 6.6 %collective-permute-start.9 = (f32[160,256]{1,0:T(8,128)S(1)}, f32[160,256]{1,0:T(8,128)S(1)}, u32[]{:S(2)}, u32[]{:S(2)}) collective-permute-start(f32[160,256]{1,0:T(8,128)S(1)} %get-tuple-element.75), channel_id=1, source_target_pairs={{0,1},{1,0},{2,3},{3,2},{4,5},{5,4},{6,7},{7,6},{8,9},{9,8},{10,11... | collective-permute-start | bytes 491528 | tf_op jit(solution)/shard_map/ppermute | solution.py:482
  74.7 5.7 %collective-permute-start.10 = (f32[160,256]{1,0:T(8,128)S(1)}, f32[160,256]{1,0:T(8,128)S(1)}, u32[]{:S(2)}, u32[]{:S(2)}) collective-permute-start(f32[160,256]{1,0:T(8,128)S(1)} %get-tuple-element.76), channel_id=1, source_target_pairs={{0,2},{1,3},{2,0},{3,1},{4,6},{5,7},{6,4},{7,5},{8,10},{9,11},{10,... | collective-permute-start | bytes 491528 | tf_op jit(solution)/shard_map/ppermute | solution.py:482
  76.1 8.1 %collective-permute-start.11 = (f32[160,256]{1,0:T(8,128)S(1)}, f32[160,256]{1,0:T(8,128)S(1)}, u32[]{:S(2)}, u32[]{:S(2)}) collective-permute-start(f32[160,256]{1,0:T(8,128)S(1)} %get-tuple-element.77), channel_id=1, source_target_pairs={{0,3},{1,2},{2,1},{3,0},{4,7},{5,6},{6,5},{7,4},{8,11},{9,10},{10,... | collective-permute-start | bytes 491528 | tf_op jit(solution)/shard_map/ppermute | solution.py:482
  87.6 18.3 %all-to-all-start.3 = ((f32[16,40,256]{2,1,0:T(8,128)}), f32[16,40,256]{2,1,0:T(8,128)S(1)}, u32[]{:S(2)}, u32[]{:S(2)}) async-start(f32[16,40,256]{2,1,0:T(8,128)} %copy-done.3), calls=%async_computation.3 | async-start | bytes 1310720 | tf_op jit(solution)/shard_map/all_to_all | solution.py:495
  94.5 6.2 %collective-permute-start.14 = (f32[128,256]{1,0:T(8,128)S(1)}, f32[128,256]{1,0:T(8,128)S(1)}, u32[]{:S(2)}, u32[]{:S(2)}) collective-permute-start(f32[128,256]{1,0:T(8,128)S(1)} %get-tuple-element.79.refs_6_), channel_id=1, source_target_pairs={{0,3},{1,2},{2,1},{3,0},{4,7},{5,6},{6,5},{7,4},{8,11},{9,10},{10,... | collective-permute-start | bytes 393224 | tf_op jit(solution)/shard_map/ppermute | solution.py:482
  96.3 6.7 %collective-permute-start.13 = (f32[128,256]{1,0:T(8,128)S(1)}, f32[128,256]{1,0:T(8,128)S(1)}, u32[]{:S(2)}, u32[]{:S(2)}) collective-permute-start(f32[128,256]{1,0:T(8,128)S(1)} %get-tuple-element.79.refs_6_), channel_id=1, source_target_pairs={{0,2},{1,3},{2,0},{3,1},{4,6},{5,7},{6,4},{7,5},{8,10},{9,11},{10,... | collective-permute-start | bytes 393224 | tf_op jit(solution)/shard_map/ppermute | solution.py:482
  96.3 7.2 %collective-permute-start.12 = (f32[128,256]{1,0:T(8,128)S(1)}, f32[128,256]{1,0:T(8,128)S(1)}, u32[]{:S(2)}, u32[]{:S(2)}) collective-permute-start(f32[128,256]{1,0:T(8,128)S(1)} %get-tuple-element.79.refs_6_), channel_id=1, source_target_pairs={{0,1},{1,0},{2,3},{3,2},{4,5},{5,4},{6,7},{7,6},{8,9},{9,8},{10,11... | collective-permute-start | bytes 393224 | tf_op jit(solution)/shard_map/ppermute | solution.py:482
  106.7 5.7 %collective-permute-start.17 = (f32[8,256]{1,0:T(8,128)S(1)}, f32[8,256]{1,0:T(8,128)S(1)}, u32[]{:S(2)}, u32[]{:S(2)}) collective-permute-start(f32[8,256]{1,0:T(8,128)S(1)} %get-tuple-element.83.refs_0_), channel_id=1, source_target_pairs={{0,12},{4,0},{8,4},{12,8},{1,13},{5,1},{9,5},{13,9},{2,14},{6,2},{... | collective-permute-start | bytes 24584 | tf_op jit(solution)/shard_map/ppermute | solution.py:489
  108.4 6.4 %collective-permute-start.16 = (f32[8,256]{1,0:T(8,128)S(1)}, f32[8,256]{1,0:T(8,128)S(1)}, u32[]{:S(2)}, u32[]{:S(2)}) collective-permute-start(f32[8,256]{1,0:T(8,128)S(1)} %get-tuple-element.83.refs_0_), channel_id=1, source_target_pairs={{0,8},{4,12},{8,0},{12,4},{1,9},{5,13},{9,1},{13,5},{2,10},{6,14},... | collective-permute-start | bytes 24584 | tf_op jit(solution)/shard_map/ppermute | solution.py:489
  111.6 4.6 %collective-permute-start.15 = (f32[8,256]{1,0:T(8,128)S(1)}, f32[8,256]{1,0:T(8,128)S(1)}, u32[]{:S(2)}, u32[]{:S(2)}) collective-permute-start(f32[8,256]{1,0:T(8,128)S(1)} %get-tuple-element.83.refs_0_), channel_id=1, source_target_pairs={{0,4},{4,8},{8,12},{12,0},{1,5},{5,9},{9,13},{13,1},{2,6},{6,10},{... | collective-permute-start | bytes 24584 | tf_op jit(solution)/shard_map/ppermute | solution.py:489
  116.2 6.3 %collective-permute-start.20 = (f32[8,256]{1,0:T(8,128)S(1)}, f32[8,256]{1,0:T(8,128)S(1)}, u32[]{:S(2)}, u32[]{:S(2)}) collective-permute-start(f32[8,256]{1,0:T(8,128)S(1)} %shard_map.87.refs_0_), channel_id=1, source_target_pairs={{0,3},{1,2},{2,1},{3,0},{4,7},{5,6},{6,5},{7,4},{8,11},{9,10},{10,... | collective-permute-start | bytes 24584 | tf_op jit(solution)/shard_map/ppermute | solution.py:482
  121.2 2.7 %collective-permute-start.19 = (f32[8,256]{1,0:T(8,128)S(1)}, f32[8,256]{1,0:T(8,128)S(1)}, u32[]{:S(2)}, u32[]{:S(2)}) collective-permute-start(f32[8,256]{1,0:T(8,128)S(1)} %shard_map.87.refs_0_), channel_id=1, source_target_pairs={{0,2},{1,3},{2,0},{3,1},{4,6},{5,7},{6,4},{7,5},{8,10},{9,11},{10,... | collective-permute-start | bytes 24584 | tf_op jit(solution)/shard_map/ppermute | solution.py:482
  121.9 2.0 %collective-permute-start.18 = (f32[8,256]{1,0:T(8,128)S(1)}, f32[8,256]{1,0:T(8,128)S(1)}, u32[]{:S(2)}, u32[]{:S(2)}) collective-permute-start(f32[8,256]{1,0:T(8,128)S(1)} %shard_map.87.refs_0_), channel_id=1, source_target_pairs={{0,1},{1,0},{2,3},{3,2},{4,5},{5,4},{6,7},{7,6},{8,9},{9,8},{10,11... | collective-permute-start | bytes 24584 | tf_op jit(solution)/shard_map/ppermute | solution.py:482
  126.6 17.6 %all-to-all-start.4 = ((f32[16,32,256]{2,1,0:T(8,128)}), f32[16,32,256]{2,1,0:T(8,128)S(1)}, u32[]{:S(2)}, u32[]{:S(2)}) async-start(f32[16,32,256]{2,1,0:T(8,128)} %copy-done.7), calls=%async_computation.4 | async-start | bytes 1048576 | tf_op jit(solution)/shard_map/all_to_all | solution.py:495
  134.3 2.1 %collective-permute-start.21 = (f32[160,256]{1,0:T(8,128)S(1)}, f32[160,256]{1,0:T(8,128)S(1)}, u32[]{:S(2)}, u32[]{:S(2)}) collective-permute-start(f32[160,256]{1,0:T(8,128)S(1)} %get-tuple-element.91), channel_id=1, source_target_pairs={{0,1},{1,0},{2,3},{3,2},{4,5},{5,4},{6,7},{7,6},{8,9},{9,8},{10,11... | collective-permute-start | bytes 491528 | tf_op jit(solution)/shard_map/ppermute | solution.py:482
  134.8 5.7 %collective-permute-start.22 = (f32[160,256]{1,0:T(8,128)S(1)}, f32[160,256]{1,0:T(8,128)S(1)}, u32[]{:S(2)}, u32[]{:S(2)}) collective-permute-start(f32[160,256]{1,0:T(8,128)S(1)} %get-tuple-element.92), channel_id=1, source_target_pairs={{0,2},{1,3},{2,0},{3,1},{4,6},{5,7},{6,4},{7,5},{8,10},{9,11},{10,... | collective-permute-start | bytes 491528 | tf_op jit(solution)/shard_map/ppermute | solution.py:482
  135.6 8.6 %collective-permute-start.23 = (f32[160,256]{1,0:T(8,128)S(1)}, f32[160,256]{1,0:T(8,128)S(1)}, u32[]{:S(2)}, u32[]{:S(2)}) collective-permute-start(f32[160,256]{1,0:T(8,128)S(1)} %get-tuple-element.93), channel_id=1, source_target_pairs={{0,3},{1,2},{2,1},{3,0},{4,7},{5,6},{6,5},{7,4},{8,11},{9,10},{10,... | collective-permute-start | bytes 491528 | tf_op jit(solution)/shard_map/ppermute | solution.py:482
  144.2 5.0 %collective-permute-start.26 = (f32[32,256]{1,0:T(8,128)S(1)}, f32[32,256]{1,0:T(8,128)S(1)}, u32[]{:S(2)}, u32[]{:S(2)}) collective-permute-start(f32[32,256]{1,0:T(8,128)S(1)} %shard_map.90.refs_0_), channel_id=1, source_target_pairs={{0,12},{4,0},{8,4},{12,8},{1,13},{5,1},{9,5},{13,9},{2,14},{6,2},{... | collective-permute-start | bytes 98312 | tf_op jit(solution)/shard_map/ppermute | solution.py:489
  144.8 6.8 %collective-permute-start.25 = (f32[32,256]{1,0:T(8,128)S(1)}, f32[32,256]{1,0:T(8,128)S(1)}, u32[]{:S(2)}, u32[]{:S(2)}) collective-permute-start(f32[32,256]{1,0:T(8,128)S(1)} %shard_map.90.refs_0_), channel_id=1, source_target_pairs={{0,8},{4,12},{8,0},{12,4},{1,9},{5,13},{9,1},{13,5},{2,10},{6,14},... | collective-permute-start | bytes 98312 | tf_op jit(solution)/shard_map/ppermute | solution.py:489
  147.2 5.9 %collective-permute-start.24 = (f32[32,256]{1,0:T(8,128)S(1)}, f32[32,256]{1,0:T(8,128)S(1)}, u32[]{:S(2)}, u32[]{:S(2)}) collective-permute-start(f32[32,256]{1,0:T(8,128)S(1)} %shard_map.90.refs_0_), channel_id=1, source_target_pairs={{0,4},{4,8},{8,12},{12,0},{1,5},{5,9},{9,13},{13,1},{2,6},{6,10},{... | collective-permute-start | bytes 98312 | tf_op jit(solution)/shard_map/ppermute | solution.py:489
  (28 other events, 97.6 us)

commit v7 on v5

--- a/solution.py
+++ b/solution.py
@@ -221,11 +221,12 @@
     for source in range(1, nxy):
         total = total + got_ref[source, : 2 * rows, :]
     sum_ref[: 2 * rows] = total
-    for source in range(nxy):
-        place = 2 * rows + source
-        sum_ref[place : place + 1, :] = got_ref[source, 2 * rows : 2 * rows + 1, :]
+    left = lax.broadcasted_iota(jnp.int32, (1, NY), 1) < HY
+    for pair in range(nxy // 2):
+        first, second = (got_ref[2 * pair + i, 2 * rows : 2 * rows + 1, :] for i in (0, 1))
+        sum_ref[2 * rows + pair : 2 * rows + pair + 1, :] = jnp.where(left, first, second)
     part = weight_ref.shape[0]
-    start = 2 * rows + nxy
+    start = 2 * rows + nxy // 2
     sum_ref[start : start + part] = weight_ref[...]
     sum_ref[start + part : start + 2 * part] = obs_ref[...]
 
@@ -233,7 +234,8 @@
 def residual_kernel(nxy, nh, *refs):
     rows = NX // nxy
     part = rows // nh
-    start = 2 * rows + nxy
+    pairs = nxy // 2
+    start = 2 * rows + pairs
     sums = refs[:nh]
     pred_ref, pull_ref, weight_ref, tops_ref, send_ref, meas_ref = refs[nh:]
     chip = lax.axis_index("h")
@@ -241,7 +243,7 @@
     for step in range(1, nh):
         total = total + sums[step][: 2 * rows]
     for step in range(nh):
-        tops_ref[step * nxy : (step + 1) * nxy] = sums[step][2 * rows : start]
+        tops_ref[step * pairs : (step + 1) * pairs] = sums[step][2 * rows : start]
         place = pl.ds(pl.multiple_of(lax.rem(chip + (nh - step), nh) * part, part), part)
         weight_ref[place, :] = sums[step][start : start + part]
         meas_ref[place, :] = sums[step][start + part :]
@@ -262,8 +264,10 @@
         double = -2.0 * ks
 
         def add(step, total):
-            for layer in range(4):
-                total = total + jnp.exp(double * tops_ref[pl.ds(4 * step + layer, 1), :])
+            for pair in range(2):
+                tops = tops_ref[pl.ds(2 * step + pair, 1), :]
+                for top in (tops[:, :HY], tops[:, HY:]):
+                    total = total + jnp.exp(double * jnp.concatenate([top, top], axis=1))
             return total
 
         total = lax.fori_loop(0, layers // 4, add, jnp.zeros_like(ks))
@@ -374,36 +378,30 @@
 
 def second_kernel(
     s0, s1, s2, s3, dens_ref, full_ref, g0, g1, g2, g3, decay_ref, gx_ref, gy_ref, fx, bx, ty,
-    out_ref, dens_out, base_out, alpha_ref, all_ref, near_ref, sems,
+    out_ref, dens_out, base_out, alpha_ref, all_ref,
 ):
-    comp = comp_index()
-    copies = [pltpu.make_async_copy(full_ref, near_ref, sems.at[4])]
-    for step, piece in enumerate((g0, g1, g2, g3)):
-        place = pl.ds(pl.multiple_of(jnp.bitwise_xor(comp, step) * QX, QX), QX)
-        copies.append(pltpu.make_async_copy(piece, all_ref.at[place, :], sems.at[step]))
-    for copy in copies:
-        copy.start()
+    gather_rows((g0, g1, g2, g3), all_ref)
     alpha = step_length(s0[:1] + s1[:1] + (s2[:1] + s3[:1]))
     alpha_ref[...] = jnp.broadcast_to(alpha, alpha_ref.shape)
     old = dens_ref[...]
-    for copy in copies:
-        copy.wait()
-    grad = all_ref[pl.ds(pl.multiple_of(comp * QX, QX), QX), :]
+    grad = g0[...]
     dens = old - alpha * grad
     dens_out[...] = dens
     data = grad - 0.5 * ((1.0 / (old * old + 0.25)) * old)
     base_out[...] = data + 0.5 * (dens * (1.0 / (dens * dens + 0.25)))
-    dens = near_ref[...] - alpha * all_ref[...]
+    dens = full_ref[...] - alpha * all_ref[...]
     all_ref[...] = 0.5 * (dens * (1.0 / (dens * dens + 0.25)))
     plane = forward_plane(all_ref[...], decay_ref, gx_ref, gy_ref, fx, bx, ty)
     out_ref[...] = plane.reshape(out_ref.shape)
 
 
-def sum_kernel(nxy, got_ref, sum_ref):
+def sum_kernel(nxy, got_ref, half_ref, sum_ref):
+    rows = NX // nxy
     total = got_ref[0]
     for source in range(1, nxy):
         total = total + got_ref[source]
-    sum_ref[...] = total
+    sum_ref[:rows] = total
+    sum_ref[rows:] = half_ref[...]
 
 
 def second_gradient_kernel(
@@ -417,25 +415,26 @@
     grad_ref[...] = grad
     image_ref[...] = line_ref[...] - alpha * total[QX:]
     square = grad * grad
-    lane = lax.broadcasted_iota(jnp.int32, (8, 128), 1)
+    lane = lax.broadcasted_iota(jnp.int32, (8, NY), 1)
     share_ref[...] = jnp.where(
         lane == 0, jnp.sum(square), jnp.where(lane == 1, jnp.sum(quad * square), 0.0)
     )
 
 
-def curvature_kernel(nh, *refs):
+def curvature_kernel(nh, part, *refs):
     parts = refs[:nh]
-    image_ref, weight_ref, part_ref, share_ref, out_ref = refs[nh:]
-    part = weight_ref.shape[0]
-    place = pl.ds(pl.multiple_of(lax.axis_index("h") * part, part), part)
-    image = image_ref[place, :]
-    for piece in parts:
-        image = image + piece[place, :]
-    out_ref[...] = image
+    image_ref, weight_ref, share_ref, out_ref, scratch = refs[nh:]
+    rows = image_ref.shape[0]
+    total = parts[0][...]
+    for piece in parts[1:]:
+        total = total + piece[...]
+    image = image_ref[...] + total[:rows]
+    scratch[...] = image
+    out_ref[...] = scratch[pl.ds(pl.multiple_of(lax.axis_index("h") * part, part), part), :]
     mine = weight_ref[...] * image
     lane = lax.broadcasted_iota(jnp.int32, (1, 128), 1)
     share_ref[...] = jnp.broadcast_to(
-        jnp.where(lane == 2, jnp.sum(mine * mine), part_ref[:1]), share_ref.shape
+        jnp.where(lane == 2, jnp.sum(mine * mine), total[rows : rows + 1, :128]), share_ref.shape
     )
 
 
@@ -466,7 +465,7 @@
     def drop(self, *values):
         self.alive = [item for item in self.alive if all(item is not value for value in values)]
 
-    def call(self, kernel, outs, *args, scratch=(), scalars=(), far=(), far_out=(), sems=0, mib=8):
+    def call(self, kernel, outs, *args, scratch=(), scalars=(), far_out=(), sems=0, mib=8):
         used = len(args)
         keep = [item for item in self.alive if all(item is not value for value in args)]
         kept = len(keep)
@@ -479,7 +478,7 @@
             inner,
             out_shape=[jax.ShapeDtypeStruct(shape, dtype) for shape, dtype in kinds],
             in_specs=[
-                SMEM if place in scalars else ANY if place in far else VMEM for place in range(used)
+                SMEM if place in scalars else VMEM for place in range(used)
             ]
             + [ANY] * kept,
             out_specs=[ANY if place in far_out else VMEM for place in range(len(outs))],
@@ -516,7 +515,6 @@
 def body(density, observed, data_weight, layer_top):
     nx, ny, nh = (lax.axis_size(axis) for axis in DEPTH)
     nxy = nx * ny
-    devices = nxy * nh * 4
     rows = NX // nxy
     part = rows // nh
     fx, ty = (jnp.asarray(table) for table in make_tables())
@@ -541,12 +539,12 @@
     )
     got = exchange(message, XY)
     (sums,) = call(
-        bind(collect_kernel, nxy), [(2 * rows + nxy + 2 * part, NY)], got, weight_own, obs_own
+        bind(collect_kernel, nxy), [(2 * rows + nxy // 2 + 2 * part, NY)], got, weight_own, obs_own
     )
     sums = from_axis([sums] * nh, "h")
     pred, pulled, weight, tops, message = call(
         bind(residual_kernel, nxy, nh),
-        [(rows, NY), (rows, NY), (rows, NY), (nxy * nh, NY), (nxy, rows, NY)],
+        [(rows, NY), (rows, NY), (rows, NY), (nxy * nh // 2, NY), (nxy, rows, NY)],
         *sums, scratch=[(rows, NY)],
     )
     program.hold(pred, pulled, weight)
@@ -564,7 +562,7 @@
         [(nxy, rows + 8, NY), (QX, NY), (rows, NY), (rows, NY)],
         *pieces, pulled, dens, weight, scratch=[(rows, NY)],
     )
-    program.drop(pulled, weight)
+    program.drop(pulled)
     program.hold(line, image)
     grads = from_comps([grad] * 4)
     got = after(exchange(message, XY), *grads)
@@ -575,23 +573,22 @@
     shares = from_comps([shares] * 4)
     message, dens, base, alpha = call(
         second_kernel, [(nxy, rows, NY), (QX, NY), (QX, NY), (8, 128)],
-        *shares, dens, full, *grads, *factors, *tables,
-        scratch=[(NX, NY)] * 2, far=(5, 6, 7, 8, 9), sems=5,
-    )
-    program.alive = [weight_own, obs_own, pred, line, image, dens, base, alpha]
+        *shares, dens, full, *grads, *factors, *tables, scratch=[(NX, NY)],
+    )
+    program.alive = [weight_own, obs_own, weight, pred, line, image, dens, base, alpha]
     got = exchange(message, XY)
     pieces = from_comps(after(pieces, message))
     grad2, image2, half = call(
-        second_gradient_kernel, [(QX, NY), (rows, NY), (8, 128)],
+        second_gradient_kernel, [(QX, NY), (rows, NY), (8, NY)],
         *pieces, alpha, base, dens, line,
     )
-    (parts,) = call(bind(sum_kernel, nxy), [(rows, NY)], got)
-    parts = after(from_axis([parts] * nh, "h"), half)
-    program.alive = [obs_own, pred, image, dens, alpha, grad2]
+    (parts,) = call(bind(sum_kernel, nxy), [(rows + 8, NY)], got, half)
+    program.alive = [weight_own, obs_own, pred, image, dens, alpha, grad2]
     shares, image2 = call(
-        bind(curvature_kernel, nh), [(devices, 128), (part, NY)], *parts, image2, weight_own, half
-    )
-    shares = exchange(shares, ALL)
+        bind(curvature_kernel, nh, part), [(nxy * 4, 128), (part, NY)],
+        *from_axis([parts] * nh, "h"), image2, weight, scratch=[(rows, NY)],
+    )
+    shares = exchange(shares, (*XY, *COMP))
     program.alive = []
     return tuple(
         call(

time: 170 us -> 164 us (0.965)
  blocking collectives: 44.4 us -> 39.7 us
  local copies, waits for them, and re-layouts: 8.07 us -> 10 us
    all_to_all x3, waiting for transfers between devices: 17.3 us -> 9.14 us  [exchange(): return lax.all_to_all(value, axes, 0, 0, tiled=True)]
    ppermute x15, waiting for transfers between devices: 15.4 us -> 22.7 us  [from_comps(): lax.ppermute(values[step], COMP, [(i, i ^ step) for i in range(4)])]
    all_to_all x2, blocking collectives: 44.4 us -> 39.7 us  [exchange(): return lax.all_to_all(value, axes, 0, 0, tiled=True)]
    unnamed x32 -> x34, local copies, waits for them, and re-layouts: 8.07 us -> 10 us
  transfers between devices with their start and end apart: 27 -> 27, of which waited for: 15 -> 17; matrix products, arithmetic and copies ran while one was open for 0% -> 0% of each run, Pallas kernels for 4% -> 4%
where the time goes in v7:
time: 164 us
  starting transfers between devices  55.1 us (34%)
  waiting for transfers between devices  41.1 us (25%)
  blocking collectives  39.7 us (24%)
  Pallas kernels  16.2 us (10%)
  local copies, waits for them, and re-layouts  10 us (6%)
    all_to_all x2, blocking collectives, exchange(): return lax.all_to_all(value, axes, 0, 0, tiled=True)  39.7 us
    ppermute x15, waiting for transfers between devices, from_comps(): lax.ppermute(values[step], COMP, [(i, i ^ step) for i in range(4)])  22.7 us
    ppermute x9, starting transfers between devices, from_axis(): lax.ppermute(values[step], axis, [(i, (i + step) % size) for i in range(s...  22.4 us
    ppermute x15, starting transfers between devices, from_comps(): lax.ppermute(values[step], COMP, [(i, i ^ step) for i in range(4)])  21.6 us
    pallas_call x15, Pallas kernels, call(): pl.pallas_call(inner, out_shape=[jax.ShapeDtypeStruct(shape, dtype) for s...  16.2 us
    all_to_all x3, starting transfers between devices, exchange(): return lax.all_to_all(value, axes, 0, 0, tiled=True)  11.1 us
    unnamed x34, local copies, waits for them, and re-layouts  10 us
    ppermute x9, waiting for transfers between devices, from_axis(): lax.ppermute(values[step], axis, [(i, (i + step) % size) for i in range(s...  9.26 us
  transfers between devices with their start and end apart: 27, of which 17 were waited for; matrix products, arithmetic and copies ran while one was open for 0% of the time, Pallas kernels for 4%

profile of v7, /device:TPU:1, one launch (start us, length us, event | category | flops | bytes accessed | tf_op | source)
XLA Modules:
  0.0 163.7 jit_solution(7889170745230423279)
XLA Ops:
  0.6 3.1 %collective-permute-start.2 = (f32[128,256]{1,0:T(8,128)}, f32[128,256]{1,0:T(8,128)S(1)}, u32[]{:S(2)}, u32[]{:S(2)}) collective-permute-start(f32[128,256]{1,0:T(8,128)} %bitcast.7), channel_id=1, source_target_pairs={{0,3},{1,2},{2,1},{3,0},{4,7},{5,6},{6,5},{7,4},{8,11},{9,10},{10,... | collective-permute-start | bytes 393224 | tf_op jit(solution)/shard_map/ppermute | solution.py:493
  3.7 1.5 collective-permute-start.1
  10.8 3.0 %shard_map.78 = (f32[16,72,256]{2,1,0:T(8,128)S(1)}, f32[512,256]{1,0:T(8,128)S(1)}) custom-call(f32[128,256]{1,0:T(8,128)S(1)} %get-tuple-element.50.refs_0_.refs_9_.refs_10_.refs_7_.refs_8_.refs_5_.refs_4_, f32[128,256]{1,0:T(8,128)S(1)} %collective-permute-done.refs_1_, f32[128,256]{1,0:T(8,128)S(1)} %collective-permute-done.1.refs_2_, ...), custom_call_target="tpu_custom_call" | custom-call | tf_op jit(solution)/shard_map/pallas_call | solution.py:477
  14.7 22.7 %all_to_all.31.refs_0_ = f32[16,72,256]{2,1,0:T(8,128)S(1)} all-to-all(f32[16,72,256]{2,1,0:T(8,128)S(1)} %get-tuple-element.59), channel_id=1, replica_groups=mesh['x'=4,'y'=4,'h'=4,'l'=2,'k'=2] {'x','y'}, dimensions={0} | all-to-all | bytes 2359296 | tf_op jit(solution)/shard_map/all_to_all | solution.py:506
  37.5 7.3 %collective-permute-start.5 = (f32[88,256]{1,0:T(8,128)S(1)}, f32[88,256]{1,0:T(8,128)S(1)}, u32[]{:S(2)}, u32[]{:S(2)}) collective-permute-start(f32[88,256]{1,0:T(8,128)S(1)} %shard_map.79.refs_0_), channel_id=1, source_target_pairs={{0,12},{4,0},{8,4},{12,8},{1,13},{5,1},{9,5},{13,9},{2,14},{6,2},{... | collective-permute-start | bytes 270344 | tf_op jit(solution)/shard_map/ppermute | solution.py:500
  45.7 2.3 %collective-permute-start.3 = (f32[88,256]{1,0:T(8,128)S(1)}, f32[88,256]{1,0:T(8,128)S(1)}, u32[]{:S(2)}, u32[]{:S(2)}) collective-permute-start(f32[88,256]{1,0:T(8,128)S(1)} %shard_map.79.refs_0_), channel_id=1, source_target_pairs={{0,4},{4,8},{8,12},{12,0},{1,5},{5,9},{9,13},{13,1},{2,6},{6,10},{... | collective-permute-start | bytes 270344 | tf_op jit(solution)/shard_map/ppermute | solution.py:500
  48.0 3.2 %collective-permute-done.5.refs_3_ = f32[88,256]{1,0:T(8,128)S(1)} collective-permute-done((f32[88,256]{1,0:T(8,128)S(1)}, f32[88,256]{1,0:T(8,128)S(1)}, u32[]{:S(2)}, u32[]{:S(2)}) %collective-permute-start.5) | collective-permute-done | bytes 90144 | tf_op jit(solution)/shard_map/ppermute | solution.py:500
  53.6 4.0 %all-to-all-start.1 = ((f32[16,32,256]{2,1,0:T(8,128)}), f32[16,32,256]{2,1,0:T(8,128)S(1)}, u32[]{:S(2)}, u32[]{:S(2)}) async-start(f32[16,32,256]{2,1,0:T(8,128)} %copy-done.4), calls=%async_computation.1 | async-start | bytes 1048576 | tf_op jit(solution)/shard_map/all_to_all | solution.py:506
  57.6 3.6 %shard_map.81.refs_4_.refs_16_.refs_12_.refs_15_.refs_20_ = f32[264,256]{1,0:T(8,128)S(1)} custom-call(f32[32,256]{1,0:T(8,128)S(1)} %get-tuple-element.61.refs_0_, bf16[4,256,256]{2,1,0:T(8,128)(2,1)S(1)} %get-tuple-element.54.refs_8_.refs_3_.refs_4_.refs_1_.refs_5_.refs_7_.refs_13_, ...), custom_call_target="tpu_custom_call" | custom-call | tf_op jit(solution)/shard_map/pallas_call | solution.py:477
  61.2 5.4 %all-to-all-done.1 = f32[16,32,256]{2,1,0:T(8,128)S(1)} async-done(((f32[16,32,256]{2,1,0:T(8,128)}), f32[16,32,256]{2,1,0:T(8,128)S(1)}, u32[]{:S(2)}, u32[]{:S(2)}) %all-to-all-start.1) | async-done | bytes 524320 | tf_op jit(solution)/shard_map/all_to_all | solution.py:506
  66.5 2.4 %shard_map.82 = (f32[160,256]{1,0:T(8,128)S(1)}, f32[160,256]{1,0:T(8,128)S(1)}, f32[160,256]{1,0:T(8,128)S(1)}, f32[160,256]{1,0:T(8,128)S(1)}) custom-call(f32[512,256]{1,0:T(8,128)S(1)} %bitcast.6, f32[264,256]{1,0:T(8,128)S(1)} %get-tuple-element.51.refs_5_.refs_6_.refs_7_.refs_4_.refs_1_.refs_10_, ...), custom_call_target="tpu_custom_call" | custom-call | tf_op jit(solution)/shard_map/pallas_call | solution.py:477
  69.0 5.5 %collective-permute-start.6 = (f32[160,256]{1,0:T(8,128)S(1)}, f32[160,256]{1,0:T(8,128)S(1)}, u32[]{:S(2)}, u32[]{:S(2)}) collective-permute-start(f32[160,256]{1,0:T(8,128)S(1)} %get-tuple-element.66), channel_id=1, source_target_pairs={{0,1},{1,0},{2,3},{3,2},{4,5},{5,4},{6,7},{7,6},{8,9},{9,8},{10,11... | collective-permute-start | bytes 491528 | tf_op jit(solution)/shard_map/ppermute | solution.py:493
  76.2 3.9 %collective-permute-done.7.refs_2_ = f32[160,256]{1,0:T(8,128)S(1)} collective-permute-done((f32[160,256]{1,0:T(8,128)S(1)}, f32[160,256]{1,0:T(8,128)S(1)}, u32[]{:S(2)}, u32[]{:S(2)}) %collective-permute-start.7) | collective-permute-done | bytes 163872 | tf_op jit(solution)/shard_map/ppermute | solution.py:493
  80.1 3.8 %collective-permute-done.8.refs_3_ = f32[160,256]{1,0:T(8,128)S(1)} collective-permute-done((f32[160,256]{1,0:T(8,128)S(1)}, f32[160,256]{1,0:T(8,128)S(1)}, u32[]{:S(2)}, u32[]{:S(2)}) %collective-permute-start.8) | collective-permute-done | bytes 163872 | tf_op jit(solution)/shard_map/ppermute | solution.py:493
  85.0 3.6 %all-to-all-start.2 = ((f32[16,40,256]{2,1,0:T(8,128)}), f32[16,40,256]{2,1,0:T(8,128)S(1)}, u32[]{:S(2)}, u32[]{:S(2)}) async-start(f32[16,40,256]{2,1,0:T(8,128)} %copy-done), calls=%async_computation.2 | async-start | bytes 1310720 | tf_op jit(solution)/shard_map/all_to_all | solution.py:506
  90.8 3.7 %collective-permute-done.11.refs_9_ = f32[128,256]{1,0:T(8,128)S(1)} collective-permute-done((f32[128,256]{1,0:T(8,128)S(1)}, f32[128,256]{1,0:T(8,128)S(1)}, u32[]{:S(2)}, u32[]{:S(2)}) %collective-permute-start.11) | collective-permute-done | bytes 131104 | tf_op jit(solution)/shard_map/ppermute | solution.py:493
  95.2 1.2 collective-permute-done.10.refs_8_
  97.7 3.1 %all-to-all-done.2.refs_0_ = f32[16,40,256]{2,1,0:T(8,128)S(1)} async-done(((f32[16,40,256]{2,1,0:T(8,128)}), f32[16,40,256]{2,1,0:T(8,128)S(1)}, u32[]{:S(2)}, u32[]{:S(2)}) %all-to-all-start.2) | async-done | bytes 655392 | tf_op jit(solution)/shard_map/all_to_all | solution.py:506
  100.8 2.2 %collective-permute-start.14 = (f32[8,256]{1,0:T(8,128)S(1)}, f32[8,256]{1,0:T(8,128)S(1)}, u32[]{:S(2)}, u32[]{:S(2)}) collective-permute-start(f32[8,256]{1,0:T(8,128)S(1)} %get-tuple-element.80.refs_0_), channel_id=1, source_target_pairs={{0,12},{4,0},{8,4},{12,8},{1,13},{5,1},{9,5},{13,9},{2,14},{6,2},{... | collective-permute-start | bytes 24584 | tf_op jit(solution)/shard_map/ppermute | solution.py:500
  104.1 2.3 %collective-permute-start.12 = (f32[8,256]{1,0:T(8,128)S(1)}, f32[8,256]{1,0:T(8,128)S(1)}, u32[]{:S(2)}, u32[]{:S(2)}) collective-permute-start(f32[8,256]{1,0:T(8,128)S(1)} %get-tuple-element.80.refs_0_), channel_id=1, source_target_pairs={{0,4},{4,8},{8,12},{12,0},{1,5},{5,9},{9,13},{13,1},{2,6},{6,10},{... | collective-permute-start | bytes 24584 | tf_op jit(solution)/shard_map/ppermute | solution.py:500
  106.4 2.4 %shard_map.85 = (f32[160,256]{1,0:T(8,128)S(1)}, f32[160,256]{1,0:T(8,128)S(1)}, f32[160,256]{1,0:T(8,128)S(1)}, f32[160,256]{1,0:T(8,128)S(1)}) custom-call(f32[512,256]{1,0:T(8,128)S(1)} %get-tuple-element.75.refs_0_, f32[264,256]{1,0:T(8,128)S(1)} %get-tuple-element.51.refs_5_.refs_6_.refs_7_.refs_4_.refs_1_.refs_10_, ...), custom_call_target="tpu_custom_call" | custom-call | tf_op jit(solution)/shard_map/pallas_call | solution.py:477
  110.2 4.8 %collective-permute-start.17 = (f32[8,256]{1,0:T(8,128)S(1)}, f32[8,256]{1,0:T(8,128)S(1)}, u32[]{:S(2)}, u32[]{:S(2)}) collective-permute-start(f32[8,256]{1,0:T(8,128)S(1)} %shard_map.86.refs_0_), channel_id=1, source_target_pairs={{0,3},{1,2},{2,1},{3,0},{4,7},{5,6},{6,5},{7,4},{8,11},{9,10},{10,... | collective-permute-start | bytes 24584 | tf_op jit(solution)/shard_map/ppermute | solution.py:493
  117.5 2.7 %shard_map.87 = (f32[16,32,256]{2,1,0:T(8,128)}, f32[128,256]{1,0:T(8,128)S(1)}, f32[128,256]{1,0:T(8,128)S(1)}, f32[8,128]{1,0:T(8,128)S(1)}) custom-call(f32[8,256]{1,0:T(8,128)S(1)} %shard_map.86.refs_0_, f32[8,256]{1,0:T(8,128)S(1)} %collective-permute-done.15.refs_1_, f32[8,256]{1,0:T(8,128)S(1)} %collective-permute-done.16.refs_2_, ...), custom_call_target="tpu_custom_call" | custom-call | tf_op jit(solution)/shard_map/pallas_call | solution.py:477
  120.3 3.6 %all-to-all-start.3 = ((f32[16,32,256]{2,1,0:T(8,128)}), f32[16,32,256]{2,1,0:T(8,128)S(1)}, u32[]{:S(2)}, u32[]{:S(2)}) async-start(f32[16,32,256]{2,1,0:T(8,128)} %get-tuple-element.85), calls=%async_computation.3 | async-start | bytes 1048576 | tf_op jit(solution)/shard_map/all_to_all | solution.py:506
  124.0 1.4 collective-permute-start.19
  126.1 3.5 %collective-permute-done.19.refs_2_ = f32[160,256]{1,0:T(8,128)S(1)} collective-permute-done((f32[160,256]{1,0:T(8,128)}, f32[160,256]{1,0:T(8,128)S(1)}, u32[]{:S(2)}, u32[]{:S(2)}) %collective-permute-start.19) | collective-permute-done | bytes 163872 | tf_op jit(solution)/shard_map/ppermute | solution.py:493
  129.6 4.4 %collective-permute-done.20.refs_3_ = f32[160,256]{1,0:T(8,128)S(1)} collective-permute-done((f32[160,256]{1,0:T(8,128)S(1)}, f32[160,256]{1,0:T(8,128)S(1)}, u32[]{:S(2)}, u32[]{:S(2)}) %collective-permute-start.20) | collective-permute-done | bytes 163872 | tf_op jit(solution)/shard_map/ppermute | solution.py:493
  134.9 1.3 collective-permute-start.23
  136.3 4.5 %collective-permute-start.22 = (f32[40,256]{1,0:T(8,128)S(1)}, f32[40,256]{1,0:T(8,128)S(1)}, u32[]{:S(2)}, u32[]{:S(2)}) collective-permute-start(f32[40,256]{1,0:T(8,128)S(1)} %shard_map.89.refs_0_), channel_id=1, source_target_pairs={{0,8},{4,12},{8,0},{12,4},{1,9},{5,13},{9,1},{13,5},{2,10},{6,14},... | collective-permute-start | bytes 122888 | tf_op jit(solution)/shard_map/ppermute | solution.py:500
  141.2 1.8 %collective-permute-done.22.refs_2_ = f32[40,256]{1,0:T(8,128)S(1)} collective-permute-done((f32[40,256]{1,0:T(8,128)S(1)}, f32[40,256]{1,0:T(8,128)S(1)}, u32[]{:S(2)}, u32[]{:S(2)}) %collective-permute-start.22) | collective-permute-done | bytes 40992 | tf_op jit(solution)/shard_map/ppermute | solution.py:500
  143.0 2.7 %collective-permute-done.21.refs_1_ = f32[40,256]{1,0:T(8,128)S(1)} collective-permute-done((f32[40,256]{1,0:T(8,128)S(1)}, f32[40,256]{1,0:T(8,128)S(1)}, u32[]{:S(2)}, u32[]{:S(2)}) %collective-permute-start.21) | collective-permute-done | bytes 40992 | tf_op jit(solution)/shard_map/ppermute | solution.py:500
  145.9 17.0 %all_to_all.32 = f32[64,1,128]{2,1,0:T(1,128)S(1)} all-to-all(f32[64,1,128]{2,1,0:T(1,128)S(1)} %bitcast.11), channel_id=1, replica_groups=mesh['x'=4,'y'=4,'h'=4,'l'=2,'k'=2] {'x','y','l','k'}, dimensions={0} | all-to-all | bytes 65536 | tf_op jit(solution)/shard_map/all_to_all | solution.py:506
  (73 shorter events, 24.2 us)
Async XLA Ops:
  0.6 10.1 %collective-permute-start.2 = (f32[128,256]{1,0:T(8,128)}, f32[128,256]{1,0:T(8,128)S(1)}, u32[]{:S(2)}, u32[]{:S(2)}) collective-permute-start(f32[128,256]{1,0:T(8,128)} %bitcast.7), channel_id=1, source_target_pairs={{0,3},{1,2},{2,1},{3,0},{4,7},{5,6},{6,5},{7,4},{8,11},{9,10},{10,... | collective-permute-start | bytes 393224 | tf_op jit(solution)/shard_map/ppermute | solution.py:493
  3.7 7.1 %collective-permute-start.1 = (f32[128,256]{1,0:T(8,128)}, f32[128,256]{1,0:T(8,128)S(1)}, u32[]{:S(2)}, u32[]{:S(2)}) collective-permute-start(f32[128,256]{1,0:T(8,128)} %bitcast.8), channel_id=1, source_target_pairs={{0,2},{1,3},{2,0},{3,1},{4,6},{5,7},{6,4},{7,5},{8,10},{9,11},{10,... | collective-permute-start | bytes 393224 | tf_op jit(solution)/shard_map/ppermute | solution.py:493
  5.3 5.5 %collective-permute-start = (f32[128,256]{1,0:T(8,128)}, f32[128,256]{1,0:T(8,128)S(1)}, u32[]{:S(2)}, u32[]{:S(2)}) collective-permute-start(f32[128,256]{1,0:T(8,128)} %bitcast.9), channel_id=1, source_target_pairs={{0,1},{1,0},{2,3},{3,2},{4,5},{5,4},{6,7},{7,6},{8,9},{9,8},{10,11... | collective-permute-start | bytes 393224 | tf_op jit(solution)/shard_map/ppermute | solution.py:493
  5.9 1.0 copy-start.3
  37.5 13.8 %collective-permute-start.5 = (f32[88,256]{1,0:T(8,128)S(1)}, f32[88,256]{1,0:T(8,128)S(1)}, u32[]{:S(2)}, u32[]{:S(2)}) collective-permute-start(f32[88,256]{1,0:T(8,128)S(1)} %shard_map.79.refs_0_), channel_id=1, source_target_pairs={{0,12},{4,0},{8,4},{12,8},{1,13},{5,1},{9,5},{13,9},{2,14},{6,2},{... | collective-permute-start | bytes 270344 | tf_op jit(solution)/shard_map/ppermute | solution.py:500
  44.7 7.5 %collective-permute-start.4 = (f32[88,256]{1,0:T(8,128)S(1)}, f32[88,256]{1,0:T(8,128)S(1)}, u32[]{:S(2)}, u32[]{:S(2)}) collective-permute-start(f32[88,256]{1,0:T(8,128)S(1)} %shard_map.79.refs_0_), channel_id=1, source_target_pairs={{0,8},{4,12},{8,0},{12,4},{1,9},{5,13},{9,1},{13,5},{2,10},{6,14},... | collective-permute-start | bytes 270344 | tf_op jit(solution)/shard_map/ppermute | solution.py:500
  45.7 7.0 %collective-permute-start.3 = (f32[88,256]{1,0:T(8,128)S(1)}, f32[88,256]{1,0:T(8,128)S(1)}, u32[]{:S(2)}, u32[]{:S(2)}) collective-permute-start(f32[88,256]{1,0:T(8,128)S(1)} %shard_map.79.refs_0_), channel_id=1, source_target_pairs={{0,4},{4,8},{8,12},{12,0},{1,5},{5,9},{9,13},{13,1},{2,6},{6,10},{... | collective-permute-start | bytes 270344 | tf_op jit(solution)/shard_map/ppermute | solution.py:500
  53.6 13.0 %all-to-all-start.1 = ((f32[16,32,256]{2,1,0:T(8,128)}), f32[16,32,256]{2,1,0:T(8,128)S(1)}, u32[]{:S(2)}, u32[]{:S(2)}) async-start(f32[16,32,256]{2,1,0:T(8,128)} %copy-done.4), calls=%async_computation.1 | async-start | bytes 1048576 | tf_op jit(solution)/shard_map/all_to_all | solution.py:506
  69.0 7.2 %collective-permute-start.6 = (f32[160,256]{1,0:T(8,128)S(1)}, f32[160,256]{1,0:T(8,128)S(1)}, u32[]{:S(2)}, u32[]{:S(2)}) collective-permute-start(f32[160,256]{1,0:T(8,128)S(1)} %get-tuple-element.66), channel_id=1, source_target_pairs={{0,1},{1,0},{2,3},{3,2},{4,5},{5,4},{6,7},{7,6},{8,9},{9,8},{10,11... | collective-permute-start | bytes 491528 | tf_op jit(solution)/shard_map/ppermute | solution.py:493
  74.5 5.7 %collective-permute-start.7 = (f32[160,256]{1,0:T(8,128)S(1)}, f32[160,256]{1,0:T(8,128)S(1)}, u32[]{:S(2)}, u32[]{:S(2)}) collective-permute-start(f32[160,256]{1,0:T(8,128)S(1)} %get-tuple-element.67), channel_id=1, source_target_pairs={{0,2},{1,3},{2,0},{3,1},{4,6},{5,7},{6,4},{7,5},{8,10},{9,11},{10,... | collective-permute-start | bytes 491528 | tf_op jit(solution)/shard_map/ppermute | solution.py:493
  75.1 8.8 %collective-permute-start.8 = (f32[160,256]{1,0:T(8,128)S(1)}, f32[160,256]{1,0:T(8,128)S(1)}, u32[]{:S(2)}, u32[]{:S(2)}) collective-permute-start(f32[160,256]{1,0:T(8,128)S(1)} %get-tuple-element.68), channel_id=1, source_target_pairs={{0,3},{1,2},{2,1},{3,0},{4,7},{5,6},{6,5},{7,4},{8,11},{9,10},{10,... | collective-permute-start | bytes 491528 | tf_op jit(solution)/shard_map/ppermute | solution.py:493
  85.0 15.8 %all-to-all-start.2 = ((f32[16,40,256]{2,1,0:T(8,128)}), f32[16,40,256]{2,1,0:T(8,128)S(1)}, u32[]{:S(2)}, u32[]{:S(2)}) async-start(f32[16,40,256]{2,1,0:T(8,128)} %copy-done), calls=%async_computation.2 | async-start | bytes 1310720 | tf_op jit(solution)/shard_map/all_to_all | solution.py:506
  88.6 6.0 %collective-permute-start.11 = (f32[128,256]{1,0:T(8,128)S(1)}, f32[128,256]{1,0:T(8,128)S(1)}, u32[]{:S(2)}, u32[]{:S(2)}) collective-permute-start(f32[128,256]{1,0:T(8,128)S(1)} %get-tuple-element.70.refs_6_), channel_id=1, source_target_pairs={{0,3},{1,2},{2,1},{3,0},{4,7},{5,6},{6,5},{7,4},{8,11},{9,10},{10,... | collective-permute-start | bytes 393224 | tf_op jit(solution)/shard_map/ppermute | solution.py:493
  89.3 7.1 %collective-permute-start.10 = (f32[128,256]{1,0:T(8,128)S(1)}, f32[128,256]{1,0:T(8,128)S(1)}, u32[]{:S(2)}, u32[]{:S(2)}) collective-permute-start(f32[128,256]{1,0:T(8,128)S(1)} %get-tuple-element.70.refs_6_), channel_id=1, source_target_pairs={{0,2},{1,3},{2,0},{3,1},{4,6},{5,7},{6,4},{7,5},{8,10},{9,11},{10,... | collective-permute-start | bytes 393224 | tf_op jit(solution)/shard_map/ppermute | solution.py:493
  90.1 6.9 %collective-permute-start.9 = (f32[128,256]{1,0:T(8,128)S(1)}, f32[128,256]{1,0:T(8,128)S(1)}, u32[]{:S(2)}, u32[]{:S(2)}) collective-permute-start(f32[128,256]{1,0:T(8,128)S(1)} %get-tuple-element.70.refs_6_), channel_id=1, source_target_pairs={{0,1},{1,0},{2,3},{3,2},{4,5},{5,4},{6,7},{7,6},{8,9},{9,8},{10,11... | collective-permute-start | bytes 393224 | tf_op jit(solution)/shard_map/ppermute | solution.py:493
  100.8 9.3 %collective-permute-start.14 = (f32[8,256]{1,0:T(8,128)S(1)}, f32[8,256]{1,0:T(8,128)S(1)}, u32[]{:S(2)}, u32[]{:S(2)}) collective-permute-start(f32[8,256]{1,0:T(8,128)S(1)} %get-tuple-element.80.refs_0_), channel_id=1, source_target_pairs={{0,12},{4,0},{8,4},{12,8},{1,13},{5,1},{9,5},{13,9},{2,14},{6,2},{... | collective-permute-start | bytes 24584 | tf_op jit(solution)/shard_map/ppermute | solution.py:500
  103.0 7.1 %collective-permute-start.13 = (f32[8,256]{1,0:T(8,128)S(1)}, f32[8,256]{1,0:T(8,128)S(1)}, u32[]{:S(2)}, u32[]{:S(2)}) collective-permute-start(f32[8,256]{1,0:T(8,128)S(1)} %get-tuple-element.80.refs_0_), channel_id=1, source_target_pairs={{0,8},{4,12},{8,0},{12,4},{1,9},{5,13},{9,1},{13,5},{2,10},{6,14},... | collective-permute-start | bytes 24584 | tf_op jit(solution)/shard_map/ppermute | solution.py:500
  104.1 6.0 %collective-permute-start.12 = (f32[8,256]{1,0:T(8,128)S(1)}, f32[8,256]{1,0:T(8,128)S(1)}, u32[]{:S(2)}, u32[]{:S(2)}) collective-permute-start(f32[8,256]{1,0:T(8,128)S(1)} %get-tuple-element.80.refs_0_), channel_id=1, source_target_pairs={{0,4},{4,8},{8,12},{12,0},{1,5},{5,9},{9,13},{13,1},{2,6},{6,10},{... | collective-permute-start | bytes 24584 | tf_op jit(solution)/shard_map/ppermute | solution.py:500
  110.2 7.4 %copy-start.2 = (f32[512,256]{1,0:T(8,128)S(1)}, f32[512,256]{1,0:T(8,128)}, u32[]{:S(2)}) copy-start(f32[512,256]{1,0:T(8,128)} %copy-done.1) | copy-start | bytes 1572868
  110.2 7.4 %copy-start.8 = (f32[128,256]{1,0:T(8,128)S(1)}, f32[128,256]{1,0:T(8,128)}, u32[]{:S(2)}) copy-start(f32[128,256]{1,0:T(8,128)} %copy-done.7) | copy-start | bytes 393220
  110.2 7.4 %copy-start.10 = (f32[128,256]{1,0:T(8,128)S(1)}, f32[128,256]{1,0:T(8,128)}, u32[]{:S(2)}) copy-start(f32[128,256]{1,0:T(8,128)} %copy-done.9) | copy-start | bytes 393220
  110.2 7.4 %copy-start.12 = (f32[128,256]{1,0:T(8,128)S(1)}, f32[128,256]{1,0:T(8,128)}, u32[]{:S(2)}) copy-start(f32[128,256]{1,0:T(8,128)} %copy-done.11) | copy-start | bytes 393220
  110.2 6.1 %collective-permute-start.17 = (f32[8,256]{1,0:T(8,128)S(1)}, f32[8,256]{1,0:T(8,128)S(1)}, u32[]{:S(2)}, u32[]{:S(2)}) collective-permute-start(f32[8,256]{1,0:T(8,128)S(1)} %shard_map.86.refs_0_), channel_id=1, source_target_pairs={{0,3},{1,2},{2,1},{3,0},{4,7},{5,6},{6,5},{7,4},{8,11},{9,10},{10,... | collective-permute-start | bytes 24584 | tf_op jit(solution)/shard_map/ppermute | solution.py:493
  115.0 2.5 %collective-permute-start.16 = (f32[8,256]{1,0:T(8,128)S(1)}, f32[8,256]{1,0:T(8,128)S(1)}, u32[]{:S(2)}, u32[]{:S(2)}) collective-permute-start(f32[8,256]{1,0:T(8,128)S(1)} %shard_map.86.refs_0_), channel_id=1, source_target_pairs={{0,2},{1,3},{2,0},{3,1},{4,6},{5,7},{6,4},{7,5},{8,10},{9,11},{10,... | collective-permute-start | bytes 24584 | tf_op jit(solution)/shard_map/ppermute | solution.py:493
  115.0 2.5 %collective-permute-start.15 = (f32[8,256]{1,0:T(8,128)S(1)}, f32[8,256]{1,0:T(8,128)S(1)}, u32[]{:S(2)}, u32[]{:S(2)}) collective-permute-start(f32[8,256]{1,0:T(8,128)S(1)} %shard_map.86.refs_0_), channel_id=1, source_target_pairs={{0,1},{1,0},{2,3},{3,2},{4,5},{5,4},{6,7},{7,6},{8,9},{9,8},{10,11... | collective-permute-start | bytes 24584 | tf_op jit(solution)/shard_map/ppermute | solution.py:493
  120.3 14.6 %all-to-all-start.3 = ((f32[16,32,256]{2,1,0:T(8,128)}), f32[16,32,256]{2,1,0:T(8,128)S(1)}, u32[]{:S(2)}, u32[]{:S(2)}) async-start(f32[16,32,256]{2,1,0:T(8,128)} %get-tuple-element.85), calls=%async_computation.3 | async-start | bytes 1048576 | tf_op jit(solution)/shard_map/all_to_all | solution.py:506
  123.9 2.2 %collective-permute-start.18 = (f32[160,256]{1,0:T(8,128)}, f32[160,256]{1,0:T(8,128)S(1)}, u32[]{:S(2)}, u32[]{:S(2)}) collective-permute-start(f32[160,256]{1,0:T(8,128)} %copy-done.16), channel_id=1, source_target_pairs={{0,1},{1,0},{2,3},{3,2},{4,5},{5,4},{6,7},{7,6},{8,9},{9,8},{10,11... | collective-permute-start | bytes 491528 | tf_op jit(solution)/shard_map/ppermute | solution.py:493
  124.0 5.6 %collective-permute-start.19 = (f32[160,256]{1,0:T(8,128)}, f32[160,256]{1,0:T(8,128)S(1)}, u32[]{:S(2)}, u32[]{:S(2)}) collective-permute-start(f32[160,256]{1,0:T(8,128)} %copy-done.15), channel_id=1, source_target_pairs={{0,2},{1,3},{2,0},{3,1},{4,6},{5,7},{6,4},{7,5},{8,10},{9,11},{10,... | collective-permute-start | bytes 491528 | tf_op jit(solution)/shard_map/ppermute | solution.py:493
  125.3 8.7 %collective-permute-start.20 = (f32[160,256]{1,0:T(8,128)S(1)}, f32[160,256]{1,0:T(8,128)S(1)}, u32[]{:S(2)}, u32[]{:S(2)}) collective-permute-start(f32[160,256]{1,0:T(8,128)S(1)} %get-tuple-element.89), channel_id=1, source_target_pairs={{0,3},{1,2},{2,1},{3,0},{4,7},{5,6},{6,5},{7,4},{8,11},{9,10},{10,... | collective-permute-start | bytes 491528 | tf_op jit(solution)/shard_map/ppermute | solution.py:493
  134.9 6.3 %collective-permute-start.23 = (f32[40,256]{1,0:T(8,128)S(1)}, f32[40,256]{1,0:T(8,128)S(1)}, u32[]{:S(2)}, u32[]{:S(2)}) collective-permute-start(f32[40,256]{1,0:T(8,128)S(1)} %shard_map.89.refs_0_), channel_id=1, source_target_pairs={{0,12},{4,0},{8,4},{12,8},{1,13},{5,1},{9,5},{13,9},{2,14},{6,2},{... | collective-permute-start | bytes 122888 | tf_op jit(solution)/shard_map/ppermute | solution.py:500
  136.3 6.8 %collective-permute-start.22 = (f32[40,256]{1,0:T(8,128)S(1)}, f32[40,256]{1,0:T(8,128)S(1)}, u32[]{:S(2)}, u32[]{:S(2)}) collective-permute-start(f32[40,256]{1,0:T(8,128)S(1)} %shard_map.89.refs_0_), channel_id=1, source_target_pairs={{0,8},{4,12},{8,0},{12,4},{1,9},{5,13},{9,1},{13,5},{2,10},{6,14},... | collective-permute-start | bytes 122888 | tf_op jit(solution)/shard_map/ppermute | solution.py:500
  140.7 5.0 %collective-permute-start.21 = (f32[40,256]{1,0:T(8,128)S(1)}, f32[40,256]{1,0:T(8,128)S(1)}, u32[]{:S(2)}, u32[]{:S(2)}) collective-permute-start(f32[40,256]{1,0:T(8,128)S(1)} %shard_map.89.refs_0_), channel_id=1, source_target_pairs={{0,4},{4,8},{8,12},{12,0},{1,5},{5,9},{9,13},{13,1},{2,6},{6,10},{... | collective-permute-start | bytes 122888 | tf_op jit(solution)/shard_map/ppermute | solution.py:500
  (12 other events, 9.0 us)

commit v8 on v7

--- a/solution.py
+++ b/solution.py
@@ -161,12 +161,9 @@
 
 
 def prepare_kernel(
-    top_ref, fx_in, ty_in, dens_in, weight_in, obs_in,
-    fx, bx, ty, dens_ref, weight_ref, obs_ref, decay_ref, gx_ref, gy_ref,
+    top_ref, fx_in, ty_in, dens_in, fx, bx, ty, dens_ref, decay_ref, gx_ref, gy_ref
 ):
     dens_ref[...] = dens_in[0]
-    weight_ref[...] = weight_in[0]
-    obs_ref[...] = obs_in[0]
     for place in range(4):
         table = fx_in[place]
         fx[place] = table
@@ -276,7 +273,7 @@
 
 
 def adjoint_kernel(
-    nxy, res_ref, decay_ref, gx_ref, gy_ref, power_ref, fx, bx, ty, o0, o1, o2, o3, z_ref, i_ref
+    nxy, res_ref, decay_ref, gx_ref, gy_ref, power_ref, fx, bx, ty, own_out, other_out, z_ref, i_ref
 ):
     rows = NX // nxy
     comp = comp_index()
@@ -310,10 +307,20 @@
         line = line + flip * table_times(bx[2, near, :], bx[3, near, :], o)
         i_ref[target * rows : (target + 1) * rows, :] = line
     i_ref[...] = times_turned(i_ref[...], ty[0], ty[1])
-    for step, out in enumerate((o0, o1, o2, o3)):
+    for step in range(4):
+        out = (own_out, other_out)[step % 2]
+        begin = (step // 2) * (QX + rows)
         other = jnp.bitwise_xor(comp, step)
-        out[:QX] = z_ref[pl.ds(pl.multiple_of(other * QX, QX), QX), :]
-        out[QX:] = i_ref[pl.ds(pl.multiple_of(other * rows, rows), rows), :]
+        out[begin : begin + QX] = z_ref[pl.ds(pl.multiple_of(other * QX, QX), QX), :]
+        out[begin + QX : begin + QX + rows] = i_ref[
+            pl.ds(pl.multiple_of(other * rows, rows), rows), :
+        ]
+
+
+def pair_kernel(own_ref, got_ref, near_ref, far_ref):
+    half = near_ref.shape[0]
+    near_ref[...] = own_ref[:half] + got_ref[:half]
+    far_ref[...] = own_ref[half:] + got_ref[half:]
 
 
 def share(grad, quad, image, weight, scratch, part):
@@ -338,10 +345,10 @@
 def gradient_kernel(nxy, nh, *refs):
     rows = NX // nxy
     part = rows // nh
-    pieces = refs[:4]
-    pull_ref, dens_ref, weight_ref = refs[4:7]
-    send_ref, grad_ref, line_ref, image_ref, scratch = refs[7:]
-    total = pieces[0][...] + pieces[1][...] + (pieces[2][...] + pieces[3][...])
+    pieces = refs[:2]
+    pull_ref, dens_ref, weight_ref = refs[2:5]
+    send_ref, grad_ref, line_ref, image_ref, scratch = refs[5:]
+    total = pieces[0][...] + pieces[1][...]
     data = total[:QX]
     line = total[QX:]
     dens = dens_ref[...]
@@ -405,10 +412,10 @@
 
 
 def second_gradient_kernel(
-    u0, u1, u2, u3, alpha_ref, base_ref, dens_ref, line_ref, grad_ref, image_ref, share_ref
+    u0, u1, alpha_ref, base_ref, dens_ref, line_ref, grad_ref, image_ref, share_ref
 ):
     alpha = alpha_ref[:1, :1]
-    total = u0[...] + u1[...] + (u2[...] + u3[...])
+    total = u0[...] + u1[...]
     dens = dens_ref[...]
     grad = base_ref[...] - alpha * total[:QX]
     quad = 1.0 / (dens * dens + 0.25)
@@ -494,6 +501,15 @@
     ]
 
 
+def flip(value, axis):
+    return lax.ppermute(value, axis, [(0, 1), (1, 0)])
+
+
+def gather_comps(value):
+    across = flip(value, "l")
+    return [value, flip(value, "k"), across, flip(across, "k")]
+
+
 def from_axis(values, axis):
     size = len(values)
     return [values[0]] + [
@@ -522,19 +538,19 @@
     program = Program()
     call = program.call
 
-    layers = from_comps([density[0]] * 4)
-    *tables, dens, weight_own, obs_own, decay, gx, gy = call(
+    near, across = flip(density[0], "k"), flip(density[0], "l")
+    *tables, dens, decay, gx, gy = call(
         prepare_kernel,
-        [
-            fx, fx, ty, (QX, NY), (part, NY), (part, NY), (KEPT, NY), (KEPT, NY), (KEPT, NY),
-        ],
-        layer_top, fx, ty, density, data_weight, observed, scalars=(0,),
-    )
+        [fx, fx, ty, (QX, NY), (KEPT, NY), (KEPT, NY), (KEPT, NY)],
+        layer_top, fx, ty, density, scalars=(0,),
+    )
+    layers = [near, across, flip(after(across, dens), "k")]
     factors = (decay, gx, gy)
-    program.hold(*tables, *factors, dens, weight_own, obs_own)
+    weight_own, obs_own = data_weight[0], observed[0]
+    program.hold(*tables, *factors, dens)
     message, full = call(
         bind(start_kernel, nxy), [(nxy, 2 * rows + 8, NY), (NX, NY)],
-        dens, *layers[1:], layer_top, *factors, *tables,
+        dens, *layers, layer_top, *factors, *tables,
         scratch=[(NX, NY)] * 2, scalars=(4,), far_out=(1,), sems=1,
     )
     got = exchange(message, XY)
@@ -552,11 +568,16 @@
     (power,) = call(bind(power_kernel, nxy * nh), [(KEPT, NY)], tops)
     program.hold(power)
     adjoint = lambda plane: call(
-        bind(adjoint_kernel, nxy), [(QX + rows, NY)] * 4,
+        bind(adjoint_kernel, nxy), [(2 * (QX + rows), NY)] * 2,
         plane.reshape(NX, NY), *factors, power, *tables,
         scratch=[(NX, NY), (4 * rows, NY)],
     )
-    pieces = from_comps(adjoint(got))
+
+    def reduce_comps(own, other):
+        near, far = call(pair_kernel, [(QX + rows, NY)] * 2, own, flip(other, "k"))
+        return near, flip(far, "l")
+
+    pieces = reduce_comps(*adjoint(got))
     message, grad, line, image = call(
         bind(gradient_kernel, nxy, nh),
         [(nxy, rows + 8, NY), (QX, NY), (rows, NY), (rows, NY)],
@@ -564,7 +585,7 @@
     )
     program.drop(pulled)
     program.hold(line, image)
-    grads = from_comps([grad] * 4)
+    grads = gather_comps(grad)
     got = after(exchange(message, XY), *grads)
     plane, shares = call(bind(part_kernel, nxy), [(NX, NY), (8, NY)], got)
     pieces = adjoint(plane)
@@ -575,15 +596,15 @@
         second_kernel, [(nxy, rows, NY), (QX, NY), (QX, NY), (8, 128)],
         *shares, dens, full, *grads, *factors, *tables, scratch=[(NX, NY)],
     )
-    program.alive = [weight_own, obs_own, weight, pred, line, image, dens, base, alpha]
+    program.alive = [weight, pred, line, image, dens, base, alpha]
     got = exchange(message, XY)
-    pieces = from_comps(after(pieces, message))
+    pieces = reduce_comps(*after(pieces, message))
     grad2, image2, half = call(
         second_gradient_kernel, [(QX, NY), (rows, NY), (8, NY)],
         *pieces, alpha, base, dens, line,
     )
     (parts,) = call(bind(sum_kernel, nxy), [(rows + 8, NY)], got, half)
-    program.alive = [weight_own, obs_own, pred, image, dens, alpha, grad2]
+    program.alive = [pred, image, dens, alpha, grad2]
     shares, image2 = call(
         bind(curvature_kernel, nh, part), [(nxy * 4, 128), (part, NY)],
         *from_axis([parts] * nh, "h"), image2, weight, scratch=[(rows, NY)],

time: 164 us -> 157 us (0.957)
  starting transfers between devices: 55.1 us -> 51.7 us
  local copies, waits for them, and re-layouts: 10 us -> 7.33 us
  waiting for transfers between devices: 41.1 us -> 38.6 us
    ppermute x15 -> x3, waiting for transfers between devices: 22.7 us -> 2.01 us  [from_comps(): lax.ppermute(values[step], COMP, [(i, i ^ step) for i in range(4)])]
    ppermute x15 -> x3, starting transfers between devices: 21.6 us -> 4.67 us  [from_comps(): lax.ppermute(values[step], COMP, [(i, i ^ step) for i in range(4)])]
    ppermute x0 -> x10, starting transfers between devices: none -> 15.2 us  [flip(): return lax.ppermute(value, axis, [(0, 1), (1, 0)])]
    ppermute x0 -> x10, waiting for transfers between devices: none -> 14.2 us  [flip(): return lax.ppermute(value, axis, [(0, 1), (1, 0)])]
    all_to_all x3, waiting for transfers between devices: 9.14 us -> 13.1 us  [exchange(): return lax.all_to_all(value, axes, 0, 0, tiled=True)]
    unnamed x34 -> x30, local copies, waits for them, and re-layouts: 10 us -> 7.33 us
    ppermute x9, starting transfers between devices: 22.4 us -> 20.7 us  [from_axis(): lax.ppermute(values[step], axis, [(i, (i + step) % size) for i in range(s...]
    pallas_call x15 -> x17, Pallas kernels: 16.2 us -> 17 us  [call(): pl.pallas_call(inner, out_shape=[jax.ShapeDtypeStruct(shape, dtype) for s...]
  transfers between devices with their start and end apart: 27 -> 25, of which waited for: 17 -> 14; matrix products, arithmetic and copies ran while one was open for 0% -> 0% of each run, Pallas kernels for 4% -> 5%
where the time goes in v8:
time: 157 us
  starting transfers between devices  51.7 us (33%)
  blocking collectives  40.4 us (26%)
  waiting for transfers between devices  38.6 us (25%)
  Pallas kernels  17 us (11%)
  local copies, waits for them, and re-layouts  7.33 us (5%)
    all_to_all x2, blocking collectives, exchange(): return lax.all_to_all(value, axes, 0, 0, tiled=True)  40.4 us
    ppermute x9, starting transfers between devices, from_axis(): lax.ppermute(values[step], axis, [(i, (i + step) % size) for i in range(s...  20.7 us
    pallas_call x17, Pallas kernels, call(): pl.pallas_call(inner, out_shape=[jax.ShapeDtypeStruct(shape, dtype) for s...  17 us
    ppermute x10, starting transfers between devices, flip(): return lax.ppermute(value, axis, [(0, 1), (1, 0)])  15.2 us
    ppermute x10, waiting for transfers between devices, flip(): return lax.ppermute(value, axis, [(0, 1), (1, 0)])  14.2 us
    all_to_all x3, waiting for transfers between devices, exchange(): return lax.all_to_all(value, axes, 0, 0, tiled=True)  13.1 us
    all_to_all x3, starting transfers between devices, exchange(): return lax.all_to_all(value, axes, 0, 0, tiled=True)  11.2 us
    ppermute x9, waiting for transfers between devices, from_axis(): lax.ppermute(values[step], axis, [(i, (i + step) % size) for i in range(s...  9.34 us
  transfers between devices with their start and end apart: 25, of which 14 were waited for; matrix products, arithmetic and copies ran while one was open for 0% of the time, Pallas kernels for 5%

profile of v8, /device:TPU:1, one launch (start us, length us, event | category | flops | bytes accessed | tf_op | source)
XLA Modules:
  0.0 156.6 jit_solution(11974026778287282104)
XLA Ops:
  0.6 2.5 %collective-permute-start.1 = (f32[128,256]{1,0:T(8,128)}, f32[128,256]{1,0:T(8,128)S(1)}, u32[]{:S(2)}, u32[]{:S(2)}) collective-permute-start(f32[128,256]{1,0:T(8,128)} %bitcast.9), channel_id=1, source_target_pairs={{0,2},{2,0},{1,3},{3,1},{4,6},{6,4},{5,7},{7,5},{8,10},{10,8},{9,1... | collective-permute-start | bytes 393224 | tf_op jit(solution)/shard_map/ppermute | solution.py:505
  10.1 3.0 %shard_map.78 = (f32[16,72,256]{2,1,0:T(8,128)S(1)}, f32[512,256]{1,0:T(8,128)S(1)}) custom-call(f32[128,256]{1,0:T(8,128)S(1)} %get-tuple-element.47.refs_0_.refs_9_.refs_10_.refs_7_.refs_8_.refs_3_.refs_4_, f32[128,256]{1,0:T(8,128)S(1)} %collective-permute-done.refs_1_, f32[128,256]{1,0:T(8,128)S(1)} %collective-permute-done.1.refs_2_, ...), custom_call_target="tpu_custom_call" | custom-call | tf_op jit(solution)/shard_map/pallas_call | solution.py:484
  14.0 24.0 %all_to_all.31.refs_0_ = f32[16,72,256]{2,1,0:T(8,128)S(1)} all-to-all(f32[16,72,256]{2,1,0:T(8,128)S(1)} %get-tuple-element.55), channel_id=1, replica_groups=mesh['x'=4,'y'=4,'h'=4,'l'=2,'k'=2] {'x','y'}, dimensions={0} | all-to-all | bytes 2359296 | tf_op jit(solution)/shard_map/all_to_all | solution.py:522
  38.1 5.0 %collective-permute-start.5 = (f32[88,256]{1,0:T(8,128)S(1)}, f32[88,256]{1,0:T(8,128)S(1)}, u32[]{:S(2)}, u32[]{:S(2)}) collective-permute-start(f32[88,256]{1,0:T(8,128)S(1)} %shard_map.79.refs_0_), channel_id=1, source_target_pairs={{0,12},{4,0},{8,4},{12,8},{1,13},{5,1},{9,5},{13,9},{2,14},{6,2},{... | collective-permute-start | bytes 270344 | tf_op jit(solution)/shard_map/ppermute | solution.py:516
  43.1 1.3 collective-permute-start.4
  44.4 1.9 %collective-permute-start.3 = (f32[88,256]{1,0:T(8,128)S(1)}, f32[88,256]{1,0:T(8,128)S(1)}, u32[]{:S(2)}, u32[]{:S(2)}) collective-permute-start(f32[88,256]{1,0:T(8,128)S(1)} %shard_map.79.refs_0_), channel_id=1, source_target_pairs={{0,4},{4,8},{8,12},{12,0},{1,5},{5,9},{9,13},{13,1},{2,6},{6,10},{... | collective-permute-start | bytes 270344 | tf_op jit(solution)/shard_map/ppermute | solution.py:516
  46.3 4.2 %collective-permute-done.4.refs_2_ = f32[88,256]{1,0:T(8,128)S(1)} collective-permute-done((f32[88,256]{1,0:T(8,128)S(1)}, f32[88,256]{1,0:T(8,128)S(1)}, u32[]{:S(2)}, u32[]{:S(2)}) %collective-permute-start.4) | collective-permute-done | bytes 90144 | tf_op jit(solution)/shard_map/ppermute | solution.py:516
  52.3 4.0 %all-to-all-start.1 = ((f32[16,32,256]{2,1,0:T(8,128)}), f32[16,32,256]{2,1,0:T(8,128)S(1)}, u32[]{:S(2)}, u32[]{:S(2)}) async-start(f32[16,32,256]{2,1,0:T(8,128)} %copy-done.4), calls=%async_computation.1 | async-start | bytes 1048576 | tf_op jit(solution)/shard_map/all_to_all | solution.py:522
  56.3 3.6 %shard_map.81.refs_4_.refs_12_.refs_10_.refs_13_.refs_18_ = f32[264,256]{1,0:T(8,128)S(1)} custom-call(f32[32,256]{1,0:T(8,128)S(1)} %get-tuple-element.57.refs_0_, bf16[4,256,256]{2,1,0:T(8,128)(2,1)S(1)} %get-tuple-element.52.refs_8_.refs_3_.refs_4_.refs_1_.refs_5_.refs_2_.refs_13_, ...), custom_call_target="tpu_custom_call" | custom-call | tf_op jit(solution)/shard_map/pallas_call | solution.py:484
  59.9 5.5 %all-to-all-done.1 = f32[16,32,256]{2,1,0:T(8,128)S(1)} async-done(((f32[16,32,256]{2,1,0:T(8,128)}), f32[16,32,256]{2,1,0:T(8,128)S(1)}, u32[]{:S(2)}, u32[]{:S(2)}) %all-to-all-start.1) | async-done | bytes 524320 | tf_op jit(solution)/shard_map/all_to_all | solution.py:522
  65.3 2.4 %shard_map.82 = (f32[320,256]{1,0:T(8,128)S(1)}, f32[320,256]{1,0:T(8,128)S(1)}) custom-call(f32[512,256]{1,0:T(8,128)S(1)} %bitcast.8, f32[264,256]{1,0:T(8,128)S(1)} %get-tuple-element.49.refs_5_.refs_6_.refs_7_.refs_4_.refs_1_.refs_8_.refs_10_, f32[264,256]{1,0:T(8,128)S(1)} %get-tuple-element.50.refs_6_.refs_7_.refs_8_.refs_5_.refs_2_.refs_9_.refs_11_, ...), custom_call_target="tpu_custom_call" | custom-call | tf_op jit(solution)/shard_map/pallas_call | solution.py:484
  67.8 5.1 %collective-permute-start.6 = (f32[320,256]{1,0:T(8,128)S(1)}, f32[320,256]{1,0:T(8,128)S(1)}, u32[]{:S(2)}, u32[]{:S(2)}) collective-permute-start(f32[320,256]{1,0:T(8,128)S(1)} %get-tuple-element.62), channel_id=1, source_target_pairs={{0,1},{1,0},{2,3},{3,2},{4,5},{5,4},{6,7},{7,6},{8,9},{9,8},{10,11... | collective-permute-start | bytes 983048 | tf_op jit(solution)/shard_map/ppermute | solution.py:505
  74.3 5.3 %collective-permute-done.7.refs_1_ = f32[160,256]{1,0:T(8,128)S(1)} collective-permute-done((f32[160,256]{1,0:T(8,128)S(1)}, f32[160,256]{1,0:T(8,128)S(1)}, u32[]{:S(2)}, u32[]{:S(2)}) %collective-permute-start.7) | collective-permute-done | bytes 163872 | tf_op jit(solution)/shard_map/ppermute | solution.py:505
  80.7 3.6 %all-to-all-start.2 = ((f32[16,40,256]{2,1,0:T(8,128)}), f32[16,40,256]{2,1,0:T(8,128)S(1)}, u32[]{:S(2)}, u32[]{:S(2)}) async-start(f32[16,40,256]{2,1,0:T(8,128)} %copy-done), calls=%async_computation.2 | async-start | bytes 1310720 | tf_op jit(solution)/shard_map/all_to_all | solution.py:522
  84.5 1.5 collective-permute-start.8
  86.0 2.3 %collective-permute-done.9.refs_8_ = f32[128,256]{1,0:T(8,128)S(1)} collective-permute-done((f32[128,256]{1,0:T(8,128)S(1)}, f32[128,256]{1,0:T(8,128)S(1)}, u32[]{:S(2)}, u32[]{:S(2)}) %collective-permute-start.9) | collective-permute-done | bytes 131104 | tf_op jit(solution)/shard_map/ppermute | solution.py:505
  88.2 2.4 %collective-permute-start.10 = (f32[128,256]{1,0:T(8,128)S(1)}, f32[128,256]{1,0:T(8,128)S(1)}, u32[]{:S(2)}, u32[]{:S(2)}) collective-permute-start(f32[128,256]{1,0:T(8,128)S(1)} %collective-permute-done.9.refs_8_), channel_id=1, source_target_pairs={{0,1},{1,0},{2,3},{3,2},{4,5},{5,4},{6,7},{7,6},{8,9},{9,8},{10,11... | collective-permute-start | bytes 393224 | tf_op jit(solution)/shard_map/ppermute | solution.py:505
  92.6 3.3 %all-to-all-done.2.refs_0_ = f32[16,40,256]{2,1,0:T(8,128)S(1)} async-done(((f32[16,40,256]{2,1,0:T(8,128)}), f32[16,40,256]{2,1,0:T(8,128)S(1)}, u32[]{:S(2)}, u32[]{:S(2)}) %all-to-all-start.2) | async-done | bytes 655392 | tf_op jit(solution)/shard_map/all_to_all | solution.py:522
  96.0 2.1 %collective-permute-start.13 = (f32[8,256]{1,0:T(8,128)S(1)}, f32[8,256]{1,0:T(8,128)S(1)}, u32[]{:S(2)}, u32[]{:S(2)}) collective-permute-start(f32[8,256]{1,0:T(8,128)S(1)} %get-tuple-element.74.refs_0_), channel_id=1, source_target_pairs={{0,12},{4,0},{8,4},{12,8},{1,13},{5,1},{9,5},{13,9},{2,14},{6,2},{... | collective-permute-start | bytes 24584 | tf_op jit(solution)/shard_map/ppermute | solution.py:516
  98.1 1.7 %collective-permute-start.12 = (f32[8,256]{1,0:T(8,128)S(1)}, f32[8,256]{1,0:T(8,128)S(1)}, u32[]{:S(2)}, u32[]{:S(2)}) collective-permute-start(f32[8,256]{1,0:T(8,128)S(1)} %get-tuple-element.74.refs_0_), channel_id=1, source_target_pairs={{0,8},{4,12},{8,0},{12,4},{1,9},{5,13},{9,1},{13,5},{2,10},{6,14},... | collective-permute-start | bytes 24584 | tf_op jit(solution)/shard_map/ppermute | solution.py:516
  99.8 2.3 %collective-permute-start.11 = (f32[8,256]{1,0:T(8,128)S(1)}, f32[8,256]{1,0:T(8,128)S(1)}, u32[]{:S(2)}, u32[]{:S(2)}) collective-permute-start(f32[8,256]{1,0:T(8,128)S(1)} %get-tuple-element.74.refs_0_), channel_id=1, source_target_pairs={{0,4},{4,8},{8,12},{12,0},{1,5},{5,9},{9,13},{13,1},{2,6},{6,10},{... | collective-permute-start | bytes 24584 | tf_op jit(solution)/shard_map/ppermute | solution.py:516
  102.1 3.2 %shard_map.86 = (f32[320,256]{1,0:T(8,128)S(1)}, f32[320,256]{1,0:T(8,128)}) custom-call(f32[512,256]{1,0:T(8,128)S(1)} %get-tuple-element.71.refs_0_, f32[264,256]{1,0:T(8,128)S(1)} %get-tuple-element.49.refs_5_.refs_6_.refs_7_.refs_4_.refs_1_.refs_8_.refs_10_, f32[264,256]{1,0:T(8,128)S(1)} %get-tuple-element.50.refs_6_.refs_7_.refs_8_.refs_5_.refs_2_.refs_9_.refs_11_, ...), custom_call_target="tpu_custom_call" | custom-call | tf_op jit(solution)/shard_map/pallas_call | solution.py:484
  105.3 4.2 %collective-permute-start.16 = (f32[8,256]{1,0:T(8,128)S(1)}, f32[8,256]{1,0:T(8,128)S(1)}, u32[]{:S(2)}, u32[]{:S(2)}) collective-permute-start(f32[8,256]{1,0:T(8,128)S(1)} %shard_map.87.refs_0_), channel_id=1, source_target_pairs={{0,3},{1,2},{2,1},{3,0},{4,7},{5,6},{6,5},{7,4},{8,11},{9,10},{10,... | collective-permute-start | bytes 24584 | tf_op jit(solution)/shard_map/ppermute | solution.py:500
  112.0 2.7 %shard_map.88 = (f32[16,32,256]{2,1,0:T(8,128)}, f32[128,256]{1,0:T(8,128)S(1)}, f32[128,256]{1,0:T(8,128)S(1)}, f32[8,128]{1,0:T(8,128)S(1)}) custom-call(f32[8,256]{1,0:T(8,128)S(1)} %shard_map.87.refs_0_, f32[8,256]{1,0:T(8,128)S(1)} %collective-permute-done.14.refs_1_, f32[8,256]{1,0:T(8,128)S(1)} %collective-permute-done.15.refs_2_, ...), custom_call_target="tpu_custom_call" | custom-call | tf_op jit(solution)/shard_map/pallas_call | solution.py:484
  115.0 3.6 %all-to-all-start.3 = ((f32[16,32,256]{2,1,0:T(8,128)}), f32[16,32,256]{2,1,0:T(8,128)S(1)}, u32[]{:S(2)}, u32[]{:S(2)}) async-start(f32[16,32,256]{2,1,0:T(8,128)} %get-tuple-element.79), calls=%async_computation.3 | async-start | bytes 1048576 | tf_op jit(solution)/shard_map/all_to_all | solution.py:522
  119.8 4.3 %collective-permute-done.18.refs_1_ = f32[160,256]{1,0:T(8,128)S(1)} collective-permute-done((f32[160,256]{1,0:T(8,128)S(1)}, f32[160,256]{1,0:T(8,128)S(1)}, u32[]{:S(2)}, u32[]{:S(2)}) %collective-permute-start.18) | collective-permute-done | bytes 163872 | tf_op jit(solution)/shard_map/ppermute | solution.py:505
  124.4 4.3 %all-to-all-done.3.refs_0_ = f32[16,32,256]{2,1,0:T(8,128)S(1)} async-done(((f32[16,32,256]{2,1,0:T(8,128)}), f32[16,32,256]{2,1,0:T(8,128)S(1)}, u32[]{:S(2)}, u32[]{:S(2)}) %all-to-all-start.3) | async-done | bytes 524320 | tf_op jit(solution)/shard_map/all_to_all | solution.py:522
  128.7 1.9 %collective-permute-start.21 = (f32[40,256]{1,0:T(8,128)S(1)}, f32[40,256]{1,0:T(8,128)S(1)}, u32[]{:S(2)}, u32[]{:S(2)}) collective-permute-start(f32[40,256]{1,0:T(8,128)S(1)} %shard_map.91.refs_0_), channel_id=1, source_target_pairs={{0,12},{4,0},{8,4},{12,8},{1,13},{5,1},{9,5},{13,9},{2,14},{6,2},{... | collective-permute-start | bytes 122888 | tf_op jit(solution)/shard_map/ppermute | solution.py:516
  130.6 3.2 %collective-permute-start.20 = (f32[40,256]{1,0:T(8,128)S(1)}, f32[40,256]{1,0:T(8,128)S(1)}, u32[]{:S(2)}, u32[]{:S(2)}) collective-permute-start(f32[40,256]{1,0:T(8,128)S(1)} %shard_map.91.refs_0_), channel_id=1, source_target_pairs={{0,8},{4,12},{8,0},{12,4},{1,9},{5,13},{9,1},{13,5},{2,10},{6,14},... | collective-permute-start | bytes 122888 | tf_op jit(solution)/shard_map/ppermute | solution.py:516
  135.0 2.4 %collective-permute-done.20.refs_2_ = f32[40,256]{1,0:T(8,128)S(1)} collective-permute-done((f32[40,256]{1,0:T(8,128)S(1)}, f32[40,256]{1,0:T(8,128)S(1)}, u32[]{:S(2)}, u32[]{:S(2)}) %collective-permute-start.20) | collective-permute-done | bytes 40992 | tf_op jit(solution)/shard_map/ppermute | solution.py:516
  137.4 1.9 %collective-permute-done.19.refs_1_ = f32[40,256]{1,0:T(8,128)S(1)} collective-permute-done((f32[40,256]{1,0:T(8,128)S(1)}, f32[40,256]{1,0:T(8,128)S(1)}, u32[]{:S(2)}, u32[]{:S(2)}) %collective-permute-start.19) | collective-permute-done | bytes 40992 | tf_op jit(solution)/shard_map/ppermute | solution.py:516
  139.4 16.4 %all_to_all.32 = f32[64,1,128]{2,1,0:T(1,128)S(1)} all-to-all(f32[64,1,128]{2,1,0:T(1,128)S(1)} %bitcast.16), channel_id=1, replica_groups=mesh['x'=4,'y'=4,'h'=4,'l'=2,'k'=2] {'x','y','l','k'}, dimensions={0} | all-to-all | bytes 65536 | tf_op jit(solution)/shard_map/all_to_all | solution.py:522
  (67 shorter events, 19.8 us)
Async XLA Ops:
  0.6 7.5 %collective-permute-start.1 = (f32[128,256]{1,0:T(8,128)}, f32[128,256]{1,0:T(8,128)S(1)}, u32[]{:S(2)}, u32[]{:S(2)}) collective-permute-start(f32[128,256]{1,0:T(8,128)} %bitcast.9), channel_id=1, source_target_pairs={{0,2},{2,0},{1,3},{3,1},{4,6},{6,4},{5,7},{7,5},{8,10},{10,8},{9,1... | collective-permute-start | bytes 393224 | tf_op jit(solution)/shard_map/ppermute | solution.py:505
  3.2 5.9 %collective-permute-start = (f32[128,256]{1,0:T(8,128)}, f32[128,256]{1,0:T(8,128)S(1)}, u32[]{:S(2)}, u32[]{:S(2)}) collective-permute-start(f32[128,256]{1,0:T(8,128)} %bitcast.10), channel_id=1, source_target_pairs={{0,1},{1,0},{2,3},{3,2},{4,5},{5,4},{6,7},{7,6},{8,9},{9,8},{10,11... | collective-permute-start | bytes 393224 | tf_op jit(solution)/shard_map/ppermute | solution.py:505
  4.8 1.0 copy-start.3
  8.2 1.9 %collective-permute-start.2 = (f32[128,256]{1,0:T(8,128)S(1)}, f32[128,256]{1,0:T(8,128)S(1)}, u32[]{:S(2)}, u32[]{:S(2)}) collective-permute-start(f32[128,256]{1,0:T(8,128)S(1)} %collective-permute-done.1.refs_2_), channel_id=1, source_target_pairs={{0,1},{1,0},{2,3},{3,2},{4,5},{5,4},{6,7},{7,6},{8,9},{9,8},{10,11... | collective-permute-start | bytes 393224 | tf_op jit(solution)/shard_map/ppermute | solution.py:505
  14.0 24.0 %copy-start.13 = (f32[1,8,256]{2,1,0:T(8,128)S(1)}, f32[1,8,256]{2,1,0:T(8,128)}, u32[]{:S(2)}) copy-start(f32[1,8,256]{2,1,0:T(8,128)} %param.8) | copy-start | bytes 24580
  14.0 24.0 %copy-start.14 = (f32[1,8,256]{2,1,0:T(8,128)S(1)}, f32[1,8,256]{2,1,0:T(8,128)}, u32[]{:S(2)}) copy-start(f32[1,8,256]{2,1,0:T(8,128)} %param.7) | copy-start | bytes 24580
  38.1 8.3 %collective-permute-start.5 = (f32[88,256]{1,0:T(8,128)S(1)}, f32[88,256]{1,0:T(8,128)S(1)}, u32[]{:S(2)}, u32[]{:S(2)}) collective-permute-start(f32[88,256]{1,0:T(8,128)S(1)} %shard_map.79.refs_0_), channel_id=1, source_target_pairs={{0,12},{4,0},{8,4},{12,8},{1,13},{5,1},{9,5},{13,9},{2,14},{6,2},{... | collective-permute-start | bytes 270344 | tf_op jit(solution)/shard_map/ppermute | solution.py:516
  43.1 7.5 %collective-permute-start.4 = (f32[88,256]{1,0:T(8,128)S(1)}, f32[88,256]{1,0:T(8,128)S(1)}, u32[]{:S(2)}, u32[]{:S(2)}) collective-permute-start(f32[88,256]{1,0:T(8,128)S(1)} %shard_map.79.refs_0_), channel_id=1, source_target_pairs={{0,8},{4,12},{8,0},{12,4},{1,9},{5,13},{9,1},{13,5},{2,10},{6,14},... | collective-permute-start | bytes 270344 | tf_op jit(solution)/shard_map/ppermute | solution.py:516
  44.4 7.0 %collective-permute-start.3 = (f32[88,256]{1,0:T(8,128)S(1)}, f32[88,256]{1,0:T(8,128)S(1)}, u32[]{:S(2)}, u32[]{:S(2)}) collective-permute-start(f32[88,256]{1,0:T(8,128)S(1)} %shard_map.79.refs_0_), channel_id=1, source_target_pairs={{0,4},{4,8},{8,12},{12,0},{1,5},{5,9},{9,13},{13,1},{2,6},{6,10},{... | collective-permute-start | bytes 270344 | tf_op jit(solution)/shard_map/ppermute | solution.py:516
  52.3 13.1 %all-to-all-start.1 = ((f32[16,32,256]{2,1,0:T(8,128)}), f32[16,32,256]{2,1,0:T(8,128)S(1)}, u32[]{:S(2)}, u32[]{:S(2)}) async-start(f32[16,32,256]{2,1,0:T(8,128)} %copy-done.4), calls=%async_computation.1 | async-start | bytes 1048576 | tf_op jit(solution)/shard_map/all_to_all | solution.py:522
  67.8 6.4 %collective-permute-start.6 = (f32[320,256]{1,0:T(8,128)S(1)}, f32[320,256]{1,0:T(8,128)S(1)}, u32[]{:S(2)}, u32[]{:S(2)}) collective-permute-start(f32[320,256]{1,0:T(8,128)S(1)} %get-tuple-element.62), channel_id=1, source_target_pairs={{0,1},{1,0},{2,3},{3,2},{4,5},{5,4},{6,7},{7,6},{8,9},{9,8},{10,11... | collective-permute-start | bytes 983048 | tf_op jit(solution)/shard_map/ppermute | solution.py:505
  74.2 5.5 %collective-permute-start.7 = (f32[160,256]{1,0:T(8,128)S(1)}, f32[160,256]{1,0:T(8,128)S(1)}, u32[]{:S(2)}, u32[]{:S(2)}) collective-permute-start(f32[160,256]{1,0:T(8,128)S(1)} %get-tuple-element.64), channel_id=1, source_target_pairs={{0,2},{2,0},{1,3},{3,1},{4,6},{6,4},{5,7},{7,5},{8,10},{10,8},{9,1... | collective-permute-start | bytes 491528 | tf_op jit(solution)/shard_map/ppermute | solution.py:505
  80.7 15.2 %all-to-all-start.2 = ((f32[16,40,256]{2,1,0:T(8,128)}), f32[16,40,256]{2,1,0:T(8,128)S(1)}, u32[]{:S(2)}, u32[]{:S(2)}) async-start(f32[16,40,256]{2,1,0:T(8,128)} %copy-done), calls=%async_computation.2 | async-start | bytes 1310720 | tf_op jit(solution)/shard_map/all_to_all | solution.py:522
  84.3 3.9 %collective-permute-start.9 = (f32[128,256]{1,0:T(8,128)S(1)}, f32[128,256]{1,0:T(8,128)S(1)}, u32[]{:S(2)}, u32[]{:S(2)}) collective-permute-start(f32[128,256]{1,0:T(8,128)S(1)} %get-tuple-element.66.refs_6_), channel_id=1, source_target_pairs={{0,2},{2,0},{1,3},{3,1},{4,6},{6,4},{5,7},{7,5},{8,10},{10,8},{9,1... | collective-permute-start | bytes 393224 | tf_op jit(solution)/shard_map/ppermute | solution.py:505
  84.5 6.8 %collective-permute-start.8 = (f32[128,256]{1,0:T(8,128)S(1)}, f32[128,256]{1,0:T(8,128)S(1)}, u32[]{:S(2)}, u32[]{:S(2)}) collective-permute-start(f32[128,256]{1,0:T(8,128)S(1)} %get-tuple-element.66.refs_6_), channel_id=1, source_target_pairs={{0,1},{1,0},{2,3},{3,2},{4,5},{5,4},{6,7},{7,6},{8,9},{9,8},{10,11... | collective-permute-start | bytes 393224 | tf_op jit(solution)/shard_map/ppermute | solution.py:505
  88.2 3.7 %collective-permute-start.10 = (f32[128,256]{1,0:T(8,128)S(1)}, f32[128,256]{1,0:T(8,128)S(1)}, u32[]{:S(2)}, u32[]{:S(2)}) collective-permute-start(f32[128,256]{1,0:T(8,128)S(1)} %collective-permute-done.9.refs_8_), channel_id=1, source_target_pairs={{0,1},{1,0},{2,3},{3,2},{4,5},{5,4},{6,7},{7,6},{8,9},{9,8},{10,11... | collective-permute-start | bytes 393224 | tf_op jit(solution)/shard_map/ppermute | solution.py:505
  96.0 9.3 %collective-permute-start.13 = (f32[8,256]{1,0:T(8,128)S(1)}, f32[8,256]{1,0:T(8,128)S(1)}, u32[]{:S(2)}, u32[]{:S(2)}) collective-permute-start(f32[8,256]{1,0:T(8,128)S(1)} %get-tuple-element.74.refs_0_), channel_id=1, source_target_pairs={{0,12},{4,0},{8,4},{12,8},{1,13},{5,1},{9,5},{13,9},{2,14},{6,2},{... | collective-permute-start | bytes 24584 | tf_op jit(solution)/shard_map/ppermute | solution.py:516
  98.1 7.1 %collective-permute-start.12 = (f32[8,256]{1,0:T(8,128)S(1)}, f32[8,256]{1,0:T(8,128)S(1)}, u32[]{:S(2)}, u32[]{:S(2)}) collective-permute-start(f32[8,256]{1,0:T(8,128)S(1)} %get-tuple-element.74.refs_0_), channel_id=1, source_target_pairs={{0,8},{4,12},{8,0},{12,4},{1,9},{5,13},{9,1},{13,5},{2,10},{6,14},... | collective-permute-start | bytes 24584 | tf_op jit(solution)/shard_map/ppermute | solution.py:516
  99.8 5.4 %collective-permute-start.11 = (f32[8,256]{1,0:T(8,128)S(1)}, f32[8,256]{1,0:T(8,128)S(1)}, u32[]{:S(2)}, u32[]{:S(2)}) collective-permute-start(f32[8,256]{1,0:T(8,128)S(1)} %get-tuple-element.74.refs_0_), channel_id=1, source_target_pairs={{0,4},{4,8},{8,12},{12,0},{1,5},{5,9},{9,13},{13,1},{2,6},{6,10},{... | collective-permute-start | bytes 24584 | tf_op jit(solution)/shard_map/ppermute | solution.py:516
  105.3 6.7 %copy-start.2 = (f32[512,256]{1,0:T(8,128)S(1)}, f32[512,256]{1,0:T(8,128)}, u32[]{:S(2)}) copy-start(f32[512,256]{1,0:T(8,128)} %copy-done.1) | copy-start | bytes 1572868
  105.3 6.7 %copy-start.8 = (f32[128,256]{1,0:T(8,128)S(1)}, f32[128,256]{1,0:T(8,128)}, u32[]{:S(2)}) copy-start(f32[128,256]{1,0:T(8,128)} %copy-done.7) | copy-start | bytes 393220
  105.3 6.7 %copy-start.10 = (f32[128,256]{1,0:T(8,128)S(1)}, f32[128,256]{1,0:T(8,128)}, u32[]{:S(2)}) copy-start(f32[128,256]{1,0:T(8,128)} %copy-done.9) | copy-start | bytes 393220
  105.3 6.7 %copy-start.12 = (f32[128,256]{1,0:T(8,128)S(1)}, f32[128,256]{1,0:T(8,128)}, u32[]{:S(2)}) copy-start(f32[128,256]{1,0:T(8,128)} %copy-done.11) | copy-start | bytes 393220
  105.3 5.9 %collective-permute-start.16 = (f32[8,256]{1,0:T(8,128)S(1)}, f32[8,256]{1,0:T(8,128)S(1)}, u32[]{:S(2)}, u32[]{:S(2)}) collective-permute-start(f32[8,256]{1,0:T(8,128)S(1)} %shard_map.87.refs_0_), channel_id=1, source_target_pairs={{0,3},{1,2},{2,1},{3,0},{4,7},{5,6},{6,5},{7,4},{8,11},{9,10},{10,... | collective-permute-start | bytes 24584 | tf_op jit(solution)/shard_map/ppermute | solution.py:500
  109.5 2.5 %collective-permute-start.15 = (f32[8,256]{1,0:T(8,128)S(1)}, f32[8,256]{1,0:T(8,128)S(1)}, u32[]{:S(2)}, u32[]{:S(2)}) collective-permute-start(f32[8,256]{1,0:T(8,128)S(1)} %shard_map.87.refs_0_), channel_id=1, source_target_pairs={{0,2},{1,3},{2,0},{3,1},{4,6},{5,7},{6,4},{7,5},{8,10},{9,11},{10,... | collective-permute-start | bytes 24584 | tf_op jit(solution)/shard_map/ppermute | solution.py:500
  109.8 2.2 %collective-permute-start.14 = (f32[8,256]{1,0:T(8,128)S(1)}, f32[8,256]{1,0:T(8,128)S(1)}, u32[]{:S(2)}, u32[]{:S(2)}) collective-permute-start(f32[8,256]{1,0:T(8,128)S(1)} %shard_map.87.refs_0_), channel_id=1, source_target_pairs={{0,1},{1,0},{2,3},{3,2},{4,5},{5,4},{6,7},{7,6},{8,9},{9,8},{10,11... | collective-permute-start | bytes 24584 | tf_op jit(solution)/shard_map/ppermute | solution.py:500
  114.8 3.8 %collective-permute-start.17 = (f32[320,256]{1,0:T(8,128)}, f32[320,256]{1,0:T(8,128)S(1)}, u32[]{:S(2)}, u32[]{:S(2)}) collective-permute-start(f32[320,256]{1,0:T(8,128)} %get-tuple-element.81), channel_id=1, source_target_pairs={{0,1},{1,0},{2,3},{3,2},{4,5},{5,4},{6,7},{7,6},{8,9},{9,8},{10,11... | collective-permute-start | bytes 983048 | tf_op jit(solution)/shard_map/ppermute | solution.py:505
  115.0 13.7 %all-to-all-start.3 = ((f32[16,32,256]{2,1,0:T(8,128)}), f32[16,32,256]{2,1,0:T(8,128)S(1)}, u32[]{:S(2)}, u32[]{:S(2)}) async-start(f32[16,32,256]{2,1,0:T(8,128)} %get-tuple-element.79), calls=%async_computation.3 | async-start | bytes 1048576 | tf_op jit(solution)/shard_map/all_to_all | solution.py:522
  118.6 5.6 %collective-permute-start.18 = (f32[160,256]{1,0:T(8,128)S(1)}, f32[160,256]{1,0:T(8,128)S(1)}, u32[]{:S(2)}, u32[]{:S(2)}) collective-permute-start(f32[160,256]{1,0:T(8,128)S(1)} %get-tuple-element.86), channel_id=1, source_target_pairs={{0,2},{2,0},{1,3},{3,1},{4,6},{6,4},{5,7},{7,5},{8,10},{10,8},{9,1... | collective-permute-start | bytes 491528 | tf_op jit(solution)/shard_map/ppermute | solution.py:505
  128.7 6.3 %collective-permute-start.21 = (f32[40,256]{1,0:T(8,128)S(1)}, f32[40,256]{1,0:T(8,128)S(1)}, u32[]{:S(2)}, u32[]{:S(2)}) collective-permute-start(f32[40,256]{1,0:T(8,128)S(1)} %shard_map.91.refs_0_), channel_id=1, source_target_pairs={{0,12},{4,0},{8,4},{12,8},{1,13},{5,1},{9,5},{13,9},{2,14},{6,2},{... | collective-permute-start | bytes 122888 | tf_op jit(solution)/shard_map/ppermute | solution.py:516
  130.6 6.8 %collective-permute-start.20 = (f32[40,256]{1,0:T(8,128)S(1)}, f32[40,256]{1,0:T(8,128)S(1)}, u32[]{:S(2)}, u32[]{:S(2)}) collective-permute-start(f32[40,256]{1,0:T(8,128)S(1)} %shard_map.91.refs_0_), channel_id=1, source_target_pairs={{0,8},{4,12},{8,0},{12,4},{1,9},{5,13},{9,1},{13,5},{2,10},{6,14},... | collective-permute-start | bytes 122888 | tf_op jit(solution)/shard_map/ppermute | solution.py:516
  133.9 5.4 %collective-permute-start.19 = (f32[40,256]{1,0:T(8,128)S(1)}, f32[40,256]{1,0:T(8,128)S(1)}, u32[]{:S(2)}, u32[]{:S(2)}) collective-permute-start(f32[40,256]{1,0:T(8,128)S(1)} %shard_map.91.refs_0_), channel_id=1, source_target_pairs={{0,4},{4,8},{8,12},{12,0},{1,5},{5,9},{9,13},{13,1},{2,6},{6,10},{... | collective-permute-start | bytes 122888 | tf_op jit(solution)/shard_map/ppermute | solution.py:516
  (8 other events, 6.3 us)

commit v9 on v8

--- a/solution.py
+++ b/solution.py
@@ -588,10 +588,9 @@
     grads = gather_comps(grad)
     got = after(exchange(message, XY), *grads)
     plane, shares = call(bind(part_kernel, nxy), [(NX, NY), (8, NY)], got)
-    pieces = adjoint(plane)
-    shares = after(from_axis([shares] * nh, "h"), *pieces)
-    (shares,) = call(add_kernel, [(8, NY)], *shares)
-    shares = from_comps([shares] * 4)
+    (shares,) = call(add_kernel, [(8, NY)], *from_axis([shares] * nh, "h"))
+    pieces = adjoint(after(plane, shares))
+    shares = after(from_comps([shares] * 4), *pieces)
     message, dens, base, alpha = call(
         second_kernel, [(nxy, rows, NY), (QX, NY), (QX, NY), (8, 128)],
         *shares, dens, full, *grads, *factors, *tables, scratch=[(NX, NY)],

time: 157 us -> 158 us (level)
    ppermute x9, waiting for transfers between devices: 9.34 us -> 11.9 us  [from_axis(): lax.ppermute(values[step], axis, [(i, (i + step) % size) for i in range(s...]
    ppermute x3, waiting for transfers between devices: 2.01 us -> 0.01 us  [from_comps(): lax.ppermute(values[step], COMP, [(i, i ^ step) for i in range(4)])]
  transfers between devices with their start and end apart: 25 -> 25, of which waited for: 14 -> 13; matrix products, arithmetic and copies ran while one was open for 0% -> 0% of each run, Pallas kernels for 5% -> 5%
where the time goes in v9:
time: 158 us; the launch traced here: 157 us
  starting transfers between devices  52.4 us (33%)
  blocking collectives  39.6 us (25%)
  waiting for transfers between devices  39 us (25%)
  Pallas kernels  17 us (11%)
  local copies, waits for them, and re-layouts  7.32 us (5%)
    all_to_all x2, blocking collectives, exchange(): return lax.all_to_all(value, axes, 0, 0, tiled=True)  39.6 us
    ppermute x9, starting transfers between devices, from_axis(): lax.ppermute(values[step], axis, [(i, (i + step) % size) for i in range(s...  20.6 us
    pallas_call x17, Pallas kernels, call(): pl.pallas_call(inner, out_shape=[jax.ShapeDtypeStruct(shape, dtype) for s...  17 us
    ppermute x10, starting transfers between devices, flip(): return lax.ppermute(value, axis, [(0, 1), (1, 0)])  15.3 us
    ppermute x10, waiting for transfers between devices, flip(): return lax.ppermute(value, axis, [(0, 1), (1, 0)])  14.1 us
    all_to_all x3, waiting for transfers between devices, exchange(): return lax.all_to_all(value, axes, 0, 0, tiled=True)  13 us
    ppermute x9, waiting for transfers between devices, from_axis(): lax.ppermute(values[step], axis, [(i, (i + step) % size) for i in range(s...  11.9 us
    all_to_all x3, starting transfers between devices, exchange(): return lax.all_to_all(value, axes, 0, 0, tiled=True)  11.2 us
  transfers between devices with their start and end apart: 25, of which 13 were waited for; matrix products, arithmetic and copies ran while one was open for 0% of the time, Pallas kernels for 5%

profile of v9, /device:TPU:1, one launch (start us, length us, event | category | flops | bytes accessed | tf_op | source)
XLA Modules:
  0.0 156.9 jit_solution(11917741083508471151)
XLA Ops:
  0.6 2.5 %collective-permute-start.1 = (f32[128,256]{1,0:T(8,128)}, f32[128,256]{1,0:T(8,128)S(1)}, u32[]{:S(2)}, u32[]{:S(2)}) collective-permute-start(f32[128,256]{1,0:T(8,128)} %bitcast.9), channel_id=1, source_target_pairs={{0,2},{2,0},{1,3},{3,1},{4,6},{6,4},{5,7},{7,5},{8,10},{10,8},{9,1... | collective-permute-start | bytes 393224 | tf_op jit(solution)/shard_map/ppermute | solution.py:505
  10.1 3.0 %shard_map.78 = (f32[16,72,256]{2,1,0:T(8,128)S(1)}, f32[512,256]{1,0:T(8,128)S(1)}) custom-call(f32[128,256]{1,0:T(8,128)S(1)} %get-tuple-element.48.refs_0_.refs_9_.refs_10_.refs_7_.refs_8_.refs_3_.refs_4_, f32[128,256]{1,0:T(8,128)S(1)} %collective-permute-done.refs_1_, f32[128,256]{1,0:T(8,128)S(1)} %collective-permute-done.1.refs_2_, ...), custom_call_target="tpu_custom_call" | custom-call | tf_op jit(solution)/shard_map/pallas_call | solution.py:484
  14.0 24.0 %all_to_all.31.refs_0_ = f32[16,72,256]{2,1,0:T(8,128)S(1)} all-to-all(f32[16,72,256]{2,1,0:T(8,128)S(1)} %get-tuple-element.56), channel_id=1, replica_groups=mesh['x'=4,'y'=4,'h'=4,'l'=2,'k'=2] {'x','y'}, dimensions={0} | all-to-all | bytes 2359296 | tf_op jit(solution)/shard_map/all_to_all | solution.py:522
  38.1 5.0 %collective-permute-start.5 = (f32[88,256]{1,0:T(8,128)S(1)}, f32[88,256]{1,0:T(8,128)S(1)}, u32[]{:S(2)}, u32[]{:S(2)}) collective-permute-start(f32[88,256]{1,0:T(8,128)S(1)} %shard_map.79.refs_0_), channel_id=1, source_target_pairs={{0,12},{4,0},{8,4},{12,8},{1,13},{5,1},{9,5},{13,9},{2,14},{6,2},{... | collective-permute-start | bytes 270344 | tf_op jit(solution)/shard_map/ppermute | solution.py:516
  44.4 1.9 %collective-permute-start.3 = (f32[88,256]{1,0:T(8,128)S(1)}, f32[88,256]{1,0:T(8,128)S(1)}, u32[]{:S(2)}, u32[]{:S(2)}) collective-permute-start(f32[88,256]{1,0:T(8,128)S(1)} %shard_map.79.refs_0_), channel_id=1, source_target_pairs={{0,4},{4,8},{8,12},{12,0},{1,5},{5,9},{9,13},{13,1},{2,6},{6,10},{... | collective-permute-start | bytes 270344 | tf_op jit(solution)/shard_map/ppermute | solution.py:516
  46.3 4.2 %collective-permute-done.4.refs_2_ = f32[88,256]{1,0:T(8,128)S(1)} collective-permute-done((f32[88,256]{1,0:T(8,128)S(1)}, f32[88,256]{1,0:T(8,128)S(1)}, u32[]{:S(2)}, u32[]{:S(2)}) %collective-permute-start.4) | collective-permute-done | bytes 90144 | tf_op jit(solution)/shard_map/ppermute | solution.py:516
  52.3 4.0 %all-to-all-start.1 = ((f32[16,32,256]{2,1,0:T(8,128)}), f32[16,32,256]{2,1,0:T(8,128)S(1)}, u32[]{:S(2)}, u32[]{:S(2)}) async-start(f32[16,32,256]{2,1,0:T(8,128)} %copy-done.4), calls=%async_computation.1 | async-start | bytes 1048576 | tf_op jit(solution)/shard_map/all_to_all | solution.py:522
  56.3 3.6 %shard_map.81.refs_4_.refs_12_.refs_10_.refs_13_.refs_18_ = f32[264,256]{1,0:T(8,128)S(1)} custom-call(f32[32,256]{1,0:T(8,128)S(1)} %get-tuple-element.58.refs_0_, bf16[4,256,256]{2,1,0:T(8,128)(2,1)S(1)} %get-tuple-element.53.refs_8_.refs_3_.refs_4_.refs_1_.refs_5_.refs_2_.refs_13_, ...), custom_call_target="tpu_custom_call" | custom-call | tf_op jit(solution)/shard_map/pallas_call | solution.py:484
  59.9 5.5 %all-to-all-done.1 = f32[16,32,256]{2,1,0:T(8,128)S(1)} async-done(((f32[16,32,256]{2,1,0:T(8,128)}), f32[16,32,256]{2,1,0:T(8,128)S(1)}, u32[]{:S(2)}, u32[]{:S(2)}) %all-to-all-start.1) | async-done | bytes 524320 | tf_op jit(solution)/shard_map/all_to_all | solution.py:522
  65.3 2.4 %shard_map.82 = (f32[320,256]{1,0:T(8,128)S(1)}, f32[320,256]{1,0:T(8,128)S(1)}) custom-call(f32[512,256]{1,0:T(8,128)S(1)} %bitcast.8, f32[264,256]{1,0:T(8,128)S(1)} %get-tuple-element.50.refs_5_.refs_6_.refs_7_.refs_4_.refs_1_.refs_8_.refs_10_, f32[264,256]{1,0:T(8,128)S(1)} %get-tuple-element.51.refs_6_.refs_7_.refs_8_.refs_5_.refs_2_.refs_9_.refs_11_, ...), custom_call_target="tpu_custom_call" | custom-call | tf_op jit(solution)/shard_map/pallas_call | solution.py:484
  67.8 5.1 %collective-permute-start.6 = (f32[320,256]{1,0:T(8,128)S(1)}, f32[320,256]{1,0:T(8,128)S(1)}, u32[]{:S(2)}, u32[]{:S(2)}) collective-permute-start(f32[320,256]{1,0:T(8,128)S(1)} %get-tuple-element.63), channel_id=1, source_target_pairs={{0,1},{1,0},{2,3},{3,2},{4,5},{5,4},{6,7},{7,6},{8,9},{9,8},{10,11... | collective-permute-start | bytes 983048 | tf_op jit(solution)/shard_map/ppermute | solution.py:505
  74.3 5.3 %collective-permute-done.7.refs_1_ = f32[160,256]{1,0:T(8,128)S(1)} collective-permute-done((f32[160,256]{1,0:T(8,128)S(1)}, f32[160,256]{1,0:T(8,128)S(1)}, u32[]{:S(2)}, u32[]{:S(2)}) %collective-permute-start.7) | collective-permute-done | bytes 163872 | tf_op jit(solution)/shard_map/ppermute | solution.py:505
  80.7 3.6 %all-to-all-start.2 = ((f32[16,40,256]{2,1,0:T(8,128)}), f32[16,40,256]{2,1,0:T(8,128)S(1)}, u32[]{:S(2)}, u32[]{:S(2)}) async-start(f32[16,40,256]{2,1,0:T(8,128)} %copy-done), calls=%async_computation.2 | async-start | bytes 1310720 | tf_op jit(solution)/shard_map/all_to_all | solution.py:522
  84.5 1.5 collective-permute-start.8
  86.0 2.3 %collective-permute-done.9.refs_8_ = f32[128,256]{1,0:T(8,128)S(1)} collective-permute-done((f32[128,256]{1,0:T(8,128)S(1)}, f32[128,256]{1,0:T(8,128)S(1)}, u32[]{:S(2)}, u32[]{:S(2)}) %collective-permute-start.9) | collective-permute-done | bytes 131104 | tf_op jit(solution)/shard_map/ppermute | solution.py:505
  88.2 2.4 %collective-permute-start.10 = (f32[128,256]{1,0:T(8,128)S(1)}, f32[128,256]{1,0:T(8,128)S(1)}, u32[]{:S(2)}, u32[]{:S(2)}) collective-permute-start(f32[128,256]{1,0:T(8,128)S(1)} %collective-permute-done.9.refs_8_), channel_id=1, source_target_pairs={{0,1},{1,0},{2,3},{3,2},{4,5},{5,4},{6,7},{7,6},{8,9},{9,8},{10,11... | collective-permute-start | bytes 393224 | tf_op jit(solution)/shard_map/ppermute | solution.py:505
  92.6 3.3 %all-to-all-done.2.refs_0_ = f32[16,40,256]{2,1,0:T(8,128)S(1)} async-done(((f32[16,40,256]{2,1,0:T(8,128)}), f32[16,40,256]{2,1,0:T(8,128)S(1)}, u32[]{:S(2)}, u32[]{:S(2)}) %all-to-all-start.2) | async-done | bytes 655392 | tf_op jit(solution)/shard_map/all_to_all | solution.py:522
  96.0 2.1 %collective-permute-start.13 = (f32[8,256]{1,0:T(8,128)S(1)}, f32[8,256]{1,0:T(8,128)S(1)}, u32[]{:S(2)}, u32[]{:S(2)}) collective-permute-start(f32[8,256]{1,0:T(8,128)S(1)} %get-tuple-element.71.refs_0_), channel_id=1, source_target_pairs={{0,12},{4,0},{8,4},{12,8},{1,13},{5,1},{9,5},{13,9},{2,14},{6,2},{... | collective-permute-start | bytes 24584 | tf_op jit(solution)/shard_map/ppermute | solution.py:516
  98.1 1.7 %collective-permute-start.12 = (f32[8,256]{1,0:T(8,128)S(1)}, f32[8,256]{1,0:T(8,128)S(1)}, u32[]{:S(2)}, u32[]{:S(2)}) collective-permute-start(f32[8,256]{1,0:T(8,128)S(1)} %get-tuple-element.71.refs_0_), channel_id=1, source_target_pairs={{0,8},{4,12},{8,0},{12,4},{1,9},{5,13},{9,1},{13,5},{2,10},{6,14},... | collective-permute-start | bytes 24584 | tf_op jit(solution)/shard_map/ppermute | solution.py:516
  99.8 2.3 %collective-permute-start.11 = (f32[8,256]{1,0:T(8,128)S(1)}, f32[8,256]{1,0:T(8,128)S(1)}, u32[]{:S(2)}, u32[]{:S(2)}) collective-permute-start(f32[8,256]{1,0:T(8,128)S(1)} %get-tuple-element.71.refs_0_), channel_id=1, source_target_pairs={{0,4},{4,8},{8,12},{12,0},{1,5},{5,9},{9,13},{13,1},{2,6},{6,10},{... | collective-permute-start | bytes 24584 | tf_op jit(solution)/shard_map/ppermute | solution.py:516
  102.1 2.5 %collective-permute-done.12.refs_2_ = f32[8,256]{1,0:T(8,128)S(1)} collective-permute-done((f32[8,256]{1,0:T(8,128)S(1)}, f32[8,256]{1,0:T(8,128)S(1)}, u32[]{:S(2)}, u32[]{:S(2)}) %collective-permute-start.12) | collective-permute-done | bytes 8224 | tf_op jit(solution)/shard_map/ppermute | solution.py:516
  104.6 4.9 %collective-permute-start.16 = (f32[8,256]{1,0:T(8,128)S(1)}, f32[8,256]{1,0:T(8,128)S(1)}, u32[]{:S(2)}, u32[]{:S(2)}) collective-permute-start(f32[8,256]{1,0:T(8,128)S(1)} %shard_map.86.refs_0_), channel_id=1, source_target_pairs={{0,3},{1,2},{2,1},{3,0},{4,7},{5,6},{6,5},{7,4},{8,11},{9,10},{10,... | collective-permute-start | bytes 24584 | tf_op jit(solution)/shard_map/ppermute | solution.py:500
  109.9 3.2 %shard_map.87 = (f32[320,256]{1,0:T(8,128)S(1)}, f32[320,256]{1,0:T(8,128)}) custom-call(f32[512,256]{1,0:T(8,128)S(1)} %get-tuple-element.73.refs_0_, f32[264,256]{1,0:T(8,128)S(1)} %get-tuple-element.50.refs_5_.refs_6_.refs_7_.refs_4_.refs_1_.refs_8_.refs_10_, f32[264,256]{1,0:T(8,128)S(1)} %get-tuple-element.51.refs_6_.refs_7_.refs_8_.refs_5_.refs_2_.refs_9_.refs_11_, ...), custom_call_target="tpu_custom_call" | custom-call | tf_op jit(solution)/shard_map/pallas_call | solution.py:484
  113.2 2.7 %shard_map.88 = (f32[16,32,256]{2,1,0:T(8,128)}, f32[128,256]{1,0:T(8,128)S(1)}, f32[128,256]{1,0:T(8,128)S(1)}, f32[8,128]{1,0:T(8,128)S(1)}) custom-call(f32[8,256]{1,0:T(8,128)S(1)} %shard_map.86.refs_0_, f32[8,256]{1,0:T(8,128)S(1)} %collective-permute-done.14.refs_1_, f32[8,256]{1,0:T(8,128)S(1)} %collective-permute-done.15.refs_2_, ...), custom_call_target="tpu_custom_call" | custom-call | tf_op jit(solution)/shard_map/pallas_call | solution.py:484
  116.1 3.6 %all-to-all-start.3 = ((f32[16,32,256]{2,1,0:T(8,128)}), f32[16,32,256]{2,1,0:T(8,128)S(1)}, u32[]{:S(2)}, u32[]{:S(2)}) async-start(f32[16,32,256]{2,1,0:T(8,128)} %get-tuple-element.81), calls=%async_computation.3 | async-start | bytes 1048576 | tf_op jit(solution)/shard_map/all_to_all | solution.py:522
  121.1 4.3 %collective-permute-done.18.refs_1_ = f32[160,256]{1,0:T(8,128)S(1)} collective-permute-done((f32[160,256]{1,0:T(8,128)S(1)}, f32[160,256]{1,0:T(8,128)S(1)}, u32[]{:S(2)}, u32[]{:S(2)}) %collective-permute-start.18) | collective-permute-done | bytes 163872 | tf_op jit(solution)/shard_map/ppermute | solution.py:505
  125.6 4.2 %all-to-all-done.3.refs_0_ = f32[16,32,256]{2,1,0:T(8,128)S(1)} async-done(((f32[16,32,256]{2,1,0:T(8,128)}), f32[16,32,256]{2,1,0:T(8,128)S(1)}, u32[]{:S(2)}, u32[]{:S(2)}) %all-to-all-start.3) | async-done | bytes 524320 | tf_op jit(solution)/shard_map/all_to_all | solution.py:522
  129.8 2.4 %collective-permute-start.21 = (f32[40,256]{1,0:T(8,128)S(1)}, f32[40,256]{1,0:T(8,128)S(1)}, u32[]{:S(2)}, u32[]{:S(2)}) collective-permute-start(f32[40,256]{1,0:T(8,128)S(1)} %shard_map.91.refs_0_), channel_id=1, source_target_pairs={{0,12},{4,0},{8,4},{12,8},{1,13},{5,1},{9,5},{13,9},{2,14},{6,2},{... | collective-permute-start | bytes 122888 | tf_op jit(solution)/shard_map/ppermute | solution.py:516
  132.2 2.6 %collective-permute-start.20 = (f32[40,256]{1,0:T(8,128)S(1)}, f32[40,256]{1,0:T(8,128)S(1)}, u32[]{:S(2)}, u32[]{:S(2)}) collective-permute-start(f32[40,256]{1,0:T(8,128)S(1)} %shard_map.91.refs_0_), channel_id=1, source_target_pairs={{0,8},{4,12},{8,0},{12,4},{1,9},{5,13},{9,1},{13,5},{2,10},{6,14},... | collective-permute-start | bytes 122888 | tf_op jit(solution)/shard_map/ppermute | solution.py:516
  136.1 2.9 %collective-permute-done.20.refs_2_ = f32[40,256]{1,0:T(8,128)S(1)} collective-permute-done((f32[40,256]{1,0:T(8,128)S(1)}, f32[40,256]{1,0:T(8,128)S(1)}, u32[]{:S(2)}, u32[]{:S(2)}) %collective-permute-start.20) | collective-permute-done | bytes 40992 | tf_op jit(solution)/shard_map/ppermute | solution.py:516
  139.0 1.4 collective-permute-done.19.refs_1_
  140.5 15.6 %all_to_all.32 = f32[64,1,128]{2,1,0:T(1,128)S(1)} all-to-all(f32[64,1,128]{2,1,0:T(1,128)S(1)} %bitcast.16), channel_id=1, replica_groups=mesh['x'=4,'y'=4,'h'=4,'l'=2,'k'=2] {'x','y','l','k'}, dimensions={0} | all-to-all | bytes 65536 | tf_op jit(solution)/shard_map/all_to_all | solution.py:522
  (67 shorter events, 19.3 us)
Async XLA Ops:
  0.6 7.5 %collective-permute-start.1 = (f32[128,256]{1,0:T(8,128)}, f32[128,256]{1,0:T(8,128)S(1)}, u32[]{:S(2)}, u32[]{:S(2)}) collective-permute-start(f32[128,256]{1,0:T(8,128)} %bitcast.9), channel_id=1, source_target_pairs={{0,2},{2,0},{1,3},{3,1},{4,6},{6,4},{5,7},{7,5},{8,10},{10,8},{9,1... | collective-permute-start | bytes 393224 | tf_op jit(solution)/shard_map/ppermute | solution.py:505
  3.2 5.9 %collective-permute-start = (f32[128,256]{1,0:T(8,128)}, f32[128,256]{1,0:T(8,128)S(1)}, u32[]{:S(2)}, u32[]{:S(2)}) collective-permute-start(f32[128,256]{1,0:T(8,128)} %bitcast.10), channel_id=1, source_target_pairs={{0,1},{1,0},{2,3},{3,2},{4,5},{5,4},{6,7},{7,6},{8,9},{9,8},{10,11... | collective-permute-start | bytes 393224 | tf_op jit(solution)/shard_map/ppermute | solution.py:505
  4.8 1.0 copy-start.3
  8.2 1.9 %collective-permute-start.2 = (f32[128,256]{1,0:T(8,128)S(1)}, f32[128,256]{1,0:T(8,128)S(1)}, u32[]{:S(2)}, u32[]{:S(2)}) collective-permute-start(f32[128,256]{1,0:T(8,128)S(1)} %collective-permute-done.1.refs_2_), channel_id=1, source_target_pairs={{0,1},{1,0},{2,3},{3,2},{4,5},{5,4},{6,7},{7,6},{8,9},{9,8},{10,11... | collective-permute-start | bytes 393224 | tf_op jit(solution)/shard_map/ppermute | solution.py:505
  14.0 24.0 %copy-start.13 = (f32[1,8,256]{2,1,0:T(8,128)S(1)}, f32[1,8,256]{2,1,0:T(8,128)}, u32[]{:S(2)}) copy-start(f32[1,8,256]{2,1,0:T(8,128)} %param.8) | copy-start | bytes 24580
  14.0 24.0 %copy-start.14 = (f32[1,8,256]{2,1,0:T(8,128)S(1)}, f32[1,8,256]{2,1,0:T(8,128)}, u32[]{:S(2)}) copy-start(f32[1,8,256]{2,1,0:T(8,128)} %param.7) | copy-start | bytes 24580
  38.1 8.3 %collective-permute-start.5 = (f32[88,256]{1,0:T(8,128)S(1)}, f32[88,256]{1,0:T(8,128)S(1)}, u32[]{:S(2)}, u32[]{:S(2)}) collective-permute-start(f32[88,256]{1,0:T(8,128)S(1)} %shard_map.79.refs_0_), channel_id=1, source_target_pairs={{0,12},{4,0},{8,4},{12,8},{1,13},{5,1},{9,5},{13,9},{2,14},{6,2},{... | collective-permute-start | bytes 270344 | tf_op jit(solution)/shard_map/ppermute | solution.py:516
  43.1 7.5 %collective-permute-start.4 = (f32[88,256]{1,0:T(8,128)S(1)}, f32[88,256]{1,0:T(8,128)S(1)}, u32[]{:S(2)}, u32[]{:S(2)}) collective-permute-start(f32[88,256]{1,0:T(8,128)S(1)} %shard_map.79.refs_0_), channel_id=1, source_target_pairs={{0,8},{4,12},{8,0},{12,4},{1,9},{5,13},{9,1},{13,5},{2,10},{6,14},... | collective-permute-start | bytes 270344 | tf_op jit(solution)/shard_map/ppermute | solution.py:516
  44.4 7.0 %collective-permute-start.3 = (f32[88,256]{1,0:T(8,128)S(1)}, f32[88,256]{1,0:T(8,128)S(1)}, u32[]{:S(2)}, u32[]{:S(2)}) collective-permute-start(f32[88,256]{1,0:T(8,128)S(1)} %shard_map.79.refs_0_), channel_id=1, source_target_pairs={{0,4},{4,8},{8,12},{12,0},{1,5},{5,9},{9,13},{13,1},{2,6},{6,10},{... | collective-permute-start | bytes 270344 | tf_op jit(solution)/shard_map/ppermute | solution.py:516
  52.3 13.1 %all-to-all-start.1 = ((f32[16,32,256]{2,1,0:T(8,128)}), f32[16,32,256]{2,1,0:T(8,128)S(1)}, u32[]{:S(2)}, u32[]{:S(2)}) async-start(f32[16,32,256]{2,1,0:T(8,128)} %copy-done.4), calls=%async_computation.1 | async-start | bytes 1048576 | tf_op jit(solution)/shard_map/all_to_all | solution.py:522
  67.8 6.4 %collective-permute-start.6 = (f32[320,256]{1,0:T(8,128)S(1)}, f32[320,256]{1,0:T(8,128)S(1)}, u32[]{:S(2)}, u32[]{:S(2)}) collective-permute-start(f32[320,256]{1,0:T(8,128)S(1)} %get-tuple-element.63), channel_id=1, source_target_pairs={{0,1},{1,0},{2,3},{3,2},{4,5},{5,4},{6,7},{7,6},{8,9},{9,8},{10,11... | collective-permute-start | bytes 983048 | tf_op jit(solution)/shard_map/ppermute | solution.py:505
  74.2 5.5 %collective-permute-start.7 = (f32[160,256]{1,0:T(8,128)S(1)}, f32[160,256]{1,0:T(8,128)S(1)}, u32[]{:S(2)}, u32[]{:S(2)}) collective-permute-start(f32[160,256]{1,0:T(8,128)S(1)} %get-tuple-element.65), channel_id=1, source_target_pairs={{0,2},{2,0},{1,3},{3,1},{4,6},{6,4},{5,7},{7,5},{8,10},{10,8},{9,1... | collective-permute-start | bytes 491528 | tf_op jit(solution)/shard_map/ppermute | solution.py:505
  80.7 15.2 %all-to-all-start.2 = ((f32[16,40,256]{2,1,0:T(8,128)}), f32[16,40,256]{2,1,0:T(8,128)S(1)}, u32[]{:S(2)}, u32[]{:S(2)}) async-start(f32[16,40,256]{2,1,0:T(8,128)} %copy-done), calls=%async_computation.2 | async-start | bytes 1310720 | tf_op jit(solution)/shard_map/all_to_all | solution.py:522
  84.3 3.9 %collective-permute-start.9 = (f32[128,256]{1,0:T(8,128)S(1)}, f32[128,256]{1,0:T(8,128)S(1)}, u32[]{:S(2)}, u32[]{:S(2)}) collective-permute-start(f32[128,256]{1,0:T(8,128)S(1)} %get-tuple-element.67.refs_6_), channel_id=1, source_target_pairs={{0,2},{2,0},{1,3},{3,1},{4,6},{6,4},{5,7},{7,5},{8,10},{10,8},{9,1... | collective-permute-start | bytes 393224 | tf_op jit(solution)/shard_map/ppermute | solution.py:505
  84.5 6.8 %collective-permute-start.8 = (f32[128,256]{1,0:T(8,128)S(1)}, f32[128,256]{1,0:T(8,128)S(1)}, u32[]{:S(2)}, u32[]{:S(2)}) collective-permute-start(f32[128,256]{1,0:T(8,128)S(1)} %get-tuple-element.67.refs_6_), channel_id=1, source_target_pairs={{0,1},{1,0},{2,3},{3,2},{4,5},{5,4},{6,7},{7,6},{8,9},{9,8},{10,11... | collective-permute-start | bytes 393224 | tf_op jit(solution)/shard_map/ppermute | solution.py:505
  88.2 3.7 %collective-permute-start.10 = (f32[128,256]{1,0:T(8,128)S(1)}, f32[128,256]{1,0:T(8,128)S(1)}, u32[]{:S(2)}, u32[]{:S(2)}) collective-permute-start(f32[128,256]{1,0:T(8,128)S(1)} %collective-permute-done.9.refs_8_), channel_id=1, source_target_pairs={{0,1},{1,0},{2,3},{3,2},{4,5},{5,4},{6,7},{7,6},{8,9},{9,8},{10,11... | collective-permute-start | bytes 393224 | tf_op jit(solution)/shard_map/ppermute | solution.py:505
  96.0 6.1 %collective-permute-start.13 = (f32[8,256]{1,0:T(8,128)S(1)}, f32[8,256]{1,0:T(8,128)S(1)}, u32[]{:S(2)}, u32[]{:S(2)}) collective-permute-start(f32[8,256]{1,0:T(8,128)S(1)} %get-tuple-element.71.refs_0_), channel_id=1, source_target_pairs={{0,12},{4,0},{8,4},{12,8},{1,13},{5,1},{9,5},{13,9},{2,14},{6,2},{... | collective-permute-start | bytes 24584 | tf_op jit(solution)/shard_map/ppermute | solution.py:516
  98.1 6.4 %collective-permute-start.12 = (f32[8,256]{1,0:T(8,128)S(1)}, f32[8,256]{1,0:T(8,128)S(1)}, u32[]{:S(2)}, u32[]{:S(2)}) collective-permute-start(f32[8,256]{1,0:T(8,128)S(1)} %get-tuple-element.71.refs_0_), channel_id=1, source_target_pairs={{0,8},{4,12},{8,0},{12,4},{1,9},{5,13},{9,1},{13,5},{2,10},{6,14},... | collective-permute-start | bytes 24584 | tf_op jit(solution)/shard_map/ppermute | solution.py:516
  99.8 4.7 %collective-permute-start.11 = (f32[8,256]{1,0:T(8,128)S(1)}, f32[8,256]{1,0:T(8,128)S(1)}, u32[]{:S(2)}, u32[]{:S(2)}) collective-permute-start(f32[8,256]{1,0:T(8,128)S(1)} %get-tuple-element.71.refs_0_), channel_id=1, source_target_pairs={{0,4},{4,8},{8,12},{12,0},{1,5},{5,9},{9,13},{13,1},{2,6},{6,10},{... | collective-permute-start | bytes 24584 | tf_op jit(solution)/shard_map/ppermute | solution.py:516
  104.6 8.5 %collective-permute-start.16 = (f32[8,256]{1,0:T(8,128)S(1)}, f32[8,256]{1,0:T(8,128)S(1)}, u32[]{:S(2)}, u32[]{:S(2)}) collective-permute-start(f32[8,256]{1,0:T(8,128)S(1)} %shard_map.86.refs_0_), channel_id=1, source_target_pairs={{0,3},{1,2},{2,1},{3,0},{4,7},{5,6},{6,5},{7,4},{8,11},{9,10},{10,... | collective-permute-start | bytes 24584 | tf_op jit(solution)/shard_map/ppermute | solution.py:500
  109.4 3.7 %collective-permute-start.15 = (f32[8,256]{1,0:T(8,128)S(1)}, f32[8,256]{1,0:T(8,128)S(1)}, u32[]{:S(2)}, u32[]{:S(2)}) collective-permute-start(f32[8,256]{1,0:T(8,128)S(1)} %shard_map.86.refs_0_), channel_id=1, source_target_pairs={{0,2},{1,3},{2,0},{3,1},{4,6},{5,7},{6,4},{7,5},{8,10},{9,11},{10,... | collective-permute-start | bytes 24584 | tf_op jit(solution)/shard_map/ppermute | solution.py:500
  109.7 3.5 %collective-permute-start.14 = (f32[8,256]{1,0:T(8,128)S(1)}, f32[8,256]{1,0:T(8,128)S(1)}, u32[]{:S(2)}, u32[]{:S(2)}) collective-permute-start(f32[8,256]{1,0:T(8,128)S(1)} %shard_map.86.refs_0_), channel_id=1, source_target_pairs={{0,1},{1,0},{2,3},{3,2},{4,5},{5,4},{6,7},{7,6},{8,9},{9,8},{10,11... | collective-permute-start | bytes 24584 | tf_op jit(solution)/shard_map/ppermute | solution.py:500
  109.9 3.2 %copy-start.2 = (f32[512,256]{1,0:T(8,128)S(1)}, f32[512,256]{1,0:T(8,128)}, u32[]{:S(2)}) copy-start(f32[512,256]{1,0:T(8,128)} %copy-done.1) | copy-start | bytes 1572868
  109.9 3.2 %copy-start.8 = (f32[128,256]{1,0:T(8,128)S(1)}, f32[128,256]{1,0:T(8,128)}, u32[]{:S(2)}) copy-start(f32[128,256]{1,0:T(8,128)} %copy-done.7) | copy-start | bytes 393220
  109.9 3.2 %copy-start.10 = (f32[128,256]{1,0:T(8,128)S(1)}, f32[128,256]{1,0:T(8,128)}, u32[]{:S(2)}) copy-start(f32[128,256]{1,0:T(8,128)} %copy-done.9) | copy-start | bytes 393220
  109.9 3.2 %copy-start.12 = (f32[128,256]{1,0:T(8,128)S(1)}, f32[128,256]{1,0:T(8,128)}, u32[]{:S(2)}) copy-start(f32[128,256]{1,0:T(8,128)} %copy-done.11) | copy-start | bytes 393220
  115.9 3.8 %collective-permute-start.17 = (f32[320,256]{1,0:T(8,128)}, f32[320,256]{1,0:T(8,128)S(1)}, u32[]{:S(2)}, u32[]{:S(2)}) collective-permute-start(f32[320,256]{1,0:T(8,128)} %get-tuple-element.83), channel_id=1, source_target_pairs={{0,1},{1,0},{2,3},{3,2},{4,5},{5,4},{6,7},{7,6},{8,9},{9,8},{10,11... | collective-permute-start | bytes 983048 | tf_op jit(solution)/shard_map/ppermute | solution.py:505
  116.1 13.7 %all-to-all-start.3 = ((f32[16,32,256]{2,1,0:T(8,128)}), f32[16,32,256]{2,1,0:T(8,128)S(1)}, u32[]{:S(2)}, u32[]{:S(2)}) async-start(f32[16,32,256]{2,1,0:T(8,128)} %get-tuple-element.81), calls=%async_computation.3 | async-start | bytes 1048576 | tf_op jit(solution)/shard_map/all_to_all | solution.py:522
  119.8 5.6 %collective-permute-start.18 = (f32[160,256]{1,0:T(8,128)S(1)}, f32[160,256]{1,0:T(8,128)S(1)}, u32[]{:S(2)}, u32[]{:S(2)}) collective-permute-start(f32[160,256]{1,0:T(8,128)S(1)} %get-tuple-element.88), channel_id=1, source_target_pairs={{0,2},{2,0},{1,3},{3,1},{4,6},{6,4},{5,7},{7,5},{8,10},{10,8},{9,1... | collective-permute-start | bytes 491528 | tf_op jit(solution)/shard_map/ppermute | solution.py:505
  129.8 6.2 %collective-permute-start.21 = (f32[40,256]{1,0:T(8,128)S(1)}, f32[40,256]{1,0:T(8,128)S(1)}, u32[]{:S(2)}, u32[]{:S(2)}) collective-permute-start(f32[40,256]{1,0:T(8,128)S(1)} %shard_map.91.refs_0_), channel_id=1, source_target_pairs={{0,12},{4,0},{8,4},{12,8},{1,13},{5,1},{9,5},{13,9},{2,14},{6,2},{... | collective-permute-start | bytes 122888 | tf_op jit(solution)/shard_map/ppermute | solution.py:516
  132.2 6.8 %collective-permute-start.20 = (f32[40,256]{1,0:T(8,128)S(1)}, f32[40,256]{1,0:T(8,128)S(1)}, u32[]{:S(2)}, u32[]{:S(2)}) collective-permute-start(f32[40,256]{1,0:T(8,128)S(1)} %shard_map.91.refs_0_), channel_id=1, source_target_pairs={{0,8},{4,12},{8,0},{12,4},{1,9},{5,13},{9,1},{13,5},{2,10},{6,14},... | collective-permute-start | bytes 122888 | tf_op jit(solution)/shard_map/ppermute | solution.py:516
  134.8 5.6 %collective-permute-start.19 = (f32[40,256]{1,0:T(8,128)S(1)}, f32[40,256]{1,0:T(8,128)S(1)}, u32[]{:S(2)}, u32[]{:S(2)}) collective-permute-start(f32[40,256]{1,0:T(8,128)S(1)} %shard_map.91.refs_0_), channel_id=1, source_target_pairs={{0,4},{4,8},{8,12},{12,0},{1,5},{5,9},{9,13},{13,1},{2,6},{6,10},{... | collective-permute-start | bytes 122888 | tf_op jit(solution)/shard_map/ppermute | solution.py:516
  (8 other events, 6.3 us)

commit v10 on v8

--- a/solution.py
+++ b/solution.py
@@ -228,13 +228,23 @@
     sum_ref[start + part : start + 2 * part] = obs_ref[...]
 
 
+def send_all(block_ref, far_ref, sems):
+    copies = [
+        pltpu.make_async_copy(block_ref, far_ref.at[place], sems.at[place])
+        for place in range(far_ref.shape[0])
+    ]
+    for copy in copies:
+        copy.start()
+    return copies
+
+
 def residual_kernel(nxy, nh, *refs):
     rows = NX // nxy
     part = rows // nh
     pairs = nxy // 2
     start = 2 * rows + pairs
     sums = refs[:nh]
-    pred_ref, pull_ref, weight_ref, tops_ref, send_ref, meas_ref = refs[nh:]
+    pred_ref, pull_ref, weight_ref, tops_ref, far_ref, meas_ref, block_ref, sems = refs[nh:]
     chip = lax.axis_index("h")
     total = sums[0][: 2 * rows]
     for step in range(1, nh):
@@ -246,11 +256,12 @@
         meas_ref[place, :] = sums[step][start + part :]
     weight = weight_ref[...]
     pred = total[:rows]
+    block_ref[...] = weight * (weight * (pred - meas_ref[...]))
+    copies = send_all(block_ref, far_ref, sems)
     pred_ref[...] = pred
     pull_ref[...] = total[rows:]
-    res = weight * (weight * (pred - meas_ref[...]))
-    for target in range(nxy):
-        send_ref[target] = res
+    for copy in copies:
+        copy.wait()
 
 
 def power_kernel(layers, tops_ref, power_ref):
@@ -347,7 +358,7 @@
     part = rows // nh
     pieces = refs[:2]
     pull_ref, dens_ref, weight_ref = refs[2:5]
-    send_ref, grad_ref, line_ref, image_ref, scratch = refs[5:]
+    far_ref, grad_ref, line_ref, image_ref, scratch, block_ref, sems = refs[5:]
     total = pieces[0][...] + pieces[1][...]
     data = total[:QX]
     line = total[QX:]
@@ -356,14 +367,14 @@
     grad = data + 0.5 * (quad * dens)
     image = line + pull_ref[...]
     weight = weight_ref[...]
-    mine = jnp.broadcast_to(share(grad, quad, image, weight, scratch, part), (8, NY))
+    block_ref[:rows] = weight * (weight * image)
+    block_ref[rows:] = jnp.broadcast_to(share(grad, quad, image, weight, scratch, part), (8, NY))
+    copies = send_all(block_ref, far_ref, sems)
     grad_ref[...] = grad
     line_ref[...] = line
     image_ref[...] = image
-    back = weight * (weight * image)
-    for target in range(nxy):
-        send_ref[target, :rows] = back
-        send_ref[target, rows:] = mine
+    for copy in copies:
+        copy.wait()
 
 
 def part_kernel(nxy, got_ref, plane_ref, share_ref):
@@ -460,6 +471,7 @@
 VMEM = pl.BlockSpec(memory_space=pltpu.VMEM)
 SMEM = pl.BlockSpec(memory_space=pltpu.SMEM)
 ANY = pl.BlockSpec(memory_space=pl.ANY)
+FAR = pl.BlockSpec(memory_space=pltpu.HBM)
 
 
 class Program:
@@ -483,12 +495,15 @@
         kinds = [(item, F32) if isinstance(item, tuple) else (item.shape, item.dtype) for item in outs]
         return pl.pallas_call(
             inner,
-            out_shape=[jax.ShapeDtypeStruct(shape, dtype) for shape, dtype in kinds],
+            out_shape=[
+                (pltpu.HBM if place in far_out else jax.ShapeDtypeStruct)(*kind)
+                for place, kind in enumerate(kinds)
+            ],
             in_specs=[
                 SMEM if place in scalars else VMEM for place in range(used)
             ]
             + [ANY] * kept,
-            out_specs=[ANY if place in far_out else VMEM for place in range(len(outs))],
+            out_specs=[FAR if place in far_out else VMEM for place in range(len(outs))],
             scratch_shapes=[pltpu.VMEM(shape, F32) for shape in scratch]
             + [pltpu.SemaphoreType.DMA((sems,) if sems > 1 else ())] * (sems > 0),
             compiler_params=pltpu.CompilerParams(vmem_limit_bytes=mib << 20),
@@ -512,10 +527,10 @@
 
 def from_axis(values, axis):
     size = len(values)
-    return [values[0]] + [
-        lax.ppermute(values[step], axis, [(i, (i + step) % size) for i in range(size)])
-        for step in range(1, size)
-    ]
+    got = {0: values[0]}
+    for step in sorted(range(1, size), key=lambda step: min(step, size - step)):
+        got[step] = lax.ppermute(values[step], axis, [(i, (i + step) % size) for i in range(size)])
+    return [got[step] for step in range(size)]
 
 
 def exchange(value, axes):
@@ -561,7 +576,7 @@
     pred, pulled, weight, tops, message = call(
         bind(residual_kernel, nxy, nh),
         [(rows, NY), (rows, NY), (rows, NY), (nxy * nh // 2, NY), (nxy, rows, NY)],
-        *sums, scratch=[(rows, NY)],
+        *sums, scratch=[(rows, NY)] * 2, far_out=(4,), sems=nxy,
     )
     program.hold(pred, pulled, weight)
     got = exchange(message, XY)
@@ -581,7 +596,8 @@
     message, grad, line, image = call(
         bind(gradient_kernel, nxy, nh),
         [(nxy, rows + 8, NY), (QX, NY), (rows, NY), (rows, NY)],
-        *pieces, pulled, dens, weight, scratch=[(rows, NY)],
+        *pieces, pulled, dens, weight,
+        scratch=[(rows, NY), (rows + 8, NY)], far_out=(0,), sems=nxy,
     )
     program.drop(pulled)
     program.hold(line, image)

time: 157 us -> 157 us (level)
  local copies, waits for them, and re-layouts: 7.33 us -> 4.87 us
  Pallas kernels: 17 us -> 19 us
    unnamed x30 -> x24, local copies, waits for them, and re-layouts: 7.33 us -> 4.87 us
    pallas_call x17, Pallas kernels: 17 us -> 19 us  [call(): pl.pallas_call(inner, out_shape=[(pltpu.HBM if place in far_out else jax....]
where the time goes in v10:
time: 157 us; the launch traced here: 156 us
  starting transfers between devices  51.8 us (33%)
  blocking collectives  40.3 us (26%)
  waiting for transfers between devices  38.5 us (25%)
  Pallas kernels  19 us (12%)
  local copies, waits for them, and re-layouts  4.87 us (3%)
    all_to_all x2, blocking collectives, exchange(): return lax.all_to_all(value, axes, 0, 0, tiled=True)  40.3 us
    ppermute x9, starting transfers between devices, from_axis(): lax.ppermute(values[step], axis, [(i, (i + step) % size) for i in range(s...  20.7 us
    pallas_call x17, Pallas kernels, call(): pl.pallas_call(inner, out_shape=[(pltpu.HBM if place in far_out else jax....  19 us
    ppermute x10, starting transfers between devices, flip(): return lax.ppermute(value, axis, [(0, 1), (1, 0)])  15.2 us
    ppermute x10, waiting for transfers between devices, flip(): return lax.ppermute(value, axis, [(0, 1), (1, 0)])  14.1 us
    all_to_all x3, waiting for transfers between devices, exchange(): return lax.all_to_all(value, axes, 0, 0, tiled=True)  13.1 us
    all_to_all x3, starting transfers between devices, exchange(): return lax.all_to_all(value, axes, 0, 0, tiled=True)  11.2 us
    ppermute x9, waiting for transfers between devices, from_axis(): lax.ppermute(values[step], axis, [(i, (i + step) % size) for i in range(s...  9.31 us
  transfers between devices with their start and end apart: 25, of which 14 were waited for; matrix products, arithmetic and copies ran while one was open for 0% of the time, Pallas kernels for 5%

profile of v10, /device:TPU:1, one launch (start us, length us, event | category | flops | bytes accessed | tf_op | source)
XLA Modules:
  0.0 156.0 jit_solution(14715426837892555286)
XLA Ops:
  0.6 2.5 %collective-permute-start.1 = (f32[128,256]{1,0:T(8,128)}, f32[128,256]{1,0:T(8,128)S(1)}, u32[]{:S(2)}, u32[]{:S(2)}) collective-permute-start(f32[128,256]{1,0:T(8,128)} %bitcast.9), channel_id=1, source_target_pairs={{0,2},{2,0},{1,3},{3,1},{4,6},{6,4},{5,7},{7,5},{8,10},{10,8},{9,1... | collective-permute-start | bytes 393224 | tf_op jit(solution)/shard_map/ppermute | solution.py:520
  10.1 3.1 %shard_map.78 = (f32[16,72,256]{2,1,0:T(8,128)S(1)}, f32[512,256]{1,0:T(8,128)}) custom-call(f32[128,256]{1,0:T(8,128)S(1)} %get-tuple-element.47.refs_0_.refs_9_.refs_10_.refs_7_.refs_8_.refs_3_.refs_4_, f32[128,256]{1,0:T(8,128)S(1)} %collective-permute-done.refs_1_, f32[128,256]{1,0:T(8,128)S(1)} %collective-permute-done.1.refs_2_, ...), custom_call_target="tpu_custom_call" | custom-call | tf_op jit(solution)/shard_map/pallas_call | solution.py:496
  13.2 23.9 %all_to_all.31.refs_0_ = f32[16,72,256]{2,1,0:T(8,128)S(1)} all-to-all(f32[16,72,256]{2,1,0:T(8,128)S(1)} %get-tuple-element.55), channel_id=1, replica_groups=mesh['x'=4,'y'=4,'h'=4,'l'=2,'k'=2] {'x','y'}, dimensions={0} | all-to-all | bytes 2359296 | tf_op jit(solution)/shard_map/all_to_all | solution.py:537
  37.2 5.0 %collective-permute-start.5 = (f32[88,256]{1,0:T(8,128)S(1)}, f32[88,256]{1,0:T(8,128)S(1)}, u32[]{:S(2)}, u32[]{:S(2)}) collective-permute-start(f32[88,256]{1,0:T(8,128)S(1)} %shard_map.79.refs_0_), channel_id=1, source_target_pairs={{0,12},{4,0},{8,4},{12,8},{1,13},{5,1},{9,5},{13,9},{2,14},{6,2},{... | collective-permute-start | bytes 270344 | tf_op jit(solution)/shard_map/ppermute | solution.py:532
  42.2 1.3 collective-permute-start.4
  43.5 1.9 %collective-permute-start.3 = (f32[88,256]{1,0:T(8,128)S(1)}, f32[88,256]{1,0:T(8,128)S(1)}, u32[]{:S(2)}, u32[]{:S(2)}) collective-permute-start(f32[88,256]{1,0:T(8,128)S(1)} %shard_map.79.refs_0_), channel_id=1, source_target_pairs={{0,4},{4,8},{8,12},{12,0},{1,5},{5,9},{9,13},{13,1},{2,6},{6,10},{... | collective-permute-start | bytes 270344 | tf_op jit(solution)/shard_map/ppermute | solution.py:532
  45.5 4.2 %collective-permute-done.4.refs_2_ = f32[88,256]{1,0:T(8,128)S(1)} collective-permute-done((f32[88,256]{1,0:T(8,128)S(1)}, f32[88,256]{1,0:T(8,128)S(1)}, u32[]{:S(2)}, u32[]{:S(2)}) %collective-permute-start.4) | collective-permute-done | bytes 90144 | tf_op jit(solution)/shard_map/ppermute | solution.py:532
  51.5 4.0 %all-to-all-start.1 = ((f32[16,32,256]{2,1,0:T(8,128)}), f32[16,32,256]{2,1,0:T(8,128)S(1)}, u32[]{:S(2)}, u32[]{:S(2)}) async-start(f32[16,32,256]{2,1,0:T(8,128)} %get-tuple-element.56), calls=%async_computation.1 | async-start | bytes 1048576 | tf_op jit(solution)/shard_map/all_to_all | solution.py:537
  55.6 3.6 %shard_map.81.refs_4_.refs_12_.refs_10_.refs_13_.refs_18_ = f32[264,256]{1,0:T(8,128)S(1)} custom-call(f32[32,256]{1,0:T(8,128)S(1)} %get-tuple-element.57.refs_0_, bf16[4,256,256]{2,1,0:T(8,128)(2,1)S(1)} %get-tuple-element.52.refs_8_.refs_3_.refs_4_.refs_1_.refs_5_.refs_2_.refs_13_, ...), custom_call_target="tpu_custom_call" | custom-call | tf_op jit(solution)/shard_map/pallas_call | solution.py:496
  59.1 5.5 %all-to-all-done.1 = f32[16,32,256]{2,1,0:T(8,128)S(1)} async-done(((f32[16,32,256]{2,1,0:T(8,128)}), f32[16,32,256]{2,1,0:T(8,128)S(1)}, u32[]{:S(2)}, u32[]{:S(2)}) %all-to-all-start.1) | async-done | bytes 524320 | tf_op jit(solution)/shard_map/all_to_all | solution.py:537
  64.6 2.4 %shard_map.82 = (f32[320,256]{1,0:T(8,128)S(1)}, f32[320,256]{1,0:T(8,128)S(1)}) custom-call(f32[512,256]{1,0:T(8,128)S(1)} %bitcast.8, f32[264,256]{1,0:T(8,128)S(1)} %get-tuple-element.49.refs_5_.refs_6_.refs_7_.refs_4_.refs_1_.refs_8_.refs_10_, f32[264,256]{1,0:T(8,128)S(1)} %get-tuple-element.50.refs_6_.refs_7_.refs_8_.refs_5_.refs_2_.refs_9_.refs_11_, ...), custom_call_target="tpu_custom_call" | custom-call | tf_op jit(solution)/shard_map/pallas_call | solution.py:496
  67.0 5.1 %collective-permute-start.6 = (f32[320,256]{1,0:T(8,128)S(1)}, f32[320,256]{1,0:T(8,128)S(1)}, u32[]{:S(2)}, u32[]{:S(2)}) collective-permute-start(f32[320,256]{1,0:T(8,128)S(1)} %get-tuple-element.62), channel_id=1, source_target_pairs={{0,1},{1,0},{2,3},{3,2},{4,5},{5,4},{6,7},{7,6},{8,9},{9,8},{10,11... | collective-permute-start | bytes 983048 | tf_op jit(solution)/shard_map/ppermute | solution.py:520
  73.6 5.3 %collective-permute-done.7.refs_1_ = f32[160,256]{1,0:T(8,128)S(1)} collective-permute-done((f32[160,256]{1,0:T(8,128)S(1)}, f32[160,256]{1,0:T(8,128)S(1)}, u32[]{:S(2)}, u32[]{:S(2)}) %collective-permute-start.7) | collective-permute-done | bytes 163872 | tf_op jit(solution)/shard_map/ppermute | solution.py:520
  80.1 3.6 %all-to-all-start.2 = ((f32[16,40,256]{2,1,0:T(8,128)}), f32[16,40,256]{2,1,0:T(8,128)S(1)}, u32[]{:S(2)}, u32[]{:S(2)}) async-start(f32[16,40,256]{2,1,0:T(8,128)} %get-tuple-element.65), calls=%async_computation.2 | async-start | bytes 1310720 | tf_op jit(solution)/shard_map/all_to_all | solution.py:537
  83.9 1.5 collective-permute-start.8
  85.4 2.2 %collective-permute-done.9.refs_8_ = f32[128,256]{1,0:T(8,128)S(1)} collective-permute-done((f32[128,256]{1,0:T(8,128)S(1)}, f32[128,256]{1,0:T(8,128)S(1)}, u32[]{:S(2)}, u32[]{:S(2)}) %collective-permute-start.9) | collective-permute-done | bytes 131104 | tf_op jit(solution)/shard_map/ppermute | solution.py:520
  87.6 2.4 %collective-permute-start.10 = (f32[128,256]{1,0:T(8,128)S(1)}, f32[128,256]{1,0:T(8,128)S(1)}, u32[]{:S(2)}, u32[]{:S(2)}) collective-permute-start(f32[128,256]{1,0:T(8,128)S(1)} %collective-permute-done.9.refs_8_), channel_id=1, source_target_pairs={{0,1},{1,0},{2,3},{3,2},{4,5},{5,4},{6,7},{7,6},{8,9},{9,8},{10,11... | collective-permute-start | bytes 393224 | tf_op jit(solution)/shard_map/ppermute | solution.py:520
  92.0 3.3 %all-to-all-done.2.refs_0_ = f32[16,40,256]{2,1,0:T(8,128)S(1)} async-done(((f32[16,40,256]{2,1,0:T(8,128)}), f32[16,40,256]{2,1,0:T(8,128)S(1)}, u32[]{:S(2)}, u32[]{:S(2)}) %all-to-all-start.2) | async-done | bytes 655392 | tf_op jit(solution)/shard_map/all_to_all | solution.py:537
  95.4 2.2 %collective-permute-start.13 = (f32[8,256]{1,0:T(8,128)S(1)}, f32[8,256]{1,0:T(8,128)S(1)}, u32[]{:S(2)}, u32[]{:S(2)}) collective-permute-start(f32[8,256]{1,0:T(8,128)S(1)} %get-tuple-element.74.refs_0_), channel_id=1, source_target_pairs={{0,12},{4,0},{8,4},{12,8},{1,13},{5,1},{9,5},{13,9},{2,14},{6,2},{... | collective-permute-start | bytes 24584 | tf_op jit(solution)/shard_map/ppermute | solution.py:532
  97.5 1.7 %collective-permute-start.12 = (f32[8,256]{1,0:T(8,128)S(1)}, f32[8,256]{1,0:T(8,128)S(1)}, u32[]{:S(2)}, u32[]{:S(2)}) collective-permute-start(f32[8,256]{1,0:T(8,128)S(1)} %get-tuple-element.74.refs_0_), channel_id=1, source_target_pairs={{0,8},{4,12},{8,0},{12,4},{1,9},{5,13},{9,1},{13,5},{2,10},{6,14},... | collective-permute-start | bytes 24584 | tf_op jit(solution)/shard_map/ppermute | solution.py:532
  99.2 2.3 %collective-permute-start.11 = (f32[8,256]{1,0:T(8,128)S(1)}, f32[8,256]{1,0:T(8,128)S(1)}, u32[]{:S(2)}, u32[]{:S(2)}) collective-permute-start(f32[8,256]{1,0:T(8,128)S(1)} %get-tuple-element.74.refs_0_), channel_id=1, source_target_pairs={{0,4},{4,8},{8,12},{12,0},{1,5},{5,9},{9,13},{13,1},{2,6},{6,10},{... | collective-permute-start | bytes 24584 | tf_op jit(solution)/shard_map/ppermute | solution.py:532
  101.5 3.2 %shard_map.86 = (f32[320,256]{1,0:T(8,128)S(1)}, f32[320,256]{1,0:T(8,128)}) custom-call(f32[512,256]{1,0:T(8,128)S(1)} %get-tuple-element.71.refs_0_, f32[264,256]{1,0:T(8,128)S(1)} %get-tuple-element.49.refs_5_.refs_6_.refs_7_.refs_4_.refs_1_.refs_8_.refs_10_, f32[264,256]{1,0:T(8,128)S(1)} %get-tuple-element.50.refs_6_.refs_7_.refs_8_.refs_5_.refs_2_.refs_9_.refs_11_, ...), custom_call_target="tpu_custom_call" | custom-call | tf_op jit(solution)/shard_map/pallas_call | solution.py:496
  104.7 4.2 %collective-permute-start.16 = (f32[8,256]{1,0:T(8,128)S(1)}, f32[8,256]{1,0:T(8,128)S(1)}, u32[]{:S(2)}, u32[]{:S(2)}) collective-permute-start(f32[8,256]{1,0:T(8,128)S(1)} %shard_map.87.refs_0_), channel_id=1, source_target_pairs={{0,3},{1,2},{2,1},{3,0},{4,7},{5,6},{6,5},{7,4},{8,11},{9,10},{10,... | collective-permute-start | bytes 24584 | tf_op jit(solution)/shard_map/ppermute | solution.py:515
  111.5 2.7 %shard_map.88 = (f32[16,32,256]{2,1,0:T(8,128)}, f32[128,256]{1,0:T(8,128)S(1)}, f32[128,256]{1,0:T(8,128)S(1)}, f32[8,128]{1,0:T(8,128)S(1)}) custom-call(f32[8,256]{1,0:T(8,128)S(1)} %shard_map.87.refs_0_, f32[8,256]{1,0:T(8,128)S(1)} %collective-permute-done.14.refs_1_, f32[8,256]{1,0:T(8,128)S(1)} %collective-permute-done.15.refs_2_, ...), custom_call_target="tpu_custom_call" | custom-call | tf_op jit(solution)/shard_map/pallas_call | solution.py:496
  114.4 3.6 %all-to-all-start.3 = ((f32[16,32,256]{2,1,0:T(8,128)}), f32[16,32,256]{2,1,0:T(8,128)S(1)}, u32[]{:S(2)}, u32[]{:S(2)}) async-start(f32[16,32,256]{2,1,0:T(8,128)} %get-tuple-element.79), calls=%async_computation.3 | async-start | bytes 1048576 | tf_op jit(solution)/shard_map/all_to_all | solution.py:537
  119.3 4.3 %collective-permute-done.18.refs_1_ = f32[160,256]{1,0:T(8,128)S(1)} collective-permute-done((f32[160,256]{1,0:T(8,128)S(1)}, f32[160,256]{1,0:T(8,128)S(1)}, u32[]{:S(2)}, u32[]{:S(2)}) %collective-permute-start.18) | collective-permute-done | bytes 163872 | tf_op jit(solution)/shard_map/ppermute | solution.py:520
  123.8 4.3 %all-to-all-done.3.refs_0_ = f32[16,32,256]{2,1,0:T(8,128)S(1)} async-done(((f32[16,32,256]{2,1,0:T(8,128)}), f32[16,32,256]{2,1,0:T(8,128)S(1)}, u32[]{:S(2)}, u32[]{:S(2)}) %all-to-all-start.3) | async-done | bytes 524320 | tf_op jit(solution)/shard_map/all_to_all | solution.py:537
  128.1 1.9 %collective-permute-start.21 = (f32[40,256]{1,0:T(8,128)S(1)}, f32[40,256]{1,0:T(8,128)S(1)}, u32[]{:S(2)}, u32[]{:S(2)}) collective-permute-start(f32[40,256]{1,0:T(8,128)S(1)} %shard_map.91.refs_0_), channel_id=1, source_target_pairs={{0,12},{4,0},{8,4},{12,8},{1,13},{5,1},{9,5},{13,9},{2,14},{6,2},{... | collective-permute-start | bytes 122888 | tf_op jit(solution)/shard_map/ppermute | solution.py:532
  130.0 3.2 %collective-permute-start.20 = (f32[40,256]{1,0:T(8,128)S(1)}, f32[40,256]{1,0:T(8,128)S(1)}, u32[]{:S(2)}, u32[]{:S(2)}) collective-permute-start(f32[40,256]{1,0:T(8,128)S(1)} %shard_map.91.refs_0_), channel_id=1, source_target_pairs={{0,8},{4,12},{8,0},{12,4},{1,9},{5,13},{9,1},{13,5},{2,10},{6,14},... | collective-permute-start | bytes 122888 | tf_op jit(solution)/shard_map/ppermute | solution.py:532
  134.4 2.4 %collective-permute-done.20.refs_2_ = f32[40,256]{1,0:T(8,128)S(1)} collective-permute-done((f32[40,256]{1,0:T(8,128)S(1)}, f32[40,256]{1,0:T(8,128)S(1)}, u32[]{:S(2)}, u32[]{:S(2)}) %collective-permute-start.20) | collective-permute-done | bytes 40992 | tf_op jit(solution)/shard_map/ppermute | solution.py:532
  136.8 1.8 %collective-permute-done.19.refs_1_ = f32[40,256]{1,0:T(8,128)S(1)} collective-permute-done((f32[40,256]{1,0:T(8,128)S(1)}, f32[40,256]{1,0:T(8,128)S(1)}, u32[]{:S(2)}, u32[]{:S(2)}) %collective-permute-start.19) | collective-permute-done | bytes 40992 | tf_op jit(solution)/shard_map/ppermute | solution.py:532
  138.8 16.4 %all_to_all.32 = f32[64,1,128]{2,1,0:T(1,128)S(1)} all-to-all(f32[64,1,128]{2,1,0:T(1,128)S(1)} %bitcast.16), channel_id=1, replica_groups=mesh['x'=4,'y'=4,'h'=4,'l'=2,'k'=2] {'x','y','l','k'}, dimensions={0} | all-to-all | bytes 65536 | tf_op jit(solution)/shard_map/all_to_all | solution.py:537
  (61 shorter events, 19.3 us)
Async XLA Ops:
  0.6 7.5 %collective-permute-start.1 = (f32[128,256]{1,0:T(8,128)}, f32[128,256]{1,0:T(8,128)S(1)}, u32[]{:S(2)}, u32[]{:S(2)}) collective-permute-start(f32[128,256]{1,0:T(8,128)} %bitcast.9), channel_id=1, source_target_pairs={{0,2},{2,0},{1,3},{3,1},{4,6},{6,4},{5,7},{7,5},{8,10},{10,8},{9,1... | collective-permute-start | bytes 393224 | tf_op jit(solution)/shard_map/ppermute | solution.py:520
  3.2 5.9 %collective-permute-start = (f32[128,256]{1,0:T(8,128)}, f32[128,256]{1,0:T(8,128)S(1)}, u32[]{:S(2)}, u32[]{:S(2)}) collective-permute-start(f32[128,256]{1,0:T(8,128)} %bitcast.10), channel_id=1, source_target_pairs={{0,1},{1,0},{2,3},{3,2},{4,5},{5,4},{6,7},{7,6},{8,9},{9,8},{10,11... | collective-permute-start | bytes 393224 | tf_op jit(solution)/shard_map/ppermute | solution.py:520
  4.8 1.0 copy-start.1
  8.2 1.9 %collective-permute-start.2 = (f32[128,256]{1,0:T(8,128)S(1)}, f32[128,256]{1,0:T(8,128)S(1)}, u32[]{:S(2)}, u32[]{:S(2)}) collective-permute-start(f32[128,256]{1,0:T(8,128)S(1)} %collective-permute-done.1.refs_2_), channel_id=1, source_target_pairs={{0,1},{1,0},{2,3},{3,2},{4,5},{5,4},{6,7},{7,6},{8,9},{9,8},{10,11... | collective-permute-start | bytes 393224 | tf_op jit(solution)/shard_map/ppermute | solution.py:520
  13.2 23.9 %copy-start.10 = (f32[1,8,256]{2,1,0:T(8,128)S(1)}, f32[1,8,256]{2,1,0:T(8,128)}, u32[]{:S(2)}) copy-start(f32[1,8,256]{2,1,0:T(8,128)} %param.8) | copy-start | bytes 24580
  13.2 23.9 %copy-start.11 = (f32[1,8,256]{2,1,0:T(8,128)S(1)}, f32[1,8,256]{2,1,0:T(8,128)}, u32[]{:S(2)}) copy-start(f32[1,8,256]{2,1,0:T(8,128)} %param.7) | copy-start | bytes 24580
  37.2 8.3 %collective-permute-start.5 = (f32[88,256]{1,0:T(8,128)S(1)}, f32[88,256]{1,0:T(8,128)S(1)}, u32[]{:S(2)}, u32[]{:S(2)}) collective-permute-start(f32[88,256]{1,0:T(8,128)S(1)} %shard_map.79.refs_0_), channel_id=1, source_target_pairs={{0,12},{4,0},{8,4},{12,8},{1,13},{5,1},{9,5},{13,9},{2,14},{6,2},{... | collective-permute-start | bytes 270344 | tf_op jit(solution)/shard_map/ppermute | solution.py:532
  42.2 7.5 %collective-permute-start.4 = (f32[88,256]{1,0:T(8,128)S(1)}, f32[88,256]{1,0:T(8,128)S(1)}, u32[]{:S(2)}, u32[]{:S(2)}) collective-permute-start(f32[88,256]{1,0:T(8,128)S(1)} %shard_map.79.refs_0_), channel_id=1, source_target_pairs={{0,8},{4,12},{8,0},{12,4},{1,9},{5,13},{9,1},{13,5},{2,10},{6,14},... | collective-permute-start | bytes 270344 | tf_op jit(solution)/shard_map/ppermute | solution.py:532
  43.5 7.0 %collective-permute-start.3 = (f32[88,256]{1,0:T(8,128)S(1)}, f32[88,256]{1,0:T(8,128)S(1)}, u32[]{:S(2)}, u32[]{:S(2)}) collective-permute-start(f32[88,256]{1,0:T(8,128)S(1)} %shard_map.79.refs_0_), channel_id=1, source_target_pairs={{0,4},{4,8},{8,12},{12,0},{1,5},{5,9},{9,13},{13,1},{2,6},{6,10},{... | collective-permute-start | bytes 270344 | tf_op jit(solution)/shard_map/ppermute | solution.py:532
  51.5 13.1 %all-to-all-start.1 = ((f32[16,32,256]{2,1,0:T(8,128)}), f32[16,32,256]{2,1,0:T(8,128)S(1)}, u32[]{:S(2)}, u32[]{:S(2)}) async-start(f32[16,32,256]{2,1,0:T(8,128)} %get-tuple-element.56), calls=%async_computation.1 | async-start | bytes 1048576 | tf_op jit(solution)/shard_map/all_to_all | solution.py:537
  67.0 6.4 %collective-permute-start.6 = (f32[320,256]{1,0:T(8,128)S(1)}, f32[320,256]{1,0:T(8,128)S(1)}, u32[]{:S(2)}, u32[]{:S(2)}) collective-permute-start(f32[320,256]{1,0:T(8,128)S(1)} %get-tuple-element.62), channel_id=1, source_target_pairs={{0,1},{1,0},{2,3},{3,2},{4,5},{5,4},{6,7},{7,6},{8,9},{9,8},{10,11... | collective-permute-start | bytes 983048 | tf_op jit(solution)/shard_map/ppermute | solution.py:520
  73.4 5.5 %collective-permute-start.7 = (f32[160,256]{1,0:T(8,128)S(1)}, f32[160,256]{1,0:T(8,128)S(1)}, u32[]{:S(2)}, u32[]{:S(2)}) collective-permute-start(f32[160,256]{1,0:T(8,128)S(1)} %get-tuple-element.64), channel_id=1, source_target_pairs={{0,2},{2,0},{1,3},{3,1},{4,6},{6,4},{5,7},{7,5},{8,10},{10,8},{9,1... | collective-permute-start | bytes 491528 | tf_op jit(solution)/shard_map/ppermute | solution.py:520
  80.1 15.2 %all-to-all-start.2 = ((f32[16,40,256]{2,1,0:T(8,128)}), f32[16,40,256]{2,1,0:T(8,128)S(1)}, u32[]{:S(2)}, u32[]{:S(2)}) async-start(f32[16,40,256]{2,1,0:T(8,128)} %get-tuple-element.65), calls=%async_computation.2 | async-start | bytes 1310720 | tf_op jit(solution)/shard_map/all_to_all | solution.py:537
  83.7 3.9 %collective-permute-start.9 = (f32[128,256]{1,0:T(8,128)S(1)}, f32[128,256]{1,0:T(8,128)S(1)}, u32[]{:S(2)}, u32[]{:S(2)}) collective-permute-start(f32[128,256]{1,0:T(8,128)S(1)} %get-tuple-element.66.refs_6_), channel_id=1, source_target_pairs={{0,2},{2,0},{1,3},{3,1},{4,6},{6,4},{5,7},{7,5},{8,10},{10,8},{9,1... | collective-permute-start | bytes 393224 | tf_op jit(solution)/shard_map/ppermute | solution.py:520
  83.9 6.8 %collective-permute-start.8 = (f32[128,256]{1,0:T(8,128)S(1)}, f32[128,256]{1,0:T(8,128)S(1)}, u32[]{:S(2)}, u32[]{:S(2)}) collective-permute-start(f32[128,256]{1,0:T(8,128)S(1)} %get-tuple-element.66.refs_6_), channel_id=1, source_target_pairs={{0,1},{1,0},{2,3},{3,2},{4,5},{5,4},{6,7},{7,6},{8,9},{9,8},{10,11... | collective-permute-start | bytes 393224 | tf_op jit(solution)/shard_map/ppermute | solution.py:520
  87.6 3.7 %collective-permute-start.10 = (f32[128,256]{1,0:T(8,128)S(1)}, f32[128,256]{1,0:T(8,128)S(1)}, u32[]{:S(2)}, u32[]{:S(2)}) collective-permute-start(f32[128,256]{1,0:T(8,128)S(1)} %collective-permute-done.9.refs_8_), channel_id=1, source_target_pairs={{0,1},{1,0},{2,3},{3,2},{4,5},{5,4},{6,7},{7,6},{8,9},{9,8},{10,11... | collective-permute-start | bytes 393224 | tf_op jit(solution)/shard_map/ppermute | solution.py:520
  95.4 9.3 %collective-permute-start.13 = (f32[8,256]{1,0:T(8,128)S(1)}, f32[8,256]{1,0:T(8,128)S(1)}, u32[]{:S(2)}, u32[]{:S(2)}) collective-permute-start(f32[8,256]{1,0:T(8,128)S(1)} %get-tuple-element.74.refs_0_), channel_id=1, source_target_pairs={{0,12},{4,0},{8,4},{12,8},{1,13},{5,1},{9,5},{13,9},{2,14},{6,2},{... | collective-permute-start | bytes 24584 | tf_op jit(solution)/shard_map/ppermute | solution.py:532
  97.5 7.1 %collective-permute-start.12 = (f32[8,256]{1,0:T(8,128)S(1)}, f32[8,256]{1,0:T(8,128)S(1)}, u32[]{:S(2)}, u32[]{:S(2)}) collective-permute-start(f32[8,256]{1,0:T(8,128)S(1)} %get-tuple-element.74.refs_0_), channel_id=1, source_target_pairs={{0,8},{4,12},{8,0},{12,4},{1,9},{5,13},{9,1},{13,5},{2,10},{6,14},... | collective-permute-start | bytes 24584 | tf_op jit(solution)/shard_map/ppermute | solution.py:532
  99.2 5.4 %collective-permute-start.11 = (f32[8,256]{1,0:T(8,128)S(1)}, f32[8,256]{1,0:T(8,128)S(1)}, u32[]{:S(2)}, u32[]{:S(2)}) collective-permute-start(f32[8,256]{1,0:T(8,128)S(1)} %get-tuple-element.74.refs_0_), channel_id=1, source_target_pairs={{0,4},{4,8},{8,12},{12,0},{1,5},{5,9},{9,13},{13,1},{2,6},{6,10},{... | collective-permute-start | bytes 24584 | tf_op jit(solution)/shard_map/ppermute | solution.py:532
  104.7 6.8 %copy-start = (f32[512,256]{1,0:T(8,128)S(1)}, f32[512,256]{1,0:T(8,128)}, u32[]{:S(2)}) copy-start(f32[512,256]{1,0:T(8,128)} %get-tuple-element.78.refs_5_) | copy-start | bytes 1572868
  104.7 6.7 %copy-start.5 = (f32[128,256]{1,0:T(8,128)S(1)}, f32[128,256]{1,0:T(8,128)}, u32[]{:S(2)}) copy-start(f32[128,256]{1,0:T(8,128)} %copy-done.4) | copy-start | bytes 393220
  104.7 6.7 %copy-start.7 = (f32[128,256]{1,0:T(8,128)S(1)}, f32[128,256]{1,0:T(8,128)}, u32[]{:S(2)}) copy-start(f32[128,256]{1,0:T(8,128)} %copy-done.6) | copy-start | bytes 393220
  104.7 6.7 %copy-start.9 = (f32[128,256]{1,0:T(8,128)S(1)}, f32[128,256]{1,0:T(8,128)}, u32[]{:S(2)}) copy-start(f32[128,256]{1,0:T(8,128)} %copy-done.8) | copy-start | bytes 393220
  104.7 5.9 %collective-permute-start.16 = (f32[8,256]{1,0:T(8,128)S(1)}, f32[8,256]{1,0:T(8,128)S(1)}, u32[]{:S(2)}, u32[]{:S(2)}) collective-permute-start(f32[8,256]{1,0:T(8,128)S(1)} %shard_map.87.refs_0_), channel_id=1, source_target_pairs={{0,3},{1,2},{2,1},{3,0},{4,7},{5,6},{6,5},{7,4},{8,11},{9,10},{10,... | collective-permute-start | bytes 24584 | tf_op jit(solution)/shard_map/ppermute | solution.py:515
  108.9 2.5 %collective-permute-start.15 = (f32[8,256]{1,0:T(8,128)S(1)}, f32[8,256]{1,0:T(8,128)S(1)}, u32[]{:S(2)}, u32[]{:S(2)}) collective-permute-start(f32[8,256]{1,0:T(8,128)S(1)} %shard_map.87.refs_0_), channel_id=1, source_target_pairs={{0,2},{1,3},{2,0},{3,1},{4,6},{5,7},{6,4},{7,5},{8,10},{9,11},{10,... | collective-permute-start | bytes 24584 | tf_op jit(solution)/shard_map/ppermute | solution.py:515
  109.2 2.2 %collective-permute-start.14 = (f32[8,256]{1,0:T(8,128)S(1)}, f32[8,256]{1,0:T(8,128)S(1)}, u32[]{:S(2)}, u32[]{:S(2)}) collective-permute-start(f32[8,256]{1,0:T(8,128)S(1)} %shard_map.87.refs_0_), channel_id=1, source_target_pairs={{0,1},{1,0},{2,3},{3,2},{4,5},{5,4},{6,7},{7,6},{8,9},{9,8},{10,11... | collective-permute-start | bytes 24584 | tf_op jit(solution)/shard_map/ppermute | solution.py:515
  114.2 3.8 %collective-permute-start.17 = (f32[320,256]{1,0:T(8,128)}, f32[320,256]{1,0:T(8,128)S(1)}, u32[]{:S(2)}, u32[]{:S(2)}) collective-permute-start(f32[320,256]{1,0:T(8,128)} %get-tuple-element.81), channel_id=1, source_target_pairs={{0,1},{1,0},{2,3},{3,2},{4,5},{5,4},{6,7},{7,6},{8,9},{9,8},{10,11... | collective-permute-start | bytes 983048 | tf_op jit(solution)/shard_map/ppermute | solution.py:520
  114.4 13.7 %all-to-all-start.3 = ((f32[16,32,256]{2,1,0:T(8,128)}), f32[16,32,256]{2,1,0:T(8,128)S(1)}, u32[]{:S(2)}, u32[]{:S(2)}) async-start(f32[16,32,256]{2,1,0:T(8,128)} %get-tuple-element.79), calls=%async_computation.3 | async-start | bytes 1048576 | tf_op jit(solution)/shard_map/all_to_all | solution.py:537
  118.0 5.6 %collective-permute-start.18 = (f32[160,256]{1,0:T(8,128)S(1)}, f32[160,256]{1,0:T(8,128)S(1)}, u32[]{:S(2)}, u32[]{:S(2)}) collective-permute-start(f32[160,256]{1,0:T(8,128)S(1)} %get-tuple-element.86), channel_id=1, source_target_pairs={{0,2},{2,0},{1,3},{3,1},{4,6},{6,4},{5,7},{7,5},{8,10},{10,8},{9,1... | collective-permute-start | bytes 491528 | tf_op jit(solution)/shard_map/ppermute | solution.py:520
  128.1 6.3 %collective-permute-start.21 = (f32[40,256]{1,0:T(8,128)S(1)}, f32[40,256]{1,0:T(8,128)S(1)}, u32[]{:S(2)}, u32[]{:S(2)}) collective-permute-start(f32[40,256]{1,0:T(8,128)S(1)} %shard_map.91.refs_0_), channel_id=1, source_target_pairs={{0,12},{4,0},{8,4},{12,8},{1,13},{5,1},{9,5},{13,9},{2,14},{6,2},{... | collective-permute-start | bytes 122888 | tf_op jit(solution)/shard_map/ppermute | solution.py:532
  130.0 6.8 %collective-permute-start.20 = (f32[40,256]{1,0:T(8,128)S(1)}, f32[40,256]{1,0:T(8,128)S(1)}, u32[]{:S(2)}, u32[]{:S(2)}) collective-permute-start(f32[40,256]{1,0:T(8,128)S(1)} %shard_map.91.refs_0_), channel_id=1, source_target_pairs={{0,8},{4,12},{8,0},{12,4},{1,9},{5,13},{9,1},{13,5},{2,10},{6,14},... | collective-permute-start | bytes 122888 | tf_op jit(solution)/shard_map/ppermute | solution.py:532
  133.3 5.4 %collective-permute-start.19 = (f32[40,256]{1,0:T(8,128)S(1)}, f32[40,256]{1,0:T(8,128)S(1)}, u32[]{:S(2)}, u32[]{:S(2)}) collective-permute-start(f32[40,256]{1,0:T(8,128)S(1)} %shard_map.91.refs_0_), channel_id=1, source_target_pairs={{0,4},{4,8},{8,12},{12,0},{1,5},{5,9},{9,13},{13,1},{2,6},{6,10},{... | collective-permute-start | bytes 122888 | tf_op jit(solution)/shard_map/ppermute | solution.py:532
  (5 other events, 3.8 us)

commit v11 on v10

--- a/solution.py
+++ b/solution.py
@@ -218,14 +218,14 @@
     for source in range(1, nxy):
         total = total + got_ref[source, : 2 * rows, :]
     sum_ref[: 2 * rows] = total
+    part = weight_ref.shape[0]
+    place = pl.ds(pl.multiple_of(lax.axis_index("h") * part, part), part)
+    sum_ref[place, :] = sum_ref[place, :] - obs_ref[...]
     left = lax.broadcasted_iota(jnp.int32, (1, NY), 1) < HY
     for pair in range(nxy // 2):
         first, second = (got_ref[2 * pair + i, 2 * rows : 2 * rows + 1, :] for i in (0, 1))
         sum_ref[2 * rows + pair : 2 * rows + pair + 1, :] = jnp.where(left, first, second)
-    part = weight_ref.shape[0]
-    start = 2 * rows + nxy // 2
-    sum_ref[start : start + part] = weight_ref[...]
-    sum_ref[start + part : start + 2 * part] = obs_ref[...]
+    sum_ref[2 * rows + nxy // 2 :] = weight_ref[...]
 
 
 def send_all(block_ref, far_ref, sems):
@@ -244,7 +244,7 @@
     pairs = nxy // 2
     start = 2 * rows + pairs
     sums = refs[:nh]
-    pred_ref, pull_ref, weight_ref, tops_ref, far_ref, meas_ref, block_ref, sems = refs[nh:]
+    error_ref, pull_ref, weight_ref, tops_ref, far_ref, block_ref, sems = refs[nh:]
     chip = lax.axis_index("h")
     total = sums[0][: 2 * rows]
     for step in range(1, nh):
@@ -252,13 +252,12 @@
     for step in range(nh):
         tops_ref[step * pairs : (step + 1) * pairs] = sums[step][2 * rows : start]
         place = pl.ds(pl.multiple_of(lax.rem(chip + (nh - step), nh) * part, part), part)
-        weight_ref[place, :] = sums[step][start : start + part]
-        meas_ref[place, :] = sums[step][start + part :]
+        weight_ref[place, :] = sums[step][start:]
     weight = weight_ref[...]
-    pred = total[:rows]
-    block_ref[...] = weight * (weight * (pred - meas_ref[...]))
+    error = total[:rows]
+    block_ref[...] = weight * (weight * error)
     copies = send_all(block_ref, far_ref, sems)
-    pred_ref[...] = pred
+    error_ref[...] = error
     pull_ref[...] = total[rows:]
     for copy in copies:
         copy.wait()
@@ -457,15 +456,14 @@
 
 
 def finish_kernel(
-    shares_ref, dens_ref, grad_ref, alpha_ref, pred_ref, first_ref, second_ref, obs_ref, w_ref, dens_out, err_out
+    shares_ref, dens_ref, grad_ref, alpha_ref, error_ref, first_ref, second_ref, w_ref, dens_out, err_out
 ):
-    part = obs_ref.shape[0]
+    part = w_ref.shape[0]
     alpha = step_length(shares_ref[...])
     dens_out[0] = dens_ref[...] - alpha * grad_ref[...]
     place = pl.ds(pl.multiple_of(lax.axis_index("h") * part, part), part)
-    pred = pred_ref[place, :] - alpha_ref[:1, :1] * first_ref[place, :]
-    pred = pred - alpha * second_ref[...]
-    err_out[0] = w_ref[...] * (pred - obs_ref[...])
+    error = error_ref[place, :] - alpha_ref[:1, :1] * first_ref[place, :]
+    err_out[0] = w_ref[...] * (error - alpha * second_ref[...])
 
 
 VMEM = pl.BlockSpec(memory_space=pltpu.VMEM)
@@ -570,15 +568,15 @@
     )
     got = exchange(message, XY)
     (sums,) = call(
-        bind(collect_kernel, nxy), [(2 * rows + nxy // 2 + 2 * part, NY)], got, weight_own, obs_own
+        bind(collect_kernel, nxy), [(2 * rows + nxy // 2 + part, NY)], got, weight_own, obs_own
     )
     sums = from_axis([sums] * nh, "h")
-    pred, pulled, weight, tops, message = call(
+    error, pulled, weight, tops, message = call(
         bind(residual_kernel, nxy, nh),
         [(rows, NY), (rows, NY), (rows, NY), (nxy * nh // 2, NY), (nxy, rows, NY)],
-        *sums, scratch=[(rows, NY)] * 2, far_out=(4,), sems=nxy,
-    )
-    program.hold(pred, pulled, weight)
+        *sums, scratch=[(rows, NY)], far_out=(4,), sems=nxy,
+    )
+    program.hold(error, pulled, weight)
     got = exchange(message, XY)
     (power,) = call(bind(power_kernel, nxy * nh), [(KEPT, NY)], tops)
     program.hold(power)
@@ -612,7 +610,7 @@
         second_kernel, [(nxy, rows, NY), (QX, NY), (QX, NY), (8, 128)],
         *shares, dens, full, *grads, *factors, *tables, scratch=[(NX, NY)],
     )
-    program.alive = [weight, pred, line, image, dens, base, alpha]
+    program.alive = [weight, error, line, image, dens, base, alpha]
     got = exchange(message, XY)
     pieces = reduce_comps(*after(pieces, message))
     grad2, image2, half = call(
@@ -620,7 +618,7 @@
         *pieces, alpha, base, dens, line,
     )
     (parts,) = call(bind(sum_kernel, nxy), [(rows + 8, NY)], got, half)
-    program.alive = [pred, image, dens, alpha, grad2]
+    program.alive = [error, image, dens, alpha, grad2]
     shares, image2 = call(
         bind(curvature_kernel, nh, part), [(nxy * 4, 128), (part, NY)],
         *from_axis([parts] * nh, "h"), image2, weight, scratch=[(rows, NY)],
@@ -630,7 +628,7 @@
     return tuple(
         call(
             finish_kernel, [density.shape, observed.shape],
-            shares, dens, grad2, alpha, pred, image, image2, obs_own, weight_own,
+            shares, dens, grad2, alpha, error, image, image2, weight_own,
         )
     )
 

time: 157 us -> 156 us (level)
  no operation moved by 1% of the time
where the time goes in v11:
time: 156 us; the launch traced here: 155 us
  starting transfers between devices  51.4 us (33%)
  blocking collectives  39.8 us (26%)
  waiting for transfers between devices  38.5 us (25%)
  Pallas kernels  19 us (12%)
  local copies, waits for them, and re-layouts  4.87 us (3%)
    all_to_all x2, blocking collectives, exchange(): return lax.all_to_all(value, axes, 0, 0, tiled=True)  39.8 us
    ppermute x9, starting transfers between devices, from_axis(): lax.ppermute(values[step], axis, [(i, (i + step) % size) for i in range(s...  20.4 us
    pallas_call x17, Pallas kernels, call(): pl.pallas_call(inner, out_shape=[(pltpu.HBM if place in far_out else jax....  19 us
    ppermute x10, starting transfers between devices, flip(): return lax.ppermute(value, axis, [(0, 1), (1, 0)])  15.4 us
    ppermute x10, waiting for transfers between devices, flip(): return lax.ppermute(value, axis, [(0, 1), (1, 0)])  14.1 us
    all_to_all x3, waiting for transfers between devices, exchange(): return lax.all_to_all(value, axes, 0, 0, tiled=True)  12.9 us
    all_to_all x3, starting transfers between devices, exchange(): return lax.all_to_all(value, axes, 0, 0, tiled=True)  11 us
    ppermute x9, waiting for transfers between devices, from_axis(): lax.ppermute(values[step], axis, [(i, (i + step) % size) for i in range(s...  9.47 us
  transfers between devices with their start and end apart: 25, of which 14 were waited for; matrix products, arithmetic and copies ran while one was open for 0% of the time, Pallas kernels for 5%

profile of v11, /device:TPU:1, one launch (start us, length us, event | category | flops | bytes accessed | tf_op | source)
XLA Modules:
  0.0 155.1 jit_solution(11469305508953758245)
XLA Ops:
  0.6 2.5 %collective-permute-start.1 = (f32[128,256]{1,0:T(8,128)}, f32[128,256]{1,0:T(8,128)S(1)}, u32[]{:S(2)}, u32[]{:S(2)}) collective-permute-start(f32[128,256]{1,0:T(8,128)} %bitcast.9), channel_id=1, source_target_pairs={{0,2},{2,0},{1,3},{3,1},{4,6},{6,4},{5,7},{7,5},{8,10},{10,8},{9,1... | collective-permute-start | bytes 393224 | tf_op jit(solution)/shard_map/ppermute | solution.py:518
  10.1 3.1 %shard_map.78 = (f32[16,72,256]{2,1,0:T(8,128)S(1)}, f32[512,256]{1,0:T(8,128)}) custom-call(f32[128,256]{1,0:T(8,128)S(1)} %get-tuple-element.47.refs_0_.refs_9_.refs_10_.refs_7_.refs_8_.refs_3_.refs_4_, f32[128,256]{1,0:T(8,128)S(1)} %collective-permute-done.refs_1_, f32[128,256]{1,0:T(8,128)S(1)} %collective-permute-done.1.refs_2_, ...), custom_call_target="tpu_custom_call" | custom-call | tf_op jit(solution)/shard_map/pallas_call | solution.py:494
  13.2 23.9 %all_to_all.31.refs_0_ = f32[16,72,256]{2,1,0:T(8,128)S(1)} all-to-all(f32[16,72,256]{2,1,0:T(8,128)S(1)} %get-tuple-element.55), channel_id=1, replica_groups=mesh['x'=4,'y'=4,'h'=4,'l'=2,'k'=2] {'x','y'}, dimensions={0} | all-to-all | bytes 2359296 | tf_op jit(solution)/shard_map/all_to_all | solution.py:535
  37.2 5.1 %collective-permute-start.5 = (f32[80,256]{1,0:T(8,128)S(1)}, f32[80,256]{1,0:T(8,128)S(1)}, u32[]{:S(2)}, u32[]{:S(2)}) collective-permute-start(f32[80,256]{1,0:T(8,128)S(1)} %shard_map.79.refs_0_), channel_id=1, source_target_pairs={{0,12},{4,0},{8,4},{12,8},{1,13},{5,1},{9,5},{13,9},{2,14},{6,2},{... | collective-permute-start | bytes 245768 | tf_op jit(solution)/shard_map/ppermute | solution.py:530
  42.2 1.3 collective-permute-start.4
  43.5 1.9 %collective-permute-start.3 = (f32[80,256]{1,0:T(8,128)S(1)}, f32[80,256]{1,0:T(8,128)S(1)}, u32[]{:S(2)}, u32[]{:S(2)}) collective-permute-start(f32[80,256]{1,0:T(8,128)S(1)} %shard_map.79.refs_0_), channel_id=1, source_target_pairs={{0,4},{4,8},{8,12},{12,0},{1,5},{5,9},{9,13},{13,1},{2,6},{6,10},{... | collective-permute-start | bytes 245768 | tf_op jit(solution)/shard_map/ppermute | solution.py:530
  45.5 4.2 %collective-permute-done.4.refs_2_ = f32[80,256]{1,0:T(8,128)S(1)} collective-permute-done((f32[80,256]{1,0:T(8,128)S(1)}, f32[80,256]{1,0:T(8,128)S(1)}, u32[]{:S(2)}, u32[]{:S(2)}) %collective-permute-start.4) | collective-permute-done | bytes 81952 | tf_op jit(solution)/shard_map/ppermute | solution.py:530
  51.4 3.8 %all-to-all-start.1 = ((f32[16,32,256]{2,1,0:T(8,128)}), f32[16,32,256]{2,1,0:T(8,128)S(1)}, u32[]{:S(2)}, u32[]{:S(2)}) async-start(f32[16,32,256]{2,1,0:T(8,128)} %get-tuple-element.56), calls=%async_computation.1 | async-start | bytes 1048576 | tf_op jit(solution)/shard_map/all_to_all | solution.py:535
  55.2 3.6 %shard_map.81.refs_4_.refs_12_.refs_10_.refs_13_.refs_18_ = f32[264,256]{1,0:T(8,128)S(1)} custom-call(f32[32,256]{1,0:T(8,128)S(1)} %get-tuple-element.57.refs_0_, bf16[4,256,256]{2,1,0:T(8,128)(2,1)S(1)} %get-tuple-element.52.refs_8_.refs_3_.refs_4_.refs_1_.refs_5_.refs_2_.refs_13_, ...), custom_call_target="tpu_custom_call" | custom-call | tf_op jit(solution)/shard_map/pallas_call | solution.py:494
  58.8 5.4 %all-to-all-done.1 = f32[16,32,256]{2,1,0:T(8,128)S(1)} async-done(((f32[16,32,256]{2,1,0:T(8,128)}), f32[16,32,256]{2,1,0:T(8,128)S(1)}, u32[]{:S(2)}, u32[]{:S(2)}) %all-to-all-start.1) | async-done | bytes 524320 | tf_op jit(solution)/shard_map/all_to_all | solution.py:535
  64.2 2.4 %shard_map.82 = (f32[320,256]{1,0:T(8,128)S(1)}, f32[320,256]{1,0:T(8,128)S(1)}) custom-call(f32[512,256]{1,0:T(8,128)S(1)} %bitcast.8, f32[264,256]{1,0:T(8,128)S(1)} %get-tuple-element.49.refs_5_.refs_6_.refs_7_.refs_4_.refs_1_.refs_8_.refs_10_, f32[264,256]{1,0:T(8,128)S(1)} %get-tuple-element.50.refs_6_.refs_7_.refs_8_.refs_5_.refs_2_.refs_9_.refs_11_, ...), custom_call_target="tpu_custom_call" | custom-call | tf_op jit(solution)/shard_map/pallas_call | solution.py:494
  66.6 5.0 %collective-permute-start.6 = (f32[320,256]{1,0:T(8,128)S(1)}, f32[320,256]{1,0:T(8,128)S(1)}, u32[]{:S(2)}, u32[]{:S(2)}) collective-permute-start(f32[320,256]{1,0:T(8,128)S(1)} %get-tuple-element.62), channel_id=1, source_target_pairs={{0,1},{1,0},{2,3},{3,2},{4,5},{5,4},{6,7},{7,6},{8,9},{9,8},{10,11... | collective-permute-start | bytes 983048 | tf_op jit(solution)/shard_map/ppermute | solution.py:518
  73.2 5.2 %collective-permute-done.7.refs_1_ = f32[160,256]{1,0:T(8,128)S(1)} collective-permute-done((f32[160,256]{1,0:T(8,128)S(1)}, f32[160,256]{1,0:T(8,128)S(1)}, u32[]{:S(2)}, u32[]{:S(2)}) %collective-permute-start.7) | collective-permute-done | bytes 163872 | tf_op jit(solution)/shard_map/ppermute | solution.py:518
  79.6 3.6 %all-to-all-start.2 = ((f32[16,40,256]{2,1,0:T(8,128)}), f32[16,40,256]{2,1,0:T(8,128)S(1)}, u32[]{:S(2)}, u32[]{:S(2)}) async-start(f32[16,40,256]{2,1,0:T(8,128)} %get-tuple-element.65), calls=%async_computation.2 | async-start | bytes 1310720 | tf_op jit(solution)/shard_map/all_to_all | solution.py:535
  83.5 1.5 collective-permute-start.8
  85.1 2.1 %collective-permute-done.9.refs_8_ = f32[128,256]{1,0:T(8,128)S(1)} collective-permute-done((f32[128,256]{1,0:T(8,128)S(1)}, f32[128,256]{1,0:T(8,128)S(1)}, u32[]{:S(2)}, u32[]{:S(2)}) %collective-permute-start.9) | collective-permute-done | bytes 131104 | tf_op jit(solution)/shard_map/ppermute | solution.py:518
  87.1 2.4 %collective-permute-start.10 = (f32[128,256]{1,0:T(8,128)S(1)}, f32[128,256]{1,0:T(8,128)S(1)}, u32[]{:S(2)}, u32[]{:S(2)}) collective-permute-start(f32[128,256]{1,0:T(8,128)S(1)} %collective-permute-done.9.refs_8_), channel_id=1, source_target_pairs={{0,1},{1,0},{2,3},{3,2},{4,5},{5,4},{6,7},{7,6},{8,9},{9,8},{10,11... | collective-permute-start | bytes 393224 | tf_op jit(solution)/shard_map/ppermute | solution.py:518
  91.5 3.3 %all-to-all-done.2.refs_0_ = f32[16,40,256]{2,1,0:T(8,128)S(1)} async-done(((f32[16,40,256]{2,1,0:T(8,128)}), f32[16,40,256]{2,1,0:T(8,128)S(1)}, u32[]{:S(2)}, u32[]{:S(2)}) %all-to-all-start.2) | async-done | bytes 655392 | tf_op jit(solution)/shard_map/all_to_all | solution.py:535
  94.8 1.8 %collective-permute-start.13 = (f32[8,256]{1,0:T(8,128)S(1)}, f32[8,256]{1,0:T(8,128)S(1)}, u32[]{:S(2)}, u32[]{:S(2)}) collective-permute-start(f32[8,256]{1,0:T(8,128)S(1)} %get-tuple-element.74.refs_0_), channel_id=1, source_target_pairs={{0,12},{4,0},{8,4},{12,8},{1,13},{5,1},{9,5},{13,9},{2,14},{6,2},{... | collective-permute-start | bytes 24584 | tf_op jit(solution)/shard_map/ppermute | solution.py:530
  96.6 2.1 %collective-permute-start.12 = (f32[8,256]{1,0:T(8,128)S(1)}, f32[8,256]{1,0:T(8,128)S(1)}, u32[]{:S(2)}, u32[]{:S(2)}) collective-permute-start(f32[8,256]{1,0:T(8,128)S(1)} %get-tuple-element.74.refs_0_), channel_id=1, source_target_pairs={{0,8},{4,12},{8,0},{12,4},{1,9},{5,13},{9,1},{13,5},{2,10},{6,14},... | collective-permute-start | bytes 24584 | tf_op jit(solution)/shard_map/ppermute | solution.py:530
  98.7 2.3 %collective-permute-start.11 = (f32[8,256]{1,0:T(8,128)S(1)}, f32[8,256]{1,0:T(8,128)S(1)}, u32[]{:S(2)}, u32[]{:S(2)}) collective-permute-start(f32[8,256]{1,0:T(8,128)S(1)} %get-tuple-element.74.refs_0_), channel_id=1, source_target_pairs={{0,4},{4,8},{8,12},{12,0},{1,5},{5,9},{9,13},{13,1},{2,6},{6,10},{... | collective-permute-start | bytes 24584 | tf_op jit(solution)/shard_map/ppermute | solution.py:530
  101.0 3.2 %shard_map.86 = (f32[320,256]{1,0:T(8,128)S(1)}, f32[320,256]{1,0:T(8,128)}) custom-call(f32[512,256]{1,0:T(8,128)S(1)} %get-tuple-element.71.refs_0_, f32[264,256]{1,0:T(8,128)S(1)} %get-tuple-element.49.refs_5_.refs_6_.refs_7_.refs_4_.refs_1_.refs_8_.refs_10_, f32[264,256]{1,0:T(8,128)S(1)} %get-tuple-element.50.refs_6_.refs_7_.refs_8_.refs_5_.refs_2_.refs_9_.refs_11_, ...), custom_call_target="tpu_custom_call" | custom-call | tf_op jit(solution)/shard_map/pallas_call | solution.py:494
  104.2 4.0 %collective-permute-start.16 = (f32[8,256]{1,0:T(8,128)S(1)}, f32[8,256]{1,0:T(8,128)S(1)}, u32[]{:S(2)}, u32[]{:S(2)}) collective-permute-start(f32[8,256]{1,0:T(8,128)S(1)} %shard_map.87.refs_0_), channel_id=1, source_target_pairs={{0,3},{1,2},{2,1},{3,0},{4,7},{5,6},{6,5},{7,4},{8,11},{9,10},{10,... | collective-permute-start | bytes 24584 | tf_op jit(solution)/shard_map/ppermute | solution.py:513
  110.8 2.7 %shard_map.88 = (f32[16,32,256]{2,1,0:T(8,128)}, f32[128,256]{1,0:T(8,128)S(1)}, f32[128,256]{1,0:T(8,128)S(1)}, f32[8,128]{1,0:T(8,128)S(1)}) custom-call(f32[8,256]{1,0:T(8,128)S(1)} %shard_map.87.refs_0_, f32[8,256]{1,0:T(8,128)S(1)} %collective-permute-done.14.refs_1_, f32[8,256]{1,0:T(8,128)S(1)} %collective-permute-done.15.refs_2_, ...), custom_call_target="tpu_custom_call" | custom-call | tf_op jit(solution)/shard_map/pallas_call | solution.py:494
  113.9 3.6 %all-to-all-start.3 = ((f32[16,32,256]{2,1,0:T(8,128)}), f32[16,32,256]{2,1,0:T(8,128)S(1)}, u32[]{:S(2)}, u32[]{:S(2)}) async-start(f32[16,32,256]{2,1,0:T(8,128)} %get-tuple-element.79), calls=%async_computation.3 | async-start | bytes 1048576 | tf_op jit(solution)/shard_map/all_to_all | solution.py:535
  118.6 4.6 %collective-permute-done.18.refs_1_ = f32[160,256]{1,0:T(8,128)S(1)} collective-permute-done((f32[160,256]{1,0:T(8,128)S(1)}, f32[160,256]{1,0:T(8,128)S(1)}, u32[]{:S(2)}, u32[]{:S(2)}) %collective-permute-start.18) | collective-permute-done | bytes 163872 | tf_op jit(solution)/shard_map/ppermute | solution.py:518
  123.5 4.2 %all-to-all-done.3.refs_0_ = f32[16,32,256]{2,1,0:T(8,128)S(1)} async-done(((f32[16,32,256]{2,1,0:T(8,128)}), f32[16,32,256]{2,1,0:T(8,128)S(1)}, u32[]{:S(2)}, u32[]{:S(2)}) %all-to-all-start.3) | async-done | bytes 524320 | tf_op jit(solution)/shard_map/all_to_all | solution.py:535
  127.7 1.9 %collective-permute-start.21 = (f32[40,256]{1,0:T(8,128)S(1)}, f32[40,256]{1,0:T(8,128)S(1)}, u32[]{:S(2)}, u32[]{:S(2)}) collective-permute-start(f32[40,256]{1,0:T(8,128)S(1)} %shard_map.91.refs_0_), channel_id=1, source_target_pairs={{0,12},{4,0},{8,4},{12,8},{1,13},{5,1},{9,5},{13,9},{2,14},{6,2},{... | collective-permute-start | bytes 122888 | tf_op jit(solution)/shard_map/ppermute | solution.py:530
  129.5 3.1 %collective-permute-start.20 = (f32[40,256]{1,0:T(8,128)S(1)}, f32[40,256]{1,0:T(8,128)S(1)}, u32[]{:S(2)}, u32[]{:S(2)}) collective-permute-start(f32[40,256]{1,0:T(8,128)S(1)} %shard_map.91.refs_0_), channel_id=1, source_target_pairs={{0,8},{4,12},{8,0},{12,4},{1,9},{5,13},{9,1},{13,5},{2,10},{6,14},... | collective-permute-start | bytes 122888 | tf_op jit(solution)/shard_map/ppermute | solution.py:530
  133.7 2.6 %collective-permute-done.20.refs_2_ = f32[40,256]{1,0:T(8,128)S(1)} collective-permute-done((f32[40,256]{1,0:T(8,128)S(1)}, f32[40,256]{1,0:T(8,128)S(1)}, u32[]{:S(2)}, u32[]{:S(2)}) %collective-permute-start.20) | collective-permute-done | bytes 40992 | tf_op jit(solution)/shard_map/ppermute | solution.py:530
  136.3 1.9 %collective-permute-done.19.refs_1_ = f32[40,256]{1,0:T(8,128)S(1)} collective-permute-done((f32[40,256]{1,0:T(8,128)S(1)}, f32[40,256]{1,0:T(8,128)S(1)}, u32[]{:S(2)}, u32[]{:S(2)}) %collective-permute-start.19) | collective-permute-done | bytes 40992 | tf_op jit(solution)/shard_map/ppermute | solution.py:530
  138.4 15.9 %all_to_all.32 = f32[64,1,128]{2,1,0:T(1,128)S(1)} all-to-all(f32[64,1,128]{2,1,0:T(1,128)S(1)} %bitcast.14), channel_id=1, replica_groups=mesh['x'=4,'y'=4,'h'=4,'l'=2,'k'=2] {'x','y','l','k'}, dimensions={0} | all-to-all | bytes 65536 | tf_op jit(solution)/shard_map/all_to_all | solution.py:535
  (61 shorter events, 19.5 us)
Async XLA Ops:
  0.6 7.5 %collective-permute-start.1 = (f32[128,256]{1,0:T(8,128)}, f32[128,256]{1,0:T(8,128)S(1)}, u32[]{:S(2)}, u32[]{:S(2)}) collective-permute-start(f32[128,256]{1,0:T(8,128)} %bitcast.9), channel_id=1, source_target_pairs={{0,2},{2,0},{1,3},{3,1},{4,6},{6,4},{5,7},{7,5},{8,10},{10,8},{9,1... | collective-permute-start | bytes 393224 | tf_op jit(solution)/shard_map/ppermute | solution.py:518
  3.2 5.9 %collective-permute-start = (f32[128,256]{1,0:T(8,128)}, f32[128,256]{1,0:T(8,128)S(1)}, u32[]{:S(2)}, u32[]{:S(2)}) collective-permute-start(f32[128,256]{1,0:T(8,128)} %bitcast.10), channel_id=1, source_target_pairs={{0,1},{1,0},{2,3},{3,2},{4,5},{5,4},{6,7},{7,6},{8,9},{9,8},{10,11... | collective-permute-start | bytes 393224 | tf_op jit(solution)/shard_map/ppermute | solution.py:518
  4.8 1.0 copy-start.1
  8.2 1.9 %collective-permute-start.2 = (f32[128,256]{1,0:T(8,128)S(1)}, f32[128,256]{1,0:T(8,128)S(1)}, u32[]{:S(2)}, u32[]{:S(2)}) collective-permute-start(f32[128,256]{1,0:T(8,128)S(1)} %collective-permute-done.1.refs_2_), channel_id=1, source_target_pairs={{0,1},{1,0},{2,3},{3,2},{4,5},{5,4},{6,7},{7,6},{8,9},{9,8},{10,11... | collective-permute-start | bytes 393224 | tf_op jit(solution)/shard_map/ppermute | solution.py:518
  13.2 23.9 %copy-start.10 = (f32[1,8,256]{2,1,0:T(8,128)S(1)}, f32[1,8,256]{2,1,0:T(8,128)}, u32[]{:S(2)}) copy-start(f32[1,8,256]{2,1,0:T(8,128)} %param.8) | copy-start | bytes 24580
  13.2 23.9 %copy-start.11 = (f32[1,8,256]{2,1,0:T(8,128)S(1)}, f32[1,8,256]{2,1,0:T(8,128)}, u32[]{:S(2)}) copy-start(f32[1,8,256]{2,1,0:T(8,128)} %param.7) | copy-start | bytes 24580
  37.2 8.3 %collective-permute-start.5 = (f32[80,256]{1,0:T(8,128)S(1)}, f32[80,256]{1,0:T(8,128)S(1)}, u32[]{:S(2)}, u32[]{:S(2)}) collective-permute-start(f32[80,256]{1,0:T(8,128)S(1)} %shard_map.79.refs_0_), channel_id=1, source_target_pairs={{0,12},{4,0},{8,4},{12,8},{1,13},{5,1},{9,5},{13,9},{2,14},{6,2},{... | collective-permute-start | bytes 245768 | tf_op jit(solution)/shard_map/ppermute | solution.py:530
  42.2 7.4 %collective-permute-start.4 = (f32[80,256]{1,0:T(8,128)S(1)}, f32[80,256]{1,0:T(8,128)S(1)}, u32[]{:S(2)}, u32[]{:S(2)}) collective-permute-start(f32[80,256]{1,0:T(8,128)S(1)} %shard_map.79.refs_0_), channel_id=1, source_target_pairs={{0,8},{4,12},{8,0},{12,4},{1,9},{5,13},{9,1},{13,5},{2,10},{6,14},... | collective-permute-start | bytes 245768 | tf_op jit(solution)/shard_map/ppermute | solution.py:530
  43.5 6.8 %collective-permute-start.3 = (f32[80,256]{1,0:T(8,128)S(1)}, f32[80,256]{1,0:T(8,128)S(1)}, u32[]{:S(2)}, u32[]{:S(2)}) collective-permute-start(f32[80,256]{1,0:T(8,128)S(1)} %shard_map.79.refs_0_), channel_id=1, source_target_pairs={{0,4},{4,8},{8,12},{12,0},{1,5},{5,9},{9,13},{13,1},{2,6},{6,10},{... | collective-permute-start | bytes 245768 | tf_op jit(solution)/shard_map/ppermute | solution.py:530
  51.4 12.8 %all-to-all-start.1 = ((f32[16,32,256]{2,1,0:T(8,128)}), f32[16,32,256]{2,1,0:T(8,128)S(1)}, u32[]{:S(2)}, u32[]{:S(2)}) async-start(f32[16,32,256]{2,1,0:T(8,128)} %get-tuple-element.56), calls=%async_computation.1 | async-start | bytes 1048576 | tf_op jit(solution)/shard_map/all_to_all | solution.py:535
  66.6 6.3 %collective-permute-start.6 = (f32[320,256]{1,0:T(8,128)S(1)}, f32[320,256]{1,0:T(8,128)S(1)}, u32[]{:S(2)}, u32[]{:S(2)}) collective-permute-start(f32[320,256]{1,0:T(8,128)S(1)} %get-tuple-element.62), channel_id=1, source_target_pairs={{0,1},{1,0},{2,3},{3,2},{4,5},{5,4},{6,7},{7,6},{8,9},{9,8},{10,11... | collective-permute-start | bytes 983048 | tf_op jit(solution)/shard_map/ppermute | solution.py:518
  72.9 5.5 %collective-permute-start.7 = (f32[160,256]{1,0:T(8,128)S(1)}, f32[160,256]{1,0:T(8,128)S(1)}, u32[]{:S(2)}, u32[]{:S(2)}) collective-permute-start(f32[160,256]{1,0:T(8,128)S(1)} %get-tuple-element.64), channel_id=1, source_target_pairs={{0,2},{2,0},{1,3},{3,1},{4,6},{6,4},{5,7},{7,5},{8,10},{10,8},{9,1... | collective-permute-start | bytes 491528 | tf_op jit(solution)/shard_map/ppermute | solution.py:518
  79.6 15.2 %all-to-all-start.2 = ((f32[16,40,256]{2,1,0:T(8,128)}), f32[16,40,256]{2,1,0:T(8,128)S(1)}, u32[]{:S(2)}, u32[]{:S(2)}) async-start(f32[16,40,256]{2,1,0:T(8,128)} %get-tuple-element.65), calls=%async_computation.2 | async-start | bytes 1310720 | tf_op jit(solution)/shard_map/all_to_all | solution.py:535
  83.2 3.9 %collective-permute-start.9 = (f32[128,256]{1,0:T(8,128)S(1)}, f32[128,256]{1,0:T(8,128)S(1)}, u32[]{:S(2)}, u32[]{:S(2)}) collective-permute-start(f32[128,256]{1,0:T(8,128)S(1)} %get-tuple-element.66.refs_6_), channel_id=1, source_target_pairs={{0,2},{2,0},{1,3},{3,1},{4,6},{6,4},{5,7},{7,5},{8,10},{10,8},{9,1... | collective-permute-start | bytes 393224 | tf_op jit(solution)/shard_map/ppermute | solution.py:518
  83.5 6.6 %collective-permute-start.8 = (f32[128,256]{1,0:T(8,128)S(1)}, f32[128,256]{1,0:T(8,128)S(1)}, u32[]{:S(2)}, u32[]{:S(2)}) collective-permute-start(f32[128,256]{1,0:T(8,128)S(1)} %get-tuple-element.66.refs_6_), channel_id=1, source_target_pairs={{0,1},{1,0},{2,3},{3,2},{4,5},{5,4},{6,7},{7,6},{8,9},{9,8},{10,11... | collective-permute-start | bytes 393224 | tf_op jit(solution)/shard_map/ppermute | solution.py:518
  87.1 3.7 %collective-permute-start.10 = (f32[128,256]{1,0:T(8,128)S(1)}, f32[128,256]{1,0:T(8,128)S(1)}, u32[]{:S(2)}, u32[]{:S(2)}) collective-permute-start(f32[128,256]{1,0:T(8,128)S(1)} %collective-permute-done.9.refs_8_), channel_id=1, source_target_pairs={{0,1},{1,0},{2,3},{3,2},{4,5},{5,4},{6,7},{7,6},{8,9},{9,8},{10,11... | collective-permute-start | bytes 393224 | tf_op jit(solution)/shard_map/ppermute | solution.py:518
  94.8 9.3 %collective-permute-start.13 = (f32[8,256]{1,0:T(8,128)S(1)}, f32[8,256]{1,0:T(8,128)S(1)}, u32[]{:S(2)}, u32[]{:S(2)}) collective-permute-start(f32[8,256]{1,0:T(8,128)S(1)} %get-tuple-element.74.refs_0_), channel_id=1, source_target_pairs={{0,12},{4,0},{8,4},{12,8},{1,13},{5,1},{9,5},{13,9},{2,14},{6,2},{... | collective-permute-start | bytes 24584 | tf_op jit(solution)/shard_map/ppermute | solution.py:530
  96.6 7.6 %collective-permute-start.12 = (f32[8,256]{1,0:T(8,128)S(1)}, f32[8,256]{1,0:T(8,128)S(1)}, u32[]{:S(2)}, u32[]{:S(2)}) collective-permute-start(f32[8,256]{1,0:T(8,128)S(1)} %get-tuple-element.74.refs_0_), channel_id=1, source_target_pairs={{0,8},{4,12},{8,0},{12,4},{1,9},{5,13},{9,1},{13,5},{2,10},{6,14},... | collective-permute-start | bytes 24584 | tf_op jit(solution)/shard_map/ppermute | solution.py:530
  98.7 5.4 %collective-permute-start.11 = (f32[8,256]{1,0:T(8,128)S(1)}, f32[8,256]{1,0:T(8,128)S(1)}, u32[]{:S(2)}, u32[]{:S(2)}) collective-permute-start(f32[8,256]{1,0:T(8,128)S(1)} %get-tuple-element.74.refs_0_), channel_id=1, source_target_pairs={{0,4},{4,8},{8,12},{12,0},{1,5},{5,9},{9,13},{13,1},{2,6},{6,10},{... | collective-permute-start | bytes 24584 | tf_op jit(solution)/shard_map/ppermute | solution.py:530
  104.2 6.6 %copy-start = (f32[512,256]{1,0:T(8,128)S(1)}, f32[512,256]{1,0:T(8,128)}, u32[]{:S(2)}) copy-start(f32[512,256]{1,0:T(8,128)} %get-tuple-element.78.refs_5_) | copy-start | bytes 1572868
  104.2 6.6 %copy-start.5 = (f32[128,256]{1,0:T(8,128)S(1)}, f32[128,256]{1,0:T(8,128)}, u32[]{:S(2)}) copy-start(f32[128,256]{1,0:T(8,128)} %copy-done.4) | copy-start | bytes 393220
  104.2 6.6 %copy-start.7 = (f32[128,256]{1,0:T(8,128)S(1)}, f32[128,256]{1,0:T(8,128)}, u32[]{:S(2)}) copy-start(f32[128,256]{1,0:T(8,128)} %copy-done.6) | copy-start | bytes 393220
  104.2 6.6 %copy-start.9 = (f32[128,256]{1,0:T(8,128)S(1)}, f32[128,256]{1,0:T(8,128)}, u32[]{:S(2)}) copy-start(f32[128,256]{1,0:T(8,128)} %copy-done.8) | copy-start | bytes 393220
  104.2 5.4 %collective-permute-start.16 = (f32[8,256]{1,0:T(8,128)S(1)}, f32[8,256]{1,0:T(8,128)S(1)}, u32[]{:S(2)}, u32[]{:S(2)}) collective-permute-start(f32[8,256]{1,0:T(8,128)S(1)} %shard_map.87.refs_0_), channel_id=1, source_target_pairs={{0,3},{1,2},{2,1},{3,0},{4,7},{5,6},{6,5},{7,4},{8,11},{9,10},{10,... | collective-permute-start | bytes 24584 | tf_op jit(solution)/shard_map/ppermute | solution.py:513
  108.3 2.5 %collective-permute-start.15 = (f32[8,256]{1,0:T(8,128)S(1)}, f32[8,256]{1,0:T(8,128)S(1)}, u32[]{:S(2)}, u32[]{:S(2)}) collective-permute-start(f32[8,256]{1,0:T(8,128)S(1)} %shard_map.87.refs_0_), channel_id=1, source_target_pairs={{0,2},{1,3},{2,0},{3,1},{4,6},{5,7},{6,4},{7,5},{8,10},{9,11},{10,... | collective-permute-start | bytes 24584 | tf_op jit(solution)/shard_map/ppermute | solution.py:513
  108.7 2.0 %collective-permute-start.14 = (f32[8,256]{1,0:T(8,128)S(1)}, f32[8,256]{1,0:T(8,128)S(1)}, u32[]{:S(2)}, u32[]{:S(2)}) collective-permute-start(f32[8,256]{1,0:T(8,128)S(1)} %shard_map.87.refs_0_), channel_id=1, source_target_pairs={{0,1},{1,0},{2,3},{3,2},{4,5},{5,4},{6,7},{7,6},{8,9},{9,8},{10,11... | collective-permute-start | bytes 24584 | tf_op jit(solution)/shard_map/ppermute | solution.py:513
  113.5 3.9 %collective-permute-start.17 = (f32[320,256]{1,0:T(8,128)}, f32[320,256]{1,0:T(8,128)S(1)}, u32[]{:S(2)}, u32[]{:S(2)}) collective-permute-start(f32[320,256]{1,0:T(8,128)} %get-tuple-element.81), channel_id=1, source_target_pairs={{0,1},{1,0},{2,3},{3,2},{4,5},{5,4},{6,7},{7,6},{8,9},{9,8},{10,11... | collective-permute-start | bytes 983048 | tf_op jit(solution)/shard_map/ppermute | solution.py:518
  113.9 13.7 %all-to-all-start.3 = ((f32[16,32,256]{2,1,0:T(8,128)}), f32[16,32,256]{2,1,0:T(8,128)S(1)}, u32[]{:S(2)}, u32[]{:S(2)}) async-start(f32[16,32,256]{2,1,0:T(8,128)} %get-tuple-element.79), calls=%async_computation.3 | async-start | bytes 1048576 | tf_op jit(solution)/shard_map/all_to_all | solution.py:535
  117.5 5.7 %collective-permute-start.18 = (f32[160,256]{1,0:T(8,128)S(1)}, f32[160,256]{1,0:T(8,128)S(1)}, u32[]{:S(2)}, u32[]{:S(2)}) collective-permute-start(f32[160,256]{1,0:T(8,128)S(1)} %get-tuple-element.86), channel_id=1, source_target_pairs={{0,2},{2,0},{1,3},{3,1},{4,6},{6,4},{5,7},{7,5},{8,10},{10,8},{9,1... | collective-permute-start | bytes 491528 | tf_op jit(solution)/shard_map/ppermute | solution.py:518
  127.7 6.0 %collective-permute-start.21 = (f32[40,256]{1,0:T(8,128)S(1)}, f32[40,256]{1,0:T(8,128)S(1)}, u32[]{:S(2)}, u32[]{:S(2)}) collective-permute-start(f32[40,256]{1,0:T(8,128)S(1)} %shard_map.91.refs_0_), channel_id=1, source_target_pairs={{0,12},{4,0},{8,4},{12,8},{1,13},{5,1},{9,5},{13,9},{2,14},{6,2},{... | collective-permute-start | bytes 122888 | tf_op jit(solution)/shard_map/ppermute | solution.py:530
  129.5 6.8 %collective-permute-start.20 = (f32[40,256]{1,0:T(8,128)S(1)}, f32[40,256]{1,0:T(8,128)S(1)}, u32[]{:S(2)}, u32[]{:S(2)}) collective-permute-start(f32[40,256]{1,0:T(8,128)S(1)} %shard_map.91.refs_0_), channel_id=1, source_target_pairs={{0,8},{4,12},{8,0},{12,4},{1,9},{5,13},{9,1},{13,5},{2,10},{6,14},... | collective-permute-start | bytes 122888 | tf_op jit(solution)/shard_map/ppermute | solution.py:530
  132.6 5.6 %collective-permute-start.19 = (f32[40,256]{1,0:T(8,128)S(1)}, f32[40,256]{1,0:T(8,128)S(1)}, u32[]{:S(2)}, u32[]{:S(2)}) collective-permute-start(f32[40,256]{1,0:T(8,128)S(1)} %shard_map.91.refs_0_), channel_id=1, source_target_pairs={{0,4},{4,8},{8,12},{12,0},{1,5},{5,9},{9,13},{13,1},{2,6},{6,10},{... | collective-permute-start | bytes 122888 | tf_op jit(solution)/shard_map/ppermute | solution.py:530
  (5 other events, 3.8 us)

commit v12 on v11

--- a/solution.py
+++ b/solution.py
@@ -381,35 +381,45 @@
     total = got_ref[0, rows:, :]
     for source in range(1, nxy):
         total = total + got_ref[source, rows:, :]
-    share_ref[...] = total
+    share_ref[...] = jnp.broadcast_to(total[:1, :128], share_ref.shape)
     for source in range(nxy):
         plane_ref[source * rows : (source + 1) * rows] = got_ref[source, :rows, :]
 
 
-def add_kernel(*refs):
-    total = refs[0][...]
-    for part in refs[1:-1]:
-        total = total + part[...]
-    refs[-1][...] = total
-
-
 def second_kernel(
-    s0, s1, s2, s3, dens_ref, full_ref, g0, g1, g2, g3, decay_ref, gx_ref, gy_ref, fx, bx, ty,
-    out_ref, dens_out, base_out, alpha_ref, all_ref,
+    shares_ref, dens_ref, full_ref, g0, g1, g2, g3, decay_ref, gx_ref, gy_ref, fx, bx, ty,
+    out_ref, dens_out, base_out, alpha_ref, all_ref, near_ref, sems,
 ):
-    gather_rows((g0, g1, g2, g3), all_ref)
-    alpha = step_length(s0[:1] + s1[:1] + (s2[:1] + s3[:1]))
+    comp = comp_index()
+    copies = [pltpu.make_async_copy(full_ref, near_ref, sems.at[4])]
+    for step, piece in enumerate((g0, g1, g2, g3)):
+        place = pl.ds(pl.multiple_of(jnp.bitwise_xor(comp, step) * QX, QX), QX)
+        copies.append(pltpu.make_async_copy(piece, all_ref.at[place, :], sems.at[step]))
+    for copy in copies:
+        copy.start()
+    alpha = step_length(shares_ref[...])
     alpha_ref[...] = jnp.broadcast_to(alpha, alpha_ref.shape)
     old = dens_ref[...]
-    grad = g0[...]
+    for copy in copies:
+        copy.wait()
+    grad = all_ref[pl.ds(pl.multiple_of(comp * QX, QX), QX), :]
     dens = old - alpha * grad
     dens_out[...] = dens
     data = grad - 0.5 * ((1.0 / (old * old + 0.25)) * old)
     base_out[...] = data + 0.5 * (dens * (1.0 / (dens * dens + 0.25)))
-    dens = full_ref[...] - alpha * all_ref[...]
+    dens = near_ref[...] - alpha * all_ref[...]
     all_ref[...] = 0.5 * (dens * (1.0 / (dens * dens + 0.25)))
     plane = forward_plane(all_ref[...], decay_ref, gx_ref, gy_ref, fx, bx, ty)
-    out_ref[...] = plane.reshape(out_ref.shape)
+    near_ref[...] = plane
+    rows = out_ref.shape[1]
+    copies = [
+        pltpu.make_async_copy(near_ref.at[pl.ds(place * rows, rows), :], out_ref.at[place], sems.at[place])
+        for place in range(out_ref.shape[0])
+    ]
+    for copy in copies:
+        copy.start()
+    for copy in copies:
+        copy.wait()
 
 
 def sum_kernel(nxy, got_ref, half_ref, sum_ref):
@@ -482,7 +492,7 @@
     def drop(self, *values):
         self.alive = [item for item in self.alive if all(item is not value for value in values)]
 
-    def call(self, kernel, outs, *args, scratch=(), scalars=(), far_out=(), sems=0, mib=8):
+    def call(self, kernel, outs, *args, scratch=(), scalars=(), far=(), far_out=(), sems=0, mib=8):
         used = len(args)
         keep = [item for item in self.alive if all(item is not value for value in args)]
         kept = len(keep)
@@ -490,6 +500,10 @@
         def inner(*refs):
             kernel(*refs[:used], *refs[used + kept :])
 
+        args = [
+            pltpu.with_memory_space_constraint(item, pltpu.HBM) if place in far else item
+            for place, item in enumerate(args)
+        ]
         kinds = [(item, F32) if isinstance(item, tuple) else (item.shape, item.dtype) for item in outs]
         return pl.pallas_call(
             inner,
@@ -498,7 +512,8 @@
                 for place, kind in enumerate(kinds)
             ],
             in_specs=[
-                SMEM if place in scalars else VMEM for place in range(used)
+                SMEM if place in scalars else FAR if place in far else VMEM
+                for place in range(used)
             ]
             + [ANY] * kept,
             out_specs=[FAR if place in far_out else VMEM for place in range(len(outs))],
@@ -601,14 +616,13 @@
     program.hold(line, image)
     grads = gather_comps(grad)
     got = after(exchange(message, XY), *grads)
-    plane, shares = call(bind(part_kernel, nxy), [(NX, NY), (8, NY)], got)
+    plane, shares = call(bind(part_kernel, nxy), [(NX, NY), (nh * 4, 128)], got)
     pieces = adjoint(plane)
-    shares = after(from_axis([shares] * nh, "h"), *pieces)
-    (shares,) = call(add_kernel, [(8, NY)], *shares)
-    shares = from_comps([shares] * 4)
+    shares = after(exchange(shares, ("h", *COMP)), *pieces)
     message, dens, base, alpha = call(
         second_kernel, [(nxy, rows, NY), (QX, NY), (QX, NY), (8, 128)],
-        *shares, dens, full, *grads, *factors, *tables, scratch=[(NX, NY)],
+        shares, dens, full, *grads, *factors, *tables,
+        scratch=[(NX, NY)] * 2, far=(2, 3, 4, 5, 6), far_out=(0,), sems=max(nxy, 5),
     )
     program.alive = [weight, error, line, image, dens, base, alpha]
     got = exchange(message, XY)

time: 156 us -> 156 us (level)
  starting transfers between devices: 51.4 us -> 46.9 us
  Pallas kernels: 19 us -> 20.8 us
  waiting for transfers between devices: 38.5 us -> 40.1 us
    all_to_all x3 -> x4, starting transfers between devices: 11 us -> 18.5 us  [exchange(): return lax.all_to_all(value, axes, 0, 0, tiled=True)]
    ppermute x9 -> x6, starting transfers between devices: 20.4 us -> 13.3 us  [from_axis(): lax.ppermute(values[step], axis, [(i, (i + step) % size) for i in range(s...]
    ppermute x3 -> x0, starting transfers between devices: 4.54 us -> none  [from_comps(): lax.ppermute(values[step], COMP, [(i, i ^ step) for i in range(4)])]
    all_to_all x3 -> x4, waiting for transfers between devices: 12.9 us -> 16.1 us  [exchange(): return lax.all_to_all(value, axes, 0, 0, tiled=True)]
    ppermute x3 -> x0, waiting for transfers between devices: 2.01 us -> none  [from_comps(): lax.ppermute(values[step], COMP, [(i, i ^ step) for i in range(4)])]
    pallas_call x17 -> x16, Pallas kernels: 19 us -> 20.8 us  [call(): pl.pallas_call(inner, out_shape=[(pltpu.HBM if place in far_out else jax....]
    ppermute x9 -> x6, waiting for transfers between devices: 9.47 us -> 8.59 us  [from_axis(): lax.ppermute(values[step], axis, [(i, (i + step) % size) for i in range(s...]
  transfers between devices with their start and end apart: 25 -> 20, of which waited for: 14 -> 14; matrix products, arithmetic and copies ran while one was open for 0% -> 0% of each run, Pallas kernels for 5% -> 5%
where the time goes in v12:
time: 156 us; the launch traced here: 155 us
  starting transfers between devices  46.9 us (30%)
  waiting for transfers between devices  40.1 us (26%)
  blocking collectives  39.8 us (26%)
  Pallas kernels  20.8 us (13%)
  local copies, waits for them, and re-layouts  6.12 us (4%)
    all_to_all x2, blocking collectives, exchange(): return lax.all_to_all(value, axes, 0, 0, tiled=True)  39.8 us
    pallas_call x16, Pallas kernels, call(): pl.pallas_call(inner, out_shape=[(pltpu.HBM if place in far_out else jax....  20.8 us
    all_to_all x4, starting transfers between devices, exchange(): return lax.all_to_all(value, axes, 0, 0, tiled=True)  18.5 us
    all_to_all x4, waiting for transfers between devices, exchange(): return lax.all_to_all(value, axes, 0, 0, tiled=True)  16.1 us
    ppermute x10, waiting for transfers between devices, flip(): return lax.ppermute(value, axis, [(0, 1), (1, 0)])  15.4 us
    ppermute x10, starting transfers between devices, flip(): return lax.ppermute(value, axis, [(0, 1), (1, 0)])  15.1 us
    ppermute x6, starting transfers between devices, from_axis(): lax.ppermute(values[step], axis, [(i, (i + step) % size) for i in range(s...  13.3 us
    ppermute x6, waiting for transfers between devices, from_axis(): lax.ppermute(values[step], axis, [(i, (i + step) % size) for i in range(s...  8.59 us
  transfers between devices with their start and end apart: 20, of which 14 were waited for; matrix products, arithmetic and copies ran while one was open for 0% of the time, Pallas kernels for 5%

profile of v12, /device:TPU:1, one launch (start us, length us, event | category | flops | bytes accessed | tf_op | source)
XLA Modules:
  0.0 155.2 jit_solution(8872868068070171790)
XLA Ops:
  0.6 2.5 %collective-permute-start.1 = (f32[128,256]{1,0:T(8,128)}, f32[128,256]{1,0:T(8,128)S(1)}, u32[]{:S(2)}, u32[]{:S(2)}) collective-permute-start(f32[128,256]{1,0:T(8,128)} %bitcast.13), channel_id=1, source_target_pairs={{0,2},{2,0},{1,3},{3,1},{4,6},{6,4},{5,7},{7,5},{8,10},{10,8},{9,1... | collective-permute-start | bytes 393224 | tf_op jit(solution)/shard_map/ppermute | solution.py:533
  10.1 3.1 %shard_map.78 = (f32[16,72,256]{2,1,0:T(8,128)S(1)}, f32[512,256]{1,0:T(8,128)}) custom-call(f32[128,256]{1,0:T(8,128)S(1)} %get-tuple-element.44.refs_0_.refs_9_.refs_10_.refs_7_.refs_8_.refs_3_.refs_1_, f32[128,256]{1,0:T(8,128)S(1)} %collective-permute-done.refs_1_, f32[128,256]{1,0:T(8,128)S(1)} %collective-permute-done.1.refs_2_, ...), custom_call_target="tpu_custom_call" | custom-call | tf_op jit(solution)/shard_map/pallas_call | solution.py:508
  13.2 23.9 %all_to_all.43.refs_0_ = f32[16,72,256]{2,1,0:T(8,128)S(1)} all-to-all(f32[16,72,256]{2,1,0:T(8,128)S(1)} %get-tuple-element.52), channel_id=1, replica_groups=mesh['x'=4,'y'=4,'h'=4,'l'=2,'k'=2] {'x','y'}, dimensions={0} | all-to-all | bytes 2359296 | tf_op jit(solution)/shard_map/all_to_all | solution.py:550
  37.2 5.1 %collective-permute-start.5 = (f32[80,256]{1,0:T(8,128)S(1)}, f32[80,256]{1,0:T(8,128)S(1)}, u32[]{:S(2)}, u32[]{:S(2)}) collective-permute-start(f32[80,256]{1,0:T(8,128)S(1)} %shard_map.79.refs_0_), channel_id=1, source_target_pairs={{0,12},{4,0},{8,4},{12,8},{1,13},{5,1},{9,5},{13,9},{2,14},{6,2},{... | collective-permute-start | bytes 245768 | tf_op jit(solution)/shard_map/ppermute | solution.py:545
  42.2 1.3 collective-permute-start.4
  43.5 1.9 %collective-permute-start.3 = (f32[80,256]{1,0:T(8,128)S(1)}, f32[80,256]{1,0:T(8,128)S(1)}, u32[]{:S(2)}, u32[]{:S(2)}) collective-permute-start(f32[80,256]{1,0:T(8,128)S(1)} %shard_map.79.refs_0_), channel_id=1, source_target_pairs={{0,4},{4,8},{8,12},{12,0},{1,5},{5,9},{9,13},{13,1},{2,6},{6,10},{... | collective-permute-start | bytes 245768 | tf_op jit(solution)/shard_map/ppermute | solution.py:545
  45.5 4.2 %collective-permute-done.4.refs_2_ = f32[80,256]{1,0:T(8,128)S(1)} collective-permute-done((f32[80,256]{1,0:T(8,128)S(1)}, f32[80,256]{1,0:T(8,128)S(1)}, u32[]{:S(2)}, u32[]{:S(2)}) %collective-permute-start.4) | collective-permute-done | bytes 81952 | tf_op jit(solution)/shard_map/ppermute | solution.py:545
  51.4 3.8 %all-to-all-start.1 = ((f32[16,32,256]{2,1,0:T(8,128)}), f32[16,32,256]{2,1,0:T(8,128)S(1)}, u32[]{:S(2)}, u32[]{:S(2)}) async-start(f32[16,32,256]{2,1,0:T(8,128)} %get-tuple-element.53), calls=%async_computation.1 | async-start | bytes 1048576 | tf_op jit(solution)/shard_map/all_to_all | solution.py:550
  55.2 3.6 %shard_map.81.refs_4_.refs_12_.refs_10_.refs_15_ = f32[264,256]{1,0:T(8,128)S(1)} custom-call(f32[32,256]{1,0:T(8,128)S(1)} %get-tuple-element.54.refs_0_, bf16[4,256,256]{2,1,0:T(8,128)(2,1)S(1)} %get-tuple-element.49.refs_8_.refs_3_.refs_4_.refs_1_.refs_5_.refs_2_.refs_10_, ...), custom_call_target="tpu_custom_call" | custom-call | tf_op jit(solution)/shard_map/pallas_call | solution.py:508
  58.8 5.4 %all-to-all-done.1 = f32[16,32,256]{2,1,0:T(8,128)S(1)} async-done(((f32[16,32,256]{2,1,0:T(8,128)}), f32[16,32,256]{2,1,0:T(8,128)S(1)}, u32[]{:S(2)}, u32[]{:S(2)}) %all-to-all-start.1) | async-done | bytes 524320 | tf_op jit(solution)/shard_map/all_to_all | solution.py:550
  64.2 2.4 %shard_map.82 = (f32[320,256]{1,0:T(8,128)S(1)}, f32[320,256]{1,0:T(8,128)S(1)}) custom-call(f32[512,256]{1,0:T(8,128)S(1)} %bitcast.12, f32[264,256]{1,0:T(8,128)S(1)} %get-tuple-element.46.refs_5_.refs_6_.refs_7_.refs_4_.refs_1_.refs_8_, f32[264,256]{1,0:T(8,128)S(1)} %get-tuple-element.47.refs_6_.refs_7_.refs_8_.refs_5_.refs_2_.refs_9_, ...), custom_call_target="tpu_custom_call" | custom-call | tf_op jit(solution)/shard_map/pallas_call | solution.py:508
  66.6 5.0 %collective-permute-start.6 = (f32[320,256]{1,0:T(8,128)S(1)}, f32[320,256]{1,0:T(8,128)S(1)}, u32[]{:S(2)}, u32[]{:S(2)}) collective-permute-start(f32[320,256]{1,0:T(8,128)S(1)} %get-tuple-element.59), channel_id=1, source_target_pairs={{0,1},{1,0},{2,3},{3,2},{4,5},{5,4},{6,7},{7,6},{8,9},{9,8},{10,11... | collective-permute-start | bytes 983048 | tf_op jit(solution)/shard_map/ppermute | solution.py:533
  71.7 1.3 collective-permute-done.6.refs_1_
  73.3 5.2 %collective-permute-done.7.refs_1_ = f32[160,256]{1,0:T(8,128)S(1)} collective-permute-done((f32[160,256]{1,0:T(8,128)S(1)}, f32[160,256]{1,0:T(8,128)S(1)}, u32[]{:S(2)}, u32[]{:S(2)}) %collective-permute-start.7) | collective-permute-done | bytes 163872 | tf_op jit(solution)/shard_map/ppermute | solution.py:533
  78.4 1.2 shard_map.84
  79.7 3.6 %all-to-all-start.2 = ((f32[16,40,256]{2,1,0:T(8,128)}), f32[16,40,256]{2,1,0:T(8,128)S(1)}, u32[]{:S(2)}, u32[]{:S(2)}) async-start(f32[16,40,256]{2,1,0:T(8,128)} %get-tuple-element.62), calls=%async_computation.2 | async-start | bytes 1310720 | tf_op jit(solution)/shard_map/all_to_all | solution.py:550
  83.6 1.5 collective-permute-start.8
  85.1 2.1 %collective-permute-done.9.refs_5_ = f32[128,256]{1,0:T(8,128)S(1)} collective-permute-done((f32[128,256]{1,0:T(8,128)S(1)}, f32[128,256]{1,0:T(8,128)S(1)}, u32[]{:S(2)}, u32[]{:S(2)}) %collective-permute-start.9) | collective-permute-done | bytes 131104 | tf_op jit(solution)/shard_map/ppermute | solution.py:533
  87.2 2.4 %collective-permute-start.10 = (f32[128,256]{1,0:T(8,128)S(1)}, f32[128,256]{1,0:T(8,128)}, u32[]{:S(2)}, u32[]{:S(2)}) collective-permute-start(f32[128,256]{1,0:T(8,128)S(1)} %collective-permute-done.9.refs_5_), channel_id=1, source_target_pairs={{0,1},{1,0},{2,3},{3,2},{4,5},{5,4},{6,7},{7,6},{8,9},{9,8},{10,11... | collective-permute-start | bytes 393224 | tf_op jit(solution)/shard_map/ppermute | solution.py:533
  90.7 4.2 %all-to-all-done.2.refs_0_ = f32[16,40,256]{2,1,0:T(8,128)S(1)} async-done(((f32[16,40,256]{2,1,0:T(8,128)}), f32[16,40,256]{2,1,0:T(8,128)S(1)}, u32[]{:S(2)}, u32[]{:S(2)}) %all-to-all-start.2) | async-done | bytes 655392 | tf_op jit(solution)/shard_map/all_to_all | solution.py:550
  96.3 7.5 %all-to-all-start.3 = ((f32[16,1,128]{2,1,0:T(1,128)}), f32[16,1,128]{2,1,0:T(1,128)S(1)}, u32[]{:S(2)}, u32[]{:S(2)}) async-start(f32[16,1,128]{2,1,0:T(1,128)} %bitcast.5), calls=%async_computation.3 | async-start | bytes 16384 | tf_op jit(solution)/shard_map/all_to_all | solution.py:550
  104.8 3.1 %shard_map.86 = (f32[320,256]{1,0:T(8,128)S(1)}, f32[320,256]{1,0:T(8,128)}) custom-call(f32[512,256]{1,0:T(8,128)S(1)} %copy-done.1, f32[264,256]{1,0:T(8,128)S(1)} %get-tuple-element.46.refs_5_.refs_6_.refs_7_.refs_4_.refs_1_.refs_8_, f32[264,256]{1,0:T(8,128)S(1)} %get-tuple-element.47.refs_6_.refs_7_.refs_8_.refs_5_.refs_2_.refs_9_, ...), custom_call_target="tpu_custom_call" | custom-call | tf_op jit(solution)/shard_map/pallas_call | solution.py:508
  108.7 2.1 %all-to-all-done.3 = f32[16,1,128]{2,1,0:T(1,128)S(1)} async-done(((f32[16,1,128]{2,1,0:T(1,128)}), f32[16,1,128]{2,1,0:T(1,128)S(1)}, u32[]{:S(2)}, u32[]{:S(2)}) %all-to-all-start.3) | async-done | bytes 8224 | tf_op jit(solution)/shard_map/all_to_all | solution.py:550
  110.8 3.9 %shard_map.87 = (f32[16,32,256]{2,1,0:T(8,128)}, f32[128,256]{1,0:T(8,128)S(1)}, f32[128,256]{1,0:T(8,128)S(1)}, f32[8,128]{1,0:T(8,128)S(1)}) custom-call(f32[16,128]{1,0:T(8,128)S(1)} %bitcast.18, f32[128,256]{1,0:T(8,128)S(1)} %get-tuple-element.44.refs_0_.refs_9_.refs_10_.refs_7_.refs_8_.refs_3_.refs_1_, f32[512,256]{1,0:T(8,128)} %get-tuple-element.72.refs_2_, ...), custom_call_target="tpu_custom_call" | custom-call | tf_op jit(solution)/shard_map/pallas_call | solution.py:508
  115.5 3.6 %all-to-all-start.4 = ((f32[16,32,256]{2,1,0:T(8,128)}), f32[16,32,256]{2,1,0:T(8,128)S(1)}, u32[]{:S(2)}, u32[]{:S(2)}) async-start(f32[16,32,256]{2,1,0:T(8,128)} %get-tuple-element.73), calls=%async_computation.4 | async-start | bytes 1048576 | tf_op jit(solution)/shard_map/all_to_all | solution.py:550
  119.5 5.5 %collective-permute-done.12.refs_1_ = f32[160,256]{1,0:T(8,128)S(1)} collective-permute-done((f32[160,256]{1,0:T(8,128)S(1)}, f32[160,256]{1,0:T(8,128)S(1)}, u32[]{:S(2)}, u32[]{:S(2)}) %collective-permute-start.12) | collective-permute-done | bytes 163872 | tf_op jit(solution)/shard_map/ppermute | solution.py:533
  125.1 4.4 %all-to-all-done.4.refs_0_ = f32[16,32,256]{2,1,0:T(8,128)S(1)} async-done(((f32[16,32,256]{2,1,0:T(8,128)}), f32[16,32,256]{2,1,0:T(8,128)S(1)}, u32[]{:S(2)}, u32[]{:S(2)}) %all-to-all-start.4) | async-done | bytes 524320 | tf_op jit(solution)/shard_map/all_to_all | solution.py:550
  130.5 2.8 %collective-permute-start.14 = (f32[40,256]{1,0:T(8,128)S(1)}, f32[40,256]{1,0:T(8,128)S(1)}, u32[]{:S(2)}, u32[]{:S(2)}) collective-permute-start(f32[40,256]{1,0:T(8,128)S(1)} %shard_map.90.refs_0_), channel_id=1, source_target_pairs={{0,8},{4,12},{8,0},{12,4},{1,9},{5,13},{9,1},{13,5},{2,10},{6,14},... | collective-permute-start | bytes 122888 | tf_op jit(solution)/shard_map/ppermute | solution.py:545
  133.3 1.4 collective-permute-start.13
  134.7 2.6 %collective-permute-done.14.refs_2_ = f32[40,256]{1,0:T(8,128)S(1)} collective-permute-done((f32[40,256]{1,0:T(8,128)S(1)}, f32[40,256]{1,0:T(8,128)S(1)}, u32[]{:S(2)}, u32[]{:S(2)}) %collective-permute-start.14) | collective-permute-done | bytes 40992 | tf_op jit(solution)/shard_map/ppermute | solution.py:545
  137.3 1.1 collective-permute-done.13.refs_1_
  138.5 15.9 %all_to_all.44 = f32[64,1,128]{2,1,0:T(1,128)S(1)} all-to-all(f32[64,1,128]{2,1,0:T(1,128)S(1)} %bitcast.19), channel_id=1, replica_groups=mesh['x'=4,'y'=4,'h'=4,'l'=2,'k'=2] {'x','y','l','k'}, dimensions={0} | all-to-all | bytes 65536 | tf_op jit(solution)/shard_map/all_to_all | solution.py:550
  (50 shorter events, 16.3 us)
Async XLA Ops:
  0.6 7.5 %collective-permute-start.1 = (f32[128,256]{1,0:T(8,128)}, f32[128,256]{1,0:T(8,128)S(1)}, u32[]{:S(2)}, u32[]{:S(2)}) collective-permute-start(f32[128,256]{1,0:T(8,128)} %bitcast.13), channel_id=1, source_target_pairs={{0,2},{2,0},{1,3},{3,1},{4,6},{6,4},{5,7},{7,5},{8,10},{10,8},{9,1... | collective-permute-start | bytes 393224 | tf_op jit(solution)/shard_map/ppermute | solution.py:533
  3.2 5.9 %collective-permute-start = (f32[128,256]{1,0:T(8,128)}, f32[128,256]{1,0:T(8,128)S(1)}, u32[]{:S(2)}, u32[]{:S(2)}) collective-permute-start(f32[128,256]{1,0:T(8,128)} %bitcast.14), channel_id=1, source_target_pairs={{0,1},{1,0},{2,3},{3,2},{4,5},{5,4},{6,7},{7,6},{8,9},{9,8},{10,11... | collective-permute-start | bytes 393224 | tf_op jit(solution)/shard_map/ppermute | solution.py:533
  4.8 1.0 copy-start.2
  5.8 0.9 copy-start.5
  6.8 0.9 copy-start.6
  8.2 1.9 %collective-permute-start.2 = (f32[128,256]{1,0:T(8,128)S(1)}, f32[128,256]{1,0:T(8,128)S(1)}, u32[]{:S(2)}, u32[]{:S(2)}) collective-permute-start(f32[128,256]{1,0:T(8,128)S(1)} %collective-permute-done.1.refs_2_), channel_id=1, source_target_pairs={{0,1},{1,0},{2,3},{3,2},{4,5},{5,4},{6,7},{7,6},{8,9},{9,8},{10,11... | collective-permute-start | bytes 393224 | tf_op jit(solution)/shard_map/ppermute | solution.py:533
  13.2 23.9 %copy-start.8 = (f32[1,8,256]{2,1,0:T(8,128)S(1)}, f32[1,8,256]{2,1,0:T(8,128)}, u32[]{:S(2)}) copy-start(f32[1,8,256]{2,1,0:T(8,128)} %param.8) | copy-start | bytes 24580
  13.2 23.9 %copy-start.9 = (f32[1,8,256]{2,1,0:T(8,128)S(1)}, f32[1,8,256]{2,1,0:T(8,128)}, u32[]{:S(2)}) copy-start(f32[1,8,256]{2,1,0:T(8,128)} %param.7) | copy-start | bytes 24580
  37.2 8.3 %collective-permute-start.5 = (f32[80,256]{1,0:T(8,128)S(1)}, f32[80,256]{1,0:T(8,128)S(1)}, u32[]{:S(2)}, u32[]{:S(2)}) collective-permute-start(f32[80,256]{1,0:T(8,128)S(1)} %shard_map.79.refs_0_), channel_id=1, source_target_pairs={{0,12},{4,0},{8,4},{12,8},{1,13},{5,1},{9,5},{13,9},{2,14},{6,2},{... | collective-permute-start | bytes 245768 | tf_op jit(solution)/shard_map/ppermute | solution.py:545
  42.2 7.4 %collective-permute-start.4 = (f32[80,256]{1,0:T(8,128)S(1)}, f32[80,256]{1,0:T(8,128)S(1)}, u32[]{:S(2)}, u32[]{:S(2)}) collective-permute-start(f32[80,256]{1,0:T(8,128)S(1)} %shard_map.79.refs_0_), channel_id=1, source_target_pairs={{0,8},{4,12},{8,0},{12,4},{1,9},{5,13},{9,1},{13,5},{2,10},{6,14},... | collective-permute-start | bytes 245768 | tf_op jit(solution)/shard_map/ppermute | solution.py:545
  43.5 6.8 %collective-permute-start.3 = (f32[80,256]{1,0:T(8,128)S(1)}, f32[80,256]{1,0:T(8,128)S(1)}, u32[]{:S(2)}, u32[]{:S(2)}) collective-permute-start(f32[80,256]{1,0:T(8,128)S(1)} %shard_map.79.refs_0_), channel_id=1, source_target_pairs={{0,4},{4,8},{8,12},{12,0},{1,5},{5,9},{9,13},{13,1},{2,6},{6,10},{... | collective-permute-start | bytes 245768 | tf_op jit(solution)/shard_map/ppermute | solution.py:545
  51.4 12.8 %all-to-all-start.1 = ((f32[16,32,256]{2,1,0:T(8,128)}), f32[16,32,256]{2,1,0:T(8,128)S(1)}, u32[]{:S(2)}, u32[]{:S(2)}) async-start(f32[16,32,256]{2,1,0:T(8,128)} %get-tuple-element.53), calls=%async_computation.1 | async-start | bytes 1048576 | tf_op jit(solution)/shard_map/all_to_all | solution.py:550
  66.6 6.3 %collective-permute-start.6 = (f32[320,256]{1,0:T(8,128)S(1)}, f32[320,256]{1,0:T(8,128)S(1)}, u32[]{:S(2)}, u32[]{:S(2)}) collective-permute-start(f32[320,256]{1,0:T(8,128)S(1)} %get-tuple-element.59), channel_id=1, source_target_pairs={{0,1},{1,0},{2,3},{3,2},{4,5},{5,4},{6,7},{7,6},{8,9},{9,8},{10,11... | collective-permute-start | bytes 983048 | tf_op jit(solution)/shard_map/ppermute | solution.py:533
  73.0 5.5 %collective-permute-start.7 = (f32[160,256]{1,0:T(8,128)S(1)}, f32[160,256]{1,0:T(8,128)S(1)}, u32[]{:S(2)}, u32[]{:S(2)}) collective-permute-start(f32[160,256]{1,0:T(8,128)S(1)} %get-tuple-element.61), channel_id=1, source_target_pairs={{0,2},{2,0},{1,3},{3,1},{4,6},{6,4},{5,7},{7,5},{8,10},{10,8},{9,1... | collective-permute-start | bytes 491528 | tf_op jit(solution)/shard_map/ppermute | solution.py:533
  79.6 15.8 %copy-start.7 = (f32[128,256]{1,0:T(8,128)}, f32[128,256]{1,0:T(8,128)S(1)}, u32[]{:S(2)}) copy-start(f32[128,256]{1,0:T(8,128)S(1)} %get-tuple-element.63.refs_3_) | copy-start | bytes 393220
  79.7 15.2 %all-to-all-start.2 = ((f32[16,40,256]{2,1,0:T(8,128)}), f32[16,40,256]{2,1,0:T(8,128)S(1)}, u32[]{:S(2)}, u32[]{:S(2)}) async-start(f32[16,40,256]{2,1,0:T(8,128)} %get-tuple-element.62), calls=%async_computation.2 | async-start | bytes 1310720 | tf_op jit(solution)/shard_map/all_to_all | solution.py:550
  83.3 3.9 %collective-permute-start.9 = (f32[128,256]{1,0:T(8,128)S(1)}, f32[128,256]{1,0:T(8,128)S(1)}, u32[]{:S(2)}, u32[]{:S(2)}) collective-permute-start(f32[128,256]{1,0:T(8,128)S(1)} %get-tuple-element.63.refs_3_), channel_id=1, source_target_pairs={{0,2},{2,0},{1,3},{3,1},{4,6},{6,4},{5,7},{7,5},{8,10},{10,8},{9,1... | collective-permute-start | bytes 393224 | tf_op jit(solution)/shard_map/ppermute | solution.py:533
  83.6 6.0 %collective-permute-start.8 = (f32[128,256]{1,0:T(8,128)S(1)}, f32[128,256]{1,0:T(8,128)S(1)}, u32[]{:S(2)}, u32[]{:S(2)}) collective-permute-start(f32[128,256]{1,0:T(8,128)S(1)} %get-tuple-element.63.refs_3_), channel_id=1, source_target_pairs={{0,1},{1,0},{2,3},{3,2},{4,5},{5,4},{6,7},{7,6},{8,9},{9,8},{10,11... | collective-permute-start | bytes 393224 | tf_op jit(solution)/shard_map/ppermute | solution.py:533
  87.2 2.4 %copy-start.10 = (f32[128,256]{1,0:T(8,128)}, f32[128,256]{1,0:T(8,128)S(1)}, u32[]{:S(2)}) copy-start(f32[128,256]{1,0:T(8,128)S(1)} %collective-permute-done.9.refs_5_) | copy-start | bytes 393220
  87.2 3.5 %collective-permute-start.10 = (f32[128,256]{1,0:T(8,128)S(1)}, f32[128,256]{1,0:T(8,128)}, u32[]{:S(2)}, u32[]{:S(2)}) collective-permute-start(f32[128,256]{1,0:T(8,128)S(1)} %collective-permute-done.9.refs_5_), channel_id=1, source_target_pairs={{0,1},{1,0},{2,3},{3,2},{4,5},{5,4},{6,7},{7,6},{8,9},{9,8},{10,11... | collective-permute-start | bytes 393224 | tf_op jit(solution)/shard_map/ppermute | solution.py:533
  89.6 0.6 copy-start.11
  95.5 0.8 copy-start
  96.3 14.5 %all-to-all-start.3 = ((f32[16,1,128]{2,1,0:T(1,128)}), f32[16,1,128]{2,1,0:T(1,128)S(1)}, u32[]{:S(2)}, u32[]{:S(2)}) async-start(f32[16,1,128]{2,1,0:T(1,128)} %bitcast.5), calls=%async_computation.3 | async-start | bytes 16384 | tf_op jit(solution)/shard_map/all_to_all | solution.py:550
  103.8 1.0 copy-start.1
  108.0 0.7 copy-start.3
  114.7 4.3 %copy-start.4 = (f32[320,256]{1,0:T(8,128)S(1)}, f32[320,256]{1,0:T(8,128)}, u32[]{:S(2)}) copy-start(f32[320,256]{1,0:T(8,128)} %copy-done.3) | copy-start | bytes 983044
  114.7 4.3 %collective-permute-start.11 = (f32[320,256]{1,0:T(8,128)}, f32[320,256]{1,0:T(8,128)S(1)}, u32[]{:S(2)}, u32[]{:S(2)}) collective-permute-start(f32[320,256]{1,0:T(8,128)} %get-tuple-element.75), channel_id=1, source_target_pairs={{0,1},{1,0},{2,3},{3,2},{4,5},{5,4},{6,7},{7,6},{8,9},{9,8},{10,11... | collective-permute-start | bytes 983048 | tf_op jit(solution)/shard_map/ppermute | solution.py:533
  115.5 14.1 %all-to-all-start.4 = ((f32[16,32,256]{2,1,0:T(8,128)}), f32[16,32,256]{2,1,0:T(8,128)S(1)}, u32[]{:S(2)}, u32[]{:S(2)}) async-start(f32[16,32,256]{2,1,0:T(8,128)} %get-tuple-element.73), calls=%async_computation.4 | async-start | bytes 1048576 | tf_op jit(solution)/shard_map/all_to_all | solution.py:550
  119.1 5.8 %collective-permute-start.12 = (f32[160,256]{1,0:T(8,128)S(1)}, f32[160,256]{1,0:T(8,128)S(1)}, u32[]{:S(2)}, u32[]{:S(2)}) collective-permute-start(f32[160,256]{1,0:T(8,128)S(1)} %get-tuple-element.80), channel_id=1, source_target_pairs={{0,2},{2,0},{1,3},{3,1},{4,6},{6,4},{5,7},{7,5},{8,10},{10,8},{9,1... | collective-permute-start | bytes 491528 | tf_op jit(solution)/shard_map/ppermute | solution.py:533
  129.6 5.0 %collective-permute-start.15 = (f32[40,256]{1,0:T(8,128)S(1)}, f32[40,256]{1,0:T(8,128)S(1)}, u32[]{:S(2)}, u32[]{:S(2)}) collective-permute-start(f32[40,256]{1,0:T(8,128)S(1)} %shard_map.90.refs_0_), channel_id=1, source_target_pairs={{0,12},{4,0},{8,4},{12,8},{1,13},{5,1},{9,5},{13,9},{2,14},{6,2},{... | collective-permute-start | bytes 122888 | tf_op jit(solution)/shard_map/ppermute | solution.py:545
  130.5 6.8 %collective-permute-start.14 = (f32[40,256]{1,0:T(8,128)S(1)}, f32[40,256]{1,0:T(8,128)S(1)}, u32[]{:S(2)}, u32[]{:S(2)}) collective-permute-start(f32[40,256]{1,0:T(8,128)S(1)} %shard_map.90.refs_0_), channel_id=1, source_target_pairs={{0,8},{4,12},{8,0},{12,4},{1,9},{5,13},{9,1},{13,5},{2,10},{6,14},... | collective-permute-start | bytes 122888 | tf_op jit(solution)/shard_map/ppermute | solution.py:545
  133.3 5.1 %collective-permute-start.13 = (f32[40,256]{1,0:T(8,128)S(1)}, f32[40,256]{1,0:T(8,128)S(1)}, u32[]{:S(2)}, u32[]{:S(2)}) collective-permute-start(f32[40,256]{1,0:T(8,128)S(1)} %shard_map.90.refs_0_), channel_id=1, source_target_pairs={{0,4},{4,8},{8,12},{12,0},{1,5},{5,9},{9,13},{13,1},{2,6},{6,10},{... | collective-permute-start | bytes 122888 | tf_op jit(solution)/shard_map/ppermute | solution.py:545

commit v13 on v11

--- a/solution.py
+++ b/solution.py
@@ -161,15 +161,16 @@
 
 
 def prepare_kernel(
-    top_ref, fx_in, ty_in, dens_in, fx, bx, ty, dens_ref, decay_ref, gx_ref, gy_ref
+    top_ref, fx_in, ty_in, dens_in, fx, bx, ty, dens_ref, decay_ref, gx_ref, gy_ref, sems
 ):
-    dens_ref[...] = dens_in[0]
-    for place in range(4):
-        table = fx_in[place]
-        fx[place] = table
-        bx[place] = table.astype(F32).T.astype(BF16)
-    for place in range(2):
-        ty[place] = ty_in[place]
+    copies = [
+        pltpu.make_async_copy(source, target, sems.at[place])
+        for place, (source, target) in enumerate(
+            ((fx_in, fx), (ty_in, ty), (dens_in.at[0], dens_ref))
+        )
+    ]
+    for copy in copies:
+        copy.start()
     kx, ky, sine_y, nyquist_y = wave_grid()
     kabs = jnp.sqrt(kx * kx + ky * ky)
     inverse = 1.0 / jnp.maximum(kabs, TWO_PI / max(NX, NY))
@@ -177,6 +178,10 @@
     gx_ref[...] = kx * inverse
     ry = ky * inverse
     gy_ref[...] = jnp.where(nyquist_y, 0.0, jnp.where(sine_y, -ry, ry))
+    for copy in copies:
+        copy.wait()
+    for place in range(4):
+        bx[place] = fx[place].astype(F32).T.astype(BF16)
 
 
 def gather_rows(pieces, full_ref):
@@ -482,7 +487,7 @@
     def drop(self, *values):
         self.alive = [item for item in self.alive if all(item is not value for value in values)]
 
-    def call(self, kernel, outs, *args, scratch=(), scalars=(), far_out=(), sems=0, mib=8):
+    def call(self, kernel, outs, *args, scratch=(), scalars=(), far=(), far_out=(), sems=0, mib=8):
         used = len(args)
         keep = [item for item in self.alive if all(item is not value for value in args)]
         kept = len(keep)
@@ -490,6 +495,10 @@
         def inner(*refs):
             kernel(*refs[:used], *refs[used + kept :])
 
+        args = [
+            pltpu.with_memory_space_constraint(item, pltpu.HBM) if place in far else item
+            for place, item in enumerate(args)
+        ]
         kinds = [(item, F32) if isinstance(item, tuple) else (item.shape, item.dtype) for item in outs]
         return pl.pallas_call(
             inner,
@@ -498,7 +507,8 @@
                 for place, kind in enumerate(kinds)
             ],
             in_specs=[
-                SMEM if place in scalars else VMEM for place in range(used)
+                SMEM if place in scalars else FAR if place in far else VMEM
+                for place in range(used)
             ]
             + [ANY] * kept,
             out_specs=[FAR if place in far_out else VMEM for place in range(len(outs))],
@@ -555,7 +565,7 @@
     *tables, dens, decay, gx, gy = call(
         prepare_kernel,
         [fx, fx, ty, (QX, NY), (KEPT, NY), (KEPT, NY), (KEPT, NY)],
-        layer_top, fx, ty, density, scalars=(0,),
+        layer_top, fx, ty, density, scalars=(0,), far=(1, 2, 3), sems=3,
     )
     layers = [near, across, flip(after(across, dens), "k")]
     factors = (decay, gx, gy)

time: 156 us -> 156 us (level)
  starting transfers between devices: 51.4 us -> 56.2 us
  local copies, waits for them, and re-layouts: 4.87 us -> 1.98 us
    ppermute x10, starting transfers between devices: 15.4 us -> 18.6 us  [flip(): return lax.ppermute(value, axis, [(0, 1), (1, 0)])]
    unnamed x24 -> x18, local copies, waits for them, and re-layouts: 4.87 us -> 1.98 us
where the time goes in v13:
time: 156 us; the launch traced here: 155 us
  starting transfers between devices  56.2 us (36%)
  blocking collectives  38.6 us (25%)
  waiting for transfers between devices  37 us (24%)
  Pallas kernels  19.9 us (13%)
  local copies, waits for them, and re-layouts  1.98 us (1%)
    all_to_all x2, blocking collectives, exchange(): return lax.all_to_all(value, axes, 0, 0, tiled=True)  38.6 us
    ppermute x9, starting transfers between devices, from_axis(): lax.ppermute(values[step], axis, [(i, (i + step) % size) for i in range(s...  21.3 us
    pallas_call x17, Pallas kernels, call(): pl.pallas_call(inner, out_shape=[(pltpu.HBM if place in far_out else jax....  19.9 us
    ppermute x10, starting transfers between devices, flip(): return lax.ppermute(value, axis, [(0, 1), (1, 0)])  18.6 us
    all_to_all x3, waiting for transfers between devices, exchange(): return lax.all_to_all(value, axes, 0, 0, tiled=True)  13 us
    ppermute x10, waiting for transfers between devices, flip(): return lax.ppermute(value, axis, [(0, 1), (1, 0)])  12.6 us
    all_to_all x3, starting transfers between devices, exchange(): return lax.all_to_all(value, axes, 0, 0, tiled=True)  11.1 us
    ppermute x9, waiting for transfers between devices, from_axis(): lax.ppermute(values[step], axis, [(i, (i + step) % size) for i in range(s...  9.42 us
  transfers between devices with their start and end apart: 25, of which 14 were waited for; matrix products, arithmetic and copies ran while one was open for 0% of the time, Pallas kernels for 5%

profile of v13, /device:TPU:1, one launch (start us, length us, event | category | flops | bytes accessed | tf_op | source)
XLA Modules:
  0.0 155.1 jit_solution(11115172915036023765)
XLA Ops:
  0.6 2.5 %collective-permute-start.1 = (f32[128,256]{1,0:T(8,128)}, f32[128,256]{1,0:T(8,128)S(1)}, u32[]{:S(2)}, u32[]{:S(2)}) collective-permute-start(f32[128,256]{1,0:T(8,128)} %bitcast.14), channel_id=1, source_target_pairs={{0,2},{2,0},{1,3},{3,1},{4,6},{6,4},{5,7},{7,5},{8,10},{10,8},{9,1... | collective-permute-start | bytes 393224 | tf_op jit(solution)/shard_map/ppermute | solution.py:528
  4.8 1.4 shard_map.77
  6.2 2.9 %collective-permute-start.2 = (f32[128,256]{1,0:T(8,128)S(1)}, f32[128,256]{1,0:T(8,128)S(1)}, u32[]{:S(2)}, u32[]{:S(2)}) collective-permute-start(f32[128,256]{1,0:T(8,128)S(1)} %collective-permute-done.1.refs_2_), channel_id=1, source_target_pairs={{0,1},{1,0},{2,3},{3,2},{4,5},{5,4},{6,7},{7,6},{8,9},{9,8},{10,11... | collective-permute-start | bytes 393224 | tf_op jit(solution)/shard_map/ppermute | solution.py:528
  10.1 3.1 %shard_map.78 = (f32[16,72,256]{2,1,0:T(8,128)S(1)}, f32[512,256]{1,0:T(8,128)}) custom-call(f32[128,256]{1,0:T(8,128)S(1)} %get-tuple-element.47.refs_0_.refs_9_.refs_10_.refs_7_.refs_8_.refs_3_.refs_4_, f32[128,256]{1,0:T(8,128)S(1)} %collective-permute-done.refs_1_, f32[128,256]{1,0:T(8,128)S(1)} %collective-permute-done.1.refs_2_, ...), custom_call_target="tpu_custom_call" | custom-call | tf_op jit(solution)/shard_map/pallas_call | solution.py:503
  13.2 22.9 %all_to_all.31.refs_0_ = f32[16,72,256]{2,1,0:T(8,128)S(1)} all-to-all(f32[16,72,256]{2,1,0:T(8,128)S(1)} %get-tuple-element.55), channel_id=1, replica_groups=mesh['x'=4,'y'=4,'h'=4,'l'=2,'k'=2] {'x','y'}, dimensions={0} | all-to-all | bytes 2359296 | tf_op jit(solution)/shard_map/all_to_all | solution.py:545
  36.2 5.9 %collective-permute-start.5 = (f32[80,256]{1,0:T(8,128)S(1)}, f32[80,256]{1,0:T(8,128)S(1)}, u32[]{:S(2)}, u32[]{:S(2)}) collective-permute-start(f32[80,256]{1,0:T(8,128)S(1)} %shard_map.79.refs_0_), channel_id=1, source_target_pairs={{0,12},{4,0},{8,4},{12,8},{1,13},{5,1},{9,5},{13,9},{2,14},{6,2},{... | collective-permute-start | bytes 245768 | tf_op jit(solution)/shard_map/ppermute | solution.py:540
  43.1 2.3 %collective-permute-start.3 = (f32[80,256]{1,0:T(8,128)S(1)}, f32[80,256]{1,0:T(8,128)S(1)}, u32[]{:S(2)}, u32[]{:S(2)}) collective-permute-start(f32[80,256]{1,0:T(8,128)S(1)} %shard_map.79.refs_0_), channel_id=1, source_target_pairs={{0,4},{4,8},{8,12},{12,0},{1,5},{5,9},{9,13},{13,1},{2,6},{6,10},{... | collective-permute-start | bytes 245768 | tf_op jit(solution)/shard_map/ppermute | solution.py:540
  45.4 4.1 %collective-permute-done.4.refs_2_ = f32[80,256]{1,0:T(8,128)S(1)} collective-permute-done((f32[80,256]{1,0:T(8,128)S(1)}, f32[80,256]{1,0:T(8,128)S(1)}, u32[]{:S(2)}, u32[]{:S(2)}) %collective-permute-start.4) | collective-permute-done | bytes 81952 | tf_op jit(solution)/shard_map/ppermute | solution.py:540
  50.9 3.9 %all-to-all-start.1 = ((f32[16,32,256]{2,1,0:T(8,128)}), f32[16,32,256]{2,1,0:T(8,128)S(1)}, u32[]{:S(2)}, u32[]{:S(2)}) async-start(f32[16,32,256]{2,1,0:T(8,128)} %get-tuple-element.56), calls=%async_computation.1 | async-start | bytes 1048576 | tf_op jit(solution)/shard_map/all_to_all | solution.py:545
  54.8 3.6 %shard_map.81.refs_4_.refs_12_.refs_10_.refs_13_.refs_18_ = f32[264,256]{1,0:T(8,128)S(1)} custom-call(f32[32,256]{1,0:T(8,128)S(1)} %get-tuple-element.57.refs_0_, bf16[4,256,256]{2,1,0:T(8,128)(2,1)S(1)} %get-tuple-element.52.refs_8_.refs_3_.refs_4_.refs_1_.refs_5_.refs_2_.refs_13_, ...), custom_call_target="tpu_custom_call" | custom-call | tf_op jit(solution)/shard_map/pallas_call | solution.py:503
  58.4 5.4 %all-to-all-done.1 = f32[16,32,256]{2,1,0:T(8,128)S(1)} async-done(((f32[16,32,256]{2,1,0:T(8,128)}), f32[16,32,256]{2,1,0:T(8,128)S(1)}, u32[]{:S(2)}, u32[]{:S(2)}) %all-to-all-start.1) | async-done | bytes 524320 | tf_op jit(solution)/shard_map/all_to_all | solution.py:545
  63.7 2.4 %shard_map.82 = (f32[320,256]{1,0:T(8,128)S(1)}, f32[320,256]{1,0:T(8,128)S(1)}) custom-call(f32[512,256]{1,0:T(8,128)S(1)} %bitcast.8, f32[264,256]{1,0:T(8,128)S(1)} %get-tuple-element.49.refs_5_.refs_6_.refs_7_.refs_4_.refs_1_.refs_8_.refs_10_, f32[264,256]{1,0:T(8,128)S(1)} %get-tuple-element.50.refs_6_.refs_7_.refs_8_.refs_5_.refs_2_.refs_9_.refs_11_, ...), custom_call_target="tpu_custom_call" | custom-call | tf_op jit(solution)/shard_map/pallas_call | solution.py:503
  66.2 4.9 %collective-permute-start.6 = (f32[320,256]{1,0:T(8,128)S(1)}, f32[320,256]{1,0:T(8,128)S(1)}, u32[]{:S(2)}, u32[]{:S(2)}) collective-permute-start(f32[320,256]{1,0:T(8,128)S(1)} %get-tuple-element.62), channel_id=1, source_target_pairs={{0,1},{1,0},{2,3},{3,2},{4,5},{5,4},{6,7},{7,6},{8,9},{9,8},{10,11... | collective-permute-start | bytes 983048 | tf_op jit(solution)/shard_map/ppermute | solution.py:528
  73.4 4.5 %collective-permute-done.7.refs_1_ = f32[160,256]{1,0:T(8,128)S(1)} collective-permute-done((f32[160,256]{1,0:T(8,128)S(1)}, f32[160,256]{1,0:T(8,128)S(1)}, u32[]{:S(2)}, u32[]{:S(2)}) %collective-permute-start.7) | collective-permute-done | bytes 163872 | tf_op jit(solution)/shard_map/ppermute | solution.py:528
  79.1 3.6 %all-to-all-start.2 = ((f32[16,40,256]{2,1,0:T(8,128)}), f32[16,40,256]{2,1,0:T(8,128)S(1)}, u32[]{:S(2)}, u32[]{:S(2)}) async-start(f32[16,40,256]{2,1,0:T(8,128)} %get-tuple-element.65), calls=%async_computation.2 | async-start | bytes 1310720 | tf_op jit(solution)/shard_map/all_to_all | solution.py:545
  83.7 1.5 collective-permute-start.8
  85.2 1.4 collective-permute-done.9.refs_8_
  86.6 2.4 %collective-permute-start.10 = (f32[128,256]{1,0:T(8,128)S(1)}, f32[128,256]{1,0:T(8,128)S(1)}, u32[]{:S(2)}, u32[]{:S(2)}) collective-permute-start(f32[128,256]{1,0:T(8,128)S(1)} %collective-permute-done.9.refs_8_), channel_id=1, source_target_pairs={{0,1},{1,0},{2,3},{3,2},{4,5},{5,4},{6,7},{7,6},{8,9},{9,8},{10,11... | collective-permute-start | bytes 393224 | tf_op jit(solution)/shard_map/ppermute | solution.py:528
  90.9 3.3 %all-to-all-done.2.refs_0_ = f32[16,40,256]{2,1,0:T(8,128)S(1)} async-done(((f32[16,40,256]{2,1,0:T(8,128)}), f32[16,40,256]{2,1,0:T(8,128)S(1)}, u32[]{:S(2)}, u32[]{:S(2)}) %all-to-all-start.2) | async-done | bytes 655392 | tf_op jit(solution)/shard_map/all_to_all | solution.py:545
  94.3 2.3 %collective-permute-start.13 = (f32[8,256]{1,0:T(8,128)S(1)}, f32[8,256]{1,0:T(8,128)S(1)}, u32[]{:S(2)}, u32[]{:S(2)}) collective-permute-start(f32[8,256]{1,0:T(8,128)S(1)} %get-tuple-element.74.refs_0_), channel_id=1, source_target_pairs={{0,12},{4,0},{8,4},{12,8},{1,13},{5,1},{9,5},{13,9},{2,14},{6,2},{... | collective-permute-start | bytes 24584 | tf_op jit(solution)/shard_map/ppermute | solution.py:540
  96.6 2.3 %collective-permute-start.12 = (f32[8,256]{1,0:T(8,128)S(1)}, f32[8,256]{1,0:T(8,128)S(1)}, u32[]{:S(2)}, u32[]{:S(2)}) collective-permute-start(f32[8,256]{1,0:T(8,128)S(1)} %get-tuple-element.74.refs_0_), channel_id=1, source_target_pairs={{0,8},{4,12},{8,0},{12,4},{1,9},{5,13},{9,1},{13,5},{2,10},{6,14},... | collective-permute-start | bytes 24584 | tf_op jit(solution)/shard_map/ppermute | solution.py:540
  99.0 1.8 %collective-permute-start.11 = (f32[8,256]{1,0:T(8,128)S(1)}, f32[8,256]{1,0:T(8,128)S(1)}, u32[]{:S(2)}, u32[]{:S(2)}) collective-permute-start(f32[8,256]{1,0:T(8,128)S(1)} %get-tuple-element.74.refs_0_), channel_id=1, source_target_pairs={{0,4},{4,8},{8,12},{12,0},{1,5},{5,9},{9,13},{13,1},{2,6},{6,10},{... | collective-permute-start | bytes 24584 | tf_op jit(solution)/shard_map/ppermute | solution.py:540
  100.8 3.2 %shard_map.86 = (f32[320,256]{1,0:T(8,128)S(1)}, f32[320,256]{1,0:T(8,128)}) custom-call(f32[512,256]{1,0:T(8,128)S(1)} %get-tuple-element.71.refs_0_, f32[264,256]{1,0:T(8,128)S(1)} %get-tuple-element.49.refs_5_.refs_6_.refs_7_.refs_4_.refs_1_.refs_8_.refs_10_, f32[264,256]{1,0:T(8,128)S(1)} %get-tuple-element.50.refs_6_.refs_7_.refs_8_.refs_5_.refs_2_.refs_9_.refs_11_, ...), custom_call_target="tpu_custom_call" | custom-call | tf_op jit(solution)/shard_map/pallas_call | solution.py:503
  104.0 4.7 %collective-permute-start.16 = (f32[8,256]{1,0:T(8,128)S(1)}, f32[8,256]{1,0:T(8,128)S(1)}, u32[]{:S(2)}, u32[]{:S(2)}) collective-permute-start(f32[8,256]{1,0:T(8,128)S(1)} %shard_map.87.refs_0_), channel_id=1, source_target_pairs={{0,3},{1,2},{2,1},{3,0},{4,7},{5,6},{6,5},{7,4},{8,11},{9,10},{10,... | collective-permute-start | bytes 24584 | tf_op jit(solution)/shard_map/ppermute | solution.py:523
  111.3 2.7 %shard_map.88 = (f32[16,32,256]{2,1,0:T(8,128)}, f32[128,256]{1,0:T(8,128)S(1)}, f32[128,256]{1,0:T(8,128)S(1)}, f32[8,128]{1,0:T(8,128)S(1)}) custom-call(f32[8,256]{1,0:T(8,128)S(1)} %shard_map.87.refs_0_, f32[8,256]{1,0:T(8,128)S(1)} %collective-permute-done.14.refs_1_, f32[8,256]{1,0:T(8,128)S(1)} %collective-permute-done.15.refs_2_, ...), custom_call_target="tpu_custom_call" | custom-call | tf_op jit(solution)/shard_map/pallas_call | solution.py:503
  114.3 3.6 %all-to-all-start.3 = ((f32[16,32,256]{2,1,0:T(8,128)}), f32[16,32,256]{2,1,0:T(8,128)S(1)}, u32[]{:S(2)}, u32[]{:S(2)}) async-start(f32[16,32,256]{2,1,0:T(8,128)} %get-tuple-element.79), calls=%async_computation.3 | async-start | bytes 1048576 | tf_op jit(solution)/shard_map/all_to_all | solution.py:545
  119.1 4.4 %collective-permute-done.18.refs_1_ = f32[160,256]{1,0:T(8,128)S(1)} collective-permute-done((f32[160,256]{1,0:T(8,128)S(1)}, f32[160,256]{1,0:T(8,128)S(1)}, u32[]{:S(2)}, u32[]{:S(2)}) %collective-permute-start.18) | collective-permute-done | bytes 163872 | tf_op jit(solution)/shard_map/ppermute | solution.py:528
  123.7 4.2 %all-to-all-done.3.refs_0_ = f32[16,32,256]{2,1,0:T(8,128)S(1)} async-done(((f32[16,32,256]{2,1,0:T(8,128)}), f32[16,32,256]{2,1,0:T(8,128)S(1)}, u32[]{:S(2)}, u32[]{:S(2)}) %all-to-all-start.3) | async-done | bytes 524320 | tf_op jit(solution)/shard_map/all_to_all | solution.py:545
  129.3 3.3 %collective-permute-start.20 = (f32[40,256]{1,0:T(8,128)S(1)}, f32[40,256]{1,0:T(8,128)S(1)}, u32[]{:S(2)}, u32[]{:S(2)}) collective-permute-start(f32[40,256]{1,0:T(8,128)S(1)} %shard_map.91.refs_0_), channel_id=1, source_target_pairs={{0,8},{4,12},{8,0},{12,4},{1,9},{5,13},{9,1},{13,5},{2,10},{6,14},... | collective-permute-start | bytes 122888 | tf_op jit(solution)/shard_map/ppermute | solution.py:540
  133.7 2.4 %collective-permute-done.20.refs_2_ = f32[40,256]{1,0:T(8,128)S(1)} collective-permute-done((f32[40,256]{1,0:T(8,128)S(1)}, f32[40,256]{1,0:T(8,128)S(1)}, u32[]{:S(2)}, u32[]{:S(2)}) %collective-permute-start.20) | collective-permute-done | bytes 40992 | tf_op jit(solution)/shard_map/ppermute | solution.py:540
  136.1 2.5 %collective-permute-done.19.refs_1_ = f32[40,256]{1,0:T(8,128)S(1)} collective-permute-done((f32[40,256]{1,0:T(8,128)S(1)}, f32[40,256]{1,0:T(8,128)S(1)}, u32[]{:S(2)}, u32[]{:S(2)}) %collective-permute-start.19) | collective-permute-done | bytes 40992 | tf_op jit(solution)/shard_map/ppermute | solution.py:540
  138.7 15.7 %all_to_all.32 = f32[64,1,128]{2,1,0:T(1,128)S(1)} all-to-all(f32[64,1,128]{2,1,0:T(1,128)S(1)} %bitcast.12), channel_id=1, replica_groups=mesh['x'=4,'y'=4,'h'=4,'l'=2,'k'=2] {'x','y','l','k'}, dimensions={0} | all-to-all | bytes 65536 | tf_op jit(solution)/shard_map/all_to_all | solution.py:545
  (55 shorter events, 18.4 us)
Async XLA Ops:
  0.6 5.5 %collective-permute-start.1 = (f32[128,256]{1,0:T(8,128)}, f32[128,256]{1,0:T(8,128)S(1)}, u32[]{:S(2)}, u32[]{:S(2)}) collective-permute-start(f32[128,256]{1,0:T(8,128)} %bitcast.14), channel_id=1, source_target_pairs={{0,2},{2,0},{1,3},{3,1},{4,6},{6,4},{5,7},{7,5},{8,10},{10,8},{9,1... | collective-permute-start | bytes 393224 | tf_op jit(solution)/shard_map/ppermute | solution.py:528
  3.2 5.9 %collective-permute-start = (f32[128,256]{1,0:T(8,128)}, f32[128,256]{1,0:T(8,128)S(1)}, u32[]{:S(2)}, u32[]{:S(2)}) collective-permute-start(f32[128,256]{1,0:T(8,128)} %bitcast.15), channel_id=1, source_target_pairs={{0,1},{1,0},{2,3},{3,2},{4,5},{5,4},{6,7},{7,6},{8,9},{9,8},{10,11... | collective-permute-start | bytes 393224 | tf_op jit(solution)/shard_map/ppermute | solution.py:528
  6.2 3.9 %collective-permute-start.2 = (f32[128,256]{1,0:T(8,128)S(1)}, f32[128,256]{1,0:T(8,128)S(1)}, u32[]{:S(2)}, u32[]{:S(2)}) collective-permute-start(f32[128,256]{1,0:T(8,128)S(1)} %collective-permute-done.1.refs_2_), channel_id=1, source_target_pairs={{0,1},{1,0},{2,3},{3,2},{4,5},{5,4},{6,7},{7,6},{8,9},{9,8},{10,11... | collective-permute-start | bytes 393224 | tf_op jit(solution)/shard_map/ppermute | solution.py:528
  13.2 22.9 %copy-start.7 = (f32[1,8,256]{2,1,0:T(8,128)S(1)}, f32[1,8,256]{2,1,0:T(8,128)}, u32[]{:S(2)}) copy-start(f32[1,8,256]{2,1,0:T(8,128)} %param.8) | copy-start | bytes 24580
  13.2 22.9 %copy-start.8 = (f32[1,8,256]{2,1,0:T(8,128)S(1)}, f32[1,8,256]{2,1,0:T(8,128)}, u32[]{:S(2)}) copy-start(f32[1,8,256]{2,1,0:T(8,128)} %param.7) | copy-start | bytes 24580
  36.2 9.2 %collective-permute-start.5 = (f32[80,256]{1,0:T(8,128)S(1)}, f32[80,256]{1,0:T(8,128)S(1)}, u32[]{:S(2)}, u32[]{:S(2)}) collective-permute-start(f32[80,256]{1,0:T(8,128)S(1)} %shard_map.79.refs_0_), channel_id=1, source_target_pairs={{0,12},{4,0},{8,4},{12,8},{1,13},{5,1},{9,5},{13,9},{2,14},{6,2},{... | collective-permute-start | bytes 245768 | tf_op jit(solution)/shard_map/ppermute | solution.py:540
  42.1 7.4 %collective-permute-start.4 = (f32[80,256]{1,0:T(8,128)S(1)}, f32[80,256]{1,0:T(8,128)S(1)}, u32[]{:S(2)}, u32[]{:S(2)}) collective-permute-start(f32[80,256]{1,0:T(8,128)S(1)} %shard_map.79.refs_0_), channel_id=1, source_target_pairs={{0,8},{4,12},{8,0},{12,4},{1,9},{5,13},{9,1},{13,5},{2,10},{6,14},... | collective-permute-start | bytes 245768 | tf_op jit(solution)/shard_map/ppermute | solution.py:540
  43.1 6.8 %collective-permute-start.3 = (f32[80,256]{1,0:T(8,128)S(1)}, f32[80,256]{1,0:T(8,128)S(1)}, u32[]{:S(2)}, u32[]{:S(2)}) collective-permute-start(f32[80,256]{1,0:T(8,128)S(1)} %shard_map.79.refs_0_), channel_id=1, source_target_pairs={{0,4},{4,8},{8,12},{12,0},{1,5},{5,9},{9,13},{13,1},{2,6},{6,10},{... | collective-permute-start | bytes 245768 | tf_op jit(solution)/shard_map/ppermute | solution.py:540
  50.9 12.8 %all-to-all-start.1 = ((f32[16,32,256]{2,1,0:T(8,128)}), f32[16,32,256]{2,1,0:T(8,128)S(1)}, u32[]{:S(2)}, u32[]{:S(2)}) async-start(f32[16,32,256]{2,1,0:T(8,128)} %get-tuple-element.56), calls=%async_computation.1 | async-start | bytes 1048576 | tf_op jit(solution)/shard_map/all_to_all | solution.py:545
  66.2 6.2 %collective-permute-start.6 = (f32[320,256]{1,0:T(8,128)S(1)}, f32[320,256]{1,0:T(8,128)S(1)}, u32[]{:S(2)}, u32[]{:S(2)}) collective-permute-start(f32[320,256]{1,0:T(8,128)S(1)} %get-tuple-element.62), channel_id=1, source_target_pairs={{0,1},{1,0},{2,3},{3,2},{4,5},{5,4},{6,7},{7,6},{8,9},{9,8},{10,11... | collective-permute-start | bytes 983048 | tf_op jit(solution)/shard_map/ppermute | solution.py:528
  72.4 5.5 %collective-permute-start.7 = (f32[160,256]{1,0:T(8,128)S(1)}, f32[160,256]{1,0:T(8,128)S(1)}, u32[]{:S(2)}, u32[]{:S(2)}) collective-permute-start(f32[160,256]{1,0:T(8,128)S(1)} %get-tuple-element.64), channel_id=1, source_target_pairs={{0,2},{2,0},{1,3},{3,1},{4,6},{6,4},{5,7},{7,5},{8,10},{10,8},{9,1... | collective-permute-start | bytes 491528 | tf_op jit(solution)/shard_map/ppermute | solution.py:528
  79.1 15.2 %all-to-all-start.2 = ((f32[16,40,256]{2,1,0:T(8,128)}), f32[16,40,256]{2,1,0:T(8,128)S(1)}, u32[]{:S(2)}, u32[]{:S(2)}) async-start(f32[16,40,256]{2,1,0:T(8,128)} %get-tuple-element.65), calls=%async_computation.2 | async-start | bytes 1310720 | tf_op jit(solution)/shard_map/all_to_all | solution.py:545
  82.7 3.9 %collective-permute-start.9 = (f32[128,256]{1,0:T(8,128)S(1)}, f32[128,256]{1,0:T(8,128)S(1)}, u32[]{:S(2)}, u32[]{:S(2)}) collective-permute-start(f32[128,256]{1,0:T(8,128)S(1)} %get-tuple-element.66.refs_6_), channel_id=1, source_target_pairs={{0,2},{2,0},{1,3},{3,1},{4,6},{6,4},{5,7},{7,5},{8,10},{10,8},{9,1... | collective-permute-start | bytes 393224 | tf_op jit(solution)/shard_map/ppermute | solution.py:528
  83.7 6.0 %collective-permute-start.8 = (f32[128,256]{1,0:T(8,128)S(1)}, f32[128,256]{1,0:T(8,128)S(1)}, u32[]{:S(2)}, u32[]{:S(2)}) collective-permute-start(f32[128,256]{1,0:T(8,128)S(1)} %get-tuple-element.66.refs_6_), channel_id=1, source_target_pairs={{0,1},{1,0},{2,3},{3,2},{4,5},{5,4},{6,7},{7,6},{8,9},{9,8},{10,11... | collective-permute-start | bytes 393224 | tf_op jit(solution)/shard_map/ppermute | solution.py:528
  86.6 3.7 %collective-permute-start.10 = (f32[128,256]{1,0:T(8,128)S(1)}, f32[128,256]{1,0:T(8,128)S(1)}, u32[]{:S(2)}, u32[]{:S(2)}) collective-permute-start(f32[128,256]{1,0:T(8,128)S(1)} %collective-permute-done.9.refs_8_), channel_id=1, source_target_pairs={{0,1},{1,0},{2,3},{3,2},{4,5},{5,4},{6,7},{7,6},{8,9},{9,8},{10,11... | collective-permute-start | bytes 393224 | tf_op jit(solution)/shard_map/ppermute | solution.py:528
  89.6 0.7 copy-start.3
  94.3 9.6 %collective-permute-start.13 = (f32[8,256]{1,0:T(8,128)S(1)}, f32[8,256]{1,0:T(8,128)S(1)}, u32[]{:S(2)}, u32[]{:S(2)}) collective-permute-start(f32[8,256]{1,0:T(8,128)S(1)} %get-tuple-element.74.refs_0_), channel_id=1, source_target_pairs={{0,12},{4,0},{8,4},{12,8},{1,13},{5,1},{9,5},{13,9},{2,14},{6,2},{... | collective-permute-start | bytes 24584 | tf_op jit(solution)/shard_map/ppermute | solution.py:540
  96.6 7.3 %collective-permute-start.12 = (f32[8,256]{1,0:T(8,128)S(1)}, f32[8,256]{1,0:T(8,128)S(1)}, u32[]{:S(2)}, u32[]{:S(2)}) collective-permute-start(f32[8,256]{1,0:T(8,128)S(1)} %get-tuple-element.74.refs_0_), channel_id=1, source_target_pairs={{0,8},{4,12},{8,0},{12,4},{1,9},{5,13},{9,1},{13,5},{2,10},{6,14},... | collective-permute-start | bytes 24584 | tf_op jit(solution)/shard_map/ppermute | solution.py:540
  99.0 5.0 %collective-permute-start.11 = (f32[8,256]{1,0:T(8,128)S(1)}, f32[8,256]{1,0:T(8,128)S(1)}, u32[]{:S(2)}, u32[]{:S(2)}) collective-permute-start(f32[8,256]{1,0:T(8,128)S(1)} %get-tuple-element.74.refs_0_), channel_id=1, source_target_pairs={{0,4},{4,8},{8,12},{12,0},{1,5},{5,9},{9,13},{13,1},{2,6},{6,10},{... | collective-permute-start | bytes 24584 | tf_op jit(solution)/shard_map/ppermute | solution.py:540
  104.0 7.3 %copy-start = (f32[512,256]{1,0:T(8,128)S(1)}, f32[512,256]{1,0:T(8,128)}, u32[]{:S(2)}) copy-start(f32[512,256]{1,0:T(8,128)} %get-tuple-element.78.refs_5_) | copy-start | bytes 1572868
  104.0 7.3 %copy-start.2 = (f32[128,256]{1,0:T(8,128)S(1)}, f32[128,256]{1,0:T(8,128)}, u32[]{:S(2)}) copy-start(f32[128,256]{1,0:T(8,128)} %copy-done.1) | copy-start | bytes 393220
  104.0 7.3 %copy-start.4 = (f32[128,256]{1,0:T(8,128)S(1)}, f32[128,256]{1,0:T(8,128)}, u32[]{:S(2)}) copy-start(f32[128,256]{1,0:T(8,128)} %copy-done.3) | copy-start | bytes 393220
  104.0 7.3 %copy-start.6 = (f32[128,256]{1,0:T(8,128)S(1)}, f32[128,256]{1,0:T(8,128)}, u32[]{:S(2)}) copy-start(f32[128,256]{1,0:T(8,128)} %copy-done.5) | copy-start | bytes 393220
  104.0 6.4 %collective-permute-start.16 = (f32[8,256]{1,0:T(8,128)S(1)}, f32[8,256]{1,0:T(8,128)S(1)}, u32[]{:S(2)}, u32[]{:S(2)}) collective-permute-start(f32[8,256]{1,0:T(8,128)S(1)} %shard_map.87.refs_0_), channel_id=1, source_target_pairs={{0,3},{1,2},{2,1},{3,0},{4,7},{5,6},{6,5},{7,4},{8,11},{9,10},{10,... | collective-permute-start | bytes 24584 | tf_op jit(solution)/shard_map/ppermute | solution.py:523
  108.8 2.5 %collective-permute-start.15 = (f32[8,256]{1,0:T(8,128)S(1)}, f32[8,256]{1,0:T(8,128)S(1)}, u32[]{:S(2)}, u32[]{:S(2)}) collective-permute-start(f32[8,256]{1,0:T(8,128)S(1)} %shard_map.87.refs_0_), channel_id=1, source_target_pairs={{0,2},{1,3},{2,0},{3,1},{4,6},{5,7},{6,4},{7,5},{8,10},{9,11},{10,... | collective-permute-start | bytes 24584 | tf_op jit(solution)/shard_map/ppermute | solution.py:523
  109.1 2.1 %collective-permute-start.14 = (f32[8,256]{1,0:T(8,128)S(1)}, f32[8,256]{1,0:T(8,128)S(1)}, u32[]{:S(2)}, u32[]{:S(2)}) collective-permute-start(f32[8,256]{1,0:T(8,128)S(1)} %shard_map.87.refs_0_), channel_id=1, source_target_pairs={{0,1},{1,0},{2,3},{3,2},{4,5},{5,4},{6,7},{7,6},{8,9},{9,8},{10,11... | collective-permute-start | bytes 24584 | tf_op jit(solution)/shard_map/ppermute | solution.py:523
  114.0 3.8 %collective-permute-start.17 = (f32[320,256]{1,0:T(8,128)}, f32[320,256]{1,0:T(8,128)S(1)}, u32[]{:S(2)}, u32[]{:S(2)}) collective-permute-start(f32[320,256]{1,0:T(8,128)} %get-tuple-element.81), channel_id=1, source_target_pairs={{0,1},{1,0},{2,3},{3,2},{4,5},{5,4},{6,7},{7,6},{8,9},{9,8},{10,11... | collective-permute-start | bytes 983048 | tf_op jit(solution)/shard_map/ppermute | solution.py:528
  114.3 13.7 %all-to-all-start.3 = ((f32[16,32,256]{2,1,0:T(8,128)}), f32[16,32,256]{2,1,0:T(8,128)S(1)}, u32[]{:S(2)}, u32[]{:S(2)}) async-start(f32[16,32,256]{2,1,0:T(8,128)} %get-tuple-element.79), calls=%async_computation.3 | async-start | bytes 1048576 | tf_op jit(solution)/shard_map/all_to_all | solution.py:545
  117.9 5.6 %collective-permute-start.18 = (f32[160,256]{1,0:T(8,128)S(1)}, f32[160,256]{1,0:T(8,128)S(1)}, u32[]{:S(2)}, u32[]{:S(2)}) collective-permute-start(f32[160,256]{1,0:T(8,128)S(1)} %get-tuple-element.86), channel_id=1, source_target_pairs={{0,2},{2,0},{1,3},{3,1},{4,6},{6,4},{5,7},{7,5},{8,10},{10,8},{9,1... | collective-permute-start | bytes 491528 | tf_op jit(solution)/shard_map/ppermute | solution.py:528
  128.0 5.7 %collective-permute-start.21 = (f32[40,256]{1,0:T(8,128)S(1)}, f32[40,256]{1,0:T(8,128)S(1)}, u32[]{:S(2)}, u32[]{:S(2)}) collective-permute-start(f32[40,256]{1,0:T(8,128)S(1)} %shard_map.91.refs_0_), channel_id=1, source_target_pairs={{0,12},{4,0},{8,4},{12,8},{1,13},{5,1},{9,5},{13,9},{2,14},{6,2},{... | collective-permute-start | bytes 122888 | tf_op jit(solution)/shard_map/ppermute | solution.py:540
  129.3 6.8 %collective-permute-start.20 = (f32[40,256]{1,0:T(8,128)S(1)}, f32[40,256]{1,0:T(8,128)S(1)}, u32[]{:S(2)}, u32[]{:S(2)}) collective-permute-start(f32[40,256]{1,0:T(8,128)S(1)} %shard_map.91.refs_0_), channel_id=1, source_target_pairs={{0,8},{4,12},{8,0},{12,4},{1,9},{5,13},{9,1},{13,5},{2,10},{6,14},... | collective-permute-start | bytes 122888 | tf_op jit(solution)/shard_map/ppermute | solution.py:540
  132.6 5.9 %collective-permute-start.19 = (f32[40,256]{1,0:T(8,128)S(1)}, f32[40,256]{1,0:T(8,128)S(1)}, u32[]{:S(2)}, u32[]{:S(2)}) collective-permute-start(f32[40,256]{1,0:T(8,128)S(1)} %shard_map.91.refs_0_), channel_id=1, source_target_pairs={{0,4},{4,8},{8,12},{12,0},{1,5},{5,9},{9,13},{13,1},{2,6},{6,10},{... | collective-permute-start | bytes 122888 | tf_op jit(solution)/shard_map/ppermute | solution.py:540
  (2 other events, 1.3 us)

commit v14 on v13

--- a/solution.py
+++ b/solution.py
@@ -615,7 +615,7 @@
     pieces = adjoint(plane)
     shares = after(from_axis([shares] * nh, "h"), *pieces)
     (shares,) = call(add_kernel, [(8, NY)], *shares)
-    shares = from_comps([shares] * 4)
+    shares = gather_comps(shares)
     message, dens, base, alpha = call(
         second_kernel, [(nxy, rows, NY), (QX, NY), (QX, NY), (8, 128)],
         *shares, dens, full, *grads, *factors, *tables, scratch=[(NX, NY)],

time: 156 us -> 157 us (level)
  starting transfers between devices: 56.2 us -> 58.2 us
  waiting for transfers between devices: 37 us -> 35 us
    ppermute x10 -> x13, starting transfers between devices: 18.6 us -> 26.1 us  [flip(): return lax.ppermute(value, axis, [(0, 1), (1, 0)])]
    ppermute x3 -> x0, starting transfers between devices: 5.24 us -> none  [from_comps(): lax.ppermute(values[step], COMP, [(i, i ^ step) for i in range(4)])]
    ppermute x3 -> x0, waiting for transfers between devices: 2.01 us -> none  [from_comps(): lax.ppermute(values[step], COMP, [(i, i ^ step) for i in range(4)])]
    ppermute x10 -> x13, waiting for transfers between devices: 12.6 us -> 13.5 us  [flip(): return lax.ppermute(value, axis, [(0, 1), (1, 0)])]
  transfers between devices with their start and end apart: 25 -> 25, of which waited for: 14 -> 13; matrix products, arithmetic and copies ran while one was open for 0% -> 0% of each run, Pallas kernels for 5% -> 5%
where the time goes in v14:
time: 157 us; the launch traced here: 156 us
  starting transfers between devices  58.2 us (37%)
  blocking collectives  39.7 us (25%)
  waiting for transfers between devices  35 us (22%)
  Pallas kernels  19.9 us (13%)
  local copies, waits for them, and re-layouts  1.98 us (1%)
    all_to_all x2, blocking collectives, exchange(): return lax.all_to_all(value, axes, 0, 0, tiled=True)  39.7 us
    ppermute x13, starting transfers between devices, flip(): return lax.ppermute(value, axis, [(0, 1), (1, 0)])  26.1 us
    ppermute x9, starting transfers between devices, from_axis(): lax.ppermute(values[step], axis, [(i, (i + step) % size) for i in range(s...  21 us
    pallas_call x17, Pallas kernels, call(): pl.pallas_call(inner, out_shape=[(pltpu.HBM if place in far_out else jax....  19.9 us
    ppermute x13, waiting for transfers between devices, flip(): return lax.ppermute(value, axis, [(0, 1), (1, 0)])  13.5 us
    all_to_all x3, waiting for transfers between devices, exchange(): return lax.all_to_all(value, axes, 0, 0, tiled=True)  12.9 us
    all_to_all x3, starting transfers between devices, exchange(): return lax.all_to_all(value, axes, 0, 0, tiled=True)  11.1 us
    ppermute x9, waiting for transfers between devices, from_axis(): lax.ppermute(values[step], axis, [(i, (i + step) % size) for i in range(s...  8.56 us
  transfers between devices with their start and end apart: 25, of which 13 were waited for; matrix products, arithmetic and copies ran while one was open for 0% of the time, Pallas kernels for 5%

profile of v14, /device:TPU:1, one launch (start us, length us, event | category | flops | bytes accessed | tf_op | source)
XLA Modules:
  0.0 156.2 jit_solution(4881935648109747602)
XLA Ops:
  0.6 2.5 %collective-permute-start.1 = (f32[128,256]{1,0:T(8,128)}, f32[128,256]{1,0:T(8,128)S(1)}, u32[]{:S(2)}, u32[]{:S(2)}) collective-permute-start(f32[128,256]{1,0:T(8,128)} %bitcast.14), channel_id=1, source_target_pairs={{0,2},{2,0},{1,3},{3,1},{4,6},{6,4},{5,7},{7,5},{8,10},{10,8},{9,1... | collective-permute-start | bytes 393224 | tf_op jit(solution)/shard_map/ppermute | solution.py:528
  4.8 1.4 shard_map.77
  6.2 2.9 %collective-permute-start.2 = (f32[128,256]{1,0:T(8,128)S(1)}, f32[128,256]{1,0:T(8,128)S(1)}, u32[]{:S(2)}, u32[]{:S(2)}) collective-permute-start(f32[128,256]{1,0:T(8,128)S(1)} %collective-permute-done.1.refs_2_), channel_id=1, source_target_pairs={{0,1},{1,0},{2,3},{3,2},{4,5},{5,4},{6,7},{7,6},{8,9},{9,8},{10,11... | collective-permute-start | bytes 393224 | tf_op jit(solution)/shard_map/ppermute | solution.py:528
  10.1 3.1 %shard_map.78 = (f32[16,72,256]{2,1,0:T(8,128)S(1)}, f32[512,256]{1,0:T(8,128)}) custom-call(f32[128,256]{1,0:T(8,128)S(1)} %get-tuple-element.47.refs_0_.refs_9_.refs_10_.refs_7_.refs_8_.refs_3_.refs_4_, f32[128,256]{1,0:T(8,128)S(1)} %collective-permute-done.refs_1_, f32[128,256]{1,0:T(8,128)S(1)} %collective-permute-done.1.refs_2_, ...), custom_call_target="tpu_custom_call" | custom-call | tf_op jit(solution)/shard_map/pallas_call | solution.py:503
  13.2 22.9 %all_to_all.31.refs_0_ = f32[16,72,256]{2,1,0:T(8,128)S(1)} all-to-all(f32[16,72,256]{2,1,0:T(8,128)S(1)} %get-tuple-element.55), channel_id=1, replica_groups=mesh['x'=4,'y'=4,'h'=4,'l'=2,'k'=2] {'x','y'}, dimensions={0} | all-to-all | bytes 2359296 | tf_op jit(solution)/shard_map/all_to_all | solution.py:545
  36.2 5.9 %collective-permute-start.5 = (f32[80,256]{1,0:T(8,128)S(1)}, f32[80,256]{1,0:T(8,128)S(1)}, u32[]{:S(2)}, u32[]{:S(2)}) collective-permute-start(f32[80,256]{1,0:T(8,128)S(1)} %shard_map.79.refs_0_), channel_id=1, source_target_pairs={{0,12},{4,0},{8,4},{12,8},{1,13},{5,1},{9,5},{13,9},{2,14},{6,2},{... | collective-permute-start | bytes 245768 | tf_op jit(solution)/shard_map/ppermute | solution.py:540
  43.1 2.3 %collective-permute-start.3 = (f32[80,256]{1,0:T(8,128)S(1)}, f32[80,256]{1,0:T(8,128)S(1)}, u32[]{:S(2)}, u32[]{:S(2)}) collective-permute-start(f32[80,256]{1,0:T(8,128)S(1)} %shard_map.79.refs_0_), channel_id=1, source_target_pairs={{0,4},{4,8},{8,12},{12,0},{1,5},{5,9},{9,13},{13,1},{2,6},{6,10},{... | collective-permute-start | bytes 245768 | tf_op jit(solution)/shard_map/ppermute | solution.py:540
  45.4 4.1 %collective-permute-done.4.refs_2_ = f32[80,256]{1,0:T(8,128)S(1)} collective-permute-done((f32[80,256]{1,0:T(8,128)S(1)}, f32[80,256]{1,0:T(8,128)S(1)}, u32[]{:S(2)}, u32[]{:S(2)}) %collective-permute-start.4) | collective-permute-done | bytes 81952 | tf_op jit(solution)/shard_map/ppermute | solution.py:540
  50.9 3.9 %all-to-all-start.1 = ((f32[16,32,256]{2,1,0:T(8,128)}), f32[16,32,256]{2,1,0:T(8,128)S(1)}, u32[]{:S(2)}, u32[]{:S(2)}) async-start(f32[16,32,256]{2,1,0:T(8,128)} %get-tuple-element.56), calls=%async_computation.1 | async-start | bytes 1048576 | tf_op jit(solution)/shard_map/all_to_all | solution.py:545
  54.8 3.6 %shard_map.81.refs_4_.refs_12_.refs_10_.refs_13_.refs_18_ = f32[264,256]{1,0:T(8,128)S(1)} custom-call(f32[32,256]{1,0:T(8,128)S(1)} %get-tuple-element.57.refs_0_, bf16[4,256,256]{2,1,0:T(8,128)(2,1)S(1)} %get-tuple-element.52.refs_8_.refs_3_.refs_4_.refs_1_.refs_5_.refs_2_.refs_13_, ...), custom_call_target="tpu_custom_call" | custom-call | tf_op jit(solution)/shard_map/pallas_call | solution.py:503
  58.4 5.4 %all-to-all-done.1 = f32[16,32,256]{2,1,0:T(8,128)S(1)} async-done(((f32[16,32,256]{2,1,0:T(8,128)}), f32[16,32,256]{2,1,0:T(8,128)S(1)}, u32[]{:S(2)}, u32[]{:S(2)}) %all-to-all-start.1) | async-done | bytes 524320 | tf_op jit(solution)/shard_map/all_to_all | solution.py:545
  63.7 2.4 %shard_map.82 = (f32[320,256]{1,0:T(8,128)S(1)}, f32[320,256]{1,0:T(8,128)S(1)}) custom-call(f32[512,256]{1,0:T(8,128)S(1)} %bitcast.8, f32[264,256]{1,0:T(8,128)S(1)} %get-tuple-element.49.refs_5_.refs_6_.refs_7_.refs_4_.refs_1_.refs_8_.refs_10_, f32[264,256]{1,0:T(8,128)S(1)} %get-tuple-element.50.refs_6_.refs_7_.refs_8_.refs_5_.refs_2_.refs_9_.refs_11_, ...), custom_call_target="tpu_custom_call" | custom-call | tf_op jit(solution)/shard_map/pallas_call | solution.py:503
  66.2 4.9 %collective-permute-start.6 = (f32[320,256]{1,0:T(8,128)S(1)}, f32[320,256]{1,0:T(8,128)S(1)}, u32[]{:S(2)}, u32[]{:S(2)}) collective-permute-start(f32[320,256]{1,0:T(8,128)S(1)} %get-tuple-element.62), channel_id=1, source_target_pairs={{0,1},{1,0},{2,3},{3,2},{4,5},{5,4},{6,7},{7,6},{8,9},{9,8},{10,11... | collective-permute-start | bytes 983048 | tf_op jit(solution)/shard_map/ppermute | solution.py:528
  73.4 4.5 %collective-permute-done.7.refs_1_ = f32[160,256]{1,0:T(8,128)S(1)} collective-permute-done((f32[160,256]{1,0:T(8,128)S(1)}, f32[160,256]{1,0:T(8,128)S(1)}, u32[]{:S(2)}, u32[]{:S(2)}) %collective-permute-start.7) | collective-permute-done | bytes 163872 | tf_op jit(solution)/shard_map/ppermute | solution.py:528
  79.1 3.6 %all-to-all-start.2 = ((f32[16,40,256]{2,1,0:T(8,128)}), f32[16,40,256]{2,1,0:T(8,128)S(1)}, u32[]{:S(2)}, u32[]{:S(2)}) async-start(f32[16,40,256]{2,1,0:T(8,128)} %get-tuple-element.65), calls=%async_computation.2 | async-start | bytes 1310720 | tf_op jit(solution)/shard_map/all_to_all | solution.py:545
  83.7 1.5 collective-permute-start.8
  85.2 1.4 collective-permute-done.9.refs_8_
  86.6 2.4 %collective-permute-start.10 = (f32[128,256]{1,0:T(8,128)S(1)}, f32[128,256]{1,0:T(8,128)S(1)}, u32[]{:S(2)}, u32[]{:S(2)}) collective-permute-start(f32[128,256]{1,0:T(8,128)S(1)} %collective-permute-done.9.refs_8_), channel_id=1, source_target_pairs={{0,1},{1,0},{2,3},{3,2},{4,5},{5,4},{6,7},{7,6},{8,9},{9,8},{10,11... | collective-permute-start | bytes 393224 | tf_op jit(solution)/shard_map/ppermute | solution.py:528
  90.9 3.3 %all-to-all-done.2.refs_0_ = f32[16,40,256]{2,1,0:T(8,128)S(1)} async-done(((f32[16,40,256]{2,1,0:T(8,128)}), f32[16,40,256]{2,1,0:T(8,128)S(1)}, u32[]{:S(2)}, u32[]{:S(2)}) %all-to-all-start.2) | async-done | bytes 655392 | tf_op jit(solution)/shard_map/all_to_all | solution.py:545
  94.3 2.3 %collective-permute-start.13 = (f32[8,256]{1,0:T(8,128)S(1)}, f32[8,256]{1,0:T(8,128)S(1)}, u32[]{:S(2)}, u32[]{:S(2)}) collective-permute-start(f32[8,256]{1,0:T(8,128)S(1)} %get-tuple-element.74.refs_0_), channel_id=1, source_target_pairs={{0,12},{4,0},{8,4},{12,8},{1,13},{5,1},{9,5},{13,9},{2,14},{6,2},{... | collective-permute-start | bytes 24584 | tf_op jit(solution)/shard_map/ppermute | solution.py:540
  96.6 2.3 %collective-permute-start.12 = (f32[8,256]{1,0:T(8,128)S(1)}, f32[8,256]{1,0:T(8,128)S(1)}, u32[]{:S(2)}, u32[]{:S(2)}) collective-permute-start(f32[8,256]{1,0:T(8,128)S(1)} %get-tuple-element.74.refs_0_), channel_id=1, source_target_pairs={{0,8},{4,12},{8,0},{12,4},{1,9},{5,13},{9,1},{13,5},{2,10},{6,14},... | collective-permute-start | bytes 24584 | tf_op jit(solution)/shard_map/ppermute | solution.py:540
  99.0 1.8 %collective-permute-start.11 = (f32[8,256]{1,0:T(8,128)S(1)}, f32[8,256]{1,0:T(8,128)S(1)}, u32[]{:S(2)}, u32[]{:S(2)}) collective-permute-start(f32[8,256]{1,0:T(8,128)S(1)} %get-tuple-element.74.refs_0_), channel_id=1, source_target_pairs={{0,4},{4,8},{8,12},{12,0},{1,5},{5,9},{9,13},{13,1},{2,6},{6,10},{... | collective-permute-start | bytes 24584 | tf_op jit(solution)/shard_map/ppermute | solution.py:540
  100.8 3.2 %shard_map.86 = (f32[320,256]{1,0:T(8,128)S(1)}, f32[320,256]{1,0:T(8,128)}) custom-call(f32[512,256]{1,0:T(8,128)S(1)} %get-tuple-element.71.refs_0_, f32[264,256]{1,0:T(8,128)S(1)} %get-tuple-element.49.refs_5_.refs_6_.refs_7_.refs_4_.refs_1_.refs_8_.refs_10_, f32[264,256]{1,0:T(8,128)S(1)} %get-tuple-element.50.refs_6_.refs_7_.refs_8_.refs_5_.refs_2_.refs_9_.refs_11_, ...), custom_call_target="tpu_custom_call" | custom-call | tf_op jit(solution)/shard_map/pallas_call | solution.py:503
  105.3 3.9 %collective-permute-start.14 = (f32[8,256]{1,0:T(8,128)S(1)}, f32[8,256]{1,0:T(8,128)S(1)}, u32[]{:S(2)}, u32[]{:S(2)}) collective-permute-start(f32[8,256]{1,0:T(8,128)S(1)} %shard_map.87.refs_0_), channel_id=1, source_target_pairs={{0,1},{1,0},{2,3},{3,2},{4,5},{5,4},{6,7},{7,6},{8,9},{9,8},{10,11... | collective-permute-start | bytes 24584 | tf_op jit(solution)/shard_map/ppermute | solution.py:528
  109.2 2.3 %collective-permute-start.16 = (f32[8,256]{1,0:T(8,128)S(1)}, f32[8,256]{1,0:T(8,128)S(1)}, u32[]{:S(2)}, u32[]{:S(2)}) collective-permute-start(f32[8,256]{1,0:T(8,128)S(1)} %collective-permute-done.15.refs_2_), channel_id=1, source_target_pairs={{0,1},{1,0},{2,3},{3,2},{4,5},{5,4},{6,7},{7,6},{8,9},{9,8},{10,11... | collective-permute-start | bytes 24584 | tf_op jit(solution)/shard_map/ppermute | solution.py:528
  112.3 2.7 %shard_map.88 = (f32[16,32,256]{2,1,0:T(8,128)}, f32[128,256]{1,0:T(8,128)S(1)}, f32[128,256]{1,0:T(8,128)S(1)}, f32[8,128]{1,0:T(8,128)S(1)}) custom-call(f32[8,256]{1,0:T(8,128)S(1)} %shard_map.87.refs_0_, f32[8,256]{1,0:T(8,128)S(1)} %collective-permute-done.14.refs_1_, f32[8,256]{1,0:T(8,128)S(1)} %collective-permute-done.15.refs_2_, ...), custom_call_target="tpu_custom_call" | custom-call | tf_op jit(solution)/shard_map/pallas_call | solution.py:503
  115.4 3.6 %all-to-all-start.3 = ((f32[16,32,256]{2,1,0:T(8,128)}), f32[16,32,256]{2,1,0:T(8,128)S(1)}, u32[]{:S(2)}, u32[]{:S(2)}) async-start(f32[16,32,256]{2,1,0:T(8,128)} %get-tuple-element.79), calls=%async_computation.3 | async-start | bytes 1048576 | tf_op jit(solution)/shard_map/all_to_all | solution.py:545
  120.2 4.5 %collective-permute-done.18.refs_1_ = f32[160,256]{1,0:T(8,128)S(1)} collective-permute-done((f32[160,256]{1,0:T(8,128)S(1)}, f32[160,256]{1,0:T(8,128)S(1)}, u32[]{:S(2)}, u32[]{:S(2)}) %collective-permute-start.18) | collective-permute-done | bytes 163872 | tf_op jit(solution)/shard_map/ppermute | solution.py:528
  124.9 4.2 %all-to-all-done.3.refs_0_ = f32[16,32,256]{2,1,0:T(8,128)S(1)} async-done(((f32[16,32,256]{2,1,0:T(8,128)}), f32[16,32,256]{2,1,0:T(8,128)S(1)}, u32[]{:S(2)}, u32[]{:S(2)}) %all-to-all-start.3) | async-done | bytes 524320 | tf_op jit(solution)/shard_map/all_to_all | solution.py:545
  130.4 3.0 %collective-permute-start.20 = (f32[40,256]{1,0:T(8,128)S(1)}, f32[40,256]{1,0:T(8,128)S(1)}, u32[]{:S(2)}, u32[]{:S(2)}) collective-permute-start(f32[40,256]{1,0:T(8,128)S(1)} %shard_map.91.refs_0_), channel_id=1, source_target_pairs={{0,8},{4,12},{8,0},{12,4},{1,9},{5,13},{9,1},{13,5},{2,10},{6,14},... | collective-permute-start | bytes 122888 | tf_op jit(solution)/shard_map/ppermute | solution.py:540
  134.5 2.7 %collective-permute-done.20.refs_2_ = f32[40,256]{1,0:T(8,128)S(1)} collective-permute-done((f32[40,256]{1,0:T(8,128)S(1)}, f32[40,256]{1,0:T(8,128)S(1)}, u32[]{:S(2)}, u32[]{:S(2)}) %collective-permute-start.20) | collective-permute-done | bytes 40992 | tf_op jit(solution)/shard_map/ppermute | solution.py:540
  138.6 16.8 %all_to_all.32 = f32[64,1,128]{2,1,0:T(1,128)S(1)} all-to-all(f32[64,1,128]{2,1,0:T(1,128)S(1)} %bitcast.12), channel_id=1, replica_groups=mesh['x'=4,'y'=4,'h'=4,'l'=2,'k'=2] {'x','y','l','k'}, dimensions={0} | all-to-all | bytes 65536 | tf_op jit(solution)/shard_map/all_to_all | solution.py:545
  (55 shorter events, 19.4 us)
Async XLA Ops:
  0.6 5.5 %collective-permute-start.1 = (f32[128,256]{1,0:T(8,128)}, f32[128,256]{1,0:T(8,128)S(1)}, u32[]{:S(2)}, u32[]{:S(2)}) collective-permute-start(f32[128,256]{1,0:T(8,128)} %bitcast.14), channel_id=1, source_target_pairs={{0,2},{2,0},{1,3},{3,1},{4,6},{6,4},{5,7},{7,5},{8,10},{10,8},{9,1... | collective-permute-start | bytes 393224 | tf_op jit(solution)/shard_map/ppermute | solution.py:528
  3.2 5.9 %collective-permute-start = (f32[128,256]{1,0:T(8,128)}, f32[128,256]{1,0:T(8,128)S(1)}, u32[]{:S(2)}, u32[]{:S(2)}) collective-permute-start(f32[128,256]{1,0:T(8,128)} %bitcast.15), channel_id=1, source_target_pairs={{0,1},{1,0},{2,3},{3,2},{4,5},{5,4},{6,7},{7,6},{8,9},{9,8},{10,11... | collective-permute-start | bytes 393224 | tf_op jit(solution)/shard_map/ppermute | solution.py:528
  6.2 3.9 %collective-permute-start.2 = (f32[128,256]{1,0:T(8,128)S(1)}, f32[128,256]{1,0:T(8,128)S(1)}, u32[]{:S(2)}, u32[]{:S(2)}) collective-permute-start(f32[128,256]{1,0:T(8,128)S(1)} %collective-permute-done.1.refs_2_), channel_id=1, source_target_pairs={{0,1},{1,0},{2,3},{3,2},{4,5},{5,4},{6,7},{7,6},{8,9},{9,8},{10,11... | collective-permute-start | bytes 393224 | tf_op jit(solution)/shard_map/ppermute | solution.py:528
  13.2 22.9 %copy-start.7 = (f32[1,8,256]{2,1,0:T(8,128)S(1)}, f32[1,8,256]{2,1,0:T(8,128)}, u32[]{:S(2)}) copy-start(f32[1,8,256]{2,1,0:T(8,128)} %param.8) | copy-start | bytes 24580
  13.2 22.9 %copy-start.8 = (f32[1,8,256]{2,1,0:T(8,128)S(1)}, f32[1,8,256]{2,1,0:T(8,128)}, u32[]{:S(2)}) copy-start(f32[1,8,256]{2,1,0:T(8,128)} %param.7) | copy-start | bytes 24580
  36.2 9.2 %collective-permute-start.5 = (f32[80,256]{1,0:T(8,128)S(1)}, f32[80,256]{1,0:T(8,128)S(1)}, u32[]{:S(2)}, u32[]{:S(2)}) collective-permute-start(f32[80,256]{1,0:T(8,128)S(1)} %shard_map.79.refs_0_), channel_id=1, source_target_pairs={{0,12},{4,0},{8,4},{12,8},{1,13},{5,1},{9,5},{13,9},{2,14},{6,2},{... | collective-permute-start | bytes 245768 | tf_op jit(solution)/shard_map/ppermute | solution.py:540
  42.1 7.4 %collective-permute-start.4 = (f32[80,256]{1,0:T(8,128)S(1)}, f32[80,256]{1,0:T(8,128)S(1)}, u32[]{:S(2)}, u32[]{:S(2)}) collective-permute-start(f32[80,256]{1,0:T(8,128)S(1)} %shard_map.79.refs_0_), channel_id=1, source_target_pairs={{0,8},{4,12},{8,0},{12,4},{1,9},{5,13},{9,1},{13,5},{2,10},{6,14},... | collective-permute-start | bytes 245768 | tf_op jit(solution)/shard_map/ppermute | solution.py:540
  43.1 6.8 %collective-permute-start.3 = (f32[80,256]{1,0:T(8,128)S(1)}, f32[80,256]{1,0:T(8,128)S(1)}, u32[]{:S(2)}, u32[]{:S(2)}) collective-permute-start(f32[80,256]{1,0:T(8,128)S(1)} %shard_map.79.refs_0_), channel_id=1, source_target_pairs={{0,4},{4,8},{8,12},{12,0},{1,5},{5,9},{9,13},{13,1},{2,6},{6,10},{... | collective-permute-start | bytes 245768 | tf_op jit(solution)/shard_map/ppermute | solution.py:540
  50.9 12.8 %all-to-all-start.1 = ((f32[16,32,256]{2,1,0:T(8,128)}), f32[16,32,256]{2,1,0:T(8,128)S(1)}, u32[]{:S(2)}, u32[]{:S(2)}) async-start(f32[16,32,256]{2,1,0:T(8,128)} %get-tuple-element.56), calls=%async_computation.1 | async-start | bytes 1048576 | tf_op jit(solution)/shard_map/all_to_all | solution.py:545
  66.2 6.2 %collective-permute-start.6 = (f32[320,256]{1,0:T(8,128)S(1)}, f32[320,256]{1,0:T(8,128)S(1)}, u32[]{:S(2)}, u32[]{:S(2)}) collective-permute-start(f32[320,256]{1,0:T(8,128)S(1)} %get-tuple-element.62), channel_id=1, source_target_pairs={{0,1},{1,0},{2,3},{3,2},{4,5},{5,4},{6,7},{7,6},{8,9},{9,8},{10,11... | collective-permute-start | bytes 983048 | tf_op jit(solution)/shard_map/ppermute | solution.py:528
  72.4 5.5 %collective-permute-start.7 = (f32[160,256]{1,0:T(8,128)S(1)}, f32[160,256]{1,0:T(8,128)S(1)}, u32[]{:S(2)}, u32[]{:S(2)}) collective-permute-start(f32[160,256]{1,0:T(8,128)S(1)} %get-tuple-element.64), channel_id=1, source_target_pairs={{0,2},{2,0},{1,3},{3,1},{4,6},{6,4},{5,7},{7,5},{8,10},{10,8},{9,1... | collective-permute-start | bytes 491528 | tf_op jit(solution)/shard_map/ppermute | solution.py:528
  79.1 15.2 %all-to-all-start.2 = ((f32[16,40,256]{2,1,0:T(8,128)}), f32[16,40,256]{2,1,0:T(8,128)S(1)}, u32[]{:S(2)}, u32[]{:S(2)}) async-start(f32[16,40,256]{2,1,0:T(8,128)} %get-tuple-element.65), calls=%async_computation.2 | async-start | bytes 1310720 | tf_op jit(solution)/shard_map/all_to_all | solution.py:545
  82.7 3.9 %collective-permute-start.9 = (f32[128,256]{1,0:T(8,128)S(1)}, f32[128,256]{1,0:T(8,128)S(1)}, u32[]{:S(2)}, u32[]{:S(2)}) collective-permute-start(f32[128,256]{1,0:T(8,128)S(1)} %get-tuple-element.66.refs_6_), channel_id=1, source_target_pairs={{0,2},{2,0},{1,3},{3,1},{4,6},{6,4},{5,7},{7,5},{8,10},{10,8},{9,1... | collective-permute-start | bytes 393224 | tf_op jit(solution)/shard_map/ppermute | solution.py:528
  83.7 6.0 %collective-permute-start.8 = (f32[128,256]{1,0:T(8,128)S(1)}, f32[128,256]{1,0:T(8,128)S(1)}, u32[]{:S(2)}, u32[]{:S(2)}) collective-permute-start(f32[128,256]{1,0:T(8,128)S(1)} %get-tuple-element.66.refs_6_), channel_id=1, source_target_pairs={{0,1},{1,0},{2,3},{3,2},{4,5},{5,4},{6,7},{7,6},{8,9},{9,8},{10,11... | collective-permute-start | bytes 393224 | tf_op jit(solution)/shard_map/ppermute | solution.py:528
  86.6 3.7 %collective-permute-start.10 = (f32[128,256]{1,0:T(8,128)S(1)}, f32[128,256]{1,0:T(8,128)S(1)}, u32[]{:S(2)}, u32[]{:S(2)}) collective-permute-start(f32[128,256]{1,0:T(8,128)S(1)} %collective-permute-done.9.refs_8_), channel_id=1, source_target_pairs={{0,1},{1,0},{2,3},{3,2},{4,5},{5,4},{6,7},{7,6},{8,9},{9,8},{10,11... | collective-permute-start | bytes 393224 | tf_op jit(solution)/shard_map/ppermute | solution.py:528
  89.6 0.7 copy-start.3
  94.3 9.6 %collective-permute-start.13 = (f32[8,256]{1,0:T(8,128)S(1)}, f32[8,256]{1,0:T(8,128)S(1)}, u32[]{:S(2)}, u32[]{:S(2)}) collective-permute-start(f32[8,256]{1,0:T(8,128)S(1)} %get-tuple-element.74.refs_0_), channel_id=1, source_target_pairs={{0,12},{4,0},{8,4},{12,8},{1,13},{5,1},{9,5},{13,9},{2,14},{6,2},{... | collective-permute-start | bytes 24584 | tf_op jit(solution)/shard_map/ppermute | solution.py:540
  96.6 7.3 %collective-permute-start.12 = (f32[8,256]{1,0:T(8,128)S(1)}, f32[8,256]{1,0:T(8,128)S(1)}, u32[]{:S(2)}, u32[]{:S(2)}) collective-permute-start(f32[8,256]{1,0:T(8,128)S(1)} %get-tuple-element.74.refs_0_), channel_id=1, source_target_pairs={{0,8},{4,12},{8,0},{12,4},{1,9},{5,13},{9,1},{13,5},{2,10},{6,14},... | collective-permute-start | bytes 24584 | tf_op jit(solution)/shard_map/ppermute | solution.py:540
  99.0 5.0 %collective-permute-start.11 = (f32[8,256]{1,0:T(8,128)S(1)}, f32[8,256]{1,0:T(8,128)S(1)}, u32[]{:S(2)}, u32[]{:S(2)}) collective-permute-start(f32[8,256]{1,0:T(8,128)S(1)} %get-tuple-element.74.refs_0_), channel_id=1, source_target_pairs={{0,4},{4,8},{8,12},{12,0},{1,5},{5,9},{9,13},{13,1},{2,6},{6,10},{... | collective-permute-start | bytes 24584 | tf_op jit(solution)/shard_map/ppermute | solution.py:540
  104.0 8.3 %copy-start = (f32[512,256]{1,0:T(8,128)S(1)}, f32[512,256]{1,0:T(8,128)}, u32[]{:S(2)}) copy-start(f32[512,256]{1,0:T(8,128)} %get-tuple-element.78.refs_5_) | copy-start | bytes 1572868
  104.0 8.3 %copy-start.2 = (f32[128,256]{1,0:T(8,128)S(1)}, f32[128,256]{1,0:T(8,128)}, u32[]{:S(2)}) copy-start(f32[128,256]{1,0:T(8,128)} %copy-done.1) | copy-start | bytes 393220
  104.0 8.3 %copy-start.4 = (f32[128,256]{1,0:T(8,128)S(1)}, f32[128,256]{1,0:T(8,128)}, u32[]{:S(2)}) copy-start(f32[128,256]{1,0:T(8,128)} %copy-done.3) | copy-start | bytes 393220
  104.0 8.3 %copy-start.6 = (f32[128,256]{1,0:T(8,128)S(1)}, f32[128,256]{1,0:T(8,128)}, u32[]{:S(2)}) copy-start(f32[128,256]{1,0:T(8,128)} %copy-done.5) | copy-start | bytes 393220
  104.0 5.1 %collective-permute-start.15 = (f32[8,256]{1,0:T(8,128)S(1)}, f32[8,256]{1,0:T(8,128)S(1)}, u32[]{:S(2)}, u32[]{:S(2)}) collective-permute-start(f32[8,256]{1,0:T(8,128)S(1)} %shard_map.87.refs_0_), channel_id=1, source_target_pairs={{0,2},{2,0},{1,3},{3,1},{4,6},{6,4},{5,7},{7,5},{8,10},{10,8},{9,1... | collective-permute-start | bytes 24584 | tf_op jit(solution)/shard_map/ppermute | solution.py:528
  105.3 6.2 %collective-permute-start.14 = (f32[8,256]{1,0:T(8,128)S(1)}, f32[8,256]{1,0:T(8,128)S(1)}, u32[]{:S(2)}, u32[]{:S(2)}) collective-permute-start(f32[8,256]{1,0:T(8,128)S(1)} %shard_map.87.refs_0_), channel_id=1, source_target_pairs={{0,1},{1,0},{2,3},{3,2},{4,5},{5,4},{6,7},{7,6},{8,9},{9,8},{10,11... | collective-permute-start | bytes 24584 | tf_op jit(solution)/shard_map/ppermute | solution.py:528
  109.2 3.1 %collective-permute-start.16 = (f32[8,256]{1,0:T(8,128)S(1)}, f32[8,256]{1,0:T(8,128)S(1)}, u32[]{:S(2)}, u32[]{:S(2)}) collective-permute-start(f32[8,256]{1,0:T(8,128)S(1)} %collective-permute-done.15.refs_2_), channel_id=1, source_target_pairs={{0,1},{1,0},{2,3},{3,2},{4,5},{5,4},{6,7},{7,6},{8,9},{9,8},{10,11... | collective-permute-start | bytes 24584 | tf_op jit(solution)/shard_map/ppermute | solution.py:528
  115.0 3.9 %collective-permute-start.17 = (f32[320,256]{1,0:T(8,128)}, f32[320,256]{1,0:T(8,128)S(1)}, u32[]{:S(2)}, u32[]{:S(2)}) collective-permute-start(f32[320,256]{1,0:T(8,128)} %get-tuple-element.81), channel_id=1, source_target_pairs={{0,1},{1,0},{2,3},{3,2},{4,5},{5,4},{6,7},{7,6},{8,9},{9,8},{10,11... | collective-permute-start | bytes 983048 | tf_op jit(solution)/shard_map/ppermute | solution.py:528
  115.4 13.7 %all-to-all-start.3 = ((f32[16,32,256]{2,1,0:T(8,128)}), f32[16,32,256]{2,1,0:T(8,128)S(1)}, u32[]{:S(2)}, u32[]{:S(2)}) async-start(f32[16,32,256]{2,1,0:T(8,128)} %get-tuple-element.79), calls=%async_computation.3 | async-start | bytes 1048576 | tf_op jit(solution)/shard_map/all_to_all | solution.py:545
  119.0 5.7 %collective-permute-start.18 = (f32[160,256]{1,0:T(8,128)S(1)}, f32[160,256]{1,0:T(8,128)S(1)}, u32[]{:S(2)}, u32[]{:S(2)}) collective-permute-start(f32[160,256]{1,0:T(8,128)S(1)} %get-tuple-element.86), channel_id=1, source_target_pairs={{0,2},{2,0},{1,3},{3,1},{4,6},{6,4},{5,7},{7,5},{8,10},{10,8},{9,1... | collective-permute-start | bytes 491528 | tf_op jit(solution)/shard_map/ppermute | solution.py:528
  129.1 5.4 %collective-permute-start.21 = (f32[40,256]{1,0:T(8,128)S(1)}, f32[40,256]{1,0:T(8,128)S(1)}, u32[]{:S(2)}, u32[]{:S(2)}) collective-permute-start(f32[40,256]{1,0:T(8,128)S(1)} %shard_map.91.refs_0_), channel_id=1, source_target_pairs={{0,12},{4,0},{8,4},{12,8},{1,13},{5,1},{9,5},{13,9},{2,14},{6,2},{... | collective-permute-start | bytes 122888 | tf_op jit(solution)/shard_map/ppermute | solution.py:540
  130.4 6.8 %collective-permute-start.20 = (f32[40,256]{1,0:T(8,128)S(1)}, f32[40,256]{1,0:T(8,128)S(1)}, u32[]{:S(2)}, u32[]{:S(2)}) collective-permute-start(f32[40,256]{1,0:T(8,128)S(1)} %shard_map.91.refs_0_), channel_id=1, source_target_pairs={{0,8},{4,12},{8,0},{12,4},{1,9},{5,13},{9,1},{13,5},{2,10},{6,14},... | collective-permute-start | bytes 122888 | tf_op jit(solution)/shard_map/ppermute | solution.py:540
  133.4 5.1 %collective-permute-start.19 = (f32[40,256]{1,0:T(8,128)S(1)}, f32[40,256]{1,0:T(8,128)S(1)}, u32[]{:S(2)}, u32[]{:S(2)}) collective-permute-start(f32[40,256]{1,0:T(8,128)S(1)} %shard_map.91.refs_0_), channel_id=1, source_target_pairs={{0,4},{4,8},{8,12},{12,0},{1,5},{5,9},{9,13},{13,1},{2,6},{6,10},{... | collective-permute-start | bytes 122888 | tf_op jit(solution)/shard_map/ppermute | solution.py:540
  (2 other events, 1.3 us)
